TPU v7x, 32 devices: a whole 2x2x4 slice. The times are simulated.
32 devices in a mesh: seq: 4 (over z), tp: 8 (over y, x, core).
Axes of the slice: x: 2, y: 2, z: 4, core: 2. Of those that a mesh axis runs over, the one named last changes fastest.
Arguments:
- tokens: bfloat16 [1024, 8192], P('tp', 'seq'), may hold values from -6 to 6
- gate_weight: bfloat16 [8192, 14336], P('seq', 'tp'), may hold values from -0.0625 to 0.0625
- up_weight: bfloat16 [8192, 14336], P('seq', 'tp'), may hold values from -0.0625 to 0.0625
- down_pool: bfloat16 [64, 64, 8192], P('tp', None, 'seq'), may hold values from -0.0625 to 0.0625
- up_pool: bfloat16 [64, 2, 64, 14336], P('seq', None, None, 'tp'), may hold values from -0.75 to 0.75
- req_len: int32 [4], replicated, may hold values from 1 to 4, 8 in all
- req_adapter: int32 [4], replicated, may hold values from 0 to 63
- owner_slot: int32 [64], replicated, may hold values from 0 to 63, each once
Outputs:
- hidden: bfloat16 [1024, 14336], P('seq', 'tp')
Inputs may be any that keep to these rules, and one draw needn't show every extreme that they name: `req_len`: lengths of the requests in segments, summing to 8; the longest is exactly 4. `req_adapter`: adapter ids; an adapter may serve several requests. `owner_slot`: each pool slot once.
All inputs are finite; a program needn't handle non-finite values.
Results may differ from a plain program's by a relative error of at most 0.015.
Values may be sent and summed in bfloat16 or wider, within the bound.
No kernel may reach another device: no remote copies, remote signals or barrier semaphores. Data moves between devices by JAX's collectives and lax.ppermute only.
A program may use at most 128 MiB of HBM per device.

v0:
```python
import jax
import jax.numpy as jnp
from jax import lax
from jax.sharding import PartitionSpec as P

SEG_ROWS = 128


low_rank_scale = 0.5


def segment_slots(req_len, req_adapter, owner_slot, segs):
    ends = jnp.cumsum(req_len)
    segment = jnp.arange(segs, dtype=jnp.int32)
    seg_request = jnp.sum((ends[None, :] <= segment[:, None]).astype(jnp.int32), axis=1)
    return jnp.take(owner_slot, jnp.take(req_adapter, seg_request))


def shards(tokens, gate_weight, up_weight, down_pool, up_pool, req_len, req_adapter, owner_slot):
    nseq = lax.axis_size("seq")
    ntp = lax.axis_size("tp")
    segs = tokens.shape[0] // SEG_ROWS * ntp
    seg_slot = segment_slots(req_len, req_adapter, owner_slot, segs)
    per_tp = down_pool.shape[0]
    per_seq = up_pool.shape[0]
    width = tokens.shape[1]
    half_width = gate_weight.shape[1]
    rank_size = down_pool.shape[1]
    own_segs = segs // nseq
    own_rows = own_segs * SEG_ROWS
    held_down = seg_slot // per_tp == lax.axis_index("tp")
    picked_down = jnp.take(down_pool, seg_slot % per_tp, axis=0).astype(jnp.float32)
    table_down = jnp.where(held_down[:, None, None], picked_down, 0.0)
    downs = lax.psum(table_down.astype(jnp.bfloat16), "tp")
    held_up = seg_slot // per_seq == lax.axis_index("seq")
    picked_up = jnp.take(up_pool, seg_slot % per_seq, axis=0).astype(jnp.float32)
    table_up = jnp.where(held_up[:, None, None, None], picked_up, 0.0)
    ups_own = lax.psum_scatter(
        table_up.astype(jnp.bfloat16), "seq", scatter_dimension=0, tiled=True
    )
    gathered = lax.all_gather(tokens, "tp", axis=0, tiled=True)
    inner_part = jnp.einsum(
        "kqd,krd->kqr",
        gathered.reshape(segs, SEG_ROWS, width),
        downs,
        preferred_element_type=jnp.float32,
    )
    inner_part = lax.optimization_barrier(inner_part.astype(jnp.bfloat16)).astype(jnp.float32)
    flat = inner_part.reshape(-1, 128)
    flat_own = own_rows * rank_size // 128
    inner_total = lax.psum(flat.astype(jnp.bfloat16), "seq").astype(jnp.float32)
    inner_own = lax.dynamic_slice_in_dim(inner_total, lax.axis_index("seq") * flat_own, flat_own, 0)
    inner_iteration = inner_own.astype(jnp.bfloat16).reshape(own_segs, SEG_ROWS, rank_size)
    low_rank_delta = jnp.einsum(
        "vcz,vwzd->vcwd", inner_iteration, ups_own, preferred_element_type=jnp.float32
    ).reshape(own_rows, 2, half_width)
    reduced_total = lax.psum_scatter(
        jnp.concatenate(
            [
                jnp.dot(gathered, gate_weight, preferred_element_type=jnp.float32),
                jnp.dot(gathered, up_weight, preferred_element_type=jnp.float32),
            ],
            axis=1,
        ).astype(jnp.bfloat16),
        "seq",
        scatter_dimension=0,
        tiled=True,
    ).astype(jnp.float32)
    gate_preactivation = reduced_total[:, :half_width] + low_rank_scale * low_rank_delta[:, 0]
    up_preactivation = reduced_total[:, half_width:] + low_rank_scale * low_rank_delta[:, 1]
    return (jax.nn.silu(gate_preactivation) * up_preactivation).astype(jnp.bfloat16)


def solution(mesh):
    placed = (
        P("tp", "seq"),
        P("seq", "tp"),
        P("seq", "tp"),
        P("tp", None, "seq"),
        P("seq", None, None, "tp"),
        P(),
        P(),
        P(),
    )
    return jax.shard_map(
        shards, mesh=mesh, in_specs=placed, out_specs=P("seq", "tp"), check_vma=False
    )
```

profile of v0, /device:TPU:0, one launch (start us, length us, event | category | flops | bytes accessed | tf_op | source)
XLA Modules:
  0.0 369.6 jit_solution(8576012177038805279)
XLA Ops:
  6.5 0.0 copy-start
  6.5 0.0 all-reduce.3.cloned.1.call-start
  6.5 1.0 reduce-window.8
  7.5 0.1 convert_reduce_fusion
  7.6 1.3 gather_fusion
  8.9 1.3 gather_fusion.1
  10.3 0.0 copy-done
  10.3 2.0 gather_fusion.2
  12.4 3.6 select_convert_fusion.1
  16.0 0.0 all-reduce.3.cloned.1.call-update
  16.0 0.0 all-gather.2.cloned.1.call-start
  16.1 0.7 all-gather.2.cloned.1.call-update
  16.8 0.0 all-reduce.5.cloned.1.call-start
  16.9 5.8 %gather_fusion.3 = bf16[8,2,64,1792]{3,2,1,0:T(8,128)(2,1)} fusion(bf16[16,2,64,1792]{3,2,1,0:T(8,128)(2,1)} %param.12, s32[1024]{0:T(1024)S(1)} %pad_clamp_fusion), kind=kCustom, calls=%fused_computation.3 | custom fusion | bytes 7340064 | tf_op jit(solution)/shard_map/jit(_take)/gather | solution.py:36
  22.6 57.7 %all-reduce.3.cloned.1.call-done = bf16[8,64,2048]{2,1,0:T(8,128)(2,1)} async-done(((bf16[8,64,2048]{2,1,0:T(8,128)(2,1)}), bf16[8,64,2048]{2,1,0:T(8,128)(2,1)}) %all-reduce.3.cloned.1.call-update) | async-done | bytes 2097168 | tf_op jit(solution)/shard_map/psum | solution.py:34
  80.3 37.8 %all-gather.2.cloned.1.call-done = bf16[1024,2048]{1,0:T(8,128)(2,1)} async-done(((bf16[128,2048]{1,0:T(8,128)(2,1)}), bf16[1024,2048]{1,0:T(8,128)(2,1)}) %all-gather.2.cloned.1.call-update) | async-done | bytes 4194320 | tf_op jit(solution)/shard_map/all_gather | solution.py:41
  118.2 4.4 %fusion.6 = bf16[8,128,64]{1,2,0:T(8,128)(2,1)S(1)} fusion(bf16[8,64,2048]{2,1,0:T(8,128)(2,1)} %all-reduce.3.cloned.1.call-done, bf16[8,128,2048]{2,1,0:T(8,128)(2,1)} %bitcast.61), kind=kOutput, calls=%fused_computation.18 | convolution fusion | flops 268500992 | bytes 6422528 | tf_op jit(solution)/shard_map/kqd,krd->kqr/dot_general | solution.py:42
  122.5 0.2 copy.13
  122.7 0.8 convert_element_type.45
  123.5 0.0 all-reduce.5.cloned.1.call-update
  123.6 0.0 reduce-scatter.5.cloned.1.call-start
  123.6 4.9 %select_convert_fusion = bf16[8,2,64,1792]{3,2,1,0:T(8,128)(2,1)} fusion(bf16[8,2,64,1792]{3,2,1,0:T(8,128)(2,1)} %gather_fusion.3, pred[8]{0:T(512)(128)(4,1)S(1)} %get-tuple-element.10, pred[8]{0:T(512)(128)(4,1)S(1)} %get-tuple-element.11), kind=kLoop, calls=%fused_computation.5 | loop fusion | flops 7340032 | bytes 7340048 | tf_op jit(solution)/shard_map/convert_element_type | solution.py:39
  128.6 0.0 reduce-scatter.5.cloned.1.call-update
  128.6 0.0 reduce-scatter.3.cloned.1.call-start
  128.6 0.0 copy-start.3
  128.6 13.1 %convolution_convert_fusion = bf16[1024,1792]{1,0:T(8,128)(2,1)} fusion(bf16[1024,2048]{1,0:T(8,128)(2,1)} %all-gather.2.cloned.1.call-done, bf16[2048,1792]{1,0:T(8,128)(2,1)} %param.10), kind=kOutput, calls=%fused_computation.7 | convolution fusion | flops 7518027776 | bytes 15204352 | tf_op jit(solution)/shard_map/dot_general | solution.py:61
  141.7 0.0 copy-done.3
  141.7 12.3 %convolution_convert_fusion.1 = bf16[1024,1792]{1,0:T(8,128)(2,1)} fusion(bf16[1024,2048]{1,0:T(8,128)(2,1)S(1)} %copy-done.3, bf16[2048,1792]{1,0:T(8,128)(2,1)} %param.9), kind=kOutput, calls=%fused_computation.8 | convolution fusion | flops 7518027776 | bytes 15204352 | tf_op jit(solution)/shard_map/dot_general | solution.py:60
  154.0 6.6 %pad_maximum_fusion = bf16[1024,3584]{1,0:T(8,128)(2,1)} fusion(bf16[1024,1792]{1,0:T(8,128)(2,1)} %convolution_convert_fusion, bf16[1024,1792]{1,0:T(8,128)(2,1)} %convolution_convert_fusion.1), kind=kLoop, calls=%fused_computation.4 | loop fusion | flops 14680064 | bytes 14680064 | tf_op jit(solution)/shard_map/concatenate | solution.py:58
  160.6 0.0 reduce-scatter.3.cloned.1.call-update
  160.6 0.0 all-reduce.5.cloned.1.call-done
  160.6 0.8 convert_convert_fusion
  161.4 0.1 reshape.295
  161.5 67.0 %reduce-scatter.5.cloned.1.call-done = bf16[2,2,64,1792]{3,2,1,0:T(8,128)(2,1)} async-done(((bf16[8,2,64,1792]{3,2,1,0:T(8,128)(2,1)}), bf16[2,2,64,1792]{3,2,1,0:T(8,128)(2,1)}) %reduce-scatter.5.cloned.1.call-update) | async-done | bytes 917520 | tf_op jit(solution)/shard_map/reduce_scatter | solution.py:38
  228.5 3.7 %fusion.7 = f32[2,128,2,1792]{3,1,0,2:T(8,128)} fusion(bf16[2,2,64,1792]{3,2,1,0:T(8,128)(2,1)} %reduce-scatter.5.cloned.1.call-done, bf16[2,128,64]{2,1,0:T(8,128)(2,1)S(1)} %reshape.295), kind=kOutput, calls=%fused_computation.19 | convolution fusion | flops 117440512 | bytes 4620288 | tf_op jit(solution)/shard_map/vcz,vwzd->vcwd/dot_general | solution.py:54
  232.2 126.7 %reduce-scatter.3.cloned.1.call-done = bf16[256,3584]{1,0:T(8,128)(2,1)} async-done(((bf16[1024,3584]{1,0:T(8,128)(2,1)}), bf16[256,3584]{1,0:T(8,128)(2,1)}) %reduce-scatter.3.cloned.1.call-update) | async-done | bytes 1835024 | tf_op jit(solution)/shard_map/reduce_scatter | solution.py:57
  358.9 0.0 copy-start.2
  358.9 2.1 convert_element_type.39
  361.0 0.0 copy-start.1
  361.0 0.5 copy-done.2
  361.5 1.6 fusion.3
  363.0 0.0 copy-done.1
  (10 shorter events, 0.1 us)
Async XLA Ops:
  6.5 3.8 %copy-start = (bf16[8,64,2048]{2,1,0:T(8,128)(2,1)S(1)}, bf16[8,64,2048]{2,1,0:T(8,128)(2,1)}, u32[]{:S(2)}) copy-start(bf16[8,64,2048]{2,1,0:T(8,128)(2,1)} %param.11) | copy-start | bytes 6291460
  6.5 73.8 %all-reduce.3.cloned.1.call-start = ((), (), s32[]{:S(2)}) async-start(), calls=%async_computation.4 | async-start | bytes 4194304 | tf_op jit(solution)/shard_map/psum | solution.py:34
  16.0 102.1 %all-gather.2.cloned.1.call-start = ((), (), s32[]{:S(2)}) async-start(), calls=%async_computation.2 | async-start | bytes 4718592 | tf_op jit(solution)/shard_map/all_gather | solution.py:41
  16.8 143.9 %all-reduce.5.cloned.1.call-start = ((), (), s32[]{:S(2)}) async-start(), calls=%async_computation.5 | async-start | bytes 262144 | tf_op jit(solution)/shard_map/psum | solution.py:51
  123.6 104.9 %reduce-scatter.5.cloned.1.call-start = ((), (), s32[]{:S(2)}) async-start(), calls=%async_computation.6 | async-start | bytes 4587520 | tf_op jit(solution)/shard_map/reduce_scatter | solution.py:38
  128.6 230.3 %reduce-scatter.3.cloned.1.call-start = ((), (), s32[]{:S(2)}) async-start(), calls=%async_computation.3 | async-start | bytes 9175040 | tf_op jit(solution)/shard_map/reduce_scatter | solution.py:57
  128.6 13.1 %copy-start.3 = (bf16[1024,2048]{1,0:T(8,128)(2,1)S(1)}, bf16[1024,2048]{1,0:T(8,128)(2,1)}, u32[]{:S(2)}) copy-start(bf16[1024,2048]{1,0:T(8,128)(2,1)} %all-gather.2.cloned.1.call-done) | copy-start | bytes 12582916
  358.9 2.6 copy-start.2
  361.0 2.1 copy-start.1
Sparse Core Ops, SparseCore 0:
  16.2 64.1 all-reduce.2
  82.2 35.9 all-gather.1
  123.7 34.4 all-reduce.4
  160.4 68.0 reduce-scatter.4
  230.7 128.1 reduce-scatter.2
where the time goes:
time: 370 us
  waiting for transfers between devices  290 us (78%)
  matrix products  33.4 us (9%)
  other arithmetic  20.8 us (6%)
  between operations  13.3 us (4%)
  local copies, waits for them, and re-layouts  12 us (3%)
    reduce_scatter x1, waiting for transfers between devices, shards(): lax.psum_scatter(jnp.concatenate([jnp.dot(gathered, gate_weight, preferre...  127 us
    reduce_scatter x1, waiting for transfers between devices, shards(): lax.psum_scatter(table_up.astype(jnp.bfloat16), 'seq', scatter_dimension=...  67 us
    psum x1, waiting for transfers between devices, shards(): downs = lax.psum(table_down.astype(jnp.bfloat16), 'tp')  57.7 us
    all_gather x1, waiting for transfers between devices, shards(): gathered = lax.all_gather(tokens, 'tp', axis=0, tiled=True)  37.8 us
    dot_general x1, matrix products, shards(): jnp.dot(gathered, up_weight, preferred_element_type=jnp.float32)  13.1 us
    dot_general x1, matrix products, shards(): jnp.dot(gathered, gate_weight, preferred_element_type=jnp.float32)  12.3 us
  transfers between devices with their start and end apart: 5, of which 4 were waited for; matrix products, arithmetic and copies ran while one was open for 13% of the time, Pallas kernels for 0%

commit v1 on v0

v1 whole, which is shorter than its diff:
```python
import jax
import jax.numpy as jnp
from jax import lax
from jax.sharding import PartitionSpec as P

SEG_ROWS = 128
SUB_BLOCKS = 2

low_rank_scale = 0.5


def segment_slots(req_len, req_adapter, owner_slot, segs):
    reqs = req_len.shape[0]
    order = jnp.arange(reqs, dtype=jnp.int32)
    ends = jnp.sum(jnp.where(order[:, None] <= order[None, :], req_len[:, None], 0), axis=0)
    segment = jnp.arange(segs, dtype=jnp.int32)
    seg_request = jnp.sum((ends[None, :] <= segment[:, None]).astype(jnp.int32), axis=1)
    adapter = jnp.sum(jnp.where(seg_request[:, None] == order[None, :], req_adapter[None, :], 0), axis=1)
    ids = jnp.arange(owner_slot.shape[0], dtype=jnp.int32)
    return jnp.sum(jnp.where(adapter[:, None] == ids[None, :], owner_slot[None, :], 0), axis=1)


def swap(x, axis, size, mask):
    return lax.ppermute(x, axis, [(i, i ^ mask) for i in range(size)])


def gather_rows(x, ntp):
    me = lax.axis_index("tp")
    mine = [x] + [swap(x, "tp", ntp, 2 * m) for m in range(1, ntp // 2)]
    out = jnp.zeros((ntp,) + x.shape, x.dtype)
    both = [(m, mine[m], swap(mine[m], "tp", ntp, 1)) for m in range(ntp // 2)]
    for m, own, other in both:
        out = lax.dynamic_update_slice_in_dim(out, own[None], me ^ (2 * m), 0)
        out = lax.dynamic_update_slice_in_dim(out, other[None], me ^ (2 * m) ^ 1, 0)
    return out


def sum_everywhere(x, nseq, ntp):
    x = x + swap(x, "tp", ntp, 1)
    x = sum([swap(x, "tp", ntp, 2 * m) for m in range(1, ntp // 2)], x)
    parts = [lax.ppermute(x, "seq", [(i, (i + k) % nseq) for i in range(nseq)]) for k in range(1, nseq)]
    total = x.astype(jnp.float32)
    for part in parts:
        total = total + part.astype(jnp.float32)
    return total.astype(jnp.bfloat16)


def slot_chunk(slot, nseq):
    me = lax.axis_index("seq")
    half = me < nseq // 2
    far = jnp.where(half, nseq - 1 - me, me)
    near = slot - far
    far_chunk = jnp.where(half, nseq - 1 - slot, slot)
    near_chunk = jnp.where(half, near, nseq - 1 - near)
    chunk = jnp.where(slot < far, far_chunk, near_chunk)
    return jnp.where(slot == nseq - 1, me, chunk)


def scatter_line(p, nseq):
    def own(slot):
        return lax.dynamic_index_in_dim(p, slot_chunk(slot, nseq), 0, keepdims=False)

    last = nseq - 2
    arrived = {}
    for step in range(nseq - 1):
        for level in range(step + 1):
            slot = step - level if level < nseq // 2 else step
            send = own(slot)
            if level > 0:
                send = (send.astype(jnp.float32) + arrived[level - 1, step - 1].astype(jnp.float32)).astype(p.dtype)
            pairs = [(level, level + 1), (nseq - 1 - level, nseq - 2 - level)]
            arrived[level, step] = lax.ppermute(send, "seq", pairs)
    total = own(nseq - 1).astype(jnp.float32)
    for level in range(nseq - 1):
        total = total + arrived[level, last].astype(jnp.float32)
    return total


def shards(tokens, gate_weight, up_weight, down_pool, up_pool, req_len, req_adapter, owner_slot):
    nseq = lax.axis_size("seq")
    ntp = lax.axis_size("tp")
    segs = ntp
    seg_slot = segment_slots(req_len, req_adapter, owner_slot, segs)
    per_tp, rank, width = down_pool.shape
    per_seq = up_pool.shape[0]
    columns = gate_weight.shape[1]
    rows = SEG_ROWS // SUB_BLOCKS
    down_local = seg_slot - lax.axis_index("tp") * per_tp
    pick_down = (down_local[None, :] == jnp.arange(per_tp, dtype=jnp.int32)[:, None]).astype(jnp.float32)
    up_local = seg_slot - lax.axis_index("seq") * per_seq
    held_up = (up_local >= 0) & (up_local < per_seq)
    ups = jnp.take(up_pool, jnp.clip(up_local, 0, per_seq - 1), axis=0)
    downs = down_pool.reshape(per_tp * rank, width)
    out = []
    for j in range(SUB_BLOCKS):
        block = tokens[j * rows:(j + 1) * rows]
        gathered = gather_rows(block, ntp)
        flat = gathered.reshape(segs * rows, width)
        every = lax.dot_general(downs, flat, (((1,), (1,)), ((), ())), preferred_element_type=jnp.float32)
        mine = jnp.sum(
            every.reshape(per_tp, rank, segs, rows) * pick_down[:, None, :, None], axis=0
        ).astype(jnp.bfloat16)
        inner = sum_everywhere(mine.reshape(rank, segs * rows), nseq, ntp).reshape(rank, segs, rows)
        inner = jnp.where(held_up[None, :, None], inner, jnp.zeros_like(inner))
        sums = []
        for which, weight in enumerate((gate_weight, up_weight)):
            part = jnp.dot(flat, weight, preferred_element_type=jnp.float32).reshape(segs, rows, columns)
            lora = jnp.einsum("zkq,kzd->kqd", inner, ups[:, which], preferred_element_type=jnp.float32)
            part = (part + low_rank_scale * lora).astype(jnp.bfloat16)
            sums.append(scatter_line(part.reshape(nseq, segs // nseq * rows, columns), nseq))
        gate, up = sums
        out.append((jax.nn.silu(gate) * up).astype(jnp.bfloat16).reshape(segs // nseq, rows, columns))
    return jnp.concatenate(out, axis=1).reshape(segs // nseq * SEG_ROWS, columns)


def solution(mesh):
    placed = (
        P("tp", "seq"),
        P("seq", "tp"),
        P("seq", "tp"),
        P("tp", None, "seq"),
        P("seq", None, None, "tp"),
        P(),
        P(),
        P(),
    )
    return jax.shard_map(
        shards, mesh=mesh, in_specs=placed, out_specs=P("seq", "tp"), check_vma=False
    )
```

time: 370 us -> 254 us (0.69)
  waiting for transfers between devices: 290 us -> 84.9 us
  starting transfers between devices: 0.17 us -> 98.3 us
  local copies, waits for them, and re-layouts: 12 us -> 28.2 us
  between operations: 13.3 us -> 0.68 us
  other arithmetic: 20.8 us -> 11.7 us
  matrix products: 33.4 us -> 29.5 us
    reduce_scatter x2 -> x0, waiting for transfers between devices: 194 us -> none  [the longest x1 127 us: shards(): lax.psum_scatter(jnp.concatenate([jnp.dot(gathered, gate_weight, preferre...]
    ppermute x0 -> x52, starting transfers between devices: none -> 98.3 us  [the longest x24 70.1 us: scatter_line(): arrived[level, step] = lax.ppermute(send, 'seq', pairs)]
    ppermute x0 -> x52, waiting for transfers between devices: none -> 84.9 us  [the longest x24 61.1 us: scatter_line(): arrived[level, step] = lax.ppermute(send, 'seq', pairs)]
    psum x2 -> x0, waiting for transfers between devices: 57.7 us -> none  [the longest x1 57.7 us: shards(): downs = lax.psum(table_down.astype(jnp.bfloat16), 'tp')]
    all_gather x1 -> x0, waiting for transfers between devices: 37.8 us -> none  [shards(): gathered = lax.all_gather(tokens, 'tp', axis=0, tiled=True)]
    dynamic_update_slice x0 -> x15, local copies, waits for them, and re-layouts: none -> 12.3 us  [the longest x7 6.25 us: gather_rows(): out = lax.dynamic_update_slice_in_dim(out, other[None], me ^ 2 * m ^ 1, 0)]
    convert_element_type x5 -> x17, other arithmetic: 13 us -> 2.91 us  [the longest x12 1.44 us: scatter_line(): (send.astype(jnp.float32) + arrived[level - 1, step - 1].astype(jnp.float...]
    concatenate x1, other arithmetic: 6.63 us -> 0.98 us  [shards(): jnp.concatenate(out, axis=1).reshape(segs // nseq * SEG_ROWS, columns)]
  transfers between devices with their start and end apart: 5 -> 52, of which waited for: 4 -> 16; matrix products, arithmetic and copies ran while one was open for 13% -> 17% of each run, Pallas kernels for 0% -> 0%
where the time goes in v1:
time: 254 us; the launch traced here: 253 us
  starting transfers between devices  98.3 us (39%)
  waiting for transfers between devices  84.9 us (33%)
  matrix products  29.5 us (12%)
  local copies, waits for them, and re-layouts  28.2 us (11%)
  other arithmetic  11.7 us (5%)
    ppermute x24, starting transfers between devices, scatter_line(): arrived[level, step] = lax.ppermute(send, 'seq', pairs)  70.1 us
    ppermute x24, waiting for transfers between devices, scatter_line(): arrived[level, step] = lax.ppermute(send, 'seq', pairs)  61.1 us
    dot_general x4, matrix products, shards(): jnp.dot(flat, weight, preferred_element_type=jnp.float32)  19.4 us
    ppermute x22, starting transfers between devices, swap(): return lax.ppermute(x, axis, [(i, i ^ mask) for i in range(size)])  19.2 us
    ppermute x6, waiting for transfers between devices, sum_everywhere(): lax.ppermute(x, 'seq', [(i, (i + k) % nseq) for i in range(nseq)])  13.6 us
    ppermute x22, waiting for transfers between devices, swap(): return lax.ppermute(x, axis, [(i, i ^ mask) for i in range(size)])  10.2 us
    ppermute x6, starting transfers between devices, sum_everywhere(): lax.ppermute(x, 'seq', [(i, (i + k) % nseq) for i in range(nseq)])  8.96 us
    dynamic_update_slice x7, local copies, waits for them, and re-layouts, gather_rows(): out = lax.dynamic_update_slice_in_dim(out, other[None], me ^ 2 * m ^ 1, 0)  6.25 us
  transfers between devices with their start and end apart: 52, of which 16 were waited for; matrix products, arithmetic and copies ran while one was open for 17% of the time, Pallas kernels for 0%

profile of v1, /device:TPU:0, one launch (start us, length us, event | category | flops | bytes accessed | tf_op | source)
XLA Modules:
  0.0 253.3 jit_solution(836951824487865356)
XLA Ops:
  0.0 2.0 fusion.38
  2.0 3.0 %collective-permute-start.29 = (bf16[64,2048]{1,0:T(8,128)(2,1)}, bf16[64,2048]{1,0:T(8,128)(2,1)S(1)}, u32[]{:S(2)}, u32[]{:S(2)}) collective-permute-start(bf16[64,2048]{1,0:T(8,128)(2,1)} %get-tuple-element.23), channel_id=1, source_target_pairs={{0,4},{1,5},{2,6},{3,7},{4,0},{5,1},{6,2},{7,3},{8,12},{9,13},{10,... | collective-permute-start | bytes 786440 | tf_op jit(solution)/shard_map/ppermute | solution.py:24
  6.5 2.0 collective-permute-start.3
  10.9 1.7 broadcast.120.clone
  15.0 5.6 %gather_fusion = bf16[8,2,64,1792]{3,2,1,0:T(8,128)(2,1)} fusion(bf16[16,2,64,1792]{3,2,1,0:T(8,128)(2,1)} %param.12, s32[1024]{0:T(1024)S(1)} %pad_clamp_fusion), kind=kCustom, calls=%fused_computation | custom fusion | bytes 7340064 | tf_op jit(solution)/shard_map/jit(_take)/gather | solution.py:92
  20.7 1.7 bitcast_dynamic-update-slice_fusion.6
  22.4 1.5 collective-permute-start.1
  24.8 1.7 bitcast_dynamic-update-slice_fusion.5
  26.5 5.2 %collective-permute-done.1 = bf16[64,2048]{1,0:T(8,128)(2,1)S(1)} collective-permute-done((bf16[64,2048]{1,0:T(8,128)(2,1)}, bf16[64,2048]{1,0:T(8,128)(2,1)S(1)}, u32[]{:S(2)}, u32[]{:S(2)}) %collective-permute-start.1) | collective-permute-done | bytes 262176 | tf_op jit(solution)/shard_map/ppermute | solution.py:24
  33.5 3.1 %collective-permute-done.5 = bf16[64,2048]{1,0:T(8,128)(2,1)S(1)} collective-permute-done((bf16[64,2048]{1,0:T(8,128)(2,1)}, bf16[64,2048]{1,0:T(8,128)(2,1)S(1)}, u32[]{:S(2)}, u32[]{:S(2)}) %collective-permute-start.5) | collective-permute-done | bytes 262176 | tf_op jit(solution)/shard_map/ppermute | solution.py:24
  43.9 2.9 %convolution_bitcast_fusion.1 = f32[512,512]{0,1:T(8,128)S(1)} fusion(bf16[512,2048]{1,0:T(8,128)(2,1)} %bitcast.136, bf16[512,2048]{1,0:T(8,128)(2,1)S(1)} %bitcast.134), kind=kOutput, calls=%fused_computation.23 | convolution fusion | flops 1073741824 | bytes 5242880 | tf_op jit(solution)/shard_map/dot_general | solution.py:99
  46.8 1.8 reshape.133
  48.6 2.9 %convolution_bitcast_fusion = f32[512,512]{0,1:T(8,128)S(1)} fusion(bf16[512,2048]{1,0:T(8,128)(2,1)} %bitcast.38, bf16[512,2048]{1,0:T(8,128)(2,1)S(1)} %bitcast.135), kind=kOutput, calls=%fused_computation.22 | convolution fusion | flops 1073741824 | bytes 5242880 | tf_op jit(solution)/shard_map/dot_general | solution.py:99
  51.5 1.8 reshape.139
  53.5 3.1 %multiply_reduce_fusion.1 = (bf16[64,8,64]{0,2,1:T(8,128)(2,1)S(1)}, bf16[64,8,64]{0,2,1:T(8,128)(2,1)S(1)}) fusion(f32[8,64,8,64]{1,0,3,2:T(8,128)S(1)} %copy-done.4, f32[8,8]{0,1:T(8,128)S(1)} %fusion.32, f32[8,64,8,64]{1,0,3,2:T(8,128)} %reshape.139), kind=kLoop, calls=%fused_computation.15 | loop fusion | flops 983040 | bytes 2228480 | tf_op jit(solution)/shard_map/reduce_sum | solution.py:100
  56.7 2.2 copy_select_fusion
  59.4 2.7 %collective-permute-start.36 = (bf16[64,512]{0,1:T(8,128)(2,1)S(1)}, bf16[64,512]{0,1:T(8,128)(2,1)S(1)}, u32[]{:S(2)}, u32[]{:S(2)}) collective-permute-start(bf16[64,512]{0,1:T(8,128)(2,1)S(1)} %bitcast_add_fusion), channel_id=1, source_target_pairs={{0,6},{1,7},{2,4},{3,5},{4,2},{5,3},{6,0},{7,1},{8,14},{9,15},{10,... | collective-permute-start | bytes 196616 | tf_op jit(solution)/shard_map/ppermute | solution.py:24
  63.0 2.7 %collective-permute-start.10 = (bf16[64,512]{0,1:T(8,128)(2,1)S(1)}, bf16[64,512]{0,1:T(8,128)(2,1)S(1)}, u32[]{:S(2)}, u32[]{:S(2)}) collective-permute-start(bf16[64,512]{0,1:T(8,128)(2,1)S(1)} %bitcast_add_fusion.1), channel_id=1, source_target_pairs={{0,6},{1,7},{2,4},{3,5},{4,2},{5,3},{6,0},{7,1},{8,14},{9,15},{10,... | collective-permute-start | bytes 196616 | tf_op jit(solution)/shard_map/ppermute | solution.py:24
  66.3 2.2 collective-permute-start.8
  68.5 1.7 collective-permute-done.35
  70.3 3.6 %collective-permute-start.39 = (bf16[64,512]{0,1:T(8,128)(2,1)S(1)}, bf16[64,512]{0,1:T(8,128)(2,1)S(1)}, u32[]{:S(2)}, u32[]{:S(2)}) collective-permute-start(bf16[64,512]{0,1:T(8,128)(2,1)S(1)} %add_add_fusion), channel_id=1, source_target_pairs={{0,24},{8,0},{16,8},{24,16},{1,25},{9,1},{17,9},{25,17},{2,26},{10... | collective-permute-start | bytes 196616 | tf_op jit(solution)/shard_map/ppermute | solution.py:41
  74.9 3.4 %collective-permute-start.13 = (bf16[64,512]{0,1:T(8,128)(2,1)S(1)}, bf16[64,512]{0,1:T(8,128)(2,1)S(1)}, u32[]{:S(2)}, u32[]{:S(2)}) collective-permute-start(bf16[64,512]{0,1:T(8,128)(2,1)S(1)} %add_add_fusion.1), channel_id=1, source_target_pairs={{0,24},{8,0},{16,8},{24,16},{1,25},{9,1},{17,9},{25,17},{2,26},{10... | collective-permute-start | bytes 196616 | tf_op jit(solution)/shard_map/ppermute | solution.py:41
  79.3 7.5 %collective-permute-done.38 = bf16[64,512]{0,1:T(8,128)(2,1)S(1)} collective-permute-done((bf16[64,512]{0,1:T(8,128)(2,1)S(1)}, bf16[64,512]{0,1:T(8,128)(2,1)S(1)}, u32[]{:S(2)}, u32[]{:S(2)}) %collective-permute-start.38) | collective-permute-done | bytes 65568 | tf_op jit(solution)/shard_map/ppermute | solution.py:41
  86.9 2.3 fusion.18
  90.2 6.1 %collective-permute-done.12 = bf16[64,512]{0,1:T(8,128)(2,1)S(1)} collective-permute-done((bf16[64,512]{0,1:T(8,128)(2,1)S(1)}, bf16[64,512]{0,1:T(8,128)(2,1)S(1)}, u32[]{:S(2)}, u32[]{:S(2)}) %collective-permute-start.12) | collective-permute-done | bytes 65568 | tf_op jit(solution)/shard_map/ppermute | solution.py:41
  98.2 5.8 %add_convert_fusion = bf16[8,64,1792]{2,1,0:T(8,128)(2,1)S(1)} fusion(f32[8,64,1792]{2,1,0:T(8,128)S(1)} %fusion.18, bf16[8,64,2048]{2,1,0:T(8,128)(2,1)} %get-tuple-element.27, bf16[2048,1792]{1,0:T(8,128)(2,1)S(1)} %bitcast.158), kind=kOutput, calls=%fused_computation.10 | convolution fusion | flops 3760848896 | bytes 14942208 | tf_op jit(solution)/shard_map/dot_general | solution.py:107
  104.1 2.6 %collective-permute-start.47 = (bf16[128,1792]{1,0:T(8,128)(2,1)S(1)}, bf16[128,1792]{1,0:T(8,128)(2,1)S(1)}, u32[]{:S(2)}, u32[]{:S(2)}) collective-permute-start(bf16[128,1792]{1,0:T(8,128)(2,1)S(1)} %get-tuple-element.21), channel_id=1, source_target_pairs={{0,8},{24,16},{1,9},{25,17},{2,10},{26,18},{3,11},{27,19},{4,12},{... | collective-permute-start | bytes 1376264 | tf_op jit(solution)/shard_map/ppermute | solution.py:72
  108.2 5.6 %add_convert_fusion.1 = bf16[8,64,1792]{2,1,0:T(8,128)(2,1)S(1)} fusion(f32[8,64,1792]{2,1,0:T(8,128)S(1)} %fusion.16, bf16[8,64,2048]{2,1,0:T(8,128)(2,1)} %get-tuple-element.27, bf16[2048,1792]{1,0:T(8,128)(2,1)S(1)} %bitcast.160), kind=kOutput, calls=%fused_computation.11 | convolution fusion | flops 3760848896 | bytes 14942208 | tf_op jit(solution)/shard_map/dot_general | solution.py:107
  115.2 1.5 collective-permute-start.43
  116.8 4.0 %add_convert_fusion.2 = bf16[8,64,1792]{2,1,0:T(8,128)(2,1)S(1)} fusion(f32[8,64,1792]{2,1,0:T(8,128)S(1)} %fusion.19, bf16[8,64,2048]{2,1,0:T(8,128)(2,1)S(1)} %copy-done.7, bf16[2048,1792]{1,0:T(8,128)(2,1)S(1)} %bitcast.158), kind=kOutput, calls=%fused_computation.12 | convolution fusion | flops 3760848896 | bytes 14942208 | tf_op jit(solution)/shard_map/dot_general | solution.py:107
  120.8 4.0 %add_convert_fusion.3 = bf16[8,64,1792]{2,1,0:T(8,128)(2,1)S(1)} fusion(f32[8,64,1792]{2,1,0:T(8,128)S(1)} %fusion.17, bf16[8,64,2048]{2,1,0:T(8,128)(2,1)S(1)} %copy-done.7, bf16[2048,1792]{1,0:T(8,128)(2,1)S(1)} %bitcast.160), kind=kOutput, calls=%fused_computation.13 | convolution fusion | flops 3760848896 | bytes 14942208 | tf_op jit(solution)/shard_map/dot_general | solution.py:107
  127.7 4.2 %collective-permute-start.15 = (bf16[128,1792]{1,0:T(8,128)(2,1)S(1)}, bf16[128,1792]{1,0:T(8,128)(2,1)S(1)}, u32[]{:S(2)}, u32[]{:S(2)}) collective-permute-start(bf16[128,1792]{1,0:T(8,128)(2,1)S(1)} %get-tuple-element.15), channel_id=1, source_target_pairs={{0,8},{24,16},{1,9},{25,17},{2,10},{26,18},{3,11},{27,19},{4,12},{... | collective-permute-start | bytes 1376264 | tf_op jit(solution)/shard_map/ppermute | solution.py:72
  132.0 5.3 %collective-permute-done.41 = bf16[128,1792]{1,0:T(8,128)(2,1)S(1)} collective-permute-done((bf16[128,1792]{1,0:T(8,128)(2,1)S(1)}, bf16[128,1792]{1,0:T(8,128)(2,1)S(1)}, u32[]{:S(2)}, u32[]{:S(2)}) %collective-permute-start.41) | collective-permute-done | bytes 458784 | tf_op jit(solution)/shard_map/ppermute | solution.py:72
  137.3 4.4 %collective-permute-start.17 = (bf16[128,1792]{1,0:T(8,128)(2,1)S(1)}, bf16[128,1792]{1,0:T(8,128)(2,1)S(1)}, u32[]{:S(2)}, u32[]{:S(2)}) collective-permute-start(bf16[128,1792]{1,0:T(8,128)(2,1)S(1)} %get-tuple-element.16), channel_id=1, source_target_pairs={{0,8},{24,16},{1,9},{25,17},{2,10},{26,18},{3,11},{27,19},{4,12},{... | collective-permute-start | bytes 1376264 | tf_op jit(solution)/shard_map/ppermute | solution.py:72
  141.9 5.3 %collective-permute-done.43 = bf16[128,1792]{1,0:T(8,128)(2,1)S(1)} collective-permute-done((bf16[128,1792]{1,0:T(8,128)(2,1)S(1)}, bf16[128,1792]{1,0:T(8,128)(2,1)S(1)}, u32[]{:S(2)}, u32[]{:S(2)}) %collective-permute-start.43) | collective-permute-done | bytes 458784 | tf_op jit(solution)/shard_map/ppermute | solution.py:72
  148.0 9.0 %collective-permute-done.21 = bf16[128,1792]{1,0:T(8,128)(2,1)S(1)} collective-permute-done((bf16[128,1792]{1,0:T(8,128)(2,1)S(1)}, bf16[128,1792]{1,0:T(8,128)(2,1)S(1)}, u32[]{:S(2)}, u32[]{:S(2)}) %collective-permute-start.21) | collective-permute-done | bytes 458784 | tf_op jit(solution)/shard_map/ppermute | solution.py:72
  157.8 9.0 %collective-permute-done.23 = bf16[128,1792]{1,0:T(8,128)(2,1)S(1)} collective-permute-done((bf16[128,1792]{1,0:T(8,128)(2,1)S(1)}, bf16[128,1792]{1,0:T(8,128)(2,1)S(1)}, u32[]{:S(2)}, u32[]{:S(2)}) %collective-permute-start.23) | collective-permute-done | bytes 458784 | tf_op jit(solution)/shard_map/ppermute | solution.py:72
  167.7 9.0 %collective-permute-done.15 = bf16[128,1792]{1,0:T(8,128)(2,1)S(1)} collective-permute-done((bf16[128,1792]{1,0:T(8,128)(2,1)S(1)}, bf16[128,1792]{1,0:T(8,128)(2,1)S(1)}, u32[]{:S(2)}, u32[]{:S(2)}) %collective-permute-start.15) | collective-permute-done | bytes 458784 | tf_op jit(solution)/shard_map/ppermute | solution.py:72
  177.5 7.2 %collective-permute-done.17 = bf16[128,1792]{1,0:T(8,128)(2,1)S(1)} collective-permute-done((bf16[128,1792]{1,0:T(8,128)(2,1)S(1)}, bf16[128,1792]{1,0:T(8,128)(2,1)S(1)}, u32[]{:S(2)}, u32[]{:S(2)}) %collective-permute-start.17) | collective-permute-done | bytes 458784 | tf_op jit(solution)/shard_map/ppermute | solution.py:72
  188.7 27.6 %collective-permute-start.46 = (bf16[128,1792]{1,0:T(8,128)(2,1)S(1)}, bf16[128,1792]{1,0:T(8,128)(2,1)S(1)}, u32[]{:S(2)}, u32[]{:S(2)}) collective-permute-start(bf16[128,1792]{1,0:T(8,128)(2,1)S(1)} %get-tuple-element.14), channel_id=1, source_target_pairs={{0,8},{24,16},{1,9},{25,17},{2,10},{26,18},{3,11},{27,19},{4,12},{... | collective-permute-start | bytes 1376264 | tf_op jit(solution)/shard_map/ppermute | solution.py:72
  217.6 4.6 %collective-permute-start.40 = (bf16[128,1792]{1,0:T(8,128)(2,1)S(1)}, bf16[128,1792]{1,0:T(8,128)(2,1)S(1)}, u32[]{:S(2)}, u32[]{:S(2)}) collective-permute-start(bf16[128,1792]{1,0:T(8,128)(2,1)S(1)} %get-tuple-element.12), channel_id=1, source_target_pairs={{0,8},{24,16},{1,9},{25,17},{2,10},{26,18},{3,11},{27,19},{4,12},{... | collective-permute-start | bytes 1376264 | tf_op jit(solution)/shard_map/ppermute | solution.py:72
  223.0 2.3 collective-permute-done.51
  226.7 4.6 %collective-permute-start.20 = (bf16[128,1792]{1,0:T(8,128)(2,1)S(1)}, bf16[128,1792]{1,0:T(8,128)(2,1)S(1)}, u32[]{:S(2)}, u32[]{:S(2)}) collective-permute-start(bf16[128,1792]{1,0:T(8,128)(2,1)S(1)} %get-tuple-element.10), channel_id=1, source_target_pairs={{0,8},{24,16},{1,9},{25,17},{2,10},{26,18},{3,11},{27,19},{4,12},{... | collective-permute-start | bytes 1376264 | tf_op jit(solution)/shard_map/ppermute | solution.py:72
  231.3 3.9 %collective-permute-done.45 = bf16[128,1792]{1,0:T(8,128)(2,1)S(1)} collective-permute-done((bf16[128,1792]{1,0:T(8,128)(2,1)S(1)}, bf16[128,1792]{1,0:T(8,128)(2,1)S(1)}, u32[]{:S(2)}, u32[]{:S(2)}) %collective-permute-start.45) | collective-permute-done | bytes 458784 | tf_op jit(solution)/shard_map/ppermute | solution.py:72
  236.5 4.6 %collective-permute-start.14 = (bf16[128,1792]{1,0:T(8,128)(2,1)S(1)}, bf16[128,1792]{1,0:T(8,128)(2,1)S(1)}, u32[]{:S(2)}, u32[]{:S(2)}) collective-permute-start(bf16[128,1792]{1,0:T(8,128)(2,1)S(1)} %get-tuple-element.8), channel_id=1, source_target_pairs={{0,8},{24,16},{1,9},{25,17},{2,10},{26,18},{3,11},{27,19},{4,12},{... | collective-permute-start | bytes 1376264 | tf_op jit(solution)/shard_map/ppermute | solution.py:72
  241.8 3.3 %collective-permute-done.25 = bf16[128,1792]{1,0:T(8,128)(2,1)S(1)} collective-permute-done((bf16[128,1792]{1,0:T(8,128)(2,1)S(1)}, bf16[128,1792]{1,0:T(8,128)(2,1)S(1)}, u32[]{:S(2)}, u32[]{:S(2)}) %collective-permute-start.25) | collective-permute-done | bytes 458784 | tf_op jit(solution)/shard_map/ppermute | solution.py:72
  245.0 5.0 %collective-permute-done.19 = bf16[128,1792]{1,0:T(8,128)(2,1)S(1)} collective-permute-done((bf16[128,1792]{1,0:T(8,128)(2,1)S(1)}, bf16[128,1792]{1,0:T(8,128)(2,1)S(1)}, u32[]{:S(2)}, u32[]{:S(2)}) %collective-permute-start.19) | collective-permute-done | bytes 458784 | tf_op jit(solution)/shard_map/ppermute | solution.py:72
  250.1 1.6 collective-permute-done.14
  (149 shorter events, 43.6 us)
Async XLA Ops:
  2.0 30.5 %collective-permute-start.29 = (bf16[64,2048]{1,0:T(8,128)(2,1)}, bf16[64,2048]{1,0:T(8,128)(2,1)S(1)}, u32[]{:S(2)}, u32[]{:S(2)}) collective-permute-start(bf16[64,2048]{1,0:T(8,128)(2,1)} %get-tuple-element.23), channel_id=1, source_target_pairs={{0,4},{1,5},{2,6},{3,7},{4,0},{5,1},{6,2},{7,3},{8,12},{9,13},{10,... | collective-permute-start | bytes 786440 | tf_op jit(solution)/shard_map/ppermute | solution.py:24
  5.0 19.7 %collective-permute-start.27 = (bf16[64,2048]{1,0:T(8,128)(2,1)}, bf16[64,2048]{1,0:T(8,128)(2,1)}, u32[]{:S(2)}, u32[]{:S(2)}) collective-permute-start(bf16[64,2048]{1,0:T(8,128)(2,1)} %get-tuple-element.23), channel_id=1, source_target_pairs={{0,2},{1,3},{2,0},{3,1},{4,6},{5,7},{6,4},{7,5},{8,10},{9,11},{10,... | collective-permute-start | bytes 786440 | tf_op jit(solution)/shard_map/ppermute | solution.py:24
  6.5 14.2 %collective-permute-start.26 = (bf16[64,2048]{1,0:T(8,128)(2,1)}, bf16[64,2048]{1,0:T(8,128)(2,1)}, u32[]{:S(2)}, u32[]{:S(2)}) collective-permute-start(bf16[64,2048]{1,0:T(8,128)(2,1)} %get-tuple-element.23), channel_id=1, source_target_pairs={{0,1},{1,0},{2,3},{3,2},{4,5},{5,4},{6,7},{7,6},{8,9},{9,8},{10,11... | collective-permute-start | bytes 786440 | tf_op jit(solution)/shard_map/ppermute | solution.py:24
  6.5 26.5 %collective-permute-start.31 = (bf16[64,2048]{1,0:T(8,128)(2,1)}, bf16[64,2048]{1,0:T(8,128)(2,1)S(1)}, u32[]{:S(2)}, u32[]{:S(2)}) collective-permute-start(bf16[64,2048]{1,0:T(8,128)(2,1)} %get-tuple-element.23), channel_id=1, source_target_pairs={{0,6},{1,7},{2,4},{3,5},{4,2},{5,3},{6,0},{7,1},{8,14},{9,15},{10,... | collective-permute-start | bytes 786440 | tf_op jit(solution)/shard_map/ppermute | solution.py:24
  6.5 26.6 %collective-permute-start.3 = (bf16[64,2048]{1,0:T(8,128)(2,1)}, bf16[64,2048]{1,0:T(8,128)(2,1)S(1)}, u32[]{:S(2)}, u32[]{:S(2)}) collective-permute-start(bf16[64,2048]{1,0:T(8,128)(2,1)} %get-tuple-element.24), channel_id=1, source_target_pairs={{0,4},{1,5},{2,6},{3,7},{4,0},{5,1},{6,2},{7,3},{8,12},{9,13},{10,... | collective-permute-start | bytes 786440 | tf_op jit(solution)/shard_map/ppermute | solution.py:24
  22.4 9.3 %collective-permute-start.1 = (bf16[64,2048]{1,0:T(8,128)(2,1)}, bf16[64,2048]{1,0:T(8,128)(2,1)S(1)}, u32[]{:S(2)}, u32[]{:S(2)}) collective-permute-start(bf16[64,2048]{1,0:T(8,128)(2,1)} %get-tuple-element.24), channel_id=1, source_target_pairs={{0,2},{1,3},{2,0},{3,1},{4,6},{5,7},{6,4},{7,5},{8,10},{9,11},{10,... | collective-permute-start | bytes 786440 | tf_op jit(solution)/shard_map/ppermute | solution.py:24
  24.7 12.0 %collective-permute-start.5 = (bf16[64,2048]{1,0:T(8,128)(2,1)}, bf16[64,2048]{1,0:T(8,128)(2,1)S(1)}, u32[]{:S(2)}, u32[]{:S(2)}) collective-permute-start(bf16[64,2048]{1,0:T(8,128)(2,1)} %get-tuple-element.24), channel_id=1, source_target_pairs={{0,6},{1,7},{2,4},{3,5},{4,2},{5,3},{6,0},{7,1},{8,14},{9,15},{10,... | collective-permute-start | bytes 786440 | tf_op jit(solution)/shard_map/ppermute | solution.py:24
  31.8 4.9 %collective-permute-start.28 = (bf16[64,2048]{1,0:T(8,128)(2,1)}, bf16[64,2048]{1,0:T(8,128)(2,1)S(1)}, u32[]{:S(2)}, u32[]{:S(2)}) collective-permute-start(bf16[64,2048]{1,0:T(8,128)(2,1)} %collective-permute-done.27), channel_id=1, source_target_pairs={{0,1},{1,0},{2,3},{3,2},{4,5},{5,4},{6,7},{7,6},{8,9},{9,8},{10,11... | collective-permute-start | bytes 786440 | tf_op jit(solution)/shard_map/ppermute | solution.py:24
  32.5 6.1 %collective-permute-start.2 = (bf16[64,2048]{1,0:T(8,128)(2,1)S(1)}, bf16[64,2048]{1,0:T(8,128)(2,1)S(1)}, u32[]{:S(2)}, u32[]{:S(2)}) collective-permute-start(bf16[64,2048]{1,0:T(8,128)(2,1)S(1)} %collective-permute-done.1), channel_id=1, source_target_pairs={{0,1},{1,0},{2,3},{3,2},{4,5},{5,4},{6,7},{7,6},{8,9},{9,8},{10,11... | collective-permute-start | bytes 786440 | tf_op jit(solution)/shard_map/ppermute | solution.py:24
  33.0 7.0 %collective-permute-start.30 = (bf16[64,2048]{1,0:T(8,128)(2,1)S(1)}, bf16[64,2048]{1,0:T(8,128)(2,1)S(1)}, u32[]{:S(2)}, u32[]{:S(2)}) collective-permute-start(bf16[64,2048]{1,0:T(8,128)(2,1)S(1)} %collective-permute-done.29), channel_id=1, source_target_pairs={{0,1},{1,0},{2,3},{3,2},{4,5},{5,4},{6,7},{7,6},{8,9},{9,8},{10,11... | collective-permute-start | bytes 786440 | tf_op jit(solution)/shard_map/ppermute | solution.py:24
  33.1 9.9 %collective-permute-start.32 = (bf16[64,2048]{1,0:T(8,128)(2,1)S(1)}, bf16[64,2048]{1,0:T(8,128)(2,1)S(1)}, u32[]{:S(2)}, u32[]{:S(2)}) collective-permute-start(bf16[64,2048]{1,0:T(8,128)(2,1)S(1)} %collective-permute-done.31), channel_id=1, source_target_pairs={{0,1},{1,0},{2,3},{3,2},{4,5},{5,4},{6,7},{7,6},{8,9},{9,8},{10,11... | collective-permute-start | bytes 786440 | tf_op jit(solution)/shard_map/ppermute | solution.py:24
  36.6 4.9 %collective-permute-start.4 = (bf16[64,2048]{1,0:T(8,128)(2,1)S(1)}, bf16[64,2048]{1,0:T(8,128)(2,1)S(1)}, u32[]{:S(2)}, u32[]{:S(2)}) collective-permute-start(bf16[64,2048]{1,0:T(8,128)(2,1)S(1)} %collective-permute-done.3), channel_id=1, source_target_pairs={{0,1},{1,0},{2,3},{3,2},{4,5},{5,4},{6,7},{7,6},{8,9},{9,8},{10,11... | collective-permute-start | bytes 786440 | tf_op jit(solution)/shard_map/ppermute | solution.py:24
  36.7 6.4 %collective-permute-start.6 = (bf16[64,2048]{1,0:T(8,128)(2,1)S(1)}, bf16[64,2048]{1,0:T(8,128)(2,1)S(1)}, u32[]{:S(2)}, u32[]{:S(2)}) collective-permute-start(bf16[64,2048]{1,0:T(8,128)(2,1)S(1)} %collective-permute-done.5), channel_id=1, source_target_pairs={{0,1},{1,0},{2,3},{3,2},{4,5},{5,4},{6,7},{7,6},{8,9},{9,8},{10,11... | collective-permute-start | bytes 786440 | tf_op jit(solution)/shard_map/ppermute | solution.py:24
  59.4 6.8 %collective-permute-start.36 = (bf16[64,512]{0,1:T(8,128)(2,1)S(1)}, bf16[64,512]{0,1:T(8,128)(2,1)S(1)}, u32[]{:S(2)}, u32[]{:S(2)}) collective-permute-start(bf16[64,512]{0,1:T(8,128)(2,1)S(1)} %bitcast_add_fusion), channel_id=1, source_target_pairs={{0,6},{1,7},{2,4},{3,5},{4,2},{5,3},{6,0},{7,1},{8,14},{9,15},{10,... | collective-permute-start | bytes 196616 | tf_op jit(solution)/shard_map/ppermute | solution.py:24
  62.1 8.1 %collective-permute-start.35 = (bf16[64,512]{0,1:T(8,128)(2,1)S(1)}, bf16[64,512]{0,1:T(8,128)(2,1)S(1)}, u32[]{:S(2)}, u32[]{:S(2)}) collective-permute-start(bf16[64,512]{0,1:T(8,128)(2,1)S(1)} %bitcast_add_fusion), channel_id=1, source_target_pairs={{0,4},{1,5},{2,6},{3,7},{4,0},{5,1},{6,2},{7,3},{8,12},{9,13},{10,... | collective-permute-start | bytes 196616 | tf_op jit(solution)/shard_map/ppermute | solution.py:24
  62.7 7.6 %collective-permute-start.34 = (bf16[64,512]{0,1:T(8,128)(2,1)S(1)}, bf16[64,512]{0,1:T(8,128)(2,1)S(1)}, u32[]{:S(2)}, u32[]{:S(2)}) collective-permute-start(bf16[64,512]{0,1:T(8,128)(2,1)S(1)} %bitcast_add_fusion), channel_id=1, source_target_pairs={{0,2},{1,3},{2,0},{3,1},{4,6},{5,7},{6,4},{7,5},{8,10},{9,11},{10,... | collective-permute-start | bytes 196616 | tf_op jit(solution)/shard_map/ppermute | solution.py:24
  63.0 10.8 %collective-permute-start.10 = (bf16[64,512]{0,1:T(8,128)(2,1)S(1)}, bf16[64,512]{0,1:T(8,128)(2,1)S(1)}, u32[]{:S(2)}, u32[]{:S(2)}) collective-permute-start(bf16[64,512]{0,1:T(8,128)(2,1)S(1)} %bitcast_add_fusion.1), channel_id=1, source_target_pairs={{0,6},{1,7},{2,4},{3,5},{4,2},{5,3},{6,0},{7,1},{8,14},{9,15},{10,... | collective-permute-start | bytes 196616 | tf_op jit(solution)/shard_map/ppermute | solution.py:24
  65.7 9.1 %collective-permute-start.9 = (bf16[64,512]{0,1:T(8,128)(2,1)S(1)}, bf16[64,512]{0,1:T(8,128)(2,1)S(1)}, u32[]{:S(2)}, u32[]{:S(2)}) collective-permute-start(bf16[64,512]{0,1:T(8,128)(2,1)S(1)} %bitcast_add_fusion.1), channel_id=1, source_target_pairs={{0,4},{1,5},{2,6},{3,7},{4,0},{5,1},{6,2},{7,3},{8,12},{9,13},{10,... | collective-permute-start | bytes 196616 | tf_op jit(solution)/shard_map/ppermute | solution.py:24
  66.3 8.6 %collective-permute-start.8 = (bf16[64,512]{0,1:T(8,128)(2,1)S(1)}, bf16[64,512]{0,1:T(8,128)(2,1)S(1)}, u32[]{:S(2)}, u32[]{:S(2)}) collective-permute-start(bf16[64,512]{0,1:T(8,128)(2,1)S(1)} %bitcast_add_fusion.1), channel_id=1, source_target_pairs={{0,2},{1,3},{2,0},{3,1},{4,6},{5,7},{6,4},{7,5},{8,10},{9,11},{10,... | collective-permute-start | bytes 196616 | tf_op jit(solution)/shard_map/ppermute | solution.py:24
  70.3 8.6 %collective-permute-start.39 = (bf16[64,512]{0,1:T(8,128)(2,1)S(1)}, bf16[64,512]{0,1:T(8,128)(2,1)S(1)}, u32[]{:S(2)}, u32[]{:S(2)}) collective-permute-start(bf16[64,512]{0,1:T(8,128)(2,1)S(1)} %add_add_fusion), channel_id=1, source_target_pairs={{0,24},{8,0},{16,8},{24,16},{1,25},{9,1},{17,9},{25,17},{2,26},{10... | collective-permute-start | bytes 196616 | tf_op jit(solution)/shard_map/ppermute | solution.py:41
  73.8 12.9 %collective-permute-start.38 = (bf16[64,512]{0,1:T(8,128)(2,1)S(1)}, bf16[64,512]{0,1:T(8,128)(2,1)S(1)}, u32[]{:S(2)}, u32[]{:S(2)}) collective-permute-start(bf16[64,512]{0,1:T(8,128)(2,1)S(1)} %add_add_fusion), channel_id=1, source_target_pairs={{0,16},{8,24},{16,0},{24,8},{1,17},{9,25},{17,1},{25,9},{2,18},{10... | collective-permute-start | bytes 196616 | tf_op jit(solution)/shard_map/ppermute | solution.py:41
  73.8 12.9 %collective-permute-start.37 = (bf16[64,512]{0,1:T(8,128)(2,1)S(1)}, bf16[64,512]{0,1:T(8,128)(2,1)S(1)}, u32[]{:S(2)}, u32[]{:S(2)}) collective-permute-start(bf16[64,512]{0,1:T(8,128)(2,1)S(1)} %add_add_fusion), channel_id=1, source_target_pairs={{0,8},{8,16},{16,24},{24,0},{1,9},{9,17},{17,25},{25,1},{2,10},{10... | collective-permute-start | bytes 196616 | tf_op jit(solution)/shard_map/ppermute | solution.py:41
  74.9 15.3 %collective-permute-start.13 = (bf16[64,512]{0,1:T(8,128)(2,1)S(1)}, bf16[64,512]{0,1:T(8,128)(2,1)S(1)}, u32[]{:S(2)}, u32[]{:S(2)}) collective-permute-start(bf16[64,512]{0,1:T(8,128)(2,1)S(1)} %add_add_fusion.1), channel_id=1, source_target_pairs={{0,24},{8,0},{16,8},{24,16},{1,25},{9,1},{17,9},{25,17},{2,26},{10... | collective-permute-start | bytes 196616 | tf_op jit(solution)/shard_map/ppermute | solution.py:41
  78.2 18.0 %collective-permute-start.12 = (bf16[64,512]{0,1:T(8,128)(2,1)S(1)}, bf16[64,512]{0,1:T(8,128)(2,1)S(1)}, u32[]{:S(2)}, u32[]{:S(2)}) collective-permute-start(bf16[64,512]{0,1:T(8,128)(2,1)S(1)} %add_add_fusion.1), channel_id=1, source_target_pairs={{0,16},{8,24},{16,0},{24,8},{1,17},{9,25},{17,1},{25,9},{2,18},{10... | collective-permute-start | bytes 196616 | tf_op jit(solution)/shard_map/ppermute | solution.py:41
  78.9 17.4 %collective-permute-start.11 = (bf16[64,512]{0,1:T(8,128)(2,1)S(1)}, bf16[64,512]{0,1:T(8,128)(2,1)S(1)}, u32[]{:S(2)}, u32[]{:S(2)}) collective-permute-start(bf16[64,512]{0,1:T(8,128)(2,1)S(1)} %add_add_fusion.1), channel_id=1, source_target_pairs={{0,8},{8,16},{16,24},{24,0},{1,9},{9,17},{17,25},{25,1},{2,10},{10... | collective-permute-start | bytes 196616 | tf_op jit(solution)/shard_map/ppermute | solution.py:41
  104.1 22.1 %collective-permute-start.47 = (bf16[128,1792]{1,0:T(8,128)(2,1)S(1)}, bf16[128,1792]{1,0:T(8,128)(2,1)S(1)}, u32[]{:S(2)}, u32[]{:S(2)}) collective-permute-start(bf16[128,1792]{1,0:T(8,128)(2,1)S(1)} %get-tuple-element.21), channel_id=1, source_target_pairs={{0,8},{24,16},{1,9},{25,17},{2,10},{26,18},{3,11},{27,19},{4,12},{... | collective-permute-start | bytes 1376264 | tf_op jit(solution)/shard_map/ppermute | solution.py:72
  106.7 21.0 %collective-permute-start.49 = (bf16[128,1792]{1,0:T(8,128)(2,1)S(1)}, bf16[128,1792]{1,0:T(8,128)(2,1)S(1)}, u32[]{:S(2)}, u32[]{:S(2)}) collective-permute-start(bf16[128,1792]{1,0:T(8,128)(2,1)S(1)} %get-tuple-element.22), channel_id=1, source_target_pairs={{0,8},{24,16},{1,9},{25,17},{2,10},{26,18},{3,11},{27,19},{4,12},{... | collective-permute-start | bytes 1376264 | tf_op jit(solution)/shard_map/ppermute | solution.py:72
  113.9 23.4 %collective-permute-start.41 = (bf16[128,1792]{1,0:T(8,128)(2,1)S(1)}, bf16[128,1792]{1,0:T(8,128)(2,1)S(1)}, u32[]{:S(2)}, u32[]{:S(2)}) collective-permute-start(bf16[128,1792]{1,0:T(8,128)(2,1)S(1)} %get-tuple-element.19), channel_id=1, source_target_pairs={{0,8},{24,16},{1,9},{25,17},{2,10},{26,18},{3,11},{27,19},{4,12},{... | collective-permute-start | bytes 1376264 | tf_op jit(solution)/shard_map/ppermute | solution.py:72
  115.2 31.9 %collective-permute-start.43 = (bf16[128,1792]{1,0:T(8,128)(2,1)S(1)}, bf16[128,1792]{1,0:T(8,128)(2,1)S(1)}, u32[]{:S(2)}, u32[]{:S(2)}) collective-permute-start(bf16[128,1792]{1,0:T(8,128)(2,1)S(1)} %get-tuple-element.20), channel_id=1, source_target_pairs={{0,8},{24,16},{1,9},{25,17},{2,10},{26,18},{3,11},{27,19},{4,12},{... | collective-permute-start | bytes 1376264 | tf_op jit(solution)/shard_map/ppermute | solution.py:72
  124.9 32.1 %collective-permute-start.21 = (bf16[128,1792]{1,0:T(8,128)(2,1)S(1)}, bf16[128,1792]{1,0:T(8,128)(2,1)S(1)}, u32[]{:S(2)}, u32[]{:S(2)}) collective-permute-start(bf16[128,1792]{1,0:T(8,128)(2,1)S(1)} %get-tuple-element.17), channel_id=1, source_target_pairs={{0,8},{24,16},{1,9},{25,17},{2,10},{26,18},{3,11},{27,19},{4,12},{... | collective-permute-start | bytes 1376264 | tf_op jit(solution)/shard_map/ppermute | solution.py:72
  126.3 40.5 %collective-permute-start.23 = (bf16[128,1792]{1,0:T(8,128)(2,1)S(1)}, bf16[128,1792]{1,0:T(8,128)(2,1)S(1)}, u32[]{:S(2)}, u32[]{:S(2)}) collective-permute-start(bf16[128,1792]{1,0:T(8,128)(2,1)S(1)} %get-tuple-element.18), channel_id=1, source_target_pairs={{0,8},{24,16},{1,9},{25,17},{2,10},{26,18},{3,11},{27,19},{4,12},{... | collective-permute-start | bytes 1376264 | tf_op jit(solution)/shard_map/ppermute | solution.py:72
  127.7 48.9 %collective-permute-start.15 = (bf16[128,1792]{1,0:T(8,128)(2,1)S(1)}, bf16[128,1792]{1,0:T(8,128)(2,1)S(1)}, u32[]{:S(2)}, u32[]{:S(2)}) collective-permute-start(bf16[128,1792]{1,0:T(8,128)(2,1)S(1)} %get-tuple-element.15), channel_id=1, source_target_pairs={{0,8},{24,16},{1,9},{25,17},{2,10},{26,18},{3,11},{27,19},{4,12},{... | collective-permute-start | bytes 1376264 | tf_op jit(solution)/shard_map/ppermute | solution.py:72
  137.3 47.4 %collective-permute-start.17 = (bf16[128,1792]{1,0:T(8,128)(2,1)S(1)}, bf16[128,1792]{1,0:T(8,128)(2,1)S(1)}, u32[]{:S(2)}, u32[]{:S(2)}) collective-permute-start(bf16[128,1792]{1,0:T(8,128)(2,1)S(1)} %get-tuple-element.16), channel_id=1, source_target_pairs={{0,8},{24,16},{1,9},{25,17},{2,10},{26,18},{3,11},{27,19},{4,12},{... | collective-permute-start | bytes 1376264 | tf_op jit(solution)/shard_map/ppermute | solution.py:72
  147.2 41.5 %collective-permute-start.48 = (bf16[128,1792]{1,0:T(8,128)(2,1)S(1)}, bf16[128,1792]{1,0:T(8,128)(2,1)S(1)}, u32[]{:S(2)}, u32[]{:S(2)}) collective-permute-start(bf16[128,1792]{1,0:T(8,128)(2,1)S(1)} %add_convert_fusion.6), channel_id=1, source_target_pairs={{8,16},{16,8},{9,17},{17,9},{10,18},{18,10},{11,19},{19,11},{12,20... | collective-permute-start | bytes 1376264 | tf_op jit(solution)/shard_map/ppermute | solution.py:72
  157.0 28.6 %collective-permute-start.50 = (bf16[128,1792]{1,0:T(8,128)(2,1)S(1)}, bf16[128,1792]{1,0:T(8,128)(2,1)S(1)}, u32[]{:S(2)}, u32[]{:S(2)}) collective-permute-start(bf16[128,1792]{1,0:T(8,128)(2,1)S(1)} %add_convert_fusion.5), channel_id=1, source_target_pairs={{8,16},{16,8},{9,17},{17,9},{10,18},{18,10},{11,19},{19,11},{12,20... | collective-permute-start | bytes 1376264 | tf_op jit(solution)/shard_map/ppermute | solution.py:72
  166.8 49.4 %collective-permute-start.42 = (bf16[128,1792]{1,0:T(8,128)(2,1)S(1)}, bf16[128,1792]{1,0:T(8,128)(2,1)S(1)}, u32[]{:S(2)}, u32[]{:S(2)}) collective-permute-start(bf16[128,1792]{1,0:T(8,128)(2,1)S(1)} %add_convert_fusion.9), channel_id=1, source_target_pairs={{8,16},{16,8},{9,17},{17,9},{10,18},{18,10},{11,19},{19,11},{12,20... | collective-permute-start | bytes 1376264 | tf_op jit(solution)/shard_map/ppermute | solution.py:72
  176.7 9.7 %collective-permute-start.44 = (bf16[128,1792]{1,0:T(8,128)(2,1)S(1)}, bf16[128,1792]{1,0:T(8,128)(2,1)S(1)}, u32[]{:S(2)}, u32[]{:S(2)}) collective-permute-start(bf16[128,1792]{1,0:T(8,128)(2,1)S(1)} %add_convert_fusion.8), channel_id=1, source_target_pairs={{8,16},{16,8},{9,17},{17,9},{10,18},{18,10},{11,19},{19,11},{12,20... | collective-permute-start | bytes 1376264 | tf_op jit(solution)/shard_map/ppermute | solution.py:72
  184.7 37.6 %collective-permute-start.22 = (bf16[128,1792]{1,0:T(8,128)(2,1)S(1)}, bf16[128,1792]{1,0:T(8,128)(2,1)S(1)}, u32[]{:S(2)}, u32[]{:S(2)}) collective-permute-start(bf16[128,1792]{1,0:T(8,128)(2,1)S(1)} %add_convert_fusion.12), channel_id=1, source_target_pairs={{8,16},{16,8},{9,17},{17,9},{10,18},{18,10},{11,19},{19,11},{12,20... | collective-permute-start | bytes 1376264 | tf_op jit(solution)/shard_map/ppermute | solution.py:72
  186.4 31.1 %collective-permute-start.18 = (bf16[128,1792]{1,0:T(8,128)(2,1)S(1)}, bf16[128,1792]{1,0:T(8,128)(2,1)S(1)}, u32[]{:S(2)}, u32[]{:S(2)}) collective-permute-start(bf16[128,1792]{1,0:T(8,128)(2,1)S(1)} %add_convert_fusion.14), channel_id=1, source_target_pairs={{8,16},{16,8},{9,17},{17,9},{10,18},{18,10},{11,19},{19,11},{12,20... | collective-permute-start | bytes 1376264 | tf_op jit(solution)/shard_map/ppermute | solution.py:72
  187.2 38.1 %collective-permute-start.51 = (bf16[128,1792]{1,0:T(8,128)(2,1)S(1)}, bf16[128,1792]{1,0:T(8,128)(2,1)S(1)}, u32[]{:S(2)}, u32[]{:S(2)}) collective-permute-start(bf16[128,1792]{1,0:T(8,128)(2,1)S(1)} %get-tuple-element.13), channel_id=1, source_target_pairs={{16,24},{8,0},{17,25},{9,1},{18,26},{10,2},{19,27},{11,3},{20,28},... | collective-permute-start | bytes 1376264 | tf_op jit(solution)/shard_map/ppermute | solution.py:72
  188.7 38.0 %collective-permute-start.46 = (bf16[128,1792]{1,0:T(8,128)(2,1)S(1)}, bf16[128,1792]{1,0:T(8,128)(2,1)S(1)}, u32[]{:S(2)}, u32[]{:S(2)}) collective-permute-start(bf16[128,1792]{1,0:T(8,128)(2,1)S(1)} %get-tuple-element.14), channel_id=1, source_target_pairs={{0,8},{24,16},{1,9},{25,17},{2,10},{26,18},{3,11},{27,19},{4,12},{... | collective-permute-start | bytes 1376264 | tf_op jit(solution)/shard_map/ppermute | solution.py:72
  216.2 19.0 %collective-permute-start.45 = (bf16[128,1792]{1,0:T(8,128)(2,1)S(1)}, bf16[128,1792]{1,0:T(8,128)(2,1)S(1)}, u32[]{:S(2)}, u32[]{:S(2)}) collective-permute-start(bf16[128,1792]{1,0:T(8,128)(2,1)S(1)} %get-tuple-element.11), channel_id=1, source_target_pairs={{16,24},{8,0},{17,25},{9,1},{18,26},{10,2},{19,27},{11,3},{20,28},... | collective-permute-start | bytes 1376264 | tf_op jit(solution)/shard_map/ppermute | solution.py:72
  217.6 18.9 %collective-permute-start.40 = (bf16[128,1792]{1,0:T(8,128)(2,1)S(1)}, bf16[128,1792]{1,0:T(8,128)(2,1)S(1)}, u32[]{:S(2)}, u32[]{:S(2)}) collective-permute-start(bf16[128,1792]{1,0:T(8,128)(2,1)S(1)} %get-tuple-element.12), channel_id=1, source_target_pairs={{0,8},{24,16},{1,9},{25,17},{2,10},{26,18},{3,11},{27,19},{4,12},{... | collective-permute-start | bytes 1376264 | tf_op jit(solution)/shard_map/ppermute | solution.py:72
  222.3 19.4 %collective-permute-start.16 = (bf16[128,1792]{1,0:T(8,128)(2,1)S(1)}, bf16[128,1792]{1,0:T(8,128)(2,1)S(1)}, u32[]{:S(2)}, u32[]{:S(2)}) collective-permute-start(bf16[128,1792]{1,0:T(8,128)(2,1)S(1)} %add_convert_fusion.15), channel_id=1, source_target_pairs={{8,16},{16,8},{9,17},{17,9},{10,18},{18,10},{11,19},{19,11},{12,20... | collective-permute-start | bytes 1376264 | tf_op jit(solution)/shard_map/ppermute | solution.py:72
  225.4 19.7 %collective-permute-start.25 = (bf16[128,1792]{1,0:T(8,128)(2,1)S(1)}, bf16[128,1792]{1,0:T(8,128)(2,1)S(1)}, u32[]{:S(2)}, u32[]{:S(2)}) collective-permute-start(bf16[128,1792]{1,0:T(8,128)(2,1)S(1)} %get-tuple-element.9), channel_id=1, source_target_pairs={{16,24},{8,0},{17,25},{9,1},{18,26},{10,2},{19,27},{11,3},{20,28},... | collective-permute-start | bytes 1376264 | tf_op jit(solution)/shard_map/ppermute | solution.py:72
  226.7 18.4 %collective-permute-start.20 = (bf16[128,1792]{1,0:T(8,128)(2,1)S(1)}, bf16[128,1792]{1,0:T(8,128)(2,1)S(1)}, u32[]{:S(2)}, u32[]{:S(2)}) collective-permute-start(bf16[128,1792]{1,0:T(8,128)(2,1)S(1)} %get-tuple-element.10), channel_id=1, source_target_pairs={{0,8},{24,16},{1,9},{25,17},{2,10},{26,18},{3,11},{27,19},{4,12},{... | collective-permute-start | bytes 1376264 | tf_op jit(solution)/shard_map/ppermute | solution.py:72
  235.2 14.9 %collective-permute-start.19 = (bf16[128,1792]{1,0:T(8,128)(2,1)S(1)}, bf16[128,1792]{1,0:T(8,128)(2,1)S(1)}, u32[]{:S(2)}, u32[]{:S(2)}) collective-permute-start(bf16[128,1792]{1,0:T(8,128)(2,1)S(1)} %get-tuple-element.7), channel_id=1, source_target_pairs={{16,24},{8,0},{17,25},{9,1},{18,26},{10,2},{19,27},{11,3},{20,28},... | collective-permute-start | bytes 1376264 | tf_op jit(solution)/shard_map/ppermute | solution.py:72
  236.5 15.2 %collective-permute-start.14 = (bf16[128,1792]{1,0:T(8,128)(2,1)S(1)}, bf16[128,1792]{1,0:T(8,128)(2,1)S(1)}, u32[]{:S(2)}, u32[]{:S(2)}) collective-permute-start(bf16[128,1792]{1,0:T(8,128)(2,1)S(1)} %get-tuple-element.8), channel_id=1, source_target_pairs={{0,8},{24,16},{1,9},{25,17},{2,10},{26,18},{3,11},{27,19},{4,12},{... | collective-permute-start | bytes 1376264 | tf_op jit(solution)/shard_map/ppermute | solution.py:72
  (16 other events, 129.5 us)

commit v2 on v1

v2 whole, which is shorter than its diff:
```python
import functools

import jax
import jax.numpy as jnp
from jax import lax
from jax.experimental import pallas as pl
from jax.experimental.pallas import tpu as pltpu
from jax.sharding import PartitionSpec as P

SEG_ROWS = 128
SPLIT = (32, 96)

low_rank_scale = 0.5


def segment_slots(req_len, req_adapter, owner_slot, segs):
    reqs = req_len.shape[0]
    order = jnp.arange(reqs, dtype=jnp.int32)
    ends = jnp.sum(jnp.where(order[:, None] <= order[None, :], req_len[:, None], 0), axis=0)
    segment = jnp.arange(segs, dtype=jnp.int32)
    seg_request = jnp.sum((ends[None, :] <= segment[:, None]).astype(jnp.int32), axis=1)
    adapter = jnp.sum(jnp.where(seg_request[:, None] == order[None, :], req_adapter[None, :], 0), axis=1)
    ids = jnp.arange(owner_slot.shape[0], dtype=jnp.int32)
    return jnp.sum(jnp.where(adapter[:, None] == ids[None, :], owner_slot[None, :], 0), axis=1)


def held(seg_slot, first, count):
    local = seg_slot - first
    here = (local >= 0) & (local < count)
    return jnp.clip(local, 0, count - 1), here.astype(jnp.int32)


def swap(x, axis, size, mask):
    return lax.ppermute(x, axis, [(i, i ^ mask) for i in range(size)])


def gather_rows(x, ntp):
    chips = [x] + [swap(x, "tp", ntp, 2 * m) for m in range(1, ntp // 2)]
    pieces = []
    for piece in chips:
        pieces += [piece, swap(piece, "tp", ntp, 1)]
    return pieces


def sum_tp(x, ntp):
    x = x + swap(x, "tp", ntp, 1)
    return sum([swap(x, "tp", ntp, 2 * m) for m in range(1, ntp // 2)], x)


def sum_seq(x, nseq):
    parts = [lax.ppermute(x, "seq", [(i, (i + k) % nseq) for i in range(nseq)]) for k in range(1, nseq)]
    total = x.astype(jnp.float32)
    for part in parts:
        total = total + part.astype(jnp.float32)
    return total.astype(jnp.bfloat16)


def assemble_kernel(segs, tab_ref, *refs):
    pieces, (down_ref, x_ref, inner_ref) = refs[:segs], refs[segs:]
    me = tab_ref[2, 0]
    for n, piece in enumerate(pieces):
        x_ref[me ^ n] = piece[...]
    for pair in range(segs // 2):
        halves = []
        for k in (2 * pair, 2 * pair + 1):
            product = lax.dot_general(
                x_ref[k], down_ref[tab_ref[0, k]], (((1,), (1,)), ((), ())), preferred_element_type=jnp.float32
            )
            halves.append(product * tab_ref[1, k].astype(jnp.float32))
        inner_ref[pair] = jnp.concatenate(halves, axis=1).astype(jnp.bfloat16)


def assemble(pieces, down_pool, table):
    segs = len(pieces)
    rows, width = pieces[0].shape
    rank = down_pool.shape[1]
    vmem = pl.BlockSpec(memory_space=pltpu.VMEM)
    return pl.pallas_call(
        functools.partial(assemble_kernel, segs),
        out_shape=(
            jax.ShapeDtypeStruct((segs, rows, width), jnp.bfloat16),
            jax.ShapeDtypeStruct((segs // 2, rows, 2 * rank), jnp.bfloat16),
        ),
        in_specs=[pl.BlockSpec(memory_space=pltpu.SMEM)] + [vmem] * (segs + 1),
        out_specs=(vmem, vmem),
        compiler_params=pltpu.CompilerParams(vmem_limit_bytes=32 << 20),
        cost_estimate=pl.CostEstimate(
            flops=2 * segs * rows * width * rank, bytes_accessed=4 * segs * rows * width, transcendentals=0
        ),
    )(table, *pieces, down_pool)


def project_kernel(segs, nseq, tab_ref, x_ref, inner_ref, gate_ref, up_ref, *refs):
    ups, out_ref = refs[:segs], refs[segs]
    rows, width = x_ref.shape[1:]
    rank = inner_ref.shape[2] // 2
    each = segs // nseq
    x = x_ref[...].reshape(segs * rows, width)
    lows = []
    for k in range(segs):
        inner = inner_ref[k // 2][:, (k % 2) * rank:(k % 2 + 1) * rank]
        scale = low_rank_scale * tab_ref[1, k].astype(jnp.float32)
        lows.append((inner, scale))
    for which, weight in enumerate((gate_ref, up_ref)):
        part = jnp.dot(x, weight[...], preferred_element_type=jnp.float32)
        for k, (inner, scale) in enumerate(lows):
            low = jnp.dot(inner, ups[k][0, which], preferred_element_type=jnp.float32)
            term = part[k * rows:(k + 1) * rows] + scale * low
            out_ref[k // each, which, k % each] = term.astype(jnp.bfloat16)


def project(x, inner, gate_weight, up_weight, up_pool, table, nseq):
    segs, rows, width = x.shape
    columns = gate_weight.shape[1]
    rank = up_pool.shape[2]
    tile = 256 if columns % 256 == 0 else 128
    each = segs // nseq

    def up_spec(k):
        return pl.BlockSpec((1, 2, rank, tile), lambda n, tab: (tab[0, k], 0, 0, n))

    return pl.pallas_call(
        functools.partial(project_kernel, segs, nseq),
        out_shape=jax.ShapeDtypeStruct((nseq, 2, each, rows, columns), jnp.bfloat16),
        grid_spec=pltpu.PrefetchScalarGridSpec(
            num_scalar_prefetch=1,
            grid=(columns // tile,),
            in_specs=[
                pl.BlockSpec((segs, rows, width), lambda n, tab: (0, 0, 0)),
                pl.BlockSpec(inner.shape, lambda n, tab: (0, 0, 0)),
                pl.BlockSpec((width, tile), lambda n, tab: (0, n)),
                pl.BlockSpec((width, tile), lambda n, tab: (0, n)),
            ]
            + [up_spec(k) for k in range(segs)],
            out_specs=pl.BlockSpec((nseq, 2, each, rows, tile), lambda n, tab: (0, 0, 0, 0, n)),
        ),
        compiler_params=pltpu.CompilerParams(vmem_limit_bytes=40 << 20),
        cost_estimate=pl.CostEstimate(
            flops=4 * segs * rows * width * columns, bytes_accessed=4 * width * columns, transcendentals=0
        ),
    )(table, x, inner, gate_weight, up_weight, *([up_pool] * segs))


def after(x, gate):
    return lax.optimization_barrier((x, gate))[0]


def shards(tokens, gate_weight, up_weight, down_pool, up_pool, req_len, req_adapter, owner_slot):
    nseq = lax.axis_size("seq")
    ntp = lax.axis_size("tp")
    seg_slot = segment_slots(req_len, req_adapter, owner_slot, ntp)
    me = lax.axis_index("tp")
    down_slot, down_here = held(seg_slot, me * down_pool.shape[0], down_pool.shape[0])
    up_slot, up_here = held(seg_slot, lax.axis_index("seq") * up_pool.shape[0], up_pool.shape[0])
    down_table = jnp.stack([down_slot, down_here, jnp.full_like(down_slot, me)])
    up_table = jnp.stack([up_slot, up_here])
    columns = gate_weight.shape[1]
    out = []
    start = 0
    shared = sent = None
    for rows in SPLIT:
        block = tokens[start:start + rows]
        if shared is not None:
            block = after(block, shared)
        pieces = gather_rows(block, ntp)
        if sent is not None:
            pieces = list(after(tuple(pieces), sent))
        x, mine = assemble(pieces, down_pool, down_table)
        flat = mine.reshape(-1, mine.shape[2])
        shared = sum_tp(flat, ntp)
        inner = sum_seq(shared, nseq).reshape(mine.shape)
        sent = project(x, inner, gate_weight, up_weight, up_pool, up_table, nseq)
        total = lax.psum_scatter(sent, "seq", scatter_dimension=0, tiled=True)[0].astype(jnp.float32)
        out.append((jax.nn.silu(total[0]) * total[1]).astype(jnp.bfloat16))
        start += rows
    return jnp.concatenate(out, axis=1).reshape(-1, columns)


def solution(mesh):
    placed = (
        P("tp", "seq"),
        P("seq", "tp"),
        P("seq", "tp"),
        P("tp", None, "seq"),
        P("seq", None, None, "tp"),
        P(),
        P(),
        P(),
    )
    return jax.shard_map(
        shards, mesh=mesh, in_specs=placed, out_specs=P("seq", "tp"), check_vma=False
    )
```

time: 254 us -> 226 us (0.89)
  starting transfers between devices: 98.3 us -> 24.1 us
  waiting for transfers between devices: 84.9 us -> 141 us
  Pallas kernels: 0 us -> 31.2 us
  matrix products: 29.5 us -> 0 us
  local copies, waits for them, and re-layouts: 28.2 us -> 9.35 us
  between operations: 0.68 us -> 13.6 us
  other arithmetic: 11.7 us -> 6.8 us
    reduce_scatter x0 -> x2, waiting for transfers between devices: none -> 95.1 us  [shards(): lax.psum_scatter(sent, 'seq', scatter_dimension=0, tiled=True)[0]]
    ppermute x30 -> x6, starting transfers between devices: 79.1 us -> 7.49 us  [sum_seq(): lax.ppermute(x, 'seq', [(i, (i + k) % nseq) for i in range(nseq)])]
    ppermute x30 -> x6, waiting for transfers between devices: 74.7 us -> 15 us  [sum_seq(): lax.ppermute(x, 'seq', [(i, (i + k) % nseq) for i in range(nseq)])]
    pallas_call x0 -> x4, Pallas kernels: none -> 31.2 us  [the longest x2 28 us: project(): pl.pallas_call(functools.partial(project_kernel, segs, nseq), out_shape=j...]
    dot_general x10 -> x0, matrix products: 29.5 us -> none  [the longest x4 19.4 us: shards(): jnp.dot(flat, weight, preferred_element_type=jnp.float32)]
    ppermute x22, waiting for transfers between devices: 10.2 us -> 30.5 us  [swap(): return lax.ppermute(x, axis, [(i, i ^ mask) for i in range(size)])]
    dynamic_update_slice x15 -> x0, local copies, waits for them, and re-layouts: 12.3 us -> none  [the longest x7 6.25 us: gather_rows(): out = lax.dynamic_update_slice_in_dim(out, other[None], me ^ 2 * m ^ 1, 0)]
    unnamed x24 -> x12, local copies, waits for them, and re-layouts: 2.4 us -> 8.33 us
  transfers between devices with their start and end apart: 52 -> 30, of which waited for: 16 -> 22; matrix products, arithmetic and copies ran while one was open for 17% -> 2% of each run, Pallas kernels for 0% -> 9%
where the time goes in v2:
time: 226 us; the launch traced here: 225 us
  waiting for transfers between devices  141 us (62%)
  Pallas kernels  31.2 us (14%)
  starting transfers between devices  24.1 us (11%)
  between operations  13.6 us (6%)
  local copies, waits for them, and re-layouts  9.35 us (4%)
  other arithmetic  6.8 us (3%)
    reduce_scatter x2, waiting for transfers between devices, shards(): lax.psum_scatter(sent, 'seq', scatter_dimension=0, tiled=True)[0]  95.1 us
    ppermute x22, waiting for transfers between devices, swap(): return lax.ppermute(x, axis, [(i, i ^ mask) for i in range(size)])  30.5 us
    pallas_call x2, Pallas kernels, project(): pl.pallas_call(functools.partial(project_kernel, segs, nseq), out_shape=j...  28 us
    ppermute x22, starting transfers between devices, swap(): return lax.ppermute(x, axis, [(i, i ^ mask) for i in range(size)])  16.5 us
    ppermute x6, waiting for transfers between devices, sum_seq(): lax.ppermute(x, 'seq', [(i, (i + k) % nseq) for i in range(nseq)])  15 us
    unnamed x12, local copies, waits for them, and re-layouts  8.33 us
    ppermute x6, starting transfers between devices, sum_seq(): lax.ppermute(x, 'seq', [(i, (i + k) % nseq) for i in range(nseq)])  7.49 us
  transfers between devices with their start and end apart: 30, of which 22 were waited for; matrix products, arithmetic and copies ran while one was open for 2% of the time, Pallas kernels for 9%

profile of v2, /device:TPU:0, one launch (start us, length us, event | category | flops | bytes accessed | tf_op | source)
XLA Modules:
  0.0 225.5 jit_solution(1284140082580614528)
XLA Ops:
  6.5 0.9 slice.22.refs_0_
  7.5 4.0 %collective-permute-start.5 = (bf16[32,2048]{1,0:T(8,128)(2,1)S(1)}, bf16[32,2048]{1,0:T(8,128)(2,1)S(1)}, u32[]{:S(2)}, u32[]{:S(2)}) collective-permute-start(bf16[32,2048]{1,0:T(8,128)(2,1)S(1)} %slice.22.refs_0_), channel_id=1, source_target_pairs={{0,6},{1,7},{2,4},{3,5},{4,2},{5,3},{6,0},{7,1},{8,14},{9,15},{10,... | collective-permute-start | bytes 393224 | tf_op jit(solution)/shard_map/ppermute | solution.py:34
  11.4 0.5 collective-permute-start.3
  12.1 0.7 select_reduce_fusion.2
  13.0 0.7 select_reduce_fusion.1
  13.7 0.8 select_reduce_fusion
  14.6 0.8 collective-permute-done.5.refs_6_
  15.3 2.4 %collective-permute-done.3.refs_4_ = bf16[32,2048]{1,0:T(8,128)(2,1)S(1)} collective-permute-done((bf16[32,2048]{1,0:T(8,128)(2,1)S(1)}, bf16[32,2048]{1,0:T(8,128)(2,1)S(1)}, u32[]{:S(2)}, u32[]{:S(2)}) %collective-permute-start.3) | collective-permute-done | bytes 131104 | tf_op jit(solution)/shard_map/ppermute | solution.py:34
  18.3 0.8 collective-permute-done.4.refs_5_
  19.3 1.6 copy-done.2
  20.9 1.4 shard_map.82
  22.6 0.9 collective-permute-done.7
  23.5 1.8 collective-permute-start.10
  25.3 1.3 collective-permute-start.9
  27.1 1.4 collective-permute-done.10
  28.5 0.8 collective-permute-done.9
  29.3 1.3 collective-permute-done.8
  30.6 3.7 %collective-permute-start.13 = (bf16[128,128]{1,0:T(8,128)(2,1)S(1)}, bf16[128,128]{1,0:T(8,128)(2,1)S(1)}, u32[]{:S(2)}, u32[]{:S(2)}) collective-permute-start(bf16[128,128]{1,0:T(8,128)(2,1)S(1)} %add_add_fusion.1), channel_id=1, source_target_pairs={{0,24},{8,0},{16,8},{24,16},{1,25},{9,1},{17,9},{25,17},{2,26},{10... | collective-permute-start | bytes 98312 | tf_op jit(solution)/shard_map/ppermute | solution.py:51
  34.2 1.0 collective-permute-start.11
  35.3 0.6 collective-permute-done.13
  35.8 3.2 %collective-permute-done.12 = bf16[128,128]{1,0:T(8,128)(2,1)S(1)} collective-permute-done((bf16[128,128]{1,0:T(8,128)(2,1)S(1)}, bf16[128,128]{1,0:T(8,128)(2,1)S(1)}, u32[]{:S(2)}, u32[]{:S(2)}) %collective-permute-start.12) | collective-permute-done | bytes 32800 | tf_op jit(solution)/shard_map/ppermute | solution.py:51
  39.1 0.9 collective-permute-done.11
  40.0 3.1 %copy-done = bf16[2048,1792]{1,0:T(8,128)(2,1)S(1)} copy-done((bf16[2048,1792]{1,0:T(8,128)(2,1)S(1)}, bf16[2048,1792]{1,0:T(8,128)(2,1)}, u32[]{:S(2)}) %copy-start) | copy-done | bytes 7340056
  43.1 10.3 %shard_map.83 = bf16[4,2,2,32,1792]{4,3,2,1,0:T(8,128)(2,1)S(1)} custom-call(s32[2,8]{1,0:T(2,128)S(1)} %pad_add_fusion.tab_ref, bf16[8,32,2048]{2,1,0:T(8,128)(2,1)S(1)} %get-tuple-element.18.x_ref, bf16[4,32,128]{2,1,0:T(8,128)(2,1)S(1)} %bitcast.37, bf16[2048,1792]{1,0:T(8,128)(2,1)S(1)} %copy-done, bf16[2048,1792]{1,0:T(8,128)(2,1)} %up_ref.3, ...), custom_call_target="tpu_custom_call" | custom-call | flops 3758096384 | bytes 14680064 | tf_op jit(solution)/shard_map/pallas_call | solution.py:122
  53.4 1.2 copy-done.4
  54.8 1.6 collective-permute-start.19
  56.4 0.5 collective-permute-start.17
  56.9 1.5 collective-permute-start.15
  58.4 9.5 %collective-permute-done.19.refs_6_ = bf16[96,2048]{1,0:T(8,128)(2,1)S(1)} collective-permute-done((bf16[96,2048]{1,0:T(8,128)(2,1)S(1)}, bf16[96,2048]{1,0:T(8,128)(2,1)S(1)}, u32[]{:S(2)}, u32[]{:S(2)}) %collective-permute-start.19) | collective-permute-done | bytes 393248 | tf_op jit(solution)/shard_map/ppermute | solution.py:34
  67.8 4.9 %collective-permute-done.17.refs_4_ = bf16[96,2048]{1,0:T(8,128)(2,1)S(1)} collective-permute-done((bf16[96,2048]{1,0:T(8,128)(2,1)S(1)}, bf16[96,2048]{1,0:T(8,128)(2,1)S(1)}, u32[]{:S(2)}, u32[]{:S(2)}) %collective-permute-start.17) | collective-permute-done | bytes 393248 | tf_op jit(solution)/shard_map/ppermute | solution.py:34
  73.2 1.2 collective-permute-done.18.refs_5_
  74.4 0.6 collective-permute-done.16.refs_3_
  75.0 1.8 shard_map.84
  77.0 1.2 collective-permute-done.21
  78.2 1.4 collective-permute-start.24
  79.6 0.8 collective-permute-start.23
  80.4 1.4 collective-permute-start.22
  81.7 3.0 %collective-permute-done.24 = bf16[384,128]{1,0:T(8,128)(2,1)S(1)} collective-permute-done((bf16[384,128]{1,0:T(8,128)(2,1)S(1)}, bf16[384,128]{1,0:T(8,128)(2,1)S(1)}, u32[]{:S(2)}, u32[]{:S(2)}) %collective-permute-start.24) | collective-permute-done | bytes 98336 | tf_op jit(solution)/shard_map/ppermute | solution.py:34
  84.8 1.3 collective-permute-done.23
  87.0 1.9 collective-permute-start.25
  89.0 3.3 %collective-permute-done.27 = bf16[384,128]{1,0:T(8,128)(2,1)S(1)} collective-permute-done((bf16[384,128]{1,0:T(8,128)(2,1)S(1)}, bf16[384,128]{1,0:T(8,128)(2,1)S(1)}, u32[]{:S(2)}, u32[]{:S(2)}) %collective-permute-start.27) | collective-permute-done | bytes 98336 | tf_op jit(solution)/shard_map/ppermute | solution.py:51
  92.2 7.0 %collective-permute-done.26 = bf16[384,128]{1,0:T(8,128)(2,1)S(1)} collective-permute-done((bf16[384,128]{1,0:T(8,128)(2,1)S(1)}, bf16[384,128]{1,0:T(8,128)(2,1)S(1)}, u32[]{:S(2)}, u32[]{:S(2)}) %collective-permute-start.26) | collective-permute-done | bytes 98336 | tf_op jit(solution)/shard_map/ppermute | solution.py:51
  99.3 17.6 %shard_map.85 = bf16[4,2,2,96,1792]{4,3,2,1,0:T(8,128)(2,1)S(1)} custom-call(s32[2,8]{1,0:T(2,128)S(1)} %pad_add_fusion.tab_ref, bf16[8,96,2048]{2,1,0:T(8,128)(2,1)S(1)} %get-tuple-element.29.x_ref, bf16[4,96,128]{2,1,0:T(8,128)(2,1)S(1)} %bitcast.36, bf16[2048,1792]{1,0:T(8,128)(2,1)} %gate_ref.3, bf16[2048,1792]{1,0:T(8,128)(2,1)} %up_ref.3, ...), custom_call_target="tpu_custom_call" | custom-call | flops 11274289152 | bytes 14680064 | tf_op jit(solution)/shard_map/pallas_call | solution.py:122
  117.0 2.4 %copy-done.1 = bf16[4,2,2,96,1792]{4,3,2,1,0:T(8,128)(2,1)} copy-done((bf16[4,2,2,96,1792]{4,3,2,1,0:T(8,128)(2,1)}, bf16[4,2,2,96,1792]{4,3,2,1,0:T(8,128)(2,1)S(1)}, u32[]{:S(2)}) %copy-start.1) | copy-done | bytes 5505048
  119.4 1.1 convert_element_type.83
  120.7 95.0 %reduce-scatter.5.cloned.1.call-done = bf16[1,2,2,96,1792]{4,3,2,1,0:T(8,128)(2,1)} async-done(((bf16[4,2,2,96,1792]{4,3,2,1,0:T(8,128)(2,1)}), bf16[1,2,2,96,1792]{4,3,2,1,0:T(8,128)(2,1)}) %reduce-scatter.5.cloned.1.call-update) | async-done | bytes 1376272 | tf_op jit(solution)/shard_map/reduce_scatter | solution.py:173
  215.7 1.6 convert_element_type.90
  217.7 1.0 pad_maximum_fusion
  (52 shorter events, 4.3 us)
Async XLA Ops:
  6.5 112.9 %reduce-scatter.3.cloned.1.call-start = ((), (), s32[]{:S(2)}) async-start(), calls=%async_computation.2 | async-start | bytes 2293760 | tf_op jit(solution)/shard_map/reduce_scatter | solution.py:173
  7.5 7.9 %collective-permute-start.5 = (bf16[32,2048]{1,0:T(8,128)(2,1)S(1)}, bf16[32,2048]{1,0:T(8,128)(2,1)S(1)}, u32[]{:S(2)}, u32[]{:S(2)}) collective-permute-start(bf16[32,2048]{1,0:T(8,128)(2,1)S(1)} %slice.22.refs_0_), channel_id=1, source_target_pairs={{0,6},{1,7},{2,4},{3,5},{4,2},{5,3},{6,0},{7,1},{8,14},{9,15},{10,... | collective-permute-start | bytes 393224 | tf_op jit(solution)/shard_map/ppermute | solution.py:34
  11.4 6.3 %collective-permute-start.3 = (bf16[32,2048]{1,0:T(8,128)(2,1)S(1)}, bf16[32,2048]{1,0:T(8,128)(2,1)S(1)}, u32[]{:S(2)}, u32[]{:S(2)}) collective-permute-start(bf16[32,2048]{1,0:T(8,128)(2,1)S(1)} %slice.22.refs_0_), channel_id=1, source_target_pairs={{0,4},{1,5},{2,6},{3,7},{4,0},{5,1},{6,2},{7,3},{8,12},{9,13},{10,... | collective-permute-start | bytes 393224 | tf_op jit(solution)/shard_map/ppermute | solution.py:34
  11.9 6.0 %collective-permute-start.1 = (bf16[32,2048]{1,0:T(8,128)(2,1)S(1)}, bf16[32,2048]{1,0:T(8,128)(2,1)S(1)}, u32[]{:S(2)}, u32[]{:S(2)}) collective-permute-start(bf16[32,2048]{1,0:T(8,128)(2,1)S(1)} %slice.22.refs_0_), channel_id=1, source_target_pairs={{0,2},{1,3},{2,0},{3,1},{4,6},{5,7},{6,4},{7,5},{8,10},{9,11},{10,... | collective-permute-start | bytes 393224 | tf_op jit(solution)/shard_map/ppermute | solution.py:34
  12.1 6.3 %collective-permute-start = (bf16[32,2048]{1,0:T(8,128)(2,1)S(1)}, bf16[32,2048]{1,0:T(8,128)(2,1)S(1)}, u32[]{:S(2)}, u32[]{:S(2)}) collective-permute-start(bf16[32,2048]{1,0:T(8,128)(2,1)S(1)} %slice.22.refs_0_), channel_id=1, source_target_pairs={{0,1},{1,0},{2,3},{3,2},{4,5},{5,4},{6,7},{7,6},{8,9},{9,8},{10,11... | collective-permute-start | bytes 393224 | tf_op jit(solution)/shard_map/ppermute | solution.py:34
  15.3 3.0 %collective-permute-start.6 = (bf16[32,2048]{1,0:T(8,128)(2,1)S(1)}, bf16[32,2048]{1,0:T(8,128)(2,1)S(1)}, u32[]{:S(2)}, u32[]{:S(2)}) collective-permute-start(bf16[32,2048]{1,0:T(8,128)(2,1)S(1)} %collective-permute-done.5.refs_6_), channel_id=1, source_target_pairs={{0,1},{1,0},{2,3},{3,2},{4,5},{5,4},{6,7},{7,6},{8,9},{9,8},{10,11... | collective-permute-start | bytes 393224 | tf_op jit(solution)/shard_map/ppermute | solution.py:34
  17.7 1.3 collective-permute-start.4
  18.0 1.3 collective-permute-start.2
  19.3 1.6 copy-start.2
  22.3 1.2 collective-permute-start.7
  23.5 5.0 %collective-permute-start.10 = (bf16[128,128]{1,0:T(8,128)(2,1)S(1)}, bf16[128,128]{1,0:T(8,128)(2,1)S(1)}, u32[]{:S(2)}, u32[]{:S(2)}) collective-permute-start(bf16[128,128]{1,0:T(8,128)(2,1)S(1)} %bitcast_add_fusion.1), channel_id=1, source_target_pairs={{0,6},{1,7},{2,4},{3,5},{4,2},{5,3},{6,0},{7,1},{8,14},{9,15},{10,... | collective-permute-start | bytes 98312 | tf_op jit(solution)/shard_map/ppermute | solution.py:34
  25.3 3.9 %collective-permute-start.9 = (bf16[128,128]{1,0:T(8,128)(2,1)S(1)}, bf16[128,128]{1,0:T(8,128)(2,1)S(1)}, u32[]{:S(2)}, u32[]{:S(2)}) collective-permute-start(bf16[128,128]{1,0:T(8,128)(2,1)S(1)} %bitcast_add_fusion.1), channel_id=1, source_target_pairs={{0,4},{1,5},{2,6},{3,7},{4,0},{5,1},{6,2},{7,3},{8,12},{9,13},{10,... | collective-permute-start | bytes 98312 | tf_op jit(solution)/shard_map/ppermute | solution.py:34
  26.7 3.9 %collective-permute-start.8 = (bf16[128,128]{1,0:T(8,128)(2,1)S(1)}, bf16[128,128]{1,0:T(8,128)(2,1)S(1)}, u32[]{:S(2)}, u32[]{:S(2)}) collective-permute-start(bf16[128,128]{1,0:T(8,128)(2,1)S(1)} %bitcast_add_fusion.1), channel_id=1, source_target_pairs={{0,2},{1,3},{2,0},{3,1},{4,6},{5,7},{6,4},{7,5},{8,10},{9,11},{10,... | collective-permute-start | bytes 98312 | tf_op jit(solution)/shard_map/ppermute | solution.py:34
  30.6 5.3 %collective-permute-start.13 = (bf16[128,128]{1,0:T(8,128)(2,1)S(1)}, bf16[128,128]{1,0:T(8,128)(2,1)S(1)}, u32[]{:S(2)}, u32[]{:S(2)}) collective-permute-start(bf16[128,128]{1,0:T(8,128)(2,1)S(1)} %add_add_fusion.1), channel_id=1, source_target_pairs={{0,24},{8,0},{16,8},{24,16},{1,25},{9,1},{17,9},{25,17},{2,26},{10... | collective-permute-start | bytes 98312 | tf_op jit(solution)/shard_map/ppermute | solution.py:51
  34.2 4.8 %collective-permute-start.12 = (bf16[128,128]{1,0:T(8,128)(2,1)S(1)}, bf16[128,128]{1,0:T(8,128)(2,1)S(1)}, u32[]{:S(2)}, u32[]{:S(2)}) collective-permute-start(bf16[128,128]{1,0:T(8,128)(2,1)S(1)} %add_add_fusion.1), channel_id=1, source_target_pairs={{0,16},{8,24},{16,0},{24,8},{1,17},{9,25},{17,1},{25,9},{2,18},{10... | collective-permute-start | bytes 98312 | tf_op jit(solution)/shard_map/ppermute | solution.py:51
  34.2 5.7 %collective-permute-start.11 = (bf16[128,128]{1,0:T(8,128)(2,1)S(1)}, bf16[128,128]{1,0:T(8,128)(2,1)S(1)}, u32[]{:S(2)}, u32[]{:S(2)}) collective-permute-start(bf16[128,128]{1,0:T(8,128)(2,1)S(1)} %add_add_fusion.1), channel_id=1, source_target_pairs={{0,8},{8,16},{16,24},{24,0},{1,9},{9,17},{17,25},{25,1},{2,10},{10... | collective-permute-start | bytes 98312 | tf_op jit(solution)/shard_map/ppermute | solution.py:51
  40.0 3.1 %copy-start = (bf16[2048,1792]{1,0:T(8,128)(2,1)S(1)}, bf16[2048,1792]{1,0:T(8,128)(2,1)}, u32[]{:S(2)}) copy-start(bf16[2048,1792]{1,0:T(8,128)(2,1)} %gate_ref.3) | copy-start | bytes 22020100
  43.1 11.7 %copy-start.5 = (bf16[128,2048]{1,0:T(8,128)(2,1)S(1)}, bf16[128,2048]{1,0:T(8,128)(2,1)}, u32[]{:S(2)}) copy-start(bf16[128,2048]{1,0:T(8,128)(2,1)} %param.8) | copy-start | bytes 1572868
  53.4 1.2 copy-start.4
  54.7 20.3 %copy-start.3 = (bf16[8,64,2048]{2,1,0:T(8,128)(2,1)S(1)}, bf16[8,64,2048]{2,1,0:T(8,128)(2,1)}, u32[]{:S(2)}) copy-start(bf16[8,64,2048]{2,1,0:T(8,128)(2,1)} %refs_8_.3) | copy-start | bytes 6291460
  54.7 161.0 %reduce-scatter.5.cloned.1.call-start = ((), (), s32[]{:S(2)}) async-start(), calls=%async_computation.3 | async-start | bytes 6881280 | tf_op jit(solution)/shard_map/reduce_scatter | solution.py:173
  54.8 13.0 %collective-permute-start.19 = (bf16[96,2048]{1,0:T(8,128)(2,1)S(1)}, bf16[96,2048]{1,0:T(8,128)(2,1)S(1)}, u32[]{:S(2)}, u32[]{:S(2)}) collective-permute-start(bf16[96,2048]{1,0:T(8,128)(2,1)S(1)} %slice.25.refs_0_), channel_id=1, source_target_pairs={{0,6},{1,7},{2,4},{3,5},{4,2},{5,3},{6,0},{7,1},{8,14},{9,15},{10,... | collective-permute-start | bytes 1179656 | tf_op jit(solution)/shard_map/ppermute | solution.py:34
  56.4 16.3 %collective-permute-start.17 = (bf16[96,2048]{1,0:T(8,128)(2,1)S(1)}, bf16[96,2048]{1,0:T(8,128)(2,1)S(1)}, u32[]{:S(2)}, u32[]{:S(2)}) collective-permute-start(bf16[96,2048]{1,0:T(8,128)(2,1)S(1)} %slice.25.refs_0_), channel_id=1, source_target_pairs={{0,4},{1,5},{2,6},{3,7},{4,0},{5,1},{6,2},{7,3},{8,12},{9,13},{10,... | collective-permute-start | bytes 1179656 | tf_op jit(solution)/shard_map/ppermute | solution.py:34
  56.9 16.0 %collective-permute-start.15 = (bf16[96,2048]{1,0:T(8,128)(2,1)S(1)}, bf16[96,2048]{1,0:T(8,128)(2,1)S(1)}, u32[]{:S(2)}, u32[]{:S(2)}) collective-permute-start(bf16[96,2048]{1,0:T(8,128)(2,1)S(1)} %slice.25.refs_0_), channel_id=1, source_target_pairs={{0,2},{1,3},{2,0},{3,1},{4,6},{5,7},{6,4},{7,5},{8,10},{9,11},{10,... | collective-permute-start | bytes 1179656 | tf_op jit(solution)/shard_map/ppermute | solution.py:34
  58.4 14.9 %collective-permute-start.14 = (bf16[96,2048]{1,0:T(8,128)(2,1)S(1)}, bf16[96,2048]{1,0:T(8,128)(2,1)S(1)}, u32[]{:S(2)}, u32[]{:S(2)}) collective-permute-start(bf16[96,2048]{1,0:T(8,128)(2,1)S(1)} %slice.25.refs_0_), channel_id=1, source_target_pairs={{0,1},{1,0},{2,3},{3,2},{4,5},{5,4},{6,7},{7,6},{8,9},{9,8},{10,11... | collective-permute-start | bytes 1179656 | tf_op jit(solution)/shard_map/ppermute | solution.py:34
  67.8 5.4 %collective-permute-start.20 = (bf16[96,2048]{1,0:T(8,128)(2,1)S(1)}, bf16[96,2048]{1,0:T(8,128)(2,1)S(1)}, u32[]{:S(2)}, u32[]{:S(2)}) collective-permute-start(bf16[96,2048]{1,0:T(8,128)(2,1)S(1)} %collective-permute-done.19.refs_6_), channel_id=1, source_target_pairs={{0,1},{1,0},{2,3},{3,2},{4,5},{5,4},{6,7},{7,6},{8,9},{9,8},{10,11... | collective-permute-start | bytes 1179656 | tf_op jit(solution)/shard_map/ppermute | solution.py:34
  72.7 1.7 collective-permute-start.18
  72.8 2.2 collective-permute-start.16
  76.8 1.4 collective-permute-start.21
  78.2 6.6 %collective-permute-start.24 = (bf16[384,128]{1,0:T(8,128)(2,1)S(1)}, bf16[384,128]{1,0:T(8,128)(2,1)S(1)}, u32[]{:S(2)}, u32[]{:S(2)}) collective-permute-start(bf16[384,128]{1,0:T(8,128)(2,1)S(1)} %bitcast_add_fusion), channel_id=1, source_target_pairs={{0,6},{1,7},{2,4},{3,5},{4,2},{5,3},{6,0},{7,1},{8,14},{9,15},{10,... | collective-permute-start | bytes 294920 | tf_op jit(solution)/shard_map/ppermute | solution.py:34
  79.6 6.6 %collective-permute-start.23 = (bf16[384,128]{1,0:T(8,128)(2,1)S(1)}, bf16[384,128]{1,0:T(8,128)(2,1)S(1)}, u32[]{:S(2)}, u32[]{:S(2)}) collective-permute-start(bf16[384,128]{1,0:T(8,128)(2,1)S(1)} %bitcast_add_fusion), channel_id=1, source_target_pairs={{0,4},{1,5},{2,6},{3,7},{4,0},{5,1},{6,2},{7,3},{8,12},{9,13},{10,... | collective-permute-start | bytes 294920 | tf_op jit(solution)/shard_map/ppermute | solution.py:34
  80.4 5.8 %collective-permute-start.22 = (bf16[384,128]{1,0:T(8,128)(2,1)S(1)}, bf16[384,128]{1,0:T(8,128)(2,1)S(1)}, u32[]{:S(2)}, u32[]{:S(2)}) collective-permute-start(bf16[384,128]{1,0:T(8,128)(2,1)S(1)} %bitcast_add_fusion), channel_id=1, source_target_pairs={{0,2},{1,3},{2,0},{3,1},{4,6},{5,7},{6,4},{7,5},{8,10},{9,11},{10,... | collective-permute-start | bytes 294920 | tf_op jit(solution)/shard_map/ppermute | solution.py:34
  86.1 6.1 %collective-permute-start.27 = (bf16[384,128]{1,0:T(8,128)(2,1)S(1)}, bf16[384,128]{1,0:T(8,128)(2,1)S(1)}, u32[]{:S(2)}, u32[]{:S(2)}) collective-permute-start(bf16[384,128]{1,0:T(8,128)(2,1)S(1)} %add_add_fusion), channel_id=1, source_target_pairs={{0,24},{8,0},{16,8},{24,16},{1,25},{9,1},{17,9},{25,17},{2,26},{10... | collective-permute-start | bytes 294920 | tf_op jit(solution)/shard_map/ppermute | solution.py:51
  86.6 12.6 %collective-permute-start.26 = (bf16[384,128]{1,0:T(8,128)(2,1)S(1)}, bf16[384,128]{1,0:T(8,128)(2,1)S(1)}, u32[]{:S(2)}, u32[]{:S(2)}) collective-permute-start(bf16[384,128]{1,0:T(8,128)(2,1)S(1)} %add_add_fusion), channel_id=1, source_target_pairs={{0,16},{8,24},{16,0},{24,8},{1,17},{9,25},{17,1},{25,9},{2,18},{10... | collective-permute-start | bytes 294920 | tf_op jit(solution)/shard_map/ppermute | solution.py:51
  87.0 12.2 %collective-permute-start.25 = (bf16[384,128]{1,0:T(8,128)(2,1)S(1)}, bf16[384,128]{1,0:T(8,128)(2,1)S(1)}, u32[]{:S(2)}, u32[]{:S(2)}) collective-permute-start(bf16[384,128]{1,0:T(8,128)(2,1)S(1)} %add_add_fusion), channel_id=1, source_target_pairs={{0,8},{8,16},{16,24},{24,0},{1,9},{9,17},{17,25},{25,1},{2,10},{10... | collective-permute-start | bytes 294920 | tf_op jit(solution)/shard_map/ppermute | solution.py:51
  117.0 2.4 %copy-start.1 = (bf16[4,2,2,96,1792]{4,3,2,1,0:T(8,128)(2,1)}, bf16[4,2,2,96,1792]{4,3,2,1,0:T(8,128)(2,1)S(1)}, u32[]{:S(2)}) copy-start(bf16[4,2,2,96,1792]{4,3,2,1,0:T(8,128)(2,1)S(1)} %shard_map.85) | copy-start | bytes 16515076
Sparse Core Ops, SparseCore 0:
  54.8 38.2 reduce-scatter.2
  119.5 96.1 reduce-scatter.4

commit v3 on v2

v3 whole, which is shorter than its diff:
```python
import functools

import jax
import jax.numpy as jnp
from jax import lax
from jax.experimental import pallas as pl
from jax.experimental.pallas import tpu as pltpu
from jax.sharding import PartitionSpec as P

SEG_ROWS = 128
GROUPS = ((32,), (48, 48))

low_rank_scale = 0.5


def slots_of(segment, req_len, req_adapter, owner_slot):
    order = jnp.arange(req_len.shape[0], dtype=jnp.int32)
    ends = jnp.sum(jnp.where(order[:, None] <= order[None, :], req_len[:, None], 0), axis=0)
    seg_request = jnp.sum((ends[None, :] <= segment[:, None]).astype(jnp.int32), axis=1)
    adapter = jnp.sum(jnp.where(seg_request[:, None] == order[None, :], req_adapter[None, :], 0), axis=1)
    ids = jnp.arange(owner_slot.shape[0], dtype=jnp.int32)
    return jnp.sum(jnp.where(adapter[:, None] == ids[None, :], owner_slot[None, :], 0), axis=1)


def chunk_of(slot, nseq):
    me = lax.axis_index("seq")
    half = me < nseq // 2
    far = jnp.where(half, nseq - 1 - me, me)
    near = slot - far
    far_chunk = jnp.where(half, nseq - 1 - slot, slot)
    near_chunk = jnp.where(half, near, nseq - 1 - near)
    chunk = jnp.where(slot < far, far_chunk, near_chunk)
    return jnp.where(slot == nseq - 1, me, chunk)


def held(seg_slot, first, count):
    local = seg_slot - first
    here = (local >= 0) & (local < count)
    return jnp.clip(local, 0, count - 1), here.astype(jnp.int32)


def swap(x, axis, size, mask):
    return lax.ppermute(x, axis, [(i, i ^ mask) for i in range(size)])


def gather_rows(x, ntp):
    chips = [x] + [swap(x, "tp", ntp, 2 * m) for m in range(1, ntp // 2)]
    pieces = []
    for piece in chips:
        pieces += [piece, swap(piece, "tp", ntp, 1)]
    return pieces


def sum_tp(x, ntp):
    x = x + swap(x, "tp", ntp, 1)
    return sum([swap(x, "tp", ntp, 2 * m) for m in range(1, ntp // 2)], x)


def sum_seq(x, nseq):
    parts = [lax.ppermute(x, "seq", [(i, (i + k) % nseq) for i in range(nseq)]) for k in range(1, nseq)]
    total = x.astype(jnp.float32)
    for part in parts:
        total = total + part.astype(jnp.float32)
    return total.astype(jnp.bfloat16)


def assemble_kernel(segs, tab_ref, *refs):
    pieces, (down_ref, x_ref, inner_ref) = refs[:segs], refs[segs:]
    me = tab_ref[2, 0]
    for n, piece in enumerate(pieces):
        x_ref[tab_ref[3, me ^ n]] = piece[...]
    for pair in range(segs // 2):
        halves = []
        for k in (2 * pair, 2 * pair + 1):
            product = lax.dot_general(
                x_ref[tab_ref[3, k]], down_ref[tab_ref[0, k]], (((1,), (1,)), ((), ())), preferred_element_type=jnp.float32
            )
            halves.append(product * tab_ref[1, k].astype(jnp.float32))
        inner_ref[pair] = jnp.concatenate(halves, axis=1).astype(jnp.bfloat16)


def assemble(pieces, down_pool, table):
    segs = len(pieces)
    rows, width = pieces[0].shape
    rank = down_pool.shape[1]
    vmem = pl.BlockSpec(memory_space=pltpu.VMEM)
    return pl.pallas_call(
        functools.partial(assemble_kernel, segs),
        out_shape=(
            jax.ShapeDtypeStruct((segs, rows, width), jnp.bfloat16),
            jax.ShapeDtypeStruct((segs // 2, rows, 2 * rank), jnp.bfloat16),
        ),
        in_specs=[pl.BlockSpec(memory_space=pltpu.SMEM)] + [vmem] * (segs + 1),
        out_specs=(vmem, vmem),
        compiler_params=pltpu.CompilerParams(vmem_limit_bytes=32 << 20),
        cost_estimate=pl.CostEstimate(
            flops=2 * segs * rows * width * rank, bytes_accessed=4 * segs * rows * width, transcendentals=0
        ),
    )(table, *pieces, down_pool)


def project_kernel(segs, nseq, tab_ref, x_ref, inner_ref, gate_ref, up_ref, *refs):
    ups, outs, low_ref = refs[:segs], refs[segs:segs + nseq], refs[segs + nseq]
    rows, width = x_ref.shape[1:]
    lanes = inner_ref.shape[2]
    rank = lanes // 2
    each = segs // nseq

    @pl.when(pl.program_id(0) == 0)
    def _():
        low_ref[...] = jnp.zeros_like(low_ref)
        lane = lax.broadcasted_iota(jnp.int32, (rows, lanes), 1)
        for k in range(segs):
            seg = tab_ref[2, k]
            mine = (lane // rank == seg % 2) & (tab_ref[1, k] == 1)
            inner = jnp.where(mine, inner_ref[seg // 2].astype(jnp.float32), 0.0) * low_rank_scale
            turned = jnp.where(seg % 2 == k % 2, inner, pltpu.roll(inner, rank, 1))
            low_ref[pl.ds(k * rows, rows), pl.ds(k // 2 * lanes, lanes)] = turned.astype(jnp.bfloat16)

    x = x_ref[...].reshape(segs * rows, width)
    for which, weight in enumerate((gate_ref, up_ref)):
        part = jnp.dot(x, weight[...], preferred_element_type=jnp.float32)
        stacked = jnp.concatenate([up[0, which] for up in ups], axis=0)
        part = part + jnp.dot(low_ref[...], stacked, preferred_element_type=jnp.float32)
        part = part.astype(jnp.bfloat16)
        for k in range(segs):
            outs[k // each][which, k % each] = part[k * rows:(k + 1) * rows]


def project(x, inner, index, rows, gate_weight, up_weight, up_pool, table, nseq):
    segs, _, width = x.shape
    columns = gate_weight.shape[1]
    rank = up_pool.shape[2]
    tile = 256 if columns % 256 == 0 else 128
    each = segs // nseq

    def up_spec(k):
        return pl.BlockSpec((1, 2, rank, tile), lambda n, tab: (tab[0, k], 0, 0, n))

    return pl.pallas_call(
        functools.partial(project_kernel, segs, nseq),
        out_shape=[jax.ShapeDtypeStruct((2, each, rows, columns), jnp.bfloat16)] * nseq,
        grid_spec=pltpu.PrefetchScalarGridSpec(
            num_scalar_prefetch=1,
            grid=(columns // tile,),
            in_specs=[
                pl.BlockSpec((segs, rows, width), lambda n, tab: (0, index, 0)),
                pl.BlockSpec((inner.shape[0], rows, inner.shape[2]), lambda n, tab: (0, index, 0)),
                pl.BlockSpec((width, tile), lambda n, tab: (0, n)),
                pl.BlockSpec((width, tile), lambda n, tab: (0, n)),
            ]
            + [up_spec(k) for k in range(segs)],
            out_specs=[pl.BlockSpec((2, each, rows, tile), lambda n, tab: (0, 0, 0, n))] * nseq,
            scratch_shapes=[pltpu.VMEM((segs * rows, segs * rank), jnp.bfloat16)],
        ),
        compiler_params=pltpu.CompilerParams(vmem_limit_bytes=40 << 20),
        cost_estimate=pl.CostEstimate(
            flops=4 * segs * rows * width * columns, bytes_accessed=4 * width * columns, transcendentals=0
        ),
    )(table, x, inner, gate_weight, up_weight, *([up_pool] * segs))


def add(x, y):
    return (x.astype(jnp.float32) + y.astype(jnp.float32)).astype(x.dtype)


def scatter_line(own, nseq):
    last = nseq - 2
    arrived = {}
    for step in range(nseq - 1):
        for level in range(step + 1):
            slot = step - level if level < nseq // 2 else step
            send = own[slot]
            if level > 0:
                send = add(send, arrived[level - 1, step - 1])
            pairs = [(level, level + 1), (nseq - 1 - level, nseq - 2 - level)]
            arrived[level, step] = lax.ppermute(send, "seq", pairs)
    total = own[nseq - 1].astype(jnp.float32)
    for level in range(nseq - 1):
        total = total + arrived[level, last].astype(jnp.float32)
    return total


def after(x, gate):
    return lax.optimization_barrier((x, gate))[0]


def shards(tokens, gate_weight, up_weight, down_pool, up_pool, req_len, req_adapter, owner_slot):
    nseq = lax.axis_size("seq")
    ntp = lax.axis_size("tp")
    each = ntp // nseq
    me = lax.axis_index("tp")
    place = jnp.arange(ntp, dtype=jnp.int32)
    ordered = chunk_of(place // each, nseq) * each + place % each
    position = jnp.sum(jnp.where(ordered[:, None] == place[None, :], place[:, None], 0), axis=0)
    down_slot, down_here = held(
        slots_of(place, req_len, req_adapter, owner_slot), me * down_pool.shape[0], down_pool.shape[0]
    )
    up_slot, up_here = held(
        slots_of(ordered, req_len, req_adapter, owner_slot),
        lax.axis_index("seq") * up_pool.shape[0],
        up_pool.shape[0],
    )
    down_table = jnp.stack([down_slot, down_here, jnp.full_like(down_slot, me), position])
    up_table = jnp.stack([up_slot, up_here, ordered])
    columns = gate_weight.shape[1]
    out = []
    start = 0
    shared = sent = None
    for group in GROUPS:
        block = tokens[start:start + sum(group)]
        if shared is not None:
            block = after(block, shared)
        pieces = gather_rows(block, ntp)
        if sent is not None:
            pieces = list(after(tuple(pieces), sent[0]))
        x, mine = assemble(pieces, down_pool, down_table)
        flat = mine.reshape(-1, mine.shape[2])
        shared = sum_tp(flat, ntp)
        inner = sum_seq(shared, nseq).reshape(mine.shape)
        for index, rows in enumerate(group):
            sent = project(x, inner, index, rows, gate_weight, up_weight, up_pool, up_table, nseq)
            total = scatter_line(sent, nseq)
            out.append((jax.nn.silu(total[0]) * total[1]).astype(jnp.bfloat16))
        start += sum(group)
    return jnp.concatenate(out, axis=1).reshape(-1, columns)


def solution(mesh):
    placed = (
        P("tp", "seq"),
        P("seq", "tp"),
        P("seq", "tp"),
        P("tp", None, "seq"),
        P("seq", None, None, "tp"),
        P(),
        P(),
        P(),
    )
    return jax.shard_map(
        shards, mesh=mesh, in_specs=placed, out_specs=P("seq", "tp"), check_vma=False
    )
```

time: 226 us -> 229 us (1.013)
  starting transfers between devices: 24.1 us -> 54.5 us
  waiting for transfers between devices: 141 us -> 120 us
  between operations: 13.6 us -> 0.51 us
  Pallas kernels: 31.2 us -> 40.1 us
  local copies, waits for them, and re-layouts: 9.35 us -> 5.7 us
    ppermute x0 -> x18, waiting for transfers between devices: none -> 100 us  [scatter_line(): arrived[level, step] = lax.ppermute(send, 'seq', pairs)]
    reduce_scatter x2 -> x0, waiting for transfers between devices: 95.1 us -> none  [shards(): lax.psum_scatter(sent, 'seq', scatter_dimension=0, tiled=True)[0]]
    ppermute x0 -> x18, starting transfers between devices: none -> 26 us  [scatter_line(): arrived[level, step] = lax.ppermute(send, 'seq', pairs)]
    ppermute x22, waiting for transfers between devices: 30.5 us -> 12.2 us  [swap(): return lax.ppermute(x, axis, [(i, i ^ mask) for i in range(size)])]
    pallas_call x2 -> x3, Pallas kernels: 28 us -> 36.9 us  [project(): pl.pallas_call(functools.partial(project_kernel, segs, nseq), out_shape=[...]
    ppermute x6, waiting for transfers between devices: 15 us -> 7.85 us  [sum_seq(): lax.ppermute(x, 'seq', [(i, (i + k) % nseq) for i in range(nseq)])]
    unnamed x12 -> x10, local copies, waits for them, and re-layouts: 8.33 us -> 4.68 us
    ppermute x6, starting transfers between devices: 7.49 us -> 10.6 us  [sum_seq(): lax.ppermute(x, 'seq', [(i, (i + k) % nseq) for i in range(nseq)])]
  transfers between devices with their start and end apart: 30 -> 46, of which waited for: 22 -> 17; matrix products, arithmetic and copies ran while one was open for 2% -> 2% of each run, Pallas kernels for 9% -> 17%
where the time goes in v3:
time: 229 us; the launch traced here: 228 us
  waiting for transfers between devices  120 us (52%)
  starting transfers between devices  54.5 us (24%)
  Pallas kernels  40.1 us (18%)
  other arithmetic  6.55 us (3%)
  local copies, waits for them, and re-layouts  5.7 us (2%)
    ppermute x18, waiting for transfers between devices, scatter_line(): arrived[level, step] = lax.ppermute(send, 'seq', pairs)  100 us
    pallas_call x3, Pallas kernels, project(): pl.pallas_call(functools.partial(project_kernel, segs, nseq), out_shape=[...  36.9 us
    ppermute x18, starting transfers between devices, scatter_line(): arrived[level, step] = lax.ppermute(send, 'seq', pairs)  26 us
    ppermute x22, starting transfers between devices, swap(): return lax.ppermute(x, axis, [(i, i ^ mask) for i in range(size)])  18 us
    ppermute x22, waiting for transfers between devices, swap(): return lax.ppermute(x, axis, [(i, i ^ mask) for i in range(size)])  12.2 us
    ppermute x6, starting transfers between devices, sum_seq(): lax.ppermute(x, 'seq', [(i, (i + k) % nseq) for i in range(nseq)])  10.6 us
    ppermute x6, waiting for transfers between devices, sum_seq(): lax.ppermute(x, 'seq', [(i, (i + k) % nseq) for i in range(nseq)])  7.85 us
    unnamed x10, local copies, waits for them, and re-layouts  4.68 us
  transfers between devices with their start and end apart: 46, of which 17 were waited for; matrix products, arithmetic and copies ran while one was open for 2% of the time, Pallas kernels for 17%

profile of v3, /device:TPU:0, one launch (start us, length us, event | category | flops | bytes accessed | tf_op | source)
XLA Modules:
  0.0 227.6 jit_solution(6549777888667793003)
XLA Ops:
  0.0 0.9 slice.24.refs_0_
  0.9 3.0 %collective-permute-start.1 = (bf16[32,2048]{1,0:T(8,128)(2,1)S(1)}, bf16[32,2048]{1,0:T(8,128)(2,1)S(1)}, u32[]{:S(2)}, u32[]{:S(2)}) collective-permute-start(bf16[32,2048]{1,0:T(8,128)(2,1)S(1)} %slice.24.refs_0_), channel_id=1, source_target_pairs={{0,2},{1,3},{2,0},{3,1},{4,6},{5,7},{6,4},{7,5},{8,10},{9,11},{10,... | collective-permute-start | bytes 393224 | tf_op jit(solution)/shard_map/ppermute | solution.py:43
  3.9 1.5 collective-permute-start.3
  8.7 3.0 %collective-permute-done.3.refs_4_ = bf16[32,2048]{1,0:T(8,128)(2,1)S(1)} collective-permute-done((bf16[32,2048]{1,0:T(8,128)(2,1)S(1)}, bf16[32,2048]{1,0:T(8,128)(2,1)S(1)}, u32[]{:S(2)}, u32[]{:S(2)}) %collective-permute-start.3) | collective-permute-done | bytes 131104 | tf_op jit(solution)/shard_map/ppermute | solution.py:43
  13.2 1.6 copy-done.2
  14.8 1.4 shard_map.82
  16.5 0.9 collective-permute-done.7
  17.4 1.5 collective-permute-start.10
  19.0 1.5 collective-permute-start.8
  21.0 1.6 collective-permute-done.10
  22.9 1.5 collective-permute-done.9
  24.4 1.6 collective-permute-start.11
  26.0 2.6 %collective-permute-start.12 = (bf16[128,128]{1,0:T(8,128)(2,1)S(1)}, bf16[128,128]{1,0:T(8,128)(2,1)S(1)}, u32[]{:S(2)}, u32[]{:S(2)}) collective-permute-start(bf16[128,128]{1,0:T(8,128)(2,1)S(1)} %add_add_fusion.1), channel_id=1, source_target_pairs={{0,16},{8,24},{16,0},{24,8},{1,17},{9,25},{17,1},{25,9},{2,18},{10... | collective-permute-start | bytes 98312 | tf_op jit(solution)/shard_map/ppermute | solution.py:60
  28.6 1.3 collective-permute-start.13
  30.6 1.0 collective-permute-start.23
  31.6 1.9 collective-permute-start.25
  33.6 3.1 %copy-done = bf16[2048,1792]{1,0:T(8,128)(2,1)S(1)} copy-done((bf16[2048,1792]{1,0:T(8,128)(2,1)S(1)}, bf16[2048,1792]{1,0:T(8,128)(2,1)}, u32[]{:S(2)}) %copy-start) | copy-done | bytes 7340056
  36.7 11.4 %shard_map.83 = (bf16[2,2,32,1792]{3,2,1,0:T(8,128)(2,1)S(1)}, bf16[2,2,32,1792]{3,2,1,0:T(8,128)(2,1)S(1)}, bf16[2,2,32,1792]{3,2,1,0:T(8,128)(2,1)S(1)}, bf16[2,2,32,1792]{3,2,1,0:T(8,128)(2,1)S(1)}) custom-call(s32[3,8]{1,0:T(4,128)S(1)} %pad_add_fusion.tab_ref, bf16[8,32,2048]{2,1,0:T(8,128)(2,1)S(1)} %get-tuple-element.30.x_ref, ...), custom_call_target="tpu_custom_call" | custom-call | flops 3758096384 | bytes 14680064 | tf_op jit(solution)/shard_map/pallas_call | solution.py:140
  48.1 2.3 %collective-permute-start.17 = (bf16[2,2,32,1792]{3,2,1,0:T(8,128)(2,1)S(1)}, bf16[2,2,32,1792]{3,2,1,0:T(8,128)(2,1)S(1)}, u32[]{:S(2)}, u32[]{:S(2)}) collective-permute-start(bf16[2,2,32,1792]{3,2,1,0:T(8,128)(2,1)S(1)} %get-tuple-element.35), channel_id=1, source_target_pairs={{0,8},{24,16},{1,9},{25,17},{2,10},{26,18},{3,11},{27,19},{4,12},{... | collective-permute-start | bytes 1376264 | tf_op jit(solution)/shard_map/ppermute | solution.py:177
  52.2 1.3 collective-permute-start.15
  53.5 1.3 collective-permute-start.14
  54.9 1.8 shard_map.84
  56.9 3.5 %collective-permute-done.17 = bf16[2,2,32,1792]{3,2,1,0:T(8,128)(2,1)S(1)} collective-permute-done((bf16[2,2,32,1792]{3,2,1,0:T(8,128)(2,1)S(1)}, bf16[2,2,32,1792]{3,2,1,0:T(8,128)(2,1)S(1)}, u32[]{:S(2)}, u32[]{:S(2)}) %collective-permute-start.17) | collective-permute-done | bytes 458784 | tf_op jit(solution)/shard_map/ppermute | solution.py:177
  61.3 1.0 collective-permute-start.28
  62.3 1.1 collective-permute-start.29
  63.4 6.8 %collective-permute-done.15 = bf16[2,2,32,1792]{3,2,1,0:T(8,128)(2,1)S(1)} collective-permute-done((bf16[2,2,32,1792]{3,2,1,0:T(8,128)(2,1)S(1)}, bf16[2,2,32,1792]{3,2,1,0:T(8,128)(2,1)S(1)}, u32[]{:S(2)}, u32[]{:S(2)}) %collective-permute-start.15) | collective-permute-done | bytes 458784 | tf_op jit(solution)/shard_map/ppermute | solution.py:177
  70.3 1.5 collective-permute-start.30
  72.6 3.2 %collective-permute-done.30 = bf16[384,128]{1,0:T(8,128)(2,1)S(1)} collective-permute-done((bf16[384,128]{1,0:T(8,128)(2,1)S(1)}, bf16[384,128]{1,0:T(8,128)(2,1)S(1)}, u32[]{:S(2)}, u32[]{:S(2)}) %collective-permute-start.30) | collective-permute-done | bytes 98336 | tf_op jit(solution)/shard_map/ppermute | solution.py:43
  75.8 2.5 %collective-permute-start.31 = (bf16[384,128]{1,0:T(8,128)(2,1)S(1)}, bf16[384,128]{1,0:T(8,128)(2,1)S(1)}, u32[]{:S(2)}, u32[]{:S(2)}) collective-permute-start(bf16[384,128]{1,0:T(8,128)(2,1)S(1)} %add_add_fusion), channel_id=1, source_target_pairs={{0,8},{8,16},{16,24},{24,0},{1,9},{9,17},{17,25},{25,1},{2,10},{10... | collective-permute-start | bytes 294920 | tf_op jit(solution)/shard_map/ppermute | solution.py:60
  78.3 2.4 %collective-permute-start.33 = (bf16[384,128]{1,0:T(8,128)(2,1)S(1)}, bf16[384,128]{1,0:T(8,128)(2,1)S(1)}, u32[]{:S(2)}, u32[]{:S(2)}) collective-permute-start(bf16[384,128]{1,0:T(8,128)(2,1)S(1)} %add_add_fusion), channel_id=1, source_target_pairs={{0,24},{8,0},{16,8},{24,16},{1,25},{9,1},{17,9},{25,17},{2,26},{10... | collective-permute-start | bytes 294920 | tf_op jit(solution)/shard_map/ppermute | solution.py:60
  80.9 1.5 collective-permute-done.31
  82.4 1.3 collective-permute-start.19
  83.7 6.3 %collective-permute-done.32 = bf16[384,128]{1,0:T(8,128)(2,1)S(1)} collective-permute-done((bf16[384,128]{1,0:T(8,128)(2,1)S(1)}, bf16[384,128]{1,0:T(8,128)(2,1)S(1)}, u32[]{:S(2)}, u32[]{:S(2)}) %collective-permute-start.32) | collective-permute-done | bytes 98336 | tf_op jit(solution)/shard_map/ppermute | solution.py:60
  90.1 12.8 %shard_map.85 = (bf16[2,2,48,1792]{3,2,1,0:T(8,128)(2,1)S(1)}, bf16[2,2,48,1792]{3,2,1,0:T(8,128)(2,1)S(1)}, bf16[2,2,48,1792]{3,2,1,0:T(8,128)(2,1)S(1)}, bf16[2,2,48,1792]{3,2,1,0:T(8,128)(2,1)S(1)}) custom-call(s32[3,8]{1,0:T(4,128)S(1)} %pad_add_fusion.tab_ref, bf16[8,96,2048]{2,1,0:T(8,128)(2,1)S(1)} %get-tuple-element.45.x_ref, ...), custom_call_target="tpu_custom_call" | custom-call | flops 5637144576 | bytes 14680064 | tf_op jit(solution)/shard_map/pallas_call | solution.py:140
  102.9 3.2 %collective-permute-start.35 = (bf16[2,2,48,1792]{3,2,1,0:T(8,128)(2,1)S(1)}, bf16[2,2,48,1792]{3,2,1,0:T(8,128)(2,1)S(1)}, u32[]{:S(2)}, u32[]{:S(2)}) collective-permute-start(bf16[2,2,48,1792]{3,2,1,0:T(8,128)(2,1)S(1)} %get-tuple-element.49), channel_id=1, source_target_pairs={{0,8},{24,16},{1,9},{25,17},{2,10},{26,18},{3,11},{27,19},{4,12},{... | collective-permute-start | bytes 2064392 | tf_op jit(solution)/shard_map/ppermute | solution.py:177
  106.1 1.3 collective-permute-start.37
  107.5 12.8 %shard_map.86 = (bf16[2,2,48,1792]{3,2,1,0:T(8,128)(2,1)S(1)}, bf16[2,2,48,1792]{3,2,1,0:T(8,128)(2,1)S(1)}, bf16[2,2,48,1792]{3,2,1,0:T(8,128)(2,1)S(1)}, bf16[2,2,48,1792]{3,2,1,0:T(8,128)(2,1)S(1)}) custom-call(s32[3,8]{1,0:T(4,128)S(1)} %pad_add_fusion.tab_ref, bf16[8,96,2048]{2,1,0:T(8,128)(2,1)S(1)} %get-tuple-element.45.x_ref, ...), custom_call_target="tpu_custom_call" | custom-call | flops 5637144576 | bytes 14680064 | tf_op jit(solution)/shard_map/pallas_call | solution.py:140
  120.3 1.3 collective-permute-start.34
  121.6 1.3 collective-permute-start.41
  123.0 1.3 collective-permute-start.43
  124.7 12.0 %collective-permute-done.37 = bf16[2,2,48,1792]{3,2,1,0:T(8,128)(2,1)S(1)} collective-permute-done((bf16[2,2,48,1792]{3,2,1,0:T(8,128)(2,1)S(1)}, bf16[2,2,48,1792]{3,2,1,0:T(8,128)(2,1)S(1)}, u32[]{:S(2)}, u32[]{:S(2)}) %collective-permute-start.37) | collective-permute-done | bytes 688160 | tf_op jit(solution)/shard_map/ppermute | solution.py:177
  136.7 4.4 %collective-permute-start.40 = (bf16[2,2,48,1792]{3,2,1,0:T(8,128)(2,1)S(1)}, bf16[2,2,48,1792]{3,2,1,0:T(8,128)(2,1)S(1)}, u32[]{:S(2)}, u32[]{:S(2)}) collective-permute-start(bf16[2,2,48,1792]{3,2,1,0:T(8,128)(2,1)S(1)} %get-tuple-element.52), channel_id=1, source_target_pairs={{0,8},{24,16},{1,9},{25,17},{2,10},{26,18},{3,11},{27,19},{4,12},{... | collective-permute-start | bytes 2064392 | tf_op jit(solution)/shard_map/ppermute | solution.py:177
  142.2 38.7 %collective-permute-done.43 = bf16[2,2,48,1792]{3,2,1,0:T(8,128)(2,1)S(1)} collective-permute-done((bf16[2,2,48,1792]{3,2,1,0:T(8,128)(2,1)S(1)}, bf16[2,2,48,1792]{3,2,1,0:T(8,128)(2,1)S(1)}, u32[]{:S(2)}, u32[]{:S(2)}) %collective-permute-start.43) | collective-permute-done | bytes 688160 | tf_op jit(solution)/shard_map/ppermute | solution.py:177
  182.7 1.3 collective-permute-start.39
  185.1 1.3 collective-permute-start.45
  186.4 13.4 %collective-permute-done.39 = bf16[2,2,48,1792]{3,2,1,0:T(8,128)(2,1)S(1)} collective-permute-done((bf16[2,2,48,1792]{3,2,1,0:T(8,128)(2,1)S(1)}, bf16[2,2,48,1792]{3,2,1,0:T(8,128)(2,1)S(1)}, u32[]{:S(2)}, u32[]{:S(2)}) %collective-permute-start.39) | collective-permute-done | bytes 688160 | tf_op jit(solution)/shard_map/ppermute | solution.py:177
  200.4 25.7 %collective-permute-done.45 = bf16[2,2,48,1792]{3,2,1,0:T(8,128)(2,1)S(1)} collective-permute-done((bf16[2,2,48,1792]{3,2,1,0:T(8,128)(2,1)S(1)}, bf16[2,2,48,1792]{3,2,1,0:T(8,128)(2,1)S(1)}, u32[]{:S(2)}, u32[]{:S(2)}) %collective-permute-start.45) | collective-permute-done | bytes 688160 | tf_op jit(solution)/shard_map/ppermute | solution.py:177
  226.6 1.0 pad_maximum_fusion
  (97 shorter events, 15.7 us)
Async XLA Ops:
  0.9 7.3 %collective-permute-start.1 = (bf16[32,2048]{1,0:T(8,128)(2,1)S(1)}, bf16[32,2048]{1,0:T(8,128)(2,1)S(1)}, u32[]{:S(2)}, u32[]{:S(2)}) collective-permute-start(bf16[32,2048]{1,0:T(8,128)(2,1)S(1)} %slice.24.refs_0_), channel_id=1, source_target_pairs={{0,2},{1,3},{2,0},{3,1},{4,6},{5,7},{6,4},{7,5},{8,10},{9,11},{10,... | collective-permute-start | bytes 393224 | tf_op jit(solution)/shard_map/ppermute | solution.py:43
  3.9 7.8 %collective-permute-start.3 = (bf16[32,2048]{1,0:T(8,128)(2,1)S(1)}, bf16[32,2048]{1,0:T(8,128)(2,1)S(1)}, u32[]{:S(2)}, u32[]{:S(2)}) collective-permute-start(bf16[32,2048]{1,0:T(8,128)(2,1)S(1)} %slice.24.refs_0_), channel_id=1, source_target_pairs={{0,4},{1,5},{2,6},{3,7},{4,0},{5,1},{6,2},{7,3},{8,12},{9,13},{10,... | collective-permute-start | bytes 393224 | tf_op jit(solution)/shard_map/ppermute | solution.py:43
  5.4 6.3 %collective-permute-start.5 = (bf16[32,2048]{1,0:T(8,128)(2,1)S(1)}, bf16[32,2048]{1,0:T(8,128)(2,1)S(1)}, u32[]{:S(2)}, u32[]{:S(2)}) collective-permute-start(bf16[32,2048]{1,0:T(8,128)(2,1)S(1)} %slice.24.refs_0_), channel_id=1, source_target_pairs={{0,6},{1,7},{2,4},{3,5},{4,2},{5,3},{6,0},{7,1},{8,14},{9,15},{10,... | collective-permute-start | bytes 393224 | tf_op jit(solution)/shard_map/ppermute | solution.py:43
  5.5 6.8 %collective-permute-start = (bf16[32,2048]{1,0:T(8,128)(2,1)S(1)}, bf16[32,2048]{1,0:T(8,128)(2,1)S(1)}, u32[]{:S(2)}, u32[]{:S(2)}) collective-permute-start(bf16[32,2048]{1,0:T(8,128)(2,1)S(1)} %slice.24.refs_0_), channel_id=1, source_target_pairs={{0,1},{1,0},{2,3},{3,2},{4,5},{5,4},{6,7},{7,6},{8,9},{9,8},{10,11... | collective-permute-start | bytes 393224 | tf_op jit(solution)/shard_map/ppermute | solution.py:43
  8.2 4.0 %collective-permute-start.2 = (bf16[32,2048]{1,0:T(8,128)(2,1)S(1)}, bf16[32,2048]{1,0:T(8,128)(2,1)S(1)}, u32[]{:S(2)}, u32[]{:S(2)}) collective-permute-start(bf16[32,2048]{1,0:T(8,128)(2,1)S(1)} %collective-permute-done.1.refs_2_), channel_id=1, source_target_pairs={{0,1},{1,0},{2,3},{3,2},{4,5},{5,4},{6,7},{7,6},{8,9},{9,8},{10,11... | collective-permute-start | bytes 393224 | tf_op jit(solution)/shard_map/ppermute | solution.py:43
  11.7 1.3 collective-permute-start.4
  11.7 1.5 collective-permute-start.6
  16.2 1.2 collective-permute-start.7
  17.4 5.2 %collective-permute-start.10 = (bf16[128,128]{1,0:T(8,128)(2,1)S(1)}, bf16[128,128]{1,0:T(8,128)(2,1)S(1)}, u32[]{:S(2)}, u32[]{:S(2)}) collective-permute-start(bf16[128,128]{1,0:T(8,128)(2,1)S(1)} %bitcast_add_fusion.1), channel_id=1, source_target_pairs={{0,6},{1,7},{2,4},{3,5},{4,2},{5,3},{6,0},{7,1},{8,14},{9,15},{10,... | collective-permute-start | bytes 98312 | tf_op jit(solution)/shard_map/ppermute | solution.py:43
  19.0 3.9 %collective-permute-start.8 = (bf16[128,128]{1,0:T(8,128)(2,1)S(1)}, bf16[128,128]{1,0:T(8,128)(2,1)S(1)}, u32[]{:S(2)}, u32[]{:S(2)}) collective-permute-start(bf16[128,128]{1,0:T(8,128)(2,1)S(1)} %bitcast_add_fusion.1), channel_id=1, source_target_pairs={{0,2},{1,3},{2,0},{3,1},{4,6},{5,7},{6,4},{7,5},{8,10},{9,11},{10,... | collective-permute-start | bytes 98312 | tf_op jit(solution)/shard_map/ppermute | solution.py:43
  20.5 3.9 %collective-permute-start.9 = (bf16[128,128]{1,0:T(8,128)(2,1)S(1)}, bf16[128,128]{1,0:T(8,128)(2,1)S(1)}, u32[]{:S(2)}, u32[]{:S(2)}) collective-permute-start(bf16[128,128]{1,0:T(8,128)(2,1)S(1)} %bitcast_add_fusion.1), channel_id=1, source_target_pairs={{0,4},{1,5},{2,6},{3,7},{4,0},{5,1},{6,2},{7,3},{8,12},{9,13},{10,... | collective-permute-start | bytes 98312 | tf_op jit(solution)/shard_map/ppermute | solution.py:43
  24.4 7.2 %collective-permute-start.11 = (bf16[128,128]{1,0:T(8,128)(2,1)S(1)}, bf16[128,128]{1,0:T(8,128)(2,1)S(1)}, u32[]{:S(2)}, u32[]{:S(2)}) collective-permute-start(bf16[128,128]{1,0:T(8,128)(2,1)S(1)} %add_add_fusion.1), channel_id=1, source_target_pairs={{0,8},{8,16},{16,24},{24,0},{1,9},{9,17},{17,25},{25,1},{2,10},{10... | collective-permute-start | bytes 98312 | tf_op jit(solution)/shard_map/ppermute | solution.py:60
  26.0 7.6 %collective-permute-start.12 = (bf16[128,128]{1,0:T(8,128)(2,1)S(1)}, bf16[128,128]{1,0:T(8,128)(2,1)S(1)}, u32[]{:S(2)}, u32[]{:S(2)}) collective-permute-start(bf16[128,128]{1,0:T(8,128)(2,1)S(1)} %add_add_fusion.1), channel_id=1, source_target_pairs={{0,16},{8,24},{16,0},{24,8},{1,17},{9,25},{17,1},{25,9},{2,18},{10... | collective-permute-start | bytes 98312 | tf_op jit(solution)/shard_map/ppermute | solution.py:60
  28.6 5.0 %collective-permute-start.13 = (bf16[128,128]{1,0:T(8,128)(2,1)S(1)}, bf16[128,128]{1,0:T(8,128)(2,1)S(1)}, u32[]{:S(2)}, u32[]{:S(2)}) collective-permute-start(bf16[128,128]{1,0:T(8,128)(2,1)S(1)} %add_add_fusion.1), channel_id=1, source_target_pairs={{0,24},{8,0},{16,8},{24,16},{1,25},{9,1},{17,9},{25,17},{2,26},{10... | collective-permute-start | bytes 98312 | tf_op jit(solution)/shard_map/ppermute | solution.py:60
  30.0 20.4 %collective-permute-start.21 = (bf16[96,2048]{1,0:T(8,128)(2,1)S(1)}, bf16[96,2048]{1,0:T(8,128)(2,1)S(1)}, u32[]{:S(2)}, u32[]{:S(2)}) collective-permute-start(bf16[96,2048]{1,0:T(8,128)(2,1)S(1)} %slice.27.refs_0_), channel_id=1, source_target_pairs={{0,2},{1,3},{2,0},{3,1},{4,6},{5,7},{6,4},{7,5},{8,10},{9,11},{10,... | collective-permute-start | bytes 1179656 | tf_op jit(solution)/shard_map/ppermute | solution.py:43
  30.6 20.3 %collective-permute-start.23 = (bf16[96,2048]{1,0:T(8,128)(2,1)S(1)}, bf16[96,2048]{1,0:T(8,128)(2,1)S(1)}, u32[]{:S(2)}, u32[]{:S(2)}) collective-permute-start(bf16[96,2048]{1,0:T(8,128)(2,1)S(1)} %slice.27.refs_0_), channel_id=1, source_target_pairs={{0,4},{1,5},{2,6},{3,7},{4,0},{5,1},{6,2},{7,3},{8,12},{9,13},{10,... | collective-permute-start | bytes 1179656 | tf_op jit(solution)/shard_map/ppermute | solution.py:43
  31.6 19.4 %collective-permute-start.25 = (bf16[96,2048]{1,0:T(8,128)(2,1)S(1)}, bf16[96,2048]{1,0:T(8,128)(2,1)S(1)}, u32[]{:S(2)}, u32[]{:S(2)}) collective-permute-start(bf16[96,2048]{1,0:T(8,128)(2,1)S(1)} %slice.27.refs_0_), channel_id=1, source_target_pairs={{0,6},{1,7},{2,4},{3,5},{4,2},{5,3},{6,0},{7,1},{8,14},{9,15},{10,... | collective-permute-start | bytes 1179656 | tf_op jit(solution)/shard_map/ppermute | solution.py:43
  36.7 18.2 %copy-start.3 = (bf16[8,64,2048]{2,1,0:T(8,128)(2,1)S(1)}, bf16[8,64,2048]{2,1,0:T(8,128)(2,1)}, u32[]{:S(2)}) copy-start(bf16[8,64,2048]{2,1,0:T(8,128)(2,1)} %refs_8_.3) | copy-start | bytes 6291460
  48.1 12.3 %collective-permute-start.17 = (bf16[2,2,32,1792]{3,2,1,0:T(8,128)(2,1)S(1)}, bf16[2,2,32,1792]{3,2,1,0:T(8,128)(2,1)S(1)}, u32[]{:S(2)}, u32[]{:S(2)}) collective-permute-start(bf16[2,2,32,1792]{3,2,1,0:T(8,128)(2,1)S(1)} %get-tuple-element.35), channel_id=1, source_target_pairs={{0,8},{24,16},{1,9},{25,17},{2,10},{26,18},{3,11},{27,19},{4,12},{... | collective-permute-start | bytes 1376264 | tf_op jit(solution)/shard_map/ppermute | solution.py:177
  50.4 1.8 collective-permute-start.20
  50.5 3.0 %collective-permute-start.22 = (bf16[96,2048]{1,0:T(8,128)(2,1)S(1)}, bf16[96,2048]{1,0:T(8,128)(2,1)S(1)}, u32[]{:S(2)}, u32[]{:S(2)}) collective-permute-start(bf16[96,2048]{1,0:T(8,128)(2,1)S(1)} %collective-permute-done.21.refs_2_), channel_id=1, source_target_pairs={{0,1},{1,0},{2,3},{3,2},{4,5},{5,4},{6,7},{7,6},{8,9},{9,8},{10,11... | collective-permute-start | bytes 1179656 | tf_op jit(solution)/shard_map/ppermute | solution.py:43
  51.0 3.9 %collective-permute-start.24 = (bf16[96,2048]{1,0:T(8,128)(2,1)S(1)}, bf16[96,2048]{1,0:T(8,128)(2,1)S(1)}, u32[]{:S(2)}, u32[]{:S(2)}) collective-permute-start(bf16[96,2048]{1,0:T(8,128)(2,1)S(1)} %collective-permute-done.23.refs_4_), channel_id=1, source_target_pairs={{0,1},{1,0},{2,3},{3,2},{4,5},{5,4},{6,7},{7,6},{8,9},{9,8},{10,11... | collective-permute-start | bytes 1179656 | tf_op jit(solution)/shard_map/ppermute | solution.py:43
  51.1 3.8 %collective-permute-start.26 = (bf16[96,2048]{1,0:T(8,128)(2,1)S(1)}, bf16[96,2048]{1,0:T(8,128)(2,1)S(1)}, u32[]{:S(2)}, u32[]{:S(2)}) collective-permute-start(bf16[96,2048]{1,0:T(8,128)(2,1)S(1)} %collective-permute-done.25.refs_6_), channel_id=1, source_target_pairs={{0,1},{1,0},{2,3},{3,2},{4,5},{5,4},{6,7},{7,6},{8,9},{9,8},{10,11... | collective-permute-start | bytes 1179656 | tf_op jit(solution)/shard_map/ppermute | solution.py:43
  52.2 18.1 %collective-permute-start.15 = (bf16[2,2,32,1792]{3,2,1,0:T(8,128)(2,1)S(1)}, bf16[2,2,32,1792]{3,2,1,0:T(8,128)(2,1)S(1)}, u32[]{:S(2)}, u32[]{:S(2)}) collective-permute-start(bf16[2,2,32,1792]{3,2,1,0:T(8,128)(2,1)S(1)} %get-tuple-element.34), channel_id=1, source_target_pairs={{0,8},{24,16},{1,9},{25,17},{2,10},{26,18},{3,11},{27,19},{4,12},{... | collective-permute-start | bytes 1376264 | tf_op jit(solution)/shard_map/ppermute | solution.py:177
  53.5 66.7 %collective-permute-start.14 = (bf16[2,2,32,1792]{3,2,1,0:T(8,128)(2,1)S(1)}, bf16[2,2,32,1792]{3,2,1,0:T(8,128)(2,1)S(1)}, u32[]{:S(2)}, u32[]{:S(2)}) collective-permute-start(bf16[2,2,32,1792]{3,2,1,0:T(8,128)(2,1)S(1)} %get-tuple-element.33), channel_id=1, source_target_pairs={{0,8},{24,16},{1,9},{25,17},{2,10},{26,18},{3,11},{27,19},{4,12},{... | collective-permute-start | bytes 1376264 | tf_op jit(solution)/shard_map/ppermute | solution.py:177
  54.9 35.2 %copy-start.1 = (bf16[2048,1792]{1,0:T(8,128)(2,1)S(1)}, bf16[2048,1792]{1,0:T(8,128)(2,1)}, u32[]{:S(2)}) copy-start(bf16[2048,1792]{1,0:T(8,128)(2,1)} %gate_ref.5) | copy-start | bytes 22020100
  56.7 4.6 %collective-permute-start.27 = (bf16[384,128]{1,0:T(8,128)(2,1)S(1)}, bf16[384,128]{1,0:T(8,128)(2,1)S(1)}, u32[]{:S(2)}, u32[]{:S(2)}) collective-permute-start(bf16[384,128]{1,0:T(8,128)(2,1)S(1)} %bitcast.50), channel_id=1, source_target_pairs={{0,1},{1,0},{2,3},{3,2},{4,5},{5,4},{6,7},{7,6},{8,9},{9,8},{10,11... | collective-permute-start | bytes 294920 | tf_op jit(solution)/shard_map/ppermute | solution.py:43
  60.5 17.8 %collective-permute-start.18 = (bf16[2,2,32,1792]{3,2,1,0:T(8,128)(2,1)S(1)}, bf16[2,2,32,1792]{3,2,1,0:T(8,128)(2,1)S(1)}, u32[]{:S(2)}, u32[]{:S(2)}) collective-permute-start(bf16[2,2,32,1792]{3,2,1,0:T(8,128)(2,1)S(1)} %add_convert_fusion.7), channel_id=1, source_target_pairs={{8,16},{16,8},{9,17},{17,9},{10,18},{18,10},{11,19},{19,11},{12,20... | collective-permute-start | bytes 1376264 | tf_op jit(solution)/shard_map/ppermute | solution.py:177
  61.3 10.6 %collective-permute-start.28 = (bf16[384,128]{1,0:T(8,128)(2,1)S(1)}, bf16[384,128]{1,0:T(8,128)(2,1)S(1)}, u32[]{:S(2)}, u32[]{:S(2)}) collective-permute-start(bf16[384,128]{1,0:T(8,128)(2,1)S(1)} %bitcast_add_fusion), channel_id=1, source_target_pairs={{0,2},{1,3},{2,0},{3,1},{4,6},{5,7},{6,4},{7,5},{8,10},{9,11},{10,... | collective-permute-start | bytes 294920 | tf_op jit(solution)/shard_map/ppermute | solution.py:43
  62.3 10.3 %collective-permute-start.29 = (bf16[384,128]{1,0:T(8,128)(2,1)S(1)}, bf16[384,128]{1,0:T(8,128)(2,1)S(1)}, u32[]{:S(2)}, u32[]{:S(2)}) collective-permute-start(bf16[384,128]{1,0:T(8,128)(2,1)S(1)} %bitcast_add_fusion), channel_id=1, source_target_pairs={{0,4},{1,5},{2,6},{3,7},{4,0},{5,1},{6,2},{7,3},{8,12},{9,13},{10,... | collective-permute-start | bytes 294920 | tf_op jit(solution)/shard_map/ppermute | solution.py:43
  70.3 5.5 %collective-permute-start.30 = (bf16[384,128]{1,0:T(8,128)(2,1)S(1)}, bf16[384,128]{1,0:T(8,128)(2,1)S(1)}, u32[]{:S(2)}, u32[]{:S(2)}) collective-permute-start(bf16[384,128]{1,0:T(8,128)(2,1)S(1)} %bitcast_add_fusion), channel_id=1, source_target_pairs={{0,6},{1,7},{2,4},{3,5},{4,2},{5,3},{6,0},{7,1},{8,14},{9,15},{10,... | collective-permute-start | bytes 294920 | tf_op jit(solution)/shard_map/ppermute | solution.py:43
  71.9 49.7 %collective-permute-start.16 = (bf16[2,2,32,1792]{3,2,1,0:T(8,128)(2,1)S(1)}, bf16[2,2,32,1792]{3,2,1,0:T(8,128)(2,1)S(1)}, u32[]{:S(2)}, u32[]{:S(2)}) collective-permute-start(bf16[2,2,32,1792]{3,2,1,0:T(8,128)(2,1)S(1)} %add_convert_fusion.8), channel_id=1, source_target_pairs={{8,16},{16,8},{9,17},{17,9},{10,18},{18,10},{11,19},{19,11},{12,20... | collective-permute-start | bytes 1376264 | tf_op jit(solution)/shard_map/ppermute | solution.py:177
  75.8 6.6 %collective-permute-start.31 = (bf16[384,128]{1,0:T(8,128)(2,1)S(1)}, bf16[384,128]{1,0:T(8,128)(2,1)S(1)}, u32[]{:S(2)}, u32[]{:S(2)}) collective-permute-start(bf16[384,128]{1,0:T(8,128)(2,1)S(1)} %add_add_fusion), channel_id=1, source_target_pairs={{0,8},{8,16},{16,24},{24,0},{1,9},{9,17},{17,25},{25,1},{2,10},{10... | collective-permute-start | bytes 294920 | tf_op jit(solution)/shard_map/ppermute | solution.py:60
  78.3 11.7 %collective-permute-start.32 = (bf16[384,128]{1,0:T(8,128)(2,1)S(1)}, bf16[384,128]{1,0:T(8,128)(2,1)S(1)}, u32[]{:S(2)}, u32[]{:S(2)}) collective-permute-start(bf16[384,128]{1,0:T(8,128)(2,1)S(1)} %add_add_fusion), channel_id=1, source_target_pairs={{0,16},{8,24},{16,0},{24,8},{1,17},{9,25},{17,1},{25,9},{2,18},{10... | collective-permute-start | bytes 294920 | tf_op jit(solution)/shard_map/ppermute | solution.py:60
  78.3 11.7 %collective-permute-start.33 = (bf16[384,128]{1,0:T(8,128)(2,1)S(1)}, bf16[384,128]{1,0:T(8,128)(2,1)S(1)}, u32[]{:S(2)}, u32[]{:S(2)}) collective-permute-start(bf16[384,128]{1,0:T(8,128)(2,1)S(1)} %add_add_fusion), channel_id=1, source_target_pairs={{0,24},{8,0},{16,8},{24,16},{1,25},{9,1},{17,9},{25,17},{2,26},{10... | collective-permute-start | bytes 294920 | tf_op jit(solution)/shard_map/ppermute | solution.py:60
  82.4 40.5 %collective-permute-start.19 = (bf16[2,2,32,1792]{3,2,1,0:T(8,128)(2,1)S(1)}, bf16[2,2,32,1792]{3,2,1,0:T(8,128)(2,1)S(1)}, u32[]{:S(2)}, u32[]{:S(2)}) collective-permute-start(bf16[2,2,32,1792]{3,2,1,0:T(8,128)(2,1)S(1)} %add_convert_fusion.6), channel_id=1, source_target_pairs={{16,24},{8,0},{17,25},{9,1},{18,26},{10,2},{19,27},{11,3},{20,28},... | collective-permute-start | bytes 1376264 | tf_op jit(solution)/shard_map/ppermute | solution.py:177
  102.9 38.4 %collective-permute-start.35 = (bf16[2,2,48,1792]{3,2,1,0:T(8,128)(2,1)S(1)}, bf16[2,2,48,1792]{3,2,1,0:T(8,128)(2,1)S(1)}, u32[]{:S(2)}, u32[]{:S(2)}) collective-permute-start(bf16[2,2,48,1792]{3,2,1,0:T(8,128)(2,1)S(1)} %get-tuple-element.49), channel_id=1, source_target_pairs={{0,8},{24,16},{1,9},{25,17},{2,10},{26,18},{3,11},{27,19},{4,12},{... | collective-permute-start | bytes 2064392 | tf_op jit(solution)/shard_map/ppermute | solution.py:177
  106.1 30.6 %collective-permute-start.37 = (bf16[2,2,48,1792]{3,2,1,0:T(8,128)(2,1)S(1)}, bf16[2,2,48,1792]{3,2,1,0:T(8,128)(2,1)S(1)}, u32[]{:S(2)}, u32[]{:S(2)}) collective-permute-start(bf16[2,2,48,1792]{3,2,1,0:T(8,128)(2,1)S(1)} %get-tuple-element.50), channel_id=1, source_target_pairs={{0,8},{24,16},{1,9},{25,17},{2,10},{26,18},{3,11},{27,19},{4,12},{... | collective-permute-start | bytes 2064392 | tf_op jit(solution)/shard_map/ppermute | solution.py:177
  120.3 64.8 %collective-permute-start.34 = (bf16[2,2,48,1792]{3,2,1,0:T(8,128)(2,1)S(1)}, bf16[2,2,48,1792]{3,2,1,0:T(8,128)(2,1)S(1)}, u32[]{:S(2)}, u32[]{:S(2)}) collective-permute-start(bf16[2,2,48,1792]{3,2,1,0:T(8,128)(2,1)S(1)} %get-tuple-element.48), channel_id=1, source_target_pairs={{0,8},{24,16},{1,9},{25,17},{2,10},{26,18},{3,11},{27,19},{4,12},{... | collective-permute-start | bytes 2064392 | tf_op jit(solution)/shard_map/ppermute | solution.py:177
  121.6 61.1 %collective-permute-start.41 = (bf16[2,2,48,1792]{3,2,1,0:T(8,128)(2,1)S(1)}, bf16[2,2,48,1792]{3,2,1,0:T(8,128)(2,1)S(1)}, u32[]{:S(2)}, u32[]{:S(2)}) collective-permute-start(bf16[2,2,48,1792]{3,2,1,0:T(8,128)(2,1)S(1)} %get-tuple-element.53), channel_id=1, source_target_pairs={{0,8},{24,16},{1,9},{25,17},{2,10},{26,18},{3,11},{27,19},{4,12},{... | collective-permute-start | bytes 2064392 | tf_op jit(solution)/shard_map/ppermute | solution.py:177
  123.0 58.0 %collective-permute-start.43 = (bf16[2,2,48,1792]{3,2,1,0:T(8,128)(2,1)S(1)}, bf16[2,2,48,1792]{3,2,1,0:T(8,128)(2,1)S(1)}, u32[]{:S(2)}, u32[]{:S(2)}) collective-permute-start(bf16[2,2,48,1792]{3,2,1,0:T(8,128)(2,1)S(1)} %get-tuple-element.54), channel_id=1, source_target_pairs={{0,8},{24,16},{1,9},{25,17},{2,10},{26,18},{3,11},{27,19},{4,12},{... | collective-permute-start | bytes 2064392 | tf_op jit(solution)/shard_map/ppermute | solution.py:177
  136.7 63.7 %collective-permute-start.40 = (bf16[2,2,48,1792]{3,2,1,0:T(8,128)(2,1)S(1)}, bf16[2,2,48,1792]{3,2,1,0:T(8,128)(2,1)S(1)}, u32[]{:S(2)}, u32[]{:S(2)}) collective-permute-start(bf16[2,2,48,1792]{3,2,1,0:T(8,128)(2,1)S(1)} %get-tuple-element.52), channel_id=1, source_target_pairs={{0,8},{24,16},{1,9},{25,17},{2,10},{26,18},{3,11},{27,19},{4,12},{... | collective-permute-start | bytes 2064392 | tf_op jit(solution)/shard_map/ppermute | solution.py:177
  141.3 40.5 %collective-permute-start.38 = (bf16[2,2,48,1792]{3,2,1,0:T(8,128)(2,1)S(1)}, bf16[2,2,48,1792]{3,2,1,0:T(8,128)(2,1)S(1)}, u32[]{:S(2)}, u32[]{:S(2)}) collective-permute-start(bf16[2,2,48,1792]{3,2,1,0:T(8,128)(2,1)S(1)} %add_convert_fusion.4), channel_id=1, source_target_pairs={{8,16},{16,8},{9,17},{17,9},{10,18},{18,10},{11,19},{19,11},{12,20... | collective-permute-start | bytes 2064392 | tf_op jit(solution)/shard_map/ppermute | solution.py:177
  180.9 5.5 %collective-permute-start.36 = (bf16[2,2,48,1792]{3,2,1,0:T(8,128)(2,1)S(1)}, bf16[2,2,48,1792]{3,2,1,0:T(8,128)(2,1)S(1)}, u32[]{:S(2)}, u32[]{:S(2)}) collective-permute-start(bf16[2,2,48,1792]{3,2,1,0:T(8,128)(2,1)S(1)} %add_convert_fusion.5), channel_id=1, source_target_pairs={{8,16},{16,8},{9,17},{17,9},{10,18},{18,10},{11,19},{19,11},{12,20... | collective-permute-start | bytes 2064392 | tf_op jit(solution)/shard_map/ppermute | solution.py:177
  181.8 2.4 %collective-permute-start.44 = (bf16[2,2,48,1792]{3,2,1,0:T(8,128)(2,1)S(1)}, bf16[2,2,48,1792]{3,2,1,0:T(8,128)(2,1)S(1)}, u32[]{:S(2)}, u32[]{:S(2)}) collective-permute-start(bf16[2,2,48,1792]{3,2,1,0:T(8,128)(2,1)S(1)} %add_convert_fusion.1), channel_id=1, source_target_pairs={{8,16},{16,8},{9,17},{17,9},{10,18},{18,10},{11,19},{19,11},{12,20... | collective-permute-start | bytes 2064392 | tf_op jit(solution)/shard_map/ppermute | solution.py:177
  182.7 17.1 %collective-permute-start.39 = (bf16[2,2,48,1792]{3,2,1,0:T(8,128)(2,1)S(1)}, bf16[2,2,48,1792]{3,2,1,0:T(8,128)(2,1)S(1)}, u32[]{:S(2)}, u32[]{:S(2)}) collective-permute-start(bf16[2,2,48,1792]{3,2,1,0:T(8,128)(2,1)S(1)} %add_convert_fusion.3), channel_id=1, source_target_pairs={{16,24},{8,0},{17,25},{9,1},{18,26},{10,2},{19,27},{11,3},{20,28},... | collective-permute-start | bytes 2064392 | tf_op jit(solution)/shard_map/ppermute | solution.py:177
  184.2 16.2 %collective-permute-start.42 = (bf16[2,2,48,1792]{3,2,1,0:T(8,128)(2,1)S(1)}, bf16[2,2,48,1792]{3,2,1,0:T(8,128)(2,1)S(1)}, u32[]{:S(2)}, u32[]{:S(2)}) collective-permute-start(bf16[2,2,48,1792]{3,2,1,0:T(8,128)(2,1)S(1)} %add_convert_fusion.2), channel_id=1, source_target_pairs={{8,16},{16,8},{9,17},{17,9},{10,18},{18,10},{11,19},{19,11},{12,20... | collective-permute-start | bytes 2064392 | tf_op jit(solution)/shard_map/ppermute | solution.py:177
  185.1 41.0 %collective-permute-start.45 = (bf16[2,2,48,1792]{3,2,1,0:T(8,128)(2,1)S(1)}, bf16[2,2,48,1792]{3,2,1,0:T(8,128)(2,1)S(1)}, u32[]{:S(2)}, u32[]{:S(2)}) collective-permute-start(bf16[2,2,48,1792]{3,2,1,0:T(8,128)(2,1)S(1)} %add_convert_fusion), channel_id=1, source_target_pairs={{16,24},{8,0},{17,25},{9,1},{18,26},{10,2},{19,27},{11,3},{20,28},... | collective-permute-start | bytes 2064392 | tf_op jit(solution)/shard_map/ppermute | solution.py:177
  (3 other events, 19.8 us)

commit v4 on v3

v4 whole, which is shorter than its diff:
```python
import functools

import jax
import jax.numpy as jnp
from jax import lax
from jax.experimental import pallas as pl
from jax.experimental.pallas import tpu as pltpu
from jax.sharding import PartitionSpec as P

SEG_ROWS = 128
GROUPS = ((48,), (48, 32))
IN_FLIGHT = 2

low_rank_scale = 0.5


def slots_of(segment, req_len, req_adapter, owner_slot):
    order = jnp.arange(req_len.shape[0], dtype=jnp.int32)
    ends = jnp.sum(jnp.where(order[:, None] <= order[None, :], req_len[:, None], 0), axis=0)
    seg_request = jnp.sum((ends[None, :] <= segment[:, None]).astype(jnp.int32), axis=1)
    adapter = jnp.sum(jnp.where(seg_request[:, None] == order[None, :], req_adapter[None, :], 0), axis=1)
    ids = jnp.arange(owner_slot.shape[0], dtype=jnp.int32)
    return jnp.sum(jnp.where(adapter[:, None] == ids[None, :], owner_slot[None, :], 0), axis=1)


def chunk_of(slot, nseq):
    me = lax.axis_index("seq")
    half = me < nseq // 2
    far = jnp.where(half, nseq - 1 - me, me)
    near = slot - far
    far_chunk = jnp.where(half, nseq - 1 - slot, slot)
    near_chunk = jnp.where(half, near, nseq - 1 - near)
    chunk = jnp.where(slot < far, far_chunk, near_chunk)
    return jnp.where(slot == nseq - 1, me, chunk)


def held(seg_slot, first, count):
    local = seg_slot - first
    here = (local >= 0) & (local < count)
    return jnp.clip(local, 0, count - 1), here.astype(jnp.int32)


def swap(x, axis, size, mask):
    return lax.ppermute(x, axis, [(i, i ^ mask) for i in range(size)])


def gather_rows(x, ntp):
    chips = [x] + [swap(x, "tp", ntp, 2 * m) for m in range(1, ntp // 2)]
    pieces = []
    for piece in chips:
        pieces += [piece, swap(piece, "tp", ntp, 1)]
    return pieces


def sum_across(x, axis, size):
    steps = []
    mask = 1
    while mask < size:
        x = add(x, swap(x, axis, size, mask))
        steps.append(x)
        mask *= 2
    return steps


def assemble_kernel(segs, group, tab_ref, *refs):
    pieces, down_ref, xs, inner_ref = refs[:segs], refs[segs], refs[segs + 1:-1], refs[-1]
    me = tab_ref[2, 0]
    for n, piece in enumerate(pieces):
        start = 0
        for x_ref, rows in zip(xs, group):
            x_ref[tab_ref[3, me ^ n]] = piece[start:start + rows]
            start += rows
    start = 0
    for x_ref, rows in zip(xs, group):
        for pair in range(segs // 2):
            halves = []
            for k in (2 * pair, 2 * pair + 1):
                product = lax.dot_general(
                    x_ref[tab_ref[3, k]],
                    down_ref[tab_ref[0, k]],
                    (((1,), (1,)), ((), ())),
                    preferred_element_type=jnp.float32,
                )
                halves.append(product * tab_ref[1, k].astype(jnp.float32))
            inner_ref[pair, start:start + rows] = jnp.concatenate(halves, axis=1).astype(jnp.bfloat16)
        start += rows


def assemble(pieces, group, down_pool, table):
    segs = len(pieces)
    total, width = pieces[0].shape
    rank = down_pool.shape[1]
    vmem = pl.BlockSpec(memory_space=pltpu.VMEM)
    *xs, mine = pl.pallas_call(
        functools.partial(assemble_kernel, segs, group),
        out_shape=[jax.ShapeDtypeStruct((segs, rows, width), jnp.bfloat16) for rows in group]
        + [jax.ShapeDtypeStruct((segs // 2, total, 2 * rank), jnp.bfloat16)],
        in_specs=[pl.BlockSpec(memory_space=pltpu.SMEM)] + [vmem] * (segs + 1),
        out_specs=[vmem] * (len(group) + 1),
        compiler_params=pltpu.CompilerParams(vmem_limit_bytes=32 << 20),
        cost_estimate=pl.CostEstimate(
            flops=2 * segs * total * width * rank, bytes_accessed=4 * segs * total * width, transcendentals=0
        ),
    )(table, *pieces, down_pool)
    return xs, mine


def low_rank_kernel(slot, each, start, tab_ref, inner_ref, gate_ref, up_ref, *refs):
    ups, out_ref, low_ref = refs[:each], refs[each], refs[each + 1]
    lanes = inner_ref.shape[2]
    rank = lanes // 2
    rows = out_ref.shape[2]

    @pl.when(pl.program_id(0) == 0)
    def _():
        lane = lax.broadcasted_iota(jnp.int32, (rows, lanes), 1)
        for e in range(each):
            seg = tab_ref[2, slot * each + e]
            mine = (lane // rank == seg % 2) & (tab_ref[1, slot * each + e] == 1)
            inner = inner_ref[seg // 2][start:start + rows].astype(jnp.float32)
            low_ref[e] = (jnp.where(mine, inner, 0.0) * low_rank_scale).astype(jnp.bfloat16)

    for which, part_ref in enumerate((gate_ref, up_ref)):
        for e in range(each):
            factor = ups[e][0, which]
            low = jnp.dot(low_ref[e], jnp.concatenate([factor, factor], axis=0), preferred_element_type=jnp.float32)
            term = part_ref[e * rows:(e + 1) * rows].astype(jnp.float32) + low
            out_ref[which, e] = term.astype(jnp.bfloat16)


def add_low_rank(gate, up, inner, start, rows, slot, up_pool, table, each):
    columns = gate.shape[1]
    rank = up_pool.shape[2]
    tile = next(t for t in (896, 512, 256, 128) if columns % t == 0)

    def up_spec(e):
        return pl.BlockSpec((1, 2, rank, tile), lambda n, tab: (tab[0, slot * each + e], 0, 0, n))

    return pl.pallas_call(
        functools.partial(low_rank_kernel, slot, each, start),
        out_shape=jax.ShapeDtypeStruct((2, each, rows, columns), jnp.bfloat16),
        grid_spec=pltpu.PrefetchScalarGridSpec(
            num_scalar_prefetch=1,
            grid=(columns // tile,),
            in_specs=[
                pl.BlockSpec(inner.shape, lambda n, tab: (0, 0, 0)),
                pl.BlockSpec((each * rows, tile), lambda n, tab: (slot, n)),
                pl.BlockSpec((each * rows, tile), lambda n, tab: (slot, n)),
            ]
            + [up_spec(e) for e in range(each)],
            out_specs=pl.BlockSpec((2, each, rows, tile), lambda n, tab: (0, 0, 0, n)),
            scratch_shapes=[pltpu.VMEM((each, rows, 2 * rank), jnp.bfloat16)],
        ),
        compiler_params=pltpu.CompilerParams(vmem_limit_bytes=16 << 20),
        cost_estimate=pl.CostEstimate(
            flops=8 * each * rows * 2 * rank * columns,
            bytes_accessed=4 * each * (2 * rows + rank) * columns,
            transcendentals=0,
        ),
    )(table, inner, gate, up, *([up_pool] * each))


def add(x, y):
    return (x.astype(jnp.float32) + y.astype(jnp.float32)).astype(x.dtype)


def scatter_line(own, nseq, first_hops):
    last = nseq - 2
    arrived = {}
    for step in range(nseq - 1):
        for level in range(step + 1):
            slot = step - level if level < nseq // 2 else step
            send = own[slot]
            if level > 0:
                send = add(send, arrived[level - 1, step - 1])
            elif len(first_hops) >= IN_FLIGHT:
                send = after(send, first_hops[-IN_FLIGHT])
            pairs = [(level, level + 1), (nseq - 1 - level, nseq - 2 - level)]
            arrived[level, step] = lax.ppermute(send, "seq", pairs)
            if level == 0:
                first_hops.append(arrived[level, step])
    total = own[nseq - 1].astype(jnp.float32)
    for level in range(nseq - 1):
        total = total + arrived[level, last].astype(jnp.float32)
    return total


def after(x, gate):
    return lax.optimization_barrier((x, gate))[0]


def shards(tokens, gate_weight, up_weight, down_pool, up_pool, req_len, req_adapter, owner_slot):
    nseq = lax.axis_size("seq")
    ntp = lax.axis_size("tp")
    each = ntp // nseq
    me = lax.axis_index("tp")
    place = jnp.arange(ntp, dtype=jnp.int32)
    ordered = chunk_of(place // each, nseq) * each + place % each
    position = jnp.sum(jnp.where(ordered[:, None] == place[None, :], place[:, None], 0), axis=0)
    down_slot, down_here = held(
        slots_of(place, req_len, req_adapter, owner_slot), me * down_pool.shape[0], down_pool.shape[0]
    )
    up_slot, up_here = held(
        slots_of(ordered, req_len, req_adapter, owner_slot),
        lax.axis_index("seq") * up_pool.shape[0],
        up_pool.shape[0],
    )
    down_table = jnp.stack([down_slot, down_here, jnp.full_like(down_slot, me), position])
    up_table = jnp.stack([up_slot, up_here, ordered])
    columns = gate_weight.shape[1]
    out = []
    start = 0
    shared = sent = None
    first_hops = []
    for group in GROUPS:
        block = tokens[start:start + sum(group)]
        if shared is not None:
            block = after(block, shared)
        pieces = gather_rows(block, ntp)
        if sent is not None:
            pieces = list(after(tuple(pieces), sent[-1]))
        xs, mine = assemble(pieces, group, down_pool, down_table)
        steps = sum_across(mine.reshape(-1, mine.shape[2]), "tp", ntp)
        shared = steps[-1]
        inner = sum_across(shared, "seq", nseq)[-1].reshape(mine.shape)
        offset = 0
        ready = steps[0]
        for x, rows in zip(xs, group):
            x = after(x.reshape(-1, x.shape[2]), ready)
            gate, up = [
                jnp.dot(x, weight, preferred_element_type=jnp.float32).astype(jnp.bfloat16)
                for weight in (gate_weight, up_weight)
            ]
            sent = []
            for slot in range(nseq):
                given = after(inner, sent[-1]) if sent else inner
                sent.append(add_low_rank(gate, up, given, offset, rows, slot, up_pool, up_table, each))
            ready = sent[-1]
            total = scatter_line(sent, nseq, first_hops)
            out.append((jax.nn.silu(total[0]) * total[1]).astype(jnp.bfloat16))
            offset += rows
        start += sum(group)
    return jnp.concatenate(out, axis=1).reshape(-1, columns)


def solution(mesh):
    placed = (
        P("tp", "seq"),
        P("seq", "tp"),
        P("seq", "tp"),
        P("tp", None, "seq"),
        P("seq", None, None, "tp"),
        P(),
        P(),
        P(),
    )
    return jax.shard_map(
        shards, mesh=mesh, in_specs=placed, out_specs=P("seq", "tp"), check_vma=False
    )
```

time: 229 us -> 208 us (0.908)
  waiting for transfers between devices: 120 us -> 91.3 us
  Pallas kernels: 40.1 us -> 20.4 us
  matrix products: 0 us -> 19.7 us
  starting transfers between devices: 54.5 us -> 65.9 us
  local copies, waits for them, and re-layouts: 5.7 us -> 2.75 us
    ppermute x18, waiting for transfers between devices: 100 us -> 62.7 us  [scatter_line(): arrived[level, step] = lax.ppermute(send, 'seq', pairs)]
    dot_general x0 -> x6, matrix products: none -> 19.7 us  [shards(): jnp.dot(x, weight, preferred_element_type=jnp.float32).astype(jnp.bfloat16)]
    pallas_call x5 -> x14, Pallas kernels: 40.1 us -> 20.4 us  [the longest x12 17.1 us: add_low_rank(): pl.pallas_call(functools.partial(low_rank_kernel, slot, each, start), out...]
    ppermute x18, starting transfers between devices: 26 us -> 43.9 us  [scatter_line(): arrived[level, step] = lax.ppermute(send, 'seq', pairs)]
    ppermute x22 -> x24, waiting for transfers between devices: 12.2 us -> 28.6 us  [swap(): return lax.ppermute(x, axis, [(i, i ^ mask) for i in range(size)])]
    ppermute x6 -> x0, starting transfers between devices: 10.6 us -> none  [sum_seq(): lax.ppermute(x, 'seq', [(i, (i + k) % nseq) for i in range(nseq)])]
    ppermute x6 -> x0, waiting for transfers between devices: 7.85 us -> none  [sum_seq(): lax.ppermute(x, 'seq', [(i, (i + k) % nseq) for i in range(nseq)])]
    ppermute x22 -> x24, starting transfers between devices: 18 us -> 22 us  [swap(): return lax.ppermute(x, axis, [(i, i ^ mask) for i in range(size)])]
  transfers between devices with their start and end apart: 46 -> 42, of which waited for: 17 -> 20; matrix products, arithmetic and copies ran while one was open for 2% -> 12% of each run, Pallas kernels for 17% -> 8%
where the time goes in v4:
time: 208 us; the launch traced here: 207 us
  waiting for transfers between devices  91.3 us (44%)
  starting transfers between devices  65.9 us (32%)
  Pallas kernels  20.4 us (10%)
  matrix products  19.7 us (9%)
  other arithmetic  6.53 us (3%)
  local copies, waits for them, and re-layouts  2.75 us (1%)
    ppermute x18, waiting for transfers between devices, scatter_line(): arrived[level, step] = lax.ppermute(send, 'seq', pairs)  62.7 us
    ppermute x18, starting transfers between devices, scatter_line(): arrived[level, step] = lax.ppermute(send, 'seq', pairs)  43.9 us
    ppermute x24, waiting for transfers between devices, swap(): return lax.ppermute(x, axis, [(i, i ^ mask) for i in range(size)])  28.6 us
    ppermute x24, starting transfers between devices, swap(): return lax.ppermute(x, axis, [(i, i ^ mask) for i in range(size)])  22 us
    dot_general x6, matrix products, shards(): jnp.dot(x, weight, preferred_element_type=jnp.float32).astype(jnp.bfloat16)  19.7 us
    pallas_call x12, Pallas kernels, add_low_rank(): pl.pallas_call(functools.partial(low_rank_kernel, slot, each, start), out...  17.1 us
  transfers between devices with their start and end apart: 42, of which 20 were waited for; matrix products, arithmetic and copies ran while one was open for 12% of the time, Pallas kernels for 8%

profile of v4, /device:TPU:0, one launch (start us, length us, event | category | flops | bytes accessed | tf_op | source)
XLA Modules:
  0.0 207.3 jit_solution(14222238554428507196)
XLA Ops:
  0.9 4.0 %collective-permute-start.5 = (bf16[48,2048]{1,0:T(8,128)(2,1)S(1)}, bf16[48,2048]{1,0:T(8,128)(2,1)S(1)}, u32[]{:S(2)}, u32[]{:S(2)}) collective-permute-start(bf16[48,2048]{1,0:T(8,128)(2,1)S(1)} %slice.24.refs_0_), channel_id=1, source_target_pairs={{0,6},{1,7},{2,4},{3,5},{4,2},{5,3},{6,0},{7,1},{8,14},{9,15},{10,... | collective-permute-start | bytes 589832 | tf_op jit(solution)/shard_map/ppermute | solution.py:44
  8.3 2.4 %collective-permute-done.5.refs_6_ = bf16[48,2048]{1,0:T(8,128)(2,1)S(1)} collective-permute-done((bf16[48,2048]{1,0:T(8,128)(2,1)S(1)}, bf16[48,2048]{1,0:T(8,128)(2,1)S(1)}, u32[]{:S(2)}, u32[]{:S(2)}) %collective-permute-start.5) | collective-permute-done | bytes 196640 | tf_op jit(solution)/shard_map/ppermute | solution.py:44
  10.7 3.3 %collective-permute-done.3.refs_4_ = bf16[48,2048]{1,0:T(8,128)(2,1)S(1)} collective-permute-done((bf16[48,2048]{1,0:T(8,128)(2,1)S(1)}, bf16[48,2048]{1,0:T(8,128)(2,1)S(1)}, u32[]{:S(2)}, u32[]{:S(2)}) %collective-permute-start.3) | collective-permute-done | bytes 196640 | tf_op jit(solution)/shard_map/ppermute | solution.py:44
  15.8 1.6 copy-done
  20.1 1.7 collective-permute-start.8
  21.8 2.4 %collective-permute-done.8 = bf16[192,128]{1,0:T(8,128)(2,1)S(1)} collective-permute-done((bf16[192,128]{1,0:T(8,128)(2,1)S(1)}, bf16[192,128]{1,0:T(8,128)(2,1)S(1)}, u32[]{:S(2)}, u32[]{:S(2)}) %collective-permute-start.8) | collective-permute-done | bytes 49184 | tf_op jit(solution)/shard_map/ppermute | solution.py:44
  24.2 1.8 collective-permute-start.9
  26.1 2.3 %collective-permute-done.9 = bf16[192,128]{1,0:T(8,128)(2,1)S(1)} collective-permute-done((bf16[192,128]{1,0:T(8,128)(2,1)S(1)}, bf16[192,128]{1,0:T(8,128)(2,1)S(1)}, u32[]{:S(2)}, u32[]{:S(2)}) %collective-permute-start.9) | collective-permute-done | bytes 49184 | tf_op jit(solution)/shard_map/ppermute | solution.py:44
  28.4 1.8 collective-permute-start.10
  30.3 1.7 collective-permute-start.23
  33.7 6.3 %convolution_convert_fusion.2.up_ref = bf16[384,1792]{1,0:T(8,128)(2,1)S(1)} fusion(bf16[384,2048]{1,0:T(8,128)(2,1)S(1)} %bitcast.78, bf16[2048,1792]{1,0:T(8,128)(2,1)} %param.10), kind=kOutput, calls=%fused_computation.2 | convolution fusion | flops 2819260416 | bytes 10289152 | tf_op jit(solution)/shard_map/dot_general | solution.py:231
  40.1 2.6 %collective-permute-start.11 = (bf16[192,128]{1,0:T(8,128)(2,1)S(1)}, bf16[192,128]{1,0:T(8,128)(2,1)S(1)}, u32[]{:S(2)}, u32[]{:S(2)}) collective-permute-start(bf16[192,128]{1,0:T(8,128)(2,1)S(1)} %add_convert_fusion.15), channel_id=1, source_target_pairs={{0,16},{8,24},{16,0},{24,8},{1,17},{9,25},{17,1},{25,9},{2,18},{10... | collective-permute-start | bytes 147464 | tf_op jit(solution)/shard_map/ppermute | solution.py:44
  43.0 2.5 %collective-permute-done.21.refs_4_ = bf16[80,2048]{1,0:T(8,128)(2,1)S(1)} collective-permute-done((bf16[80,2048]{1,0:T(8,128)(2,1)S(1)}, bf16[80,2048]{1,0:T(8,128)(2,1)S(1)}, u32[]{:S(2)}, u32[]{:S(2)}) %collective-permute-start.21) | collective-permute-done | bytes 327712 | tf_op jit(solution)/shard_map/ppermute | solution.py:44
  46.0 3.1 %convolution_convert_fusion.3.gate_ref = bf16[384,1792]{1,0:T(8,128)(2,1)S(1)} fusion(bf16[384,2048]{1,0:T(8,128)(2,1)S(1)} %bitcast.79, bf16[2048,1792]{1,0:T(8,128)(2,1)S(1)} %bitcast.88), kind=kOutput, calls=%fused_computation.3 | convolution fusion | flops 2819260416 | bytes 10289152 | tf_op jit(solution)/shard_map/dot_general | solution.py:231
  49.1 1.4 shard_map.83
  50.5 1.4 shard_map.84
  52.0 1.4 shard_map.85
  53.5 1.4 shard_map.86
  55.1 2.0 shard_map.87
  57.1 2.4 %collective-permute-start.14 = (bf16[2,2,48,1792]{3,2,1,0:T(8,128)(2,1)S(1)}, bf16[2,2,48,1792]{3,2,1,0:T(8,128)(2,1)S(1)}, u32[]{:S(2)}, u32[]{:S(2)}) collective-permute-start(bf16[2,2,48,1792]{3,2,1,0:T(8,128)(2,1)S(1)} %shard_map.84), channel_id=1, source_target_pairs={{0,8},{24,16},{1,9},{25,17},{2,10},{26,18},{3,11},{27,19},{4,12},{... | collective-permute-start | bytes 2064392 | tf_op jit(solution)/shard_map/ppermute | solution.py:179
  59.5 1.5 collective-permute-start.12
  61.1 1.5 collective-permute-start.26
  62.6 3.1 %convolution_convert_fusion.up_ref = bf16[384,1792]{1,0:T(8,128)(2,1)S(1)} fusion(bf16[384,2048]{1,0:T(8,128)(2,1)S(1)} %bitcast.80, bf16[2048,1792]{1,0:T(8,128)(2,1)S(1)} %bitcast.86), kind=kOutput, calls=%fused_computation | convolution fusion | flops 2819260416 | bytes 10289152 | tf_op jit(solution)/shard_map/dot_general | solution.py:231
  65.7 1.6 collective-permute-start.27
  67.3 3.1 %convolution_convert_fusion.1.gate_ref = bf16[384,1792]{1,0:T(8,128)(2,1)S(1)} fusion(bf16[384,2048]{1,0:T(8,128)(2,1)S(1)} %bitcast.81, bf16[2048,1792]{1,0:T(8,128)(2,1)S(1)} %bitcast.88), kind=kOutput, calls=%fused_computation.1 | convolution fusion | flops 2819260416 | bytes 10289152 | tf_op jit(solution)/shard_map/dot_general | solution.py:231
  70.5 4.8 %collective-permute-done.14 = bf16[2,2,48,1792]{3,2,1,0:T(8,128)(2,1)S(1)} collective-permute-done((bf16[2,2,48,1792]{3,2,1,0:T(8,128)(2,1)S(1)}, bf16[2,2,48,1792]{3,2,1,0:T(8,128)(2,1)S(1)}, u32[]{:S(2)}, u32[]{:S(2)}) %collective-permute-start.14) | collective-permute-done | bytes 688160 | tf_op jit(solution)/shard_map/ppermute | solution.py:179
  76.1 13.9 %collective-permute-done.12 = bf16[2,2,48,1792]{3,2,1,0:T(8,128)(2,1)S(1)} collective-permute-done((bf16[2,2,48,1792]{3,2,1,0:T(8,128)(2,1)S(1)}, bf16[2,2,48,1792]{3,2,1,0:T(8,128)(2,1)S(1)}, u32[]{:S(2)}, u32[]{:S(2)}) %collective-permute-start.12) | collective-permute-done | bytes 688160 | tf_op jit(solution)/shard_map/ppermute | solution.py:179
  90.0 4.4 %collective-permute-start.13 = (bf16[2,2,48,1792]{3,2,1,0:T(8,128)(2,1)S(1)}, bf16[2,2,48,1792]{3,2,1,0:T(8,128)(2,1)S(1)}, u32[]{:S(2)}, u32[]{:S(2)}) collective-permute-start(bf16[2,2,48,1792]{3,2,1,0:T(8,128)(2,1)S(1)} %shard_map.85), channel_id=1, source_target_pairs={{0,8},{24,16},{1,9},{25,17},{2,10},{26,18},{3,11},{27,19},{4,12},{... | collective-permute-start | bytes 2064392 | tf_op jit(solution)/shard_map/ppermute | solution.py:179
  94.5 1.5 collective-permute-start.29
  96.9 13.0 %collective-permute-done.29 = bf16[320,128]{1,0:T(8,128)(2,1)S(1)} collective-permute-done((bf16[320,128]{1,0:T(8,128)(2,1)S(1)}, bf16[320,128]{1,0:T(8,128)(2,1)S(1)}, u32[]{:S(2)}, u32[]{:S(2)}) %collective-permute-start.29) | collective-permute-done | bytes 81952 | tf_op jit(solution)/shard_map/ppermute | solution.py:44
  109.9 1.4 shard_map.88
  111.4 1.4 shard_map.89
  112.8 1.4 shard_map.90
  114.3 1.4 shard_map.91
  115.7 6.9 %collective-permute-start.30 = (bf16[2,2,48,1792]{3,2,1,0:T(8,128)(2,1)S(1)}, bf16[2,2,48,1792]{3,2,1,0:T(8,128)(2,1)S(1)}, u32[]{:S(2)}, u32[]{:S(2)}) collective-permute-start(bf16[2,2,48,1792]{3,2,1,0:T(8,128)(2,1)S(1)} %shard_map.88), channel_id=1, source_target_pairs={{0,8},{24,16},{1,9},{25,17},{2,10},{26,18},{3,11},{27,19},{4,12},{... | collective-permute-start | bytes 2064392 | tf_op jit(solution)/shard_map/ppermute | solution.py:179
  122.6 2.1 %convolution_convert_fusion.4.up_ref = bf16[256,1792]{1,0:T(8,128)(2,1)S(1)} fusion(bf16[256,2048]{1,0:T(8,128)(2,1)S(1)} %bitcast.82, bf16[2048,1792]{1,0:T(8,128)(2,1)S(1)} %bitcast.86), kind=kOutput, calls=%fused_computation.4 | convolution fusion | flops 1879506944 | bytes 9306112 | tf_op jit(solution)/shard_map/dot_general | solution.py:231
  125.0 1.5 collective-permute-start.17
  126.5 2.1 %convolution_convert_fusion.5.gate_ref = bf16[256,1792]{1,0:T(8,128)(2,1)S(1)} fusion(bf16[256,2048]{1,0:T(8,128)(2,1)S(1)} %bitcast.83, bf16[2048,1792]{1,0:T(8,128)(2,1)S(1)} %bitcast.88), kind=kOutput, calls=%fused_computation.5 | convolution fusion | flops 1879506944 | bytes 9306112 | tf_op jit(solution)/shard_map/dot_general | solution.py:231
  134.1 4.6 %collective-permute-start.32 = (bf16[2,2,48,1792]{3,2,1,0:T(8,128)(2,1)S(1)}, bf16[2,2,48,1792]{3,2,1,0:T(8,128)(2,1)S(1)}, u32[]{:S(2)}, u32[]{:S(2)}) collective-permute-start(bf16[2,2,48,1792]{3,2,1,0:T(8,128)(2,1)S(1)} %shard_map.89), channel_id=1, source_target_pairs={{0,8},{24,16},{1,9},{25,17},{2,10},{26,18},{3,11},{27,19},{4,12},{... | collective-permute-start | bytes 2064392 | tf_op jit(solution)/shard_map/ppermute | solution.py:179
  142.1 12.5 %collective-permute-done.32 = bf16[2,2,48,1792]{3,2,1,0:T(8,128)(2,1)S(1)} collective-permute-done((bf16[2,2,48,1792]{3,2,1,0:T(8,128)(2,1)S(1)}, bf16[2,2,48,1792]{3,2,1,0:T(8,128)(2,1)S(1)}, u32[]{:S(2)}, u32[]{:S(2)}) %collective-permute-start.32) | collective-permute-done | bytes 688160 | tf_op jit(solution)/shard_map/ppermute | solution.py:179
  155.7 5.6 %collective-permute-start.36 = (bf16[2,2,32,1792]{3,2,1,0:T(8,128)(2,1)S(1)}, bf16[2,2,32,1792]{3,2,1,0:T(8,128)(2,1)S(1)}, u32[]{:S(2)}, u32[]{:S(2)}) collective-permute-start(bf16[2,2,32,1792]{3,2,1,0:T(8,128)(2,1)S(1)} %shard_map.92), channel_id=1, source_target_pairs={{0,8},{24,16},{1,9},{25,17},{2,10},{26,18},{3,11},{27,19},{4,12},{... | collective-permute-start | bytes 1376264 | tf_op jit(solution)/shard_map/ppermute | solution.py:179
  162.8 6.5 %collective-permute-done.31 = bf16[2,2,48,1792]{3,2,1,0:T(8,128)(2,1)S(1)} collective-permute-done((bf16[2,2,48,1792]{3,2,1,0:T(8,128)(2,1)S(1)}, bf16[2,2,48,1792]{3,2,1,0:T(8,128)(2,1)S(1)}, u32[]{:S(2)}, u32[]{:S(2)}) %collective-permute-start.31) | collective-permute-done | bytes 688160 | tf_op jit(solution)/shard_map/ppermute | solution.py:179
  169.4 4.4 %collective-permute-start.38 = (bf16[2,2,32,1792]{3,2,1,0:T(8,128)(2,1)S(1)}, bf16[2,2,32,1792]{3,2,1,0:T(8,128)(2,1)S(1)}, u32[]{:S(2)}, u32[]{:S(2)}) collective-permute-start(bf16[2,2,32,1792]{3,2,1,0:T(8,128)(2,1)S(1)} %shard_map.93), channel_id=1, source_target_pairs={{0,8},{24,16},{1,9},{25,17},{2,10},{26,18},{3,11},{27,19},{4,12},{... | collective-permute-start | bytes 1376264 | tf_op jit(solution)/shard_map/ppermute | solution.py:179
  173.8 5.4 %collective-permute-done.36 = bf16[2,2,32,1792]{3,2,1,0:T(8,128)(2,1)S(1)} collective-permute-done((bf16[2,2,32,1792]{3,2,1,0:T(8,128)(2,1)S(1)}, bf16[2,2,32,1792]{3,2,1,0:T(8,128)(2,1)S(1)}, u32[]{:S(2)}, u32[]{:S(2)}) %collective-permute-start.36) | collective-permute-done | bytes 458784 | tf_op jit(solution)/shard_map/ppermute | solution.py:179
  179.2 4.4 %collective-permute-start.37 = (bf16[2,2,32,1792]{3,2,1,0:T(8,128)(2,1)S(1)}, bf16[2,2,32,1792]{3,2,1,0:T(8,128)(2,1)S(1)}, u32[]{:S(2)}, u32[]{:S(2)}) collective-permute-start(bf16[2,2,32,1792]{3,2,1,0:T(8,128)(2,1)S(1)} %shard_map.94), channel_id=1, source_target_pairs={{0,8},{24,16},{1,9},{25,17},{2,10},{26,18},{3,11},{27,19},{4,12},{... | collective-permute-start | bytes 1376264 | tf_op jit(solution)/shard_map/ppermute | solution.py:179
  184.4 4.6 %collective-permute-done.38 = bf16[2,2,32,1792]{3,2,1,0:T(8,128)(2,1)S(1)} collective-permute-done((bf16[2,2,32,1792]{3,2,1,0:T(8,128)(2,1)S(1)}, bf16[2,2,32,1792]{3,2,1,0:T(8,128)(2,1)S(1)}, u32[]{:S(2)}, u32[]{:S(2)}) %collective-permute-start.38) | collective-permute-done | bytes 458784 | tf_op jit(solution)/shard_map/ppermute | solution.py:179
  191.8 3.3 %collective-permute-done.37 = bf16[2,2,32,1792]{3,2,1,0:T(8,128)(2,1)S(1)} collective-permute-done((bf16[2,2,32,1792]{3,2,1,0:T(8,128)(2,1)S(1)}, bf16[2,2,32,1792]{3,2,1,0:T(8,128)(2,1)S(1)}, u32[]{:S(2)}, u32[]{:S(2)}) %collective-permute-start.37) | collective-permute-done | bytes 458784 | tf_op jit(solution)/shard_map/ppermute | solution.py:179
  195.1 10.9 %collective-permute-done.41 = bf16[2,2,32,1792]{3,2,1,0:T(8,128)(2,1)S(1)} collective-permute-done((bf16[2,2,32,1792]{3,2,1,0:T(8,128)(2,1)S(1)}, bf16[2,2,32,1792]{3,2,1,0:T(8,128)(2,1)S(1)}, u32[]{:S(2)}, u32[]{:S(2)}) %collective-permute-start.41) | collective-permute-done | bytes 458784 | tf_op jit(solution)/shard_map/ppermute | solution.py:179
  (119 shorter events, 29.9 us)
Async XLA Ops:
  0.9 9.7 %collective-permute-start.5 = (bf16[48,2048]{1,0:T(8,128)(2,1)S(1)}, bf16[48,2048]{1,0:T(8,128)(2,1)S(1)}, u32[]{:S(2)}, u32[]{:S(2)}) collective-permute-start(bf16[48,2048]{1,0:T(8,128)(2,1)S(1)} %slice.24.refs_0_), channel_id=1, source_target_pairs={{0,6},{1,7},{2,4},{3,5},{4,2},{5,3},{6,0},{7,1},{8,14},{9,15},{10,... | collective-permute-start | bytes 589832 | tf_op jit(solution)/shard_map/ppermute | solution.py:44
  4.9 9.1 %collective-permute-start.3 = (bf16[48,2048]{1,0:T(8,128)(2,1)S(1)}, bf16[48,2048]{1,0:T(8,128)(2,1)S(1)}, u32[]{:S(2)}, u32[]{:S(2)}) collective-permute-start(bf16[48,2048]{1,0:T(8,128)(2,1)S(1)} %slice.24.refs_0_), channel_id=1, source_target_pairs={{0,4},{1,5},{2,6},{3,7},{4,0},{5,1},{6,2},{7,3},{8,12},{9,13},{10,... | collective-permute-start | bytes 589832 | tf_op jit(solution)/shard_map/ppermute | solution.py:44
  5.4 8.9 %collective-permute-start.1 = (bf16[48,2048]{1,0:T(8,128)(2,1)S(1)}, bf16[48,2048]{1,0:T(8,128)(2,1)S(1)}, u32[]{:S(2)}, u32[]{:S(2)}) collective-permute-start(bf16[48,2048]{1,0:T(8,128)(2,1)S(1)} %slice.24.refs_0_), channel_id=1, source_target_pairs={{0,2},{1,3},{2,0},{3,1},{4,6},{5,7},{6,4},{7,5},{8,10},{9,11},{10,... | collective-permute-start | bytes 589832 | tf_op jit(solution)/shard_map/ppermute | solution.py:44
  5.5 9.0 %collective-permute-start = (bf16[48,2048]{1,0:T(8,128)(2,1)S(1)}, bf16[48,2048]{1,0:T(8,128)(2,1)S(1)}, u32[]{:S(2)}, u32[]{:S(2)}) collective-permute-start(bf16[48,2048]{1,0:T(8,128)(2,1)S(1)} %slice.24.refs_0_), channel_id=1, source_target_pairs={{0,1},{1,0},{2,3},{3,2},{4,5},{5,4},{6,7},{7,6},{8,9},{9,8},{10,11... | collective-permute-start | bytes 589832 | tf_op jit(solution)/shard_map/ppermute | solution.py:44
  10.7 3.9 %collective-permute-start.6 = (bf16[48,2048]{1,0:T(8,128)(2,1)S(1)}, bf16[48,2048]{1,0:T(8,128)(2,1)S(1)}, u32[]{:S(2)}, u32[]{:S(2)}) collective-permute-start(bf16[48,2048]{1,0:T(8,128)(2,1)S(1)} %collective-permute-done.5.refs_6_), channel_id=1, source_target_pairs={{0,1},{1,0},{2,3},{3,2},{4,5},{5,4},{6,7},{7,6},{8,9},{9,8},{10,11... | collective-permute-start | bytes 589832 | tf_op jit(solution)/shard_map/ppermute | solution.py:44
  14.0 1.4 collective-permute-start.4
  14.3 1.4 collective-permute-start.2
  18.8 1.3 collective-permute-start.7
  20.1 4.2 %collective-permute-start.8 = (bf16[192,128]{1,0:T(8,128)(2,1)S(1)}, bf16[192,128]{1,0:T(8,128)(2,1)S(1)}, u32[]{:S(2)}, u32[]{:S(2)}) collective-permute-start(bf16[192,128]{1,0:T(8,128)(2,1)S(1)} %add_convert_fusion.18), channel_id=1, source_target_pairs={{0,2},{1,3},{2,0},{3,1},{4,6},{5,7},{6,4},{7,5},{8,10},{9,11},{10,... | collective-permute-start | bytes 147464 | tf_op jit(solution)/shard_map/ppermute | solution.py:44
  24.2 4.2 %collective-permute-start.9 = (bf16[192,128]{1,0:T(8,128)(2,1)S(1)}, bf16[192,128]{1,0:T(8,128)(2,1)S(1)}, u32[]{:S(2)}, u32[]{:S(2)}) collective-permute-start(bf16[192,128]{1,0:T(8,128)(2,1)S(1)} %add_convert_fusion.17), channel_id=1, source_target_pairs={{0,4},{1,5},{2,6},{3,7},{4,0},{5,1},{6,2},{7,3},{8,12},{9,13},{10,... | collective-permute-start | bytes 147464 | tf_op jit(solution)/shard_map/ppermute | solution.py:44
  28.4 17.6 %slice-start.4 = ((s8[7340032]{0:T(1024)(128)(4,1)}), s8[4194304]{0:T(1024)(128)(4,1)S(1)}, s32[]{:S(2)}) async-start(s8[7340032]{0:T(1024)(128)(4,1)} %bitcast.87), calls=%async_computation.4 | async-start | bytes 8388608
  28.4 17.5 %slice-start.5 = ((s8[7340032]{0:T(1024)(128)(4,1)}), s8[3145728]{0:T(1024)(128)(4,1)S(1)}, s32[]{:S(2)}) async-start(s8[7340032]{0:T(1024)(128)(4,1)} %bitcast.87), calls=%async_computation.5 | async-start | bytes 6291456
  28.4 11.7 %collective-permute-start.10 = (bf16[192,128]{1,0:T(8,128)(2,1)S(1)}, bf16[192,128]{1,0:T(8,128)(2,1)S(1)}, u32[]{:S(2)}, u32[]{:S(2)}) collective-permute-start(bf16[192,128]{1,0:T(8,128)(2,1)S(1)} %add_convert_fusion.16), channel_id=1, source_target_pairs={{0,8},{8,0},{16,24},{24,16},{1,9},{9,1},{17,25},{25,17},{2,10},{10... | collective-permute-start | bytes 147464 | tf_op jit(solution)/shard_map/ppermute | solution.py:44
  30.3 12.5 %collective-permute-start.23 = (bf16[80,2048]{1,0:T(8,128)(2,1)S(1)}, bf16[80,2048]{1,0:T(8,128)(2,1)S(1)}, u32[]{:S(2)}, u32[]{:S(2)}) collective-permute-start(bf16[80,2048]{1,0:T(8,128)(2,1)S(1)} %slice.27.refs_0_), channel_id=1, source_target_pairs={{0,6},{1,7},{2,4},{3,5},{4,2},{5,3},{6,0},{7,1},{8,14},{9,15},{10,... | collective-permute-start | bytes 983048 | tf_op jit(solution)/shard_map/ppermute | solution.py:44
  32.0 13.4 %collective-permute-start.21 = (bf16[80,2048]{1,0:T(8,128)(2,1)S(1)}, bf16[80,2048]{1,0:T(8,128)(2,1)S(1)}, u32[]{:S(2)}, u32[]{:S(2)}) collective-permute-start(bf16[80,2048]{1,0:T(8,128)(2,1)S(1)} %slice.27.refs_0_), channel_id=1, source_target_pairs={{0,4},{1,5},{2,6},{3,7},{4,0},{5,1},{6,2},{7,3},{8,12},{9,13},{10,... | collective-permute-start | bytes 983048 | tf_op jit(solution)/shard_map/ppermute | solution.py:44
  33.2 12.3 %collective-permute-start.19 = (bf16[80,2048]{1,0:T(8,128)(2,1)S(1)}, bf16[80,2048]{1,0:T(8,128)(2,1)S(1)}, u32[]{:S(2)}, u32[]{:S(2)}) collective-permute-start(bf16[80,2048]{1,0:T(8,128)(2,1)S(1)} %slice.27.refs_0_), channel_id=1, source_target_pairs={{0,2},{1,3},{2,0},{3,1},{4,6},{5,7},{6,4},{7,5},{8,10},{9,11},{10,... | collective-permute-start | bytes 983048 | tf_op jit(solution)/shard_map/ppermute | solution.py:44
  33.7 15.3 %slice-start = ((s8[7340032]{0:T(1024)(128)(4,1)}), s8[4194304]{0:T(1024)(128)(4,1)S(1)}, s32[]{:S(2)}) async-start(s8[7340032]{0:T(1024)(128)(4,1)} %bitcast.62), calls=%async_computation | async-start | bytes 8388608
  40.0 14.9 %collective-permute-start.18 = (bf16[80,2048]{1,0:T(8,128)(2,1)S(1)}, bf16[80,2048]{1,0:T(8,128)(2,1)S(1)}, u32[]{:S(2)}, u32[]{:S(2)}) collective-permute-start(bf16[80,2048]{1,0:T(8,128)(2,1)S(1)} %slice.27.refs_0_), channel_id=1, source_target_pairs={{0,1},{1,0},{2,3},{3,2},{4,5},{5,4},{6,7},{7,6},{8,9},{9,8},{10,11... | collective-permute-start | bytes 983048 | tf_op jit(solution)/shard_map/ppermute | solution.py:44
  40.1 8.9 %slice-start.1 = ((s8[7340032]{0:T(1024)(128)(4,1)}), s8[3145728]{0:T(1024)(128)(4,1)S(1)}, s32[]{:S(2)}) async-start(s8[7340032]{0:T(1024)(128)(4,1)} %bitcast.62), calls=%async_computation.1 | async-start | bytes 6291456
  40.1 8.9 %collective-permute-start.11 = (bf16[192,128]{1,0:T(8,128)(2,1)S(1)}, bf16[192,128]{1,0:T(8,128)(2,1)S(1)}, u32[]{:S(2)}, u32[]{:S(2)}) collective-permute-start(bf16[192,128]{1,0:T(8,128)(2,1)S(1)} %add_convert_fusion.15), channel_id=1, source_target_pairs={{0,16},{8,24},{16,0},{24,8},{1,17},{9,25},{17,1},{25,9},{2,18},{10... | collective-permute-start | bytes 147464 | tf_op jit(solution)/shard_map/ppermute | solution.py:44
  42.8 12.2 %collective-permute-start.24 = (bf16[80,2048]{1,0:T(8,128)(2,1)S(1)}, bf16[80,2048]{1,0:T(8,128)(2,1)S(1)}, u32[]{:S(2)}, u32[]{:S(2)}) collective-permute-start(bf16[80,2048]{1,0:T(8,128)(2,1)S(1)} %collective-permute-done.23.refs_6_), channel_id=1, source_target_pairs={{0,1},{1,0},{2,3},{3,2},{4,5},{5,4},{6,7},{7,6},{8,9},{9,8},{10,11... | collective-permute-start | bytes 983048 | tf_op jit(solution)/shard_map/ppermute | solution.py:44
  45.4 9.5 %collective-permute-start.22 = (bf16[80,2048]{1,0:T(8,128)(2,1)S(1)}, bf16[80,2048]{1,0:T(8,128)(2,1)S(1)}, u32[]{:S(2)}, u32[]{:S(2)}) collective-permute-start(bf16[80,2048]{1,0:T(8,128)(2,1)S(1)} %collective-permute-done.21.refs_4_), channel_id=1, source_target_pairs={{0,1},{1,0},{2,3},{3,2},{4,5},{5,4},{6,7},{7,6},{8,9},{9,8},{10,11... | collective-permute-start | bytes 983048 | tf_op jit(solution)/shard_map/ppermute | solution.py:44
  45.5 9.4 %collective-permute-start.20 = (bf16[80,2048]{1,0:T(8,128)(2,1)S(1)}, bf16[80,2048]{1,0:T(8,128)(2,1)S(1)}, u32[]{:S(2)}, u32[]{:S(2)}) collective-permute-start(bf16[80,2048]{1,0:T(8,128)(2,1)S(1)} %collective-permute-done.19.refs_2_), channel_id=1, source_target_pairs={{0,1},{1,0},{2,3},{3,2},{4,5},{5,4},{6,7},{7,6},{8,9},{9,8},{10,11... | collective-permute-start | bytes 983048 | tf_op jit(solution)/shard_map/ppermute | solution.py:44
  52.0 10.6 %slice-start.2 = ((s8[7340032]{0:T(1024)(128)(4,1)}), s8[4194304]{0:T(1024)(128)(4,1)S(1)}, s32[]{:S(2)}) async-start(s8[7340032]{0:T(1024)(128)(4,1)} %bitcast.85), calls=%async_computation.2 | async-start | bytes 8388608
  53.5 9.1 %slice-start.3 = ((s8[7340032]{0:T(1024)(128)(4,1)}), s8[3145728]{0:T(1024)(128)(4,1)S(1)}, s32[]{:S(2)}) async-start(s8[7340032]{0:T(1024)(128)(4,1)} %bitcast.85), calls=%async_computation.3 | async-start | bytes 6291456
  57.0 4.0 %collective-permute-start.25 = (bf16[320,128]{1,0:T(8,128)(2,1)S(1)}, bf16[320,128]{1,0:T(8,128)(2,1)S(1)}, u32[]{:S(2)}, u32[]{:S(2)}) collective-permute-start(bf16[320,128]{1,0:T(8,128)(2,1)S(1)} %bitcast.76), channel_id=1, source_target_pairs={{0,1},{1,0},{2,3},{3,2},{4,5},{5,4},{6,7},{7,6},{8,9},{9,8},{10,11... | collective-permute-start | bytes 245768 | tf_op jit(solution)/shard_map/ppermute | solution.py:44
  57.1 18.1 %collective-permute-start.14 = (bf16[2,2,48,1792]{3,2,1,0:T(8,128)(2,1)S(1)}, bf16[2,2,48,1792]{3,2,1,0:T(8,128)(2,1)S(1)}, u32[]{:S(2)}, u32[]{:S(2)}) collective-permute-start(bf16[2,2,48,1792]{3,2,1,0:T(8,128)(2,1)S(1)} %shard_map.84), channel_id=1, source_target_pairs={{0,8},{24,16},{1,9},{25,17},{2,10},{26,18},{3,11},{27,19},{4,12},{... | collective-permute-start | bytes 2064392 | tf_op jit(solution)/shard_map/ppermute | solution.py:179
  59.5 30.5 %collective-permute-start.12 = (bf16[2,2,48,1792]{3,2,1,0:T(8,128)(2,1)S(1)}, bf16[2,2,48,1792]{3,2,1,0:T(8,128)(2,1)S(1)}, u32[]{:S(2)}, u32[]{:S(2)}) collective-permute-start(bf16[2,2,48,1792]{3,2,1,0:T(8,128)(2,1)S(1)} %shard_map.83), channel_id=1, source_target_pairs={{0,8},{24,16},{1,9},{25,17},{2,10},{26,18},{3,11},{27,19},{4,12},{... | collective-permute-start | bytes 2064392 | tf_op jit(solution)/shard_map/ppermute | solution.py:179
  61.1 4.6 %collective-permute-start.26 = (bf16[320,128]{1,0:T(8,128)(2,1)S(1)}, bf16[320,128]{1,0:T(8,128)(2,1)S(1)}, u32[]{:S(2)}, u32[]{:S(2)}) collective-permute-start(bf16[320,128]{1,0:T(8,128)(2,1)S(1)} %add_convert_fusion.13), channel_id=1, source_target_pairs={{0,2},{1,3},{2,0},{3,1},{4,6},{5,7},{6,4},{7,5},{8,10},{9,11},{10,... | collective-permute-start | bytes 245768 | tf_op jit(solution)/shard_map/ppermute | solution.py:44
  65.7 4.6 %collective-permute-start.27 = (bf16[320,128]{1,0:T(8,128)(2,1)S(1)}, bf16[320,128]{1,0:T(8,128)(2,1)S(1)}, u32[]{:S(2)}, u32[]{:S(2)}) collective-permute-start(bf16[320,128]{1,0:T(8,128)(2,1)S(1)} %add_convert_fusion.12), channel_id=1, source_target_pairs={{0,4},{1,5},{2,6},{3,7},{4,0},{5,1},{6,2},{7,3},{8,12},{9,13},{10,... | collective-permute-start | bytes 245768 | tf_op jit(solution)/shard_map/ppermute | solution.py:44
  70.4 24.0 %collective-permute-start.28 = (bf16[320,128]{1,0:T(8,128)(2,1)S(1)}, bf16[320,128]{1,0:T(8,128)(2,1)S(1)}, u32[]{:S(2)}, u32[]{:S(2)}) collective-permute-start(bf16[320,128]{1,0:T(8,128)(2,1)S(1)} %add_convert_fusion.11), channel_id=1, source_target_pairs={{0,8},{8,0},{16,24},{24,16},{1,9},{9,1},{17,25},{25,17},{2,10},{10... | collective-permute-start | bytes 245768 | tf_op jit(solution)/shard_map/ppermute | solution.py:44
  75.4 65.6 %collective-permute-start.15 = (bf16[2,2,48,1792]{3,2,1,0:T(8,128)(2,1)S(1)}, bf16[2,2,48,1792]{3,2,1,0:T(8,128)(2,1)S(1)}, u32[]{:S(2)}, u32[]{:S(2)}) collective-permute-start(bf16[2,2,48,1792]{3,2,1,0:T(8,128)(2,1)S(1)} %add_convert_fusion.5), channel_id=1, source_target_pairs={{8,16},{16,8},{9,17},{17,9},{10,18},{18,10},{11,19},{19,11},{12,20... | collective-permute-start | bytes 2064392 | tf_op jit(solution)/shard_map/ppermute | solution.py:179
  90.0 44.1 %collective-permute-start.13 = (bf16[2,2,48,1792]{3,2,1,0:T(8,128)(2,1)S(1)}, bf16[2,2,48,1792]{3,2,1,0:T(8,128)(2,1)S(1)}, u32[]{:S(2)}, u32[]{:S(2)}) collective-permute-start(bf16[2,2,48,1792]{3,2,1,0:T(8,128)(2,1)S(1)} %shard_map.85), channel_id=1, source_target_pairs={{0,8},{24,16},{1,9},{25,17},{2,10},{26,18},{3,11},{27,19},{4,12},{... | collective-permute-start | bytes 2064392 | tf_op jit(solution)/shard_map/ppermute | solution.py:179
  94.5 15.4 %collective-permute-start.29 = (bf16[320,128]{1,0:T(8,128)(2,1)S(1)}, bf16[320,128]{1,0:T(8,128)(2,1)S(1)}, u32[]{:S(2)}, u32[]{:S(2)}) collective-permute-start(bf16[320,128]{1,0:T(8,128)(2,1)S(1)} %add_convert_fusion.10), channel_id=1, source_target_pairs={{0,16},{8,24},{16,0},{24,8},{1,17},{9,25},{17,1},{25,9},{2,18},{10... | collective-permute-start | bytes 245768 | tf_op jit(solution)/shard_map/ppermute | solution.py:44
  96.2 28.6 %collective-permute-start.16 = (bf16[2,2,48,1792]{3,2,1,0:T(8,128)(2,1)S(1)}, bf16[2,2,48,1792]{3,2,1,0:T(8,128)(2,1)S(1)}, u32[]{:S(2)}, u32[]{:S(2)}) collective-permute-start(bf16[2,2,48,1792]{3,2,1,0:T(8,128)(2,1)S(1)} %add_convert_fusion.4), channel_id=1, source_target_pairs={{8,16},{16,8},{9,17},{17,9},{10,18},{18,10},{11,19},{19,11},{12,20... | collective-permute-start | bytes 2064392 | tf_op jit(solution)/shard_map/ppermute | solution.py:179
  115.7 23.0 %collective-permute-start.30 = (bf16[2,2,48,1792]{3,2,1,0:T(8,128)(2,1)S(1)}, bf16[2,2,48,1792]{3,2,1,0:T(8,128)(2,1)S(1)}, u32[]{:S(2)}, u32[]{:S(2)}) collective-permute-start(bf16[2,2,48,1792]{3,2,1,0:T(8,128)(2,1)S(1)} %shard_map.88), channel_id=1, source_target_pairs={{0,8},{24,16},{1,9},{25,17},{2,10},{26,18},{3,11},{27,19},{4,12},{... | collective-permute-start | bytes 2064392 | tf_op jit(solution)/shard_map/ppermute | solution.py:179
  125.0 16.8 %collective-permute-start.17 = (bf16[2,2,48,1792]{3,2,1,0:T(8,128)(2,1)S(1)}, bf16[2,2,48,1792]{3,2,1,0:T(8,128)(2,1)S(1)}, u32[]{:S(2)}, u32[]{:S(2)}) collective-permute-start(bf16[2,2,48,1792]{3,2,1,0:T(8,128)(2,1)S(1)} %add_convert_fusion.3), channel_id=1, source_target_pairs={{16,24},{8,0},{17,25},{9,1},{18,26},{10,2},{19,27},{11,3},{20,28},... | collective-permute-start | bytes 2064392 | tf_op jit(solution)/shard_map/ppermute | solution.py:179
  134.1 20.5 %collective-permute-start.32 = (bf16[2,2,48,1792]{3,2,1,0:T(8,128)(2,1)S(1)}, bf16[2,2,48,1792]{3,2,1,0:T(8,128)(2,1)S(1)}, u32[]{:S(2)}, u32[]{:S(2)}) collective-permute-start(bf16[2,2,48,1792]{3,2,1,0:T(8,128)(2,1)S(1)} %shard_map.89), channel_id=1, source_target_pairs={{0,8},{24,16},{1,9},{25,17},{2,10},{26,18},{3,11},{27,19},{4,12},{... | collective-permute-start | bytes 2064392 | tf_op jit(solution)/shard_map/ppermute | solution.py:179
  138.8 30.6 %collective-permute-start.31 = (bf16[2,2,48,1792]{3,2,1,0:T(8,128)(2,1)S(1)}, bf16[2,2,48,1792]{3,2,1,0:T(8,128)(2,1)S(1)}, u32[]{:S(2)}, u32[]{:S(2)}) collective-permute-start(bf16[2,2,48,1792]{3,2,1,0:T(8,128)(2,1)S(1)} %shard_map.90), channel_id=1, source_target_pairs={{0,8},{24,16},{1,9},{25,17},{2,10},{26,18},{3,11},{27,19},{4,12},{... | collective-permute-start | bytes 2064392 | tf_op jit(solution)/shard_map/ppermute | solution.py:179
  140.3 21.0 %collective-permute-start.34 = (bf16[2,2,48,1792]{3,2,1,0:T(8,128)(2,1)S(1)}, bf16[2,2,48,1792]{3,2,1,0:T(8,128)(2,1)S(1)}, u32[]{:S(2)}, u32[]{:S(2)}) collective-permute-start(bf16[2,2,48,1792]{3,2,1,0:T(8,128)(2,1)S(1)} %add_convert_fusion.1), channel_id=1, source_target_pairs={{8,16},{16,8},{9,17},{17,9},{10,18},{18,10},{11,19},{19,11},{12,20... | collective-permute-start | bytes 2064392 | tf_op jit(solution)/shard_map/ppermute | solution.py:179
  155.0 36.3 %collective-permute-start.33 = (bf16[2,2,48,1792]{3,2,1,0:T(8,128)(2,1)S(1)}, bf16[2,2,48,1792]{3,2,1,0:T(8,128)(2,1)S(1)}, u32[]{:S(2)}, u32[]{:S(2)}) collective-permute-start(bf16[2,2,48,1792]{3,2,1,0:T(8,128)(2,1)S(1)} %add_convert_fusion.2), channel_id=1, source_target_pairs={{8,16},{16,8},{9,17},{17,9},{10,18},{18,10},{11,19},{19,11},{12,20... | collective-permute-start | bytes 2064392 | tf_op jit(solution)/shard_map/ppermute | solution.py:179
  155.7 23.5 %collective-permute-start.36 = (bf16[2,2,32,1792]{3,2,1,0:T(8,128)(2,1)S(1)}, bf16[2,2,32,1792]{3,2,1,0:T(8,128)(2,1)S(1)}, u32[]{:S(2)}, u32[]{:S(2)}) collective-permute-start(bf16[2,2,32,1792]{3,2,1,0:T(8,128)(2,1)S(1)} %shard_map.92), channel_id=1, source_target_pairs={{0,8},{24,16},{1,9},{25,17},{2,10},{26,18},{3,11},{27,19},{4,12},{... | collective-permute-start | bytes 1376264 | tf_op jit(solution)/shard_map/ppermute | solution.py:179
  161.5 29.8 %collective-permute-start.35 = (bf16[2,2,48,1792]{3,2,1,0:T(8,128)(2,1)S(1)}, bf16[2,2,48,1792]{3,2,1,0:T(8,128)(2,1)S(1)}, u32[]{:S(2)}, u32[]{:S(2)}) collective-permute-start(bf16[2,2,48,1792]{3,2,1,0:T(8,128)(2,1)S(1)} %add_convert_fusion), channel_id=1, source_target_pairs={{16,24},{8,0},{17,25},{9,1},{18,26},{10,2},{19,27},{11,3},{20,28},... | collective-permute-start | bytes 2064392 | tf_op jit(solution)/shard_map/ppermute | solution.py:179
  169.4 19.7 %collective-permute-start.38 = (bf16[2,2,32,1792]{3,2,1,0:T(8,128)(2,1)S(1)}, bf16[2,2,32,1792]{3,2,1,0:T(8,128)(2,1)S(1)}, u32[]{:S(2)}, u32[]{:S(2)}) collective-permute-start(bf16[2,2,32,1792]{3,2,1,0:T(8,128)(2,1)S(1)} %shard_map.93), channel_id=1, source_target_pairs={{0,8},{24,16},{1,9},{25,17},{2,10},{26,18},{3,11},{27,19},{4,12},{... | collective-permute-start | bytes 1376264 | tf_op jit(solution)/shard_map/ppermute | solution.py:179
  179.2 15.9 %collective-permute-start.37 = (bf16[2,2,32,1792]{3,2,1,0:T(8,128)(2,1)S(1)}, bf16[2,2,32,1792]{3,2,1,0:T(8,128)(2,1)S(1)}, u32[]{:S(2)}, u32[]{:S(2)}) collective-permute-start(bf16[2,2,32,1792]{3,2,1,0:T(8,128)(2,1)S(1)} %shard_map.94), channel_id=1, source_target_pairs={{0,8},{24,16},{1,9},{25,17},{2,10},{26,18},{3,11},{27,19},{4,12},{... | collective-permute-start | bytes 1376264 | tf_op jit(solution)/shard_map/ppermute | solution.py:179
  183.7 6.1 %collective-permute-start.40 = (bf16[2,2,32,1792]{3,2,1,0:T(8,128)(2,1)S(1)}, bf16[2,2,32,1792]{3,2,1,0:T(8,128)(2,1)S(1)}, u32[]{:S(2)}, u32[]{:S(2)}) collective-permute-start(bf16[2,2,32,1792]{3,2,1,0:T(8,128)(2,1)S(1)} %add_convert_fusion.7), channel_id=1, source_target_pairs={{8,16},{16,8},{9,17},{17,9},{10,18},{18,10},{11,19},{19,11},{12,20... | collective-permute-start | bytes 1376264 | tf_op jit(solution)/shard_map/ppermute | solution.py:179
  189.1 6.0 %collective-permute-start.39 = (bf16[2,2,32,1792]{3,2,1,0:T(8,128)(2,1)S(1)}, bf16[2,2,32,1792]{3,2,1,0:T(8,128)(2,1)S(1)}, u32[]{:S(2)}, u32[]{:S(2)}) collective-permute-start(bf16[2,2,32,1792]{3,2,1,0:T(8,128)(2,1)S(1)} %add_convert_fusion.8), channel_id=1, source_target_pairs={{8,16},{16,8},{9,17},{17,9},{10,18},{18,10},{11,19},{19,11},{12,20... | collective-permute-start | bytes 1376264 | tf_op jit(solution)/shard_map/ppermute | solution.py:179
  189.9 16.1 %collective-permute-start.41 = (bf16[2,2,32,1792]{3,2,1,0:T(8,128)(2,1)S(1)}, bf16[2,2,32,1792]{3,2,1,0:T(8,128)(2,1)S(1)}, u32[]{:S(2)}, u32[]{:S(2)}) collective-permute-start(bf16[2,2,32,1792]{3,2,1,0:T(8,128)(2,1)S(1)} %add_convert_fusion.6), channel_id=1, source_target_pairs={{16,24},{8,0},{17,25},{9,1},{18,26},{10,2},{19,27},{11,3},{20,28},... | collective-permute-start | bytes 1376264 | tf_op jit(solution)/shard_map/ppermute | solution.py:179
  (3 other events, 11.9 us)

commit v5 on v4

v5 whole, which is shorter than its diff:
```python
import functools

import jax
import jax.numpy as jnp
from jax import lax
from jax.experimental import pallas as pl
from jax.experimental.pallas import tpu as pltpu
from jax.sharding import PartitionSpec as P

SEG_ROWS = 128
GROUPS = ((48,), (80,))
AHEAD = 1 << 36

low_rank_scale = 0.5


def slots_of(segment, req_len, req_adapter, owner_slot):
    order = jnp.arange(req_len.shape[0], dtype=jnp.int32)
    ends = jnp.sum(jnp.where(order[:, None] <= order[None, :], req_len[:, None], 0), axis=0)
    seg_request = jnp.sum((ends[None, :] <= segment[:, None]).astype(jnp.int32), axis=1)
    adapter = jnp.sum(jnp.where(seg_request[:, None] == order[None, :], req_adapter[None, :], 0), axis=1)
    ids = jnp.arange(owner_slot.shape[0], dtype=jnp.int32)
    return jnp.sum(jnp.where(adapter[:, None] == ids[None, :], owner_slot[None, :], 0), axis=1)


def chunk_of(slot, nseq):
    me = lax.axis_index("seq")
    half = me < nseq // 2
    far = jnp.where(half, nseq - 1 - me, me)
    near = slot - far
    far_chunk = jnp.where(half, nseq - 1 - slot, slot)
    near_chunk = jnp.where(half, near, nseq - 1 - near)
    chunk = jnp.where(slot < far, far_chunk, near_chunk)
    return jnp.where(slot == nseq - 1, me, chunk)


def held(seg_slot, first, count):
    local = seg_slot - first
    here = (local >= 0) & (local < count)
    return jnp.clip(local, 0, count - 1), here.astype(jnp.int32)


def swap(x, axis, size, mask):
    return lax.ppermute(x, axis, [(i, i ^ mask) for i in range(size)])


def gather_rows(x, ntp):
    chips = [x] + [swap(x, "tp", ntp, 2 * m) for m in range(1, ntp // 2)]
    pieces = []
    for piece in chips:
        pieces += [piece, swap(piece, "tp", ntp, 1)]
    return pieces


def sum_one_step(x, axis, size):
    parts = [lax.ppermute(x, axis, [(i, (i + k) % size) for i in range(size)]) for k in range(1, size)]
    total = x.astype(jnp.float32)
    for part in parts:
        total = total + part.astype(jnp.float32)
    return total.astype(x.dtype)


def sum_beside(x, axis, size, beside):
    done = []
    mask = 1
    while mask < size:
        other = swap(x, axis, size, mask)
        if mask > 1 or axis != "tp":
            done.append(beside(x))
            other = after(other, done[-1]) if done[-1] is not None else other
        x = add(x, other)
        mask *= 2
    return x, done


def assemble_kernel(segs, group, tab_ref, *refs):
    pieces, down_ref, xs, inner_ref = refs[:segs], refs[segs], refs[segs + 1:-1], refs[-1]
    me = tab_ref[2, 0]
    for n, piece in enumerate(pieces):
        start = 0
        for x_ref, rows in zip(xs, group):
            x_ref[tab_ref[3, me ^ n]] = piece[start:start + rows]
            start += rows
    start = 0
    for x_ref, rows in zip(xs, group):
        for pair in range(segs // 2):
            halves = []
            for k in (2 * pair, 2 * pair + 1):
                product = lax.dot_general(
                    x_ref[tab_ref[3, k]],
                    down_ref[tab_ref[0, k]],
                    (((1,), (1,)), ((), ())),
                    preferred_element_type=jnp.float32,
                )
                halves.append(product * tab_ref[1, k].astype(jnp.float32))
            inner_ref[pair, start:start + rows] = jnp.concatenate(halves, axis=1).astype(jnp.bfloat16)
        start += rows


def assemble(pieces, group, down_pool, table, hint):
    segs = len(pieces)
    total, width = pieces[0].shape
    rank = down_pool.shape[1]
    vmem = pl.BlockSpec(memory_space=pltpu.VMEM)
    *xs, mine = pl.pallas_call(
        functools.partial(assemble_kernel, segs, group),
        out_shape=[jax.ShapeDtypeStruct((segs, rows, width), jnp.bfloat16) for rows in group]
        + [jax.ShapeDtypeStruct((segs // 2, total, 2 * rank), jnp.bfloat16)],
        in_specs=[pl.BlockSpec(memory_space=pltpu.SMEM)] + [vmem] * (segs + 1),
        out_specs=[vmem] * (len(group) + 1),
        compiler_params=pltpu.CompilerParams(vmem_limit_bytes=32 << 20),
        cost_estimate=pl.CostEstimate(flops=hint, bytes_accessed=4 * segs * total * width, transcendentals=0),
    )(table, *pieces, down_pool)
    return xs, mine


def project_kernel(x_ref, weight_ref, out_ref):
    out_ref[...] = jnp.dot(x_ref[...], weight_ref[...], preferred_element_type=jnp.float32).astype(jnp.bfloat16)


def project(x, weight, first, count, tile, hint=0):
    width = weight.shape[0]
    rows = x.shape[0]
    return pl.pallas_call(
        project_kernel,
        out_shape=jax.ShapeDtypeStruct((rows, count * tile), jnp.bfloat16),
        grid=(count,),
        in_specs=[
            pl.BlockSpec((rows, width), lambda n: (0, 0)),
            pl.BlockSpec((width, tile), lambda n: (0, first + n)),
        ],
        out_specs=pl.BlockSpec((rows, tile), lambda n: (0, n)),
        compiler_params=pltpu.CompilerParams(vmem_limit_bytes=16 << 20),
        cost_estimate=pl.CostEstimate(
            flops=hint or 2 * rows * width * count * tile, bytes_accessed=2 * width * count * tile, transcendentals=0
        ),
    )(x, weight)


def low_rank_kernel(first, each, start, widths, tab_ref, inner_ref, *refs):
    parts, ups, out_ref = refs[:2 * len(widths)], refs[2 * len(widths):-1], refs[-1]
    slot = first + pl.program_id(0)
    lanes = inner_ref.shape[2]
    rank = lanes // 2
    rows = out_ref.shape[3]
    lane = lax.broadcasted_iota(jnp.int32, (rows, lanes), 1)
    for e in range(each):
        seg = tab_ref[2, slot * each + e]
        mine = (lane // rank == seg % 2) & (tab_ref[1, slot * each + e] == 1)
        inner = inner_ref[seg // 2][start:start + rows].astype(jnp.float32)
        inner = (jnp.where(mine, inner, 0.0) * low_rank_scale).astype(jnp.bfloat16)
        for which in range(2):
            column = 0
            for n, width in enumerate(widths):
                factor = ups[e][0, which, :, column:column + width]
                low = jnp.dot(inner, jnp.concatenate([factor, factor], axis=0), preferred_element_type=jnp.float32)
                term = parts[which * len(widths) + n][e * rows:(e + 1) * rows].astype(jnp.float32) + low
                out_ref[0, which, e, :, column:column + width] = term.astype(jnp.bfloat16)
                column += width


def add_low_rank(parts, inner, start, rows, first, count, up_pool, table, each, hint=1 << 10):
    columns = up_pool.shape[3]
    rank = up_pool.shape[2]
    widths = [part.shape[1] for part in parts[:len(parts) // 2]]

    def up_spec(e):
        return pl.BlockSpec((1, 2, rank, columns), lambda n, tab: (tab[0, (first + n) * each + e], 0, 0, 0))

    return pl.pallas_call(
        functools.partial(low_rank_kernel, first, each, start, widths),
        out_shape=jax.ShapeDtypeStruct((count, 2, each, rows, columns), jnp.bfloat16),
        grid_spec=pltpu.PrefetchScalarGridSpec(
            num_scalar_prefetch=1,
            grid=(count,),
            in_specs=[pl.BlockSpec(inner.shape, lambda n, tab: (0, 0, 0))]
            + [pl.BlockSpec((each * rows, part.shape[1]), lambda n, tab: (first + n, 0)) for part in parts]
            + [up_spec(e) for e in range(each)],
            out_specs=pl.BlockSpec((1, 2, each, rows, columns), lambda n, tab: (n, 0, 0, 0, 0)),
        ),
        compiler_params=pltpu.CompilerParams(vmem_limit_bytes=24 << 20),
        cost_estimate=pl.CostEstimate(flops=hint, bytes_accessed=1 << 10, transcendentals=0),
    )(table, inner, *parts, *([up_pool] * each))


def add(x, y):
    return (x.astype(jnp.float32) + y.astype(jnp.float32)).astype(x.dtype)


def hop_pairs(level, nseq):
    return [(level, level + 1), (nseq - 1 - level, nseq - 2 - level)]


def scatter_line(own, first, nseq):
    last = nseq - 2
    arrived = {(0, slot): hop for slot, hop in enumerate(first)}
    for step in range(nseq - 1):
        for level in range(1, step + 1):
            slot = step - level if level < nseq // 2 else step
            send = add(own[slot], arrived[level - 1, step - 1])
            arrived[level, step] = lax.ppermute(send, "seq", hop_pairs(level, nseq))
    total = own[nseq - 1].astype(jnp.float32)
    for level in range(nseq - 1):
        total = total + arrived[level, last].astype(jnp.float32)
    return total


def after(x, gate):
    return lax.optimization_barrier((x, gate))[0]


def shards(tokens, gate_weight, up_weight, down_pool, up_pool, req_len, req_adapter, owner_slot):
    nseq = lax.axis_size("seq")
    ntp = lax.axis_size("tp")
    each = ntp // nseq
    me = lax.axis_index("tp")
    place = jnp.arange(ntp, dtype=jnp.int32)
    ordered = chunk_of(place // each, nseq) * each + place % each
    position = jnp.sum(jnp.where(ordered[:, None] == place[None, :], place[:, None], 0), axis=0)
    down_slot, down_here = held(
        slots_of(place, req_len, req_adapter, owner_slot), me * down_pool.shape[0], down_pool.shape[0]
    )
    up_slot, up_here = held(
        slots_of(ordered, req_len, req_adapter, owner_slot),
        lax.axis_index("seq") * up_pool.shape[0],
        up_pool.shape[0],
    )
    down_table = jnp.stack([down_slot, down_here, jnp.full_like(down_slot, me), position])
    up_table = jnp.stack([up_slot, up_here, ordered])
    columns = gate_weight.shape[1]
    tile = 256 if columns % 256 == 0 else 128
    tiles = columns // tile
    first, second = GROUPS
    rows = first[0]

    pieces = gather_rows(tokens[:rows], ntp)
    (x,), mine = assemble(pieces, first, down_pool, down_table, 1 << 20)
    x = x.reshape(-1, x.shape[2])
    cuts = [(w, f, c) for w in (gate_weight, up_weight) for f, c in ((0, tiles // 2), (tiles // 2, tiles - tiles // 2))]
    left = list(cuts)

    def piece(gate):
        if not left:
            return None
        weight, begin, count = left.pop(0)
        return project(after(x, gate), weight, begin, count, tile)

    shared, parts = sum_beside(mine.reshape(-1, mine.shape[2]), "tp", ntp, piece)
    pieces = gather_rows(after(tokens[rows:], shared), ntp)
    inner, more = sum_beside(shared, "seq", nseq, piece)
    parts = [part for part in parts + more if part is not None]
    inner = inner.reshape(mine.shape)

    def terms(parts, inner, start, rows, first, count, gate, hint=1 << 10):
        given = after(inner, gate) if gate is not None else inner
        return add_low_rank(parts, given, start, rows, first, count, up_pool, up_table, each, hint)

    def first_hop(send):
        return lax.ppermute(send, "seq", hop_pairs(0, nseq))

    head = terms(parts, inner, 0, rows, 0, 1, None)
    pieces = list(after(tuple(pieces), head))
    (x,), mine = assemble(pieces, second, down_pool, down_table, AHEAD)
    head_hop = first_hop(head)
    shared, _ = sum_beside(mine.reshape(-1, mine.shape[2]), "tp", ntp, lambda gate: None)
    rest = terms(parts, inner, 0, rows, 1, nseq - 2, shared)
    rest_hop = first_hop(rest)
    kept = terms(parts, inner, 0, rows, nseq - 1, 1, rest)
    inner = sum_one_step(shared, "seq", nseq).reshape(mine.shape)
    x = after(x.reshape(-1, x.shape[2]), (head_hop, kept))
    own = [head[0]] + [rest[slot] for slot in range(nseq - 2)] + [kept[0]]

    rows = second[0]
    parts = [project(x, weight, 0, tiles, tile, AHEAD) for weight in (gate_weight, up_weight)]
    sent = [terms(parts, inner, 0, rows, 0, 1, None)]
    for slot in range(1, nseq):
        sent.append(terms(parts, inner, 0, rows, slot, 1, sent[-1]))
    head_hop = after(head_hop, sent[0])
    rest_hop = after(rest_hop, sent[-1])
    hops = []
    for slot in range(nseq - 1):
        hops.append(first_hop(after(sent[slot], hops[slot - 2] if slot > 1 else rest_hop)))

    totals = [
        scatter_line(own, [head_hop[0]] + [rest_hop[slot] for slot in range(nseq - 2)], nseq),
        scatter_line([term[0] for term in sent], [hop[0] for hop in hops], nseq),
    ]
    out = [(jax.nn.silu(total[0]) * total[1]).astype(jnp.bfloat16) for total in totals]
    return jnp.concatenate(out, axis=1).reshape(-1, columns)


def solution(mesh):
    placed = (
        P("tp", "seq"),
        P("seq", "tp"),
        P("seq", "tp"),
        P("tp", None, "seq"),
        P("seq", None, None, "tp"),
        P(),
        P(),
        P(),
    )
    return jax.shard_map(
        shards, mesh=mesh, in_specs=placed, out_specs=P("seq", "tp"), check_vma=False
    )
```

time: 208 us -> 208 us (level)
  the two profiles are of different devices: /device:TPU:0 before, /device:TPU:16 now
where the time goes in v5:
time: 208 us; the launch traced here: 207 us
  waiting for transfers between devices  118 us (57%)
  starting transfers between devices  36.9 us (18%)
  Pallas kernels  34.2 us (16%)
  other arithmetic  11.7 us (6%)
  local copies, waits for them, and re-layouts  6.34 us (3%)
    ppermute x5, waiting for transfers between devices, first_hop(): return lax.ppermute(send, 'seq', hop_pairs(0, nseq))  55.2 us
    ppermute x6, waiting for transfers between devices, scatter_line(): arrived[level, step] = lax.ppermute(send, 'seq', hop_pairs(level, nseq))  35 us
    ppermute x22, waiting for transfers between devices, swap(): return lax.ppermute(x, axis, [(i, i ^ mask) for i in range(size)])  27.5 us
    pallas_call x6, Pallas kernels, project(): pl.pallas_call(project_kernel, out_shape=jax.ShapeDtypeStruct((rows, coun...  22.8 us
    ppermute x22, starting transfers between devices, swap(): return lax.ppermute(x, axis, [(i, i ^ mask) for i in range(size)])  13.8 us
    ppermute x6, starting transfers between devices, scatter_line(): arrived[level, step] = lax.ppermute(send, 'seq', hop_pairs(level, nseq))  12.6 us
    pallas_call x7, Pallas kernels, add_low_rank(): pl.pallas_call(functools.partial(low_rank_kernel, first, each, start, wid...  8.28 us
    ppermute x5, starting transfers between devices, first_hop(): return lax.ppermute(send, 'seq', hop_pairs(0, nseq))  6.44 us
  transfers between devices with their start and end apart: 36, of which 18 were waited for; matrix products, arithmetic and copies ran while one was open for 5% of the time, Pallas kernels for 15%

profile of v5, /device:TPU:16, one launch (start us, length us, event | category | flops | bytes accessed | tf_op | source)
XLA Modules:
  0.0 207.4 jit_solution(4109807846444302699)
XLA Ops:
  0.9 1.6 collective-permute-start.1
  2.5 1.5 collective-permute-start.3
  7.2 1.6 collective-permute-done.1.refs_2_
  8.8 4.3 %collective-permute-done.3.refs_4_ = bf16[48,2048]{1,0:T(8,128)(2,1)S(1)} collective-permute-done((bf16[48,2048]{1,0:T(8,128)(2,1)S(1)}, bf16[48,2048]{1,0:T(8,128)(2,1)S(1)}, u32[]{:S(2)}, u32[]{:S(2)}) %collective-permute-start.3) | collective-permute-done | bytes 196640 | tf_op jit(solution)/shard_map/ppermute | solution.py:44
  14.8 1.6 copy-done.3
  16.4 1.4 shard_map.82
  20.1 3.1 %copy-done = bf16[2048,1792]{1,0:T(8,128)(2,1)S(1)} copy-done((bf16[2048,1792]{1,0:T(8,128)(2,1)S(1)}, bf16[2048,1792]{1,0:T(8,128)(2,1)}, u32[]{:S(2)}) %copy-start) | copy-done | bytes 7340056
  23.2 2.0 shard_map.83.refs_0_
  25.3 1.2 collective-permute-start.9
  26.4 2.7 %shard_map.84.refs_1_ = bf16[384,1024]{1,0:T(8,128)(2,1)S(1)} custom-call(bf16[384,2048]{1,0:T(8,128)(2,1)S(1)} %bitcast.72, bf16[2048,1792]{1,0:T(8,128)(2,1)S(1)} %copy-done), custom_call_target="tpu_custom_call" | custom-call | flops 1610612736 | bytes 4194304 | tf_op jit(solution)/shard_map/pallas_call | solution.py:124
  29.5 1.6 collective-permute-start.10
  31.1 1.2 collective-permute-start.13
  32.3 1.4 collective-permute-start.15
  34.6 2.0 shard_map.85.refs_2_
  37.1 4.7 %collective-permute-done.13.refs_2_ = bf16[80,2048]{1,0:T(8,128)(2,1)S(1)} collective-permute-done((bf16[80,2048]{1,0:T(8,128)(2,1)S(1)}, bf16[80,2048]{1,0:T(8,128)(2,1)S(1)}, u32[]{:S(2)}, u32[]{:S(2)}) %collective-permute-start.13) | collective-permute-done | bytes 327712 | tf_op jit(solution)/shard_map/ppermute | solution.py:44
  41.7 6.3 %collective-permute-done.15.refs_4_ = bf16[80,2048]{1,0:T(8,128)(2,1)S(1)} collective-permute-done((bf16[80,2048]{1,0:T(8,128)(2,1)S(1)}, bf16[80,2048]{1,0:T(8,128)(2,1)S(1)}, u32[]{:S(2)}, u32[]{:S(2)}) %collective-permute-start.15) | collective-permute-done | bytes 327712 | tf_op jit(solution)/shard_map/ppermute | solution.py:44
  48.6 2.7 %shard_map.86.refs_3_ = bf16[384,1024]{1,0:T(8,128)(2,1)S(1)} custom-call(bf16[384,2048]{1,0:T(8,128)(2,1)S(1)} %bitcast.74, bf16[2048,1792]{1,0:T(8,128)(2,1)S(1)} %bitcast.68), custom_call_target="tpu_custom_call" | custom-call | flops 1610612736 | bytes 4194304 | tf_op jit(solution)/shard_map/pallas_call | solution.py:124
  53.0 1.7 shard_map.88
  54.7 1.3 collective-permute-start.26
  56.7 4.3 %collective-permute-done.20 = bf16[320,128]{1,0:T(8,128)(2,1)S(1)} collective-permute-done((bf16[320,128]{1,0:T(8,128)(2,1)S(1)}, bf16[320,128]{1,0:T(8,128)(2,1)S(1)}, u32[]{:S(2)}, u32[]{:S(2)}) %collective-permute-start.20) | collective-permute-done | bytes 81952 | tf_op jit(solution)/shard_map/ppermute | solution.py:44
  61.6 3.9 %collective-permute-done.21 = bf16[320,128]{1,0:T(8,128)(2,1)S(1)} collective-permute-done((bf16[320,128]{1,0:T(8,128)(2,1)S(1)}, bf16[320,128]{1,0:T(8,128)(2,1)S(1)}, u32[]{:S(2)}, u32[]{:S(2)}) %collective-permute-start.21) | collective-permute-done | bytes 81952 | tf_op jit(solution)/shard_map/ppermute | solution.py:44
  66.2 2.4 %collective-permute-start.23 = (bf16[320,128]{1,0:T(8,128)(2,1)}, bf16[320,128]{1,0:T(8,128)(2,1)}, u32[]{:S(2)}, u32[]{:S(2)}) collective-permute-start(bf16[320,128]{1,0:T(8,128)(2,1)} %add_convert_fusion.5), channel_id=1, source_target_pairs={{0,8},{8,16},{16,24},{24,0},{1,9},{9,17},{17,25},{25,1},{2,10},{10... | collective-permute-start | bytes 245768 | tf_op jit(solution)/shard_map/ppermute | solution.py:56
  68.6 1.7 collective-permute-start.25
  70.2 2.3 %shard_map.89 = bf16[2,2,2,48,1792]{4,3,2,1,0:T(8,128)(2,1)} custom-call(s32[3,8]{1,0:T(4,128)S(1)} %pad_add_fusion.tab_ref, bf16[4,48,128]{2,1,0:T(8,128)(2,1)S(1)} %bitcast.80, bf16[384,768]{1,0:T(8,128)(2,1)S(1)} %shard_map.83.refs_0_, bf16[384,1024]{1,0:T(8,128)(2,1)S(1)} %shard_map.84.refs_1_, bf16[384,768]{1,0:T(8,128)(2,1)S(1)} %shard_map.85.refs_2_, ...), custom_call_target="tpu_custom_call" | custom-call | flops 1024 | bytes 1024 | tf_op jit(solution)/shard_map/pallas_call | solution.py:170
  72.5 1.3 collective-permute-start.22
  74.9 6.7 %shard_map.91.refs_0_ = bf16[640,1792]{1,0:T(8,128)(2,1)S(1)} custom-call(bf16[640,2048]{1,0:T(8,128)(2,1)S(1)} %bitcast.84, bf16[2048,1792]{1,0:T(8,128)(2,1)S(1)} %bitcast.66), custom_call_target="tpu_custom_call" | custom-call | flops 68719476736 | bytes 7340032 | tf_op jit(solution)/shard_map/pallas_call | solution.py:124
  81.6 6.7 %shard_map.92.refs_1_ = bf16[640,1792]{1,0:T(8,128)(2,1)S(1)} custom-call(bf16[640,2048]{1,0:T(8,128)(2,1)S(1)} %bitcast.85, bf16[2048,1792]{1,0:T(8,128)(2,1)S(1)} %bitcast.70), custom_call_target="tpu_custom_call" | custom-call | flops 68719476736 | bytes 7340032 | tf_op jit(solution)/shard_map/pallas_call | solution.py:124
  88.3 1.1 add_convert_fusion.4
  92.5 1.0 shard_map.96
  93.5 15.8 %collective-permute-done.22 = bf16[2,2,2,48,1792]{4,3,2,1,0:T(8,128)(2,1)} collective-permute-done((bf16[2,2,2,48,1792]{4,3,2,1,0:T(8,128)(2,1)}, bf16[2,2,2,48,1792]{4,3,2,1,0:T(8,128)(2,1)}, u32[]{:S(2)}, u32[]{:S(2)}) %collective-permute-start.22) | collective-permute-done | bytes 1376288 | tf_op jit(solution)/shard_map/ppermute | solution.py:259
  109.3 1.3 collective-permute-start.30
  110.8 1.9 collective-permute-start.28
  112.7 1.3 collective-permute-start.32
  114.0 25.4 %collective-permute-done.30 = bf16[1,2,2,80,1792]{4,3,2,1,0:T(8,128)(2,1)S(1)} collective-permute-done((bf16[1,2,2,80,1792]{4,3,2,1,0:T(8,128)(2,1)S(1)}, bf16[1,2,2,80,1792]{4,3,2,1,0:T(8,128)(2,1)S(1)}, u32[]{:S(2)}, u32[]{:S(2)}) %collective-permute-start.30) | collective-permute-done | bytes 1146912 | tf_op jit(solution)/shard_map/ppermute | solution.py:259
  139.7 2.1 %collective-permute-start.34 = (bf16[2,2,80,1792]{3,2,1,0:T(8,128)(2,1)S(1)}, bf16[2,2,80,1792]{3,2,1,0:T(8,128)(2,1)S(1)}, u32[]{:S(2)}, u32[]{:S(2)}) collective-permute-start(bf16[2,2,80,1792]{3,2,1,0:T(8,128)(2,1)S(1)} %fusion.5), channel_id=1, source_target_pairs={{8,16},{16,8},{9,17},{17,9},{10,18},{18,10},{11,19},{19,11},{12,20... | collective-permute-start | bytes 3440648 | tf_op jit(solution)/shard_map/ppermute | solution.py:201
  141.8 1.3 fusion.2
  143.1 1.3 collective-permute-start.29
  144.4 1.5 fusion.8
  145.9 3.9 %collective-permute-start.27 = (bf16[2,2,48,1792]{3,2,1,0:T(8,128)(2,1)S(1)}, bf16[2,2,48,1792]{3,2,1,0:T(8,128)(2,1)S(1)}, u32[]{:S(2)}, u32[]{:S(2)}) collective-permute-start(bf16[2,2,48,1792]{3,2,1,0:T(8,128)(2,1)S(1)} %fusion.8), channel_id=1, source_target_pairs={{8,16},{16,8},{9,17},{17,9},{10,18},{18,10},{11,19},{19,11},{12,20... | collective-permute-start | bytes 2064392 | tf_op jit(solution)/shard_map/ppermute | solution.py:201
  149.8 1.3 collective-permute-start.31
  151.1 12.8 %collective-permute-done.32 = bf16[1,2,2,80,1792]{4,3,2,1,0:T(8,128)(2,1)S(1)} collective-permute-done((bf16[1,2,2,80,1792]{4,3,2,1,0:T(8,128)(2,1)S(1)}, bf16[1,2,2,80,1792]{4,3,2,1,0:T(8,128)(2,1)S(1)}, u32[]{:S(2)}, u32[]{:S(2)}) %collective-permute-start.32) | collective-permute-done | bytes 1146912 | tf_op jit(solution)/shard_map/ppermute | solution.py:259
  164.2 1.9 collective-permute-start.33
  166.1 3.6 %collective-permute-done.34 = bf16[2,2,80,1792]{3,2,1,0:T(8,128)(2,1)S(1)} collective-permute-done((bf16[2,2,80,1792]{3,2,1,0:T(8,128)(2,1)S(1)}, bf16[2,2,80,1792]{3,2,1,0:T(8,128)(2,1)S(1)}, u32[]{:S(2)}, u32[]{:S(2)}) %collective-permute-start.34) | collective-permute-done | bytes 1146912 | tf_op jit(solution)/shard_map/ppermute | solution.py:201
  170.0 1.4 collective-permute-start.35
  171.4 13.1 %collective-permute-done.27 = bf16[2,2,48,1792]{3,2,1,0:T(8,128)(2,1)S(1)} collective-permute-done((bf16[2,2,48,1792]{3,2,1,0:T(8,128)(2,1)S(1)}, bf16[2,2,48,1792]{3,2,1,0:T(8,128)(2,1)S(1)}, u32[]{:S(2)}, u32[]{:S(2)}) %collective-permute-start.27) | collective-permute-done | bytes 688160 | tf_op jit(solution)/shard_map/ppermute | solution.py:201
  184.5 1.4 fusion.3
  186.1 1.1 collective-permute-done.31
  187.2 18.3 %collective-permute-done.33 = bf16[2,2,80,1792]{3,2,1,0:T(8,128)(2,1)S(1)} collective-permute-done((bf16[2,2,80,1792]{3,2,1,0:T(8,128)(2,1)S(1)}, bf16[2,2,80,1792]{3,2,1,0:T(8,128)(2,1)S(1)}, u32[]{:S(2)}, u32[]{:S(2)}) %collective-permute-start.33) | collective-permute-done | bytes 1146912 | tf_op jit(solution)/shard_map/ppermute | solution.py:201
  (111 shorter events, 21.0 us)
Async XLA Ops:
  0.9 7.9 %collective-permute-start.1 = (bf16[48,2048]{1,0:T(8,128)(2,1)S(1)}, bf16[48,2048]{1,0:T(8,128)(2,1)S(1)}, u32[]{:S(2)}, u32[]{:S(2)}) collective-permute-start(bf16[48,2048]{1,0:T(8,128)(2,1)S(1)} %slice.30.refs_0_), channel_id=1, source_target_pairs={{0,2},{1,3},{2,0},{3,1},{4,6},{5,7},{6,4},{7,5},{8,10},{9,11},{10,... | collective-permute-start | bytes 589832 | tf_op jit(solution)/shard_map/ppermute | solution.py:44
  2.5 10.6 %collective-permute-start.3 = (bf16[48,2048]{1,0:T(8,128)(2,1)S(1)}, bf16[48,2048]{1,0:T(8,128)(2,1)S(1)}, u32[]{:S(2)}, u32[]{:S(2)}) collective-permute-start(bf16[48,2048]{1,0:T(8,128)(2,1)S(1)} %slice.30.refs_0_), channel_id=1, source_target_pairs={{0,4},{1,5},{2,6},{3,7},{4,0},{5,1},{6,2},{7,3},{8,12},{9,13},{10,... | collective-permute-start | bytes 589832 | tf_op jit(solution)/shard_map/ppermute | solution.py:44
  4.0 9.1 %collective-permute-start.5 = (bf16[48,2048]{1,0:T(8,128)(2,1)S(1)}, bf16[48,2048]{1,0:T(8,128)(2,1)S(1)}, u32[]{:S(2)}, u32[]{:S(2)}) collective-permute-start(bf16[48,2048]{1,0:T(8,128)(2,1)S(1)} %slice.30.refs_0_), channel_id=1, source_target_pairs={{0,6},{1,7},{2,4},{3,5},{4,2},{5,3},{6,0},{7,1},{8,14},{9,15},{10,... | collective-permute-start | bytes 589832 | tf_op jit(solution)/shard_map/ppermute | solution.py:44
  4.5 9.1 %collective-permute-start = (bf16[48,2048]{1,0:T(8,128)(2,1)S(1)}, bf16[48,2048]{1,0:T(8,128)(2,1)S(1)}, u32[]{:S(2)}, u32[]{:S(2)}) collective-permute-start(bf16[48,2048]{1,0:T(8,128)(2,1)S(1)} %slice.30.refs_0_), channel_id=1, source_target_pairs={{0,1},{1,0},{2,3},{3,2},{4,5},{5,4},{6,7},{7,6},{8,9},{9,8},{10,11... | collective-permute-start | bytes 589832 | tf_op jit(solution)/shard_map/ppermute | solution.py:44
  8.8 4.8 %collective-permute-start.2 = (bf16[48,2048]{1,0:T(8,128)(2,1)S(1)}, bf16[48,2048]{1,0:T(8,128)(2,1)S(1)}, u32[]{:S(2)}, u32[]{:S(2)}) collective-permute-start(bf16[48,2048]{1,0:T(8,128)(2,1)S(1)} %collective-permute-done.1.refs_2_), channel_id=1, source_target_pairs={{0,1},{1,0},{2,3},{3,2},{4,5},{5,4},{6,7},{7,6},{8,9},{9,8},{10,11... | collective-permute-start | bytes 589832 | tf_op jit(solution)/shard_map/ppermute | solution.py:44
  13.1 1.4 collective-permute-start.4
  13.1 1.7 collective-permute-start.6
  17.8 1.3 collective-permute-start.7
  19.1 6.1 %collective-permute-start.8 = (bf16[192,128]{1,0:T(8,128)(2,1)S(1)}, bf16[192,128]{1,0:T(8,128)(2,1)S(1)}, u32[]{:S(2)}, u32[]{:S(2)}) collective-permute-start(bf16[192,128]{1,0:T(8,128)(2,1)S(1)} %add_convert_fusion.12), channel_id=1, source_target_pairs={{0,2},{1,3},{2,0},{3,1},{4,6},{5,7},{6,4},{7,5},{8,10},{9,11},{10,... | collective-permute-start | bytes 147464 | tf_op jit(solution)/shard_map/ppermute | solution.py:44
  20.1 3.1 %copy-start = (bf16[2048,1792]{1,0:T(8,128)(2,1)S(1)}, bf16[2048,1792]{1,0:T(8,128)(2,1)}, u32[]{:S(2)}) copy-start(bf16[2048,1792]{1,0:T(8,128)(2,1)} %weight_ref.10) | copy-start | bytes 22020100
  23.2 11.4 %slice-start.4 = ((s8[7340032]{0:T(1024)(128)(4,1)}), s8[4194304]{0:T(1024)(128)(4,1)S(1)}, s32[]{:S(2)}) async-start(s8[7340032]{0:T(1024)(128)(4,1)} %bitcast.67), calls=%async_computation.4 | async-start | bytes 8388608
  25.3 9.3 %slice-start.5 = ((s8[7340032]{0:T(1024)(128)(4,1)}), s8[3145728]{0:T(1024)(128)(4,1)S(1)}, s32[]{:S(2)}) async-start(s8[7340032]{0:T(1024)(128)(4,1)} %bitcast.67), calls=%async_computation.5 | async-start | bytes 6291456
  25.3 4.2 %collective-permute-start.9 = (bf16[192,128]{1,0:T(8,128)(2,1)S(1)}, bf16[192,128]{1,0:T(8,128)(2,1)S(1)}, u32[]{:S(2)}, u32[]{:S(2)}) collective-permute-start(bf16[192,128]{1,0:T(8,128)(2,1)S(1)} %add_convert_fusion.11), channel_id=1, source_target_pairs={{0,4},{1,5},{2,6},{3,7},{4,0},{5,1},{6,2},{7,3},{8,12},{9,13},{10,... | collective-permute-start | bytes 147464 | tf_op jit(solution)/shard_map/ppermute | solution.py:44
  29.5 7.2 %collective-permute-start.10 = (bf16[192,128]{1,0:T(8,128)(2,1)S(1)}, bf16[192,128]{1,0:T(8,128)(2,1)S(1)}, u32[]{:S(2)}, u32[]{:S(2)}) collective-permute-start(bf16[192,128]{1,0:T(8,128)(2,1)S(1)} %add_convert_fusion.10), channel_id=1, source_target_pairs={{0,8},{8,0},{16,24},{24,16},{1,9},{9,1},{17,25},{25,17},{2,10},{10... | collective-permute-start | bytes 147464 | tf_op jit(solution)/shard_map/ppermute | solution.py:44
  31.1 10.6 %collective-permute-start.13 = (bf16[80,2048]{1,0:T(8,128)(2,1)S(1)}, bf16[80,2048]{1,0:T(8,128)(2,1)S(1)}, u32[]{:S(2)}, u32[]{:S(2)}) collective-permute-start(bf16[80,2048]{1,0:T(8,128)(2,1)S(1)} %slice.31.refs_0_), channel_id=1, source_target_pairs={{0,2},{1,3},{2,0},{3,1},{4,6},{5,7},{6,4},{7,5},{8,10},{9,11},{10,... | collective-permute-start | bytes 983048 | tf_op jit(solution)/shard_map/ppermute | solution.py:44
  32.3 15.8 %collective-permute-start.15 = (bf16[80,2048]{1,0:T(8,128)(2,1)S(1)}, bf16[80,2048]{1,0:T(8,128)(2,1)S(1)}, u32[]{:S(2)}, u32[]{:S(2)}) collective-permute-start(bf16[80,2048]{1,0:T(8,128)(2,1)S(1)} %slice.31.refs_0_), channel_id=1, source_target_pairs={{0,4},{1,5},{2,6},{3,7},{4,0},{5,1},{6,2},{7,3},{8,12},{9,13},{10,... | collective-permute-start | bytes 983048 | tf_op jit(solution)/shard_map/ppermute | solution.py:44
  33.7 14.4 %collective-permute-start.17 = (bf16[80,2048]{1,0:T(8,128)(2,1)S(1)}, bf16[80,2048]{1,0:T(8,128)(2,1)S(1)}, u32[]{:S(2)}, u32[]{:S(2)}) collective-permute-start(bf16[80,2048]{1,0:T(8,128)(2,1)S(1)} %slice.31.refs_0_), channel_id=1, source_target_pairs={{0,6},{1,7},{2,4},{3,5},{4,2},{5,3},{6,0},{7,1},{8,14},{9,15},{10,... | collective-permute-start | bytes 983048 | tf_op jit(solution)/shard_map/ppermute | solution.py:44
  34.6 17.8 %collective-permute-start.12 = (bf16[80,2048]{1,0:T(8,128)(2,1)S(1)}, bf16[80,2048]{1,0:T(8,128)(2,1)S(1)}, u32[]{:S(2)}, u32[]{:S(2)}) collective-permute-start(bf16[80,2048]{1,0:T(8,128)(2,1)S(1)} %slice.31.refs_0_), channel_id=1, source_target_pairs={{0,1},{1,0},{2,3},{3,2},{4,5},{5,4},{6,7},{7,6},{8,9},{9,8},{10,11... | collective-permute-start | bytes 983048 | tf_op jit(solution)/shard_map/ppermute | solution.py:44
  34.6 16.7 %slice-start = ((s8[7340032]{0:T(1024)(128)(4,1)}), s8[4194304]{0:T(1024)(128)(4,1)S(1)}, s32[]{:S(2)}) async-start(s8[7340032]{0:T(1024)(128)(4,1)} %bitcast.63), calls=%async_computation | async-start | bytes 8388608
  36.7 14.7 %slice-start.1 = ((s8[7340032]{0:T(1024)(128)(4,1)}), s8[3145728]{0:T(1024)(128)(4,1)S(1)}, s32[]{:S(2)}) async-start(s8[7340032]{0:T(1024)(128)(4,1)} %bitcast.63), calls=%async_computation.1 | async-start | bytes 6291456
  36.7 14.6 %collective-permute-start.11 = (bf16[192,128]{1,0:T(8,128)(2,1)S(1)}, bf16[192,128]{1,0:T(8,128)(2,1)S(1)}, u32[]{:S(2)}, u32[]{:S(2)}) collective-permute-start(bf16[192,128]{1,0:T(8,128)(2,1)S(1)} %add_convert_fusion.9), channel_id=1, source_target_pairs={{0,16},{8,24},{16,0},{24,8},{1,17},{9,25},{17,1},{25,9},{2,18},{10... | collective-permute-start | bytes 147464 | tf_op jit(solution)/shard_map/ppermute | solution.py:44
  41.7 10.6 %collective-permute-start.14 = (bf16[80,2048]{1,0:T(8,128)(2,1)S(1)}, bf16[80,2048]{1,0:T(8,128)(2,1)S(1)}, u32[]{:S(2)}, u32[]{:S(2)}) collective-permute-start(bf16[80,2048]{1,0:T(8,128)(2,1)S(1)} %collective-permute-done.13.refs_2_), channel_id=1, source_target_pairs={{0,1},{1,0},{2,3},{3,2},{4,5},{5,4},{6,7},{7,6},{8,9},{9,8},{10,11... | collective-permute-start | bytes 983048 | tf_op jit(solution)/shard_map/ppermute | solution.py:44
  48.1 4.3 %collective-permute-start.16 = (bf16[80,2048]{1,0:T(8,128)(2,1)S(1)}, bf16[80,2048]{1,0:T(8,128)(2,1)S(1)}, u32[]{:S(2)}, u32[]{:S(2)}) collective-permute-start(bf16[80,2048]{1,0:T(8,128)(2,1)S(1)} %collective-permute-done.15.refs_4_), channel_id=1, source_target_pairs={{0,1},{1,0},{2,3},{3,2},{4,5},{5,4},{6,7},{7,6},{8,9},{9,8},{10,11... | collective-permute-start | bytes 983048 | tf_op jit(solution)/shard_map/ppermute | solution.py:44
  48.1 4.3 %collective-permute-start.18 = (bf16[80,2048]{1,0:T(8,128)(2,1)S(1)}, bf16[80,2048]{1,0:T(8,128)(2,1)S(1)}, u32[]{:S(2)}, u32[]{:S(2)}) collective-permute-start(bf16[80,2048]{1,0:T(8,128)(2,1)S(1)} %collective-permute-done.17.refs_6_), channel_id=1, source_target_pairs={{0,1},{1,0},{2,3},{3,2},{4,5},{5,4},{6,7},{7,6},{8,9},{9,8},{10,11... | collective-permute-start | bytes 983048 | tf_op jit(solution)/shard_map/ppermute | solution.py:44
  51.4 23.5 %slice-start.2 = ((s8[7340032]{0:T(1024)(128)(4,1)}), s8[4194304]{0:T(1024)(128)(4,1)S(1)}, s32[]{:S(2)}) async-start(s8[7340032]{0:T(1024)(128)(4,1)} %bitcast.65), calls=%async_computation.2 | async-start | bytes 8388608
  52.4 22.5 %slice-start.3 = ((s8[7340032]{0:T(1024)(128)(4,1)}), s8[3145728]{0:T(1024)(128)(4,1)S(1)}, s32[]{:S(2)}) async-start(s8[7340032]{0:T(1024)(128)(4,1)} %bitcast.65), calls=%async_computation.3 | async-start | bytes 6291456
  54.6 1.4 collective-permute-start.19
  54.7 20.1 %collective-permute-start.26 = (bf16[1,2,2,48,1792]{4,3,2,1,0:T(8,128)(2,1)S(1)}, bf16[1,2,2,48,1792]{4,3,2,1,0:T(8,128)(2,1)S(1)}, u32[]{:S(2)}, u32[]{:S(2)}) collective-permute-start(bf16[1,2,2,48,1792]{4,3,2,1,0:T(8,128)(2,1)S(1)} %shard_map.87), channel_id=1, source_target_pairs={{0,8},{24,16},{1,9},{25,17},{2,10},{26,18},{3,11},{27,19},{4,12},{... | collective-permute-start | bytes 2064392 | tf_op jit(solution)/shard_map/ppermute | solution.py:259
  56.1 4.9 %collective-permute-start.20 = (bf16[320,128]{1,0:T(8,128)(2,1)S(1)}, bf16[320,128]{1,0:T(8,128)(2,1)S(1)}, u32[]{:S(2)}, u32[]{:S(2)}) collective-permute-start(bf16[320,128]{1,0:T(8,128)(2,1)S(1)} %add_convert_fusion.7), channel_id=1, source_target_pairs={{0,2},{1,3},{2,0},{3,1},{4,6},{5,7},{6,4},{7,5},{8,10},{9,11},{10,... | collective-permute-start | bytes 245768 | tf_op jit(solution)/shard_map/ppermute | solution.py:44
  61.0 4.5 %collective-permute-start.21 = (bf16[320,128]{1,0:T(8,128)(2,1)S(1)}, bf16[320,128]{1,0:T(8,128)(2,1)S(1)}, u32[]{:S(2)}, u32[]{:S(2)}) collective-permute-start(bf16[320,128]{1,0:T(8,128)(2,1)S(1)} %add_convert_fusion.6), channel_id=1, source_target_pairs={{0,4},{1,5},{2,6},{3,7},{4,0},{5,1},{6,2},{7,3},{8,12},{9,13},{10,... | collective-permute-start | bytes 245768 | tf_op jit(solution)/shard_map/ppermute | solution.py:44
  66.2 22.1 %collective-permute-start.23 = (bf16[320,128]{1,0:T(8,128)(2,1)}, bf16[320,128]{1,0:T(8,128)(2,1)}, u32[]{:S(2)}, u32[]{:S(2)}) collective-permute-start(bf16[320,128]{1,0:T(8,128)(2,1)} %add_convert_fusion.5), channel_id=1, source_target_pairs={{0,8},{8,16},{16,24},{24,0},{1,9},{9,17},{17,25},{25,1},{2,10},{10... | collective-permute-start | bytes 245768 | tf_op jit(solution)/shard_map/ppermute | solution.py:56
  68.6 19.7 %collective-permute-start.24 = (bf16[320,128]{1,0:T(8,128)(2,1)}, bf16[320,128]{1,0:T(8,128)(2,1)}, u32[]{:S(2)}, u32[]{:S(2)}) collective-permute-start(bf16[320,128]{1,0:T(8,128)(2,1)} %add_convert_fusion.5), channel_id=1, source_target_pairs={{0,16},{8,24},{16,0},{24,8},{1,17},{9,25},{17,1},{25,9},{2,18},{10... | collective-permute-start | bytes 245768 | tf_op jit(solution)/shard_map/ppermute | solution.py:56
  68.6 19.8 %collective-permute-start.25 = (bf16[320,128]{1,0:T(8,128)(2,1)}, bf16[320,128]{1,0:T(8,128)(2,1)}, u32[]{:S(2)}, u32[]{:S(2)}) collective-permute-start(bf16[320,128]{1,0:T(8,128)(2,1)} %add_convert_fusion.5), channel_id=1, source_target_pairs={{0,24},{8,0},{16,8},{24,16},{1,25},{9,1},{17,9},{25,17},{2,26},{10... | collective-permute-start | bytes 245768 | tf_op jit(solution)/shard_map/ppermute | solution.py:56
  72.5 36.8 %collective-permute-start.22 = (bf16[2,2,2,48,1792]{4,3,2,1,0:T(8,128)(2,1)}, bf16[2,2,2,48,1792]{4,3,2,1,0:T(8,128)(2,1)}, u32[]{:S(2)}, u32[]{:S(2)}) collective-permute-start(bf16[2,2,2,48,1792]{4,3,2,1,0:T(8,128)(2,1)} %shard_map.89), channel_id=1, source_target_pairs={{0,8},{24,16},{1,9},{25,17},{2,10},{26,18},{3,11},{27,19},{4,12},{... | collective-permute-start | bytes 4128776 | tf_op jit(solution)/shard_map/ppermute | solution.py:259
  73.8 7.8 %slice-start.6 = ((s8[7340032]{0:T(1024)(128)(4,1)}), s8[3145728]{0:T(1024)(128)(4,1)S(1)}, s32[]{:S(2)}) async-start(s8[7340032]{0:T(1024)(128)(4,1)} %bitcast.69), calls=%async_computation.6 | async-start | bytes 6291456
  74.9 6.7 %copy-start.5 = (bf16[1,2,2,48,1792]{4,3,2,1,0:T(8,128)(2,1)}, bf16[1,2,2,48,1792]{4,3,2,1,0:T(8,128)(2,1)S(1)}, u32[]{:S(2)}) copy-start(bf16[1,2,2,48,1792]{4,3,2,1,0:T(8,128)(2,1)S(1)} %collective-permute-done.26) | copy-start | bytes 2064388
  74.9 6.7 %slice-start.7 = ((s8[7340032]{0:T(1024)(128)(4,1)}), s8[4194304]{0:T(1024)(128)(4,1)S(1)}, s32[]{:S(2)}) async-start(s8[7340032]{0:T(1024)(128)(4,1)} %bitcast.69), calls=%async_computation.7 | async-start | bytes 8388608
  92.5 18.1 %copy-start.2 = (bf16[1,2,2,48,1792]{4,3,2,1,0:T(8,128)(2,1)S(1)}, bf16[1,2,2,48,1792]{4,3,2,1,0:T(8,128)(2,1)}, u32[]{:S(2)}) copy-start(bf16[1,2,2,48,1792]{4,3,2,1,0:T(8,128)(2,1)} %copy-done.1) | copy-start | bytes 2064388
  92.5 18.1 %copy-start.6 = (bf16[1,2,2,48,1792]{4,3,2,1,0:T(8,128)(2,1)S(1)}, bf16[1,2,2,48,1792]{4,3,2,1,0:T(8,128)(2,1)}, u32[]{:S(2)}) copy-start(bf16[1,2,2,48,1792]{4,3,2,1,0:T(8,128)(2,1)} %copy-done.5) | copy-start | bytes 2064388
  109.3 30.1 %collective-permute-start.30 = (bf16[1,2,2,80,1792]{4,3,2,1,0:T(8,128)(2,1)S(1)}, bf16[1,2,2,80,1792]{4,3,2,1,0:T(8,128)(2,1)S(1)}, u32[]{:S(2)}, u32[]{:S(2)}) collective-permute-start(bf16[1,2,2,80,1792]{4,3,2,1,0:T(8,128)(2,1)S(1)} %shard_map.93), channel_id=1, source_target_pairs={{0,8},{24,16},{1,9},{25,17},{2,10},{26,18},{3,11},{27,19},{4,12},{... | collective-permute-start | bytes 3440648 | tf_op jit(solution)/shard_map/ppermute | solution.py:259
  110.8 31.0 %collective-permute-start.28 = (bf16[2,2,48,1792]{3,2,1,0:T(8,128)(2,1)S(1)}, bf16[2,2,48,1792]{3,2,1,0:T(8,128)(2,1)S(1)}, u32[]{:S(2)}, u32[]{:S(2)}) collective-permute-start(bf16[2,2,48,1792]{3,2,1,0:T(8,128)(2,1)S(1)} %fusion.9), channel_id=1, source_target_pairs={{8,16},{16,8},{9,17},{17,9},{10,18},{18,10},{11,19},{19,11},{12,20... | collective-permute-start | bytes 2064392 | tf_op jit(solution)/shard_map/ppermute | solution.py:201
  112.7 51.2 %collective-permute-start.32 = (bf16[1,2,2,80,1792]{4,3,2,1,0:T(8,128)(2,1)S(1)}, bf16[1,2,2,80,1792]{4,3,2,1,0:T(8,128)(2,1)S(1)}, u32[]{:S(2)}, u32[]{:S(2)}) collective-permute-start(bf16[1,2,2,80,1792]{4,3,2,1,0:T(8,128)(2,1)S(1)} %shard_map.94), channel_id=1, source_target_pairs={{0,8},{24,16},{1,9},{25,17},{2,10},{26,18},{3,11},{27,19},{4,12},{... | collective-permute-start | bytes 3440648 | tf_op jit(solution)/shard_map/ppermute | solution.py:259
  139.7 30.1 %collective-permute-start.34 = (bf16[2,2,80,1792]{3,2,1,0:T(8,128)(2,1)S(1)}, bf16[2,2,80,1792]{3,2,1,0:T(8,128)(2,1)S(1)}, u32[]{:S(2)}, u32[]{:S(2)}) collective-permute-start(bf16[2,2,80,1792]{3,2,1,0:T(8,128)(2,1)S(1)} %fusion.5), channel_id=1, source_target_pairs={{8,16},{16,8},{9,17},{17,9},{10,18},{18,10},{11,19},{19,11},{12,20... | collective-permute-start | bytes 3440648 | tf_op jit(solution)/shard_map/ppermute | solution.py:201
  143.1 28.4 %collective-permute-start.29 = (bf16[2,2,48,1792]{3,2,1,0:T(8,128)(2,1)S(1)}, bf16[2,2,48,1792]{3,2,1,0:T(8,128)(2,1)S(1)}, u32[]{:S(2)}, u32[]{:S(2)}) collective-permute-start(bf16[2,2,48,1792]{3,2,1,0:T(8,128)(2,1)S(1)} %fusion.2), channel_id=1, source_target_pairs={{16,24},{8,0},{17,25},{9,1},{18,26},{10,2},{19,27},{11,3},{20,28},... | collective-permute-start | bytes 2064392 | tf_op jit(solution)/shard_map/ppermute | solution.py:201
  145.9 38.6 %collective-permute-start.27 = (bf16[2,2,48,1792]{3,2,1,0:T(8,128)(2,1)S(1)}, bf16[2,2,48,1792]{3,2,1,0:T(8,128)(2,1)S(1)}, u32[]{:S(2)}, u32[]{:S(2)}) collective-permute-start(bf16[2,2,48,1792]{3,2,1,0:T(8,128)(2,1)S(1)} %fusion.8), channel_id=1, source_target_pairs={{8,16},{16,8},{9,17},{17,9},{10,18},{18,10},{11,19},{19,11},{12,20... | collective-permute-start | bytes 2064392 | tf_op jit(solution)/shard_map/ppermute | solution.py:201
  149.8 37.4 %collective-permute-start.31 = (bf16[1,2,2,80,1792]{4,3,2,1,0:T(8,128)(2,1)S(1)}, bf16[1,2,2,80,1792]{4,3,2,1,0:T(8,128)(2,1)S(1)}, u32[]{:S(2)}, u32[]{:S(2)}) collective-permute-start(bf16[1,2,2,80,1792]{4,3,2,1,0:T(8,128)(2,1)S(1)} %shard_map.95), channel_id=1, source_target_pairs={{0,8},{24,16},{1,9},{25,17},{2,10},{26,18},{3,11},{27,19},{4,12},{... | collective-permute-start | bytes 3440648 | tf_op jit(solution)/shard_map/ppermute | solution.py:259
  164.2 41.3 %collective-permute-start.33 = (bf16[2,2,80,1792]{3,2,1,0:T(8,128)(2,1)S(1)}, bf16[2,2,80,1792]{3,2,1,0:T(8,128)(2,1)S(1)}, u32[]{:S(2)}, u32[]{:S(2)}) collective-permute-start(bf16[2,2,80,1792]{3,2,1,0:T(8,128)(2,1)S(1)} %fusion.4), channel_id=1, source_target_pairs={{8,16},{16,8},{9,17},{17,9},{10,18},{18,10},{11,19},{19,11},{12,20... | collective-permute-start | bytes 3440648 | tf_op jit(solution)/shard_map/ppermute | solution.py:201
  170.0 35.5 %collective-permute-start.35 = (bf16[2,2,80,1792]{3,2,1,0:T(8,128)(2,1)S(1)}, bf16[2,2,80,1792]{3,2,1,0:T(8,128)(2,1)S(1)}, u32[]{:S(2)}, u32[]{:S(2)}) collective-permute-start(bf16[2,2,80,1792]{3,2,1,0:T(8,128)(2,1)S(1)} %fusion), channel_id=1, source_target_pairs={{16,24},{8,0},{17,25},{9,1},{18,26},{10,2},{19,27},{11,3},{20,28},... | collective-permute-start | bytes 3440648 | tf_op jit(solution)/shard_map/ppermute | solution.py:201
  (4 other events, 7.3 us)

commit v6 on v5

--- a/solution.py
+++ b/solution.py
@@ -44,8 +44,11 @@
     return lax.ppermute(x, axis, [(i, i ^ mask) for i in range(size)])
 
 
-def gather_rows(x, ntp):
-    chips = [x] + [swap(x, "tp", ntp, 2 * m) for m in range(1, ntp // 2)]
+def gather_chips(x, ntp):
+    return [x] + [swap(x, "tp", ntp, 2 * m) for m in range(1, ntp // 2)]
+
+
+def gather_cores(chips, ntp):
     pieces = []
     for piece in chips:
         pieces += [piece, swap(piece, "tp", ntp, 1)]
@@ -108,7 +111,7 @@
         + [jax.ShapeDtypeStruct((segs // 2, total, 2 * rank), jnp.bfloat16)],
         in_specs=[pl.BlockSpec(memory_space=pltpu.SMEM)] + [vmem] * (segs + 1),
         out_specs=[vmem] * (len(group) + 1),
-        compiler_params=pltpu.CompilerParams(vmem_limit_bytes=32 << 20),
+        compiler_params=pltpu.CompilerParams(vmem_limit_bytes=12 << 20),
         cost_estimate=pl.CostEstimate(flops=hint, bytes_accessed=4 * segs * total * width, transcendentals=0),
     )(table, *pieces, down_pool)
     return xs, mine
@@ -191,11 +194,14 @@
     return [(level, level + 1), (nseq - 1 - level, nseq - 2 - level)]
 
 
-def scatter_line(own, first, nseq):
+def scatter_line(own, first, nseq, given=None):
     last = nseq - 2
     arrived = {(0, slot): hop for slot, hop in enumerate(first)}
+    arrived.update(given or {})
     for step in range(nseq - 1):
         for level in range(1, step + 1):
+            if (level, step) in arrived:
+                continue
             slot = step - level if level < nseq // 2 else step
             send = add(own[slot], arrived[level - 1, step - 1])
             arrived[level, step] = lax.ppermute(send, "seq", hop_pairs(level, nseq))
@@ -230,11 +236,11 @@
     columns = gate_weight.shape[1]
     tile = 256 if columns % 256 == 0 else 128
     tiles = columns // tile
-    first, second = GROUPS
-    rows = first[0]
-
-    pieces = gather_rows(tokens[:rows], ntp)
-    (x,), mine = assemble(pieces, first, down_pool, down_table, 1 << 20)
+    (first,), (later,) = GROUPS
+    rows = first
+
+    pieces = gather_cores(gather_chips(tokens[:rows], ntp), ntp)
+    (x,), mine = assemble(pieces, (first,), down_pool, down_table, 1 << 20)
     x = x.reshape(-1, x.shape[2])
     cuts = [(w, f, c) for w in (gate_weight, up_weight) for f, c in ((0, tiles // 2), (tiles // 2, tiles - tiles // 2))]
     left = list(cuts)
@@ -246,7 +252,7 @@
         return project(after(x, gate), weight, begin, count, tile)
 
     shared, parts = sum_beside(mine.reshape(-1, mine.shape[2]), "tp", ntp, piece)
-    pieces = gather_rows(after(tokens[rows:], shared), ntp)
+    chips = gather_chips(after(tokens[rows:], shared), ntp)
     inner, more = sum_beside(shared, "seq", nseq, piece)
     parts = [part for part in parts + more if part is not None]
     inner = inner.reshape(mine.shape)
@@ -259,30 +265,31 @@
         return lax.ppermute(send, "seq", hop_pairs(0, nseq))
 
     head = terms(parts, inner, 0, rows, 0, 1, None)
-    pieces = list(after(tuple(pieces), head))
-    (x,), mine = assemble(pieces, second, down_pool, down_table, AHEAD)
+    pieces = gather_cores(list(after(tuple(chips), head)), ntp)
+    (x,), mine = assemble(pieces, (later,), down_pool, down_table, AHEAD)
     head_hop = first_hop(head)
     shared, _ = sum_beside(mine.reshape(-1, mine.shape[2]), "tp", ntp, lambda gate: None)
     rest = terms(parts, inner, 0, rows, 1, nseq - 2, shared)
     rest_hop = first_hop(rest)
     kept = terms(parts, inner, 0, rows, nseq - 1, 1, rest)
     inner = sum_one_step(shared, "seq", nseq).reshape(mine.shape)
-    x = after(x.reshape(-1, x.shape[2]), (head_hop, kept))
+    second = add(head[0], after(head_hop, rest)[0])
+    second_hop = lax.ppermute(second, "seq", hop_pairs(1, nseq))
+    x = after(x.reshape(-1, x.shape[2]), (second, kept))
     own = [head[0]] + [rest[slot] for slot in range(nseq - 2)] + [kept[0]]
 
-    rows = second[0]
+    rows = later
     parts = [project(x, weight, 0, tiles, tile, AHEAD) for weight in (gate_weight, up_weight)]
     sent = [terms(parts, inner, 0, rows, 0, 1, None)]
     for slot in range(1, nseq):
-        sent.append(terms(parts, inner, 0, rows, slot, 1, sent[-1]))
-    head_hop = after(head_hop, sent[0])
+        sent.append(terms(parts, inner, 0, rows, slot, 1, (sent[-1], second_hop)))
     rest_hop = after(rest_hop, sent[-1])
     hops = []
     for slot in range(nseq - 1):
         hops.append(first_hop(after(sent[slot], hops[slot - 2] if slot > 1 else rest_hop)))
 
     totals = [
-        scatter_line(own, [head_hop[0]] + [rest_hop[slot] for slot in range(nseq - 2)], nseq),
+        scatter_line(own, [head_hop[0]] + [rest_hop[slot] for slot in range(nseq - 2)], nseq, {(1, 1): second_hop}),
         scatter_line([term[0] for term in sent], [hop[0] for hop in hops], nseq),
     ]
     out = [(jax.nn.silu(total[0]) * total[1]).astype(jnp.bfloat16) for total in totals]

time: 208 us -> 206 us (level)
  waiting for transfers between devices: 118 us -> 114 us
  starting transfers between devices: 36.9 us -> 39.6 us
    ppermute x0 -> x1, starting transfers between devices: none -> 3.7 us  [shards(): second_hop = lax.ppermute(second, 'seq', hop_pairs(1, nseq))]
    ppermute x6 -> x5, starting transfers between devices: 12.6 us -> 10.6 us  [scatter_line(): arrived[level, step] = lax.ppermute(send, 'seq', hop_pairs(level, nseq))]
    unnamed x32 -> x24, local copies, waits for them, and re-layouts: 5.3 us -> 4.73 us
    ppermute x6 -> x5, waiting for transfers between devices: 35 us -> 34.9 us  [scatter_line(): arrived[level, step] = lax.ppermute(send, 'seq', hop_pairs(level, nseq))]
  transfers between devices with their start and end apart: 36 -> 36, of which waited for: 18 -> 21; matrix products, arithmetic and copies ran while one was open for 5% -> 5% of each run, Pallas kernels for 15% -> 15%
where the time goes in v6:
time: 206 us; the launch traced here: 205 us
  waiting for transfers between devices  114 us (55%)
  starting transfers between devices  39.6 us (19%)
  Pallas kernels  34 us (17%)
  other arithmetic  11.7 us (6%)
  local copies, waits for them, and re-layouts  5.77 us (3%)
    ppermute x5, waiting for transfers between devices, first_hop(): return lax.ppermute(send, 'seq', hop_pairs(0, nseq))  53.1 us
    ppermute x5, waiting for transfers between devices, scatter_line(): arrived[level, step] = lax.ppermute(send, 'seq', hop_pairs(level, nseq))  34.9 us
    ppermute x22, waiting for transfers between devices, swap(): return lax.ppermute(x, axis, [(i, i ^ mask) for i in range(size)])  25.7 us
    pallas_call x6, Pallas kernels, project(): pl.pallas_call(project_kernel, out_shape=jax.ShapeDtypeStruct((rows, coun...  22.6 us
    ppermute x22, starting transfers between devices, swap(): return lax.ppermute(x, axis, [(i, i ^ mask) for i in range(size)])  14.5 us
    ppermute x5, starting transfers between devices, scatter_line(): arrived[level, step] = lax.ppermute(send, 'seq', hop_pairs(level, nseq))  10.6 us
    pallas_call x7, Pallas kernels, add_low_rank(): pl.pallas_call(functools.partial(low_rank_kernel, first, each, start, wid...  8.28 us
    ppermute x5, starting transfers between devices, first_hop(): return lax.ppermute(send, 'seq', hop_pairs(0, nseq))  6.69 us
  transfers between devices with their start and end apart: 36, of which 21 were waited for; matrix products, arithmetic and copies ran while one was open for 5% of the time, Pallas kernels for 15%

profile of v6, /device:TPU:16, one launch (start us, length us, event | category | flops | bytes accessed | tf_op | source)
XLA Modules:
  0.0 205.2 jit_solution(12153296507682674089)
XLA Ops:
  0.9 1.6 collective-permute-start.1
  2.5 1.5 collective-permute-start.3
  7.2 1.6 collective-permute-done.1.refs_2_
  8.8 4.3 %collective-permute-done.3.refs_4_ = bf16[48,2048]{1,0:T(8,128)(2,1)S(1)} collective-permute-done((bf16[48,2048]{1,0:T(8,128)(2,1)S(1)}, bf16[48,2048]{1,0:T(8,128)(2,1)S(1)}, u32[]{:S(2)}, u32[]{:S(2)}) %collective-permute-start.3) | collective-permute-done | bytes 196640 | tf_op jit(solution)/shard_map/ppermute | solution.py:44
  14.8 1.6 copy-done.1
  16.4 1.4 shard_map.82
  20.1 3.1 %copy-done = bf16[2048,1792]{1,0:T(8,128)(2,1)S(1)} copy-done((bf16[2048,1792]{1,0:T(8,128)(2,1)S(1)}, bf16[2048,1792]{1,0:T(8,128)(2,1)}, u32[]{:S(2)}) %copy-start) | copy-done | bytes 7340056
  23.2 2.0 shard_map.83.refs_0_
  25.3 1.2 collective-permute-start.9
  26.4 2.7 %shard_map.84.refs_1_ = bf16[384,1024]{1,0:T(8,128)(2,1)S(1)} custom-call(bf16[384,2048]{1,0:T(8,128)(2,1)S(1)} %bitcast.72, bf16[2048,1792]{1,0:T(8,128)(2,1)S(1)} %copy-done), custom_call_target="tpu_custom_call" | custom-call | flops 1610612736 | bytes 4194304 | tf_op jit(solution)/shard_map/pallas_call | solution.py:127
  29.4 1.6 collective-permute-start.10
  31.1 1.2 collective-permute-start.12
  32.3 1.4 collective-permute-start.13
  34.6 2.0 shard_map.85.refs_2_
  37.1 2.7 %shard_map.86.refs_3_ = bf16[384,1024]{1,0:T(8,128)(2,1)S(1)} custom-call(bf16[384,2048]{1,0:T(8,128)(2,1)S(1)} %bitcast.74, bf16[2048,1792]{1,0:T(8,128)(2,1)S(1)} %bitcast.68), custom_call_target="tpu_custom_call" | custom-call | flops 1610612736 | bytes 4194304 | tf_op jit(solution)/shard_map/pallas_call | solution.py:127
  39.8 1.9 collective-permute-done.11
  42.7 5.3 %collective-permute-done.13.refs_4_ = bf16[80,2048]{1,0:T(8,128)(2,1)S(1)} collective-permute-done((bf16[80,2048]{1,0:T(8,128)(2,1)S(1)}, bf16[80,2048]{1,0:T(8,128)(2,1)S(1)}, u32[]{:S(2)}, u32[]{:S(2)}) %collective-permute-start.13) | collective-permute-done | bytes 327712 | tf_op jit(solution)/shard_map/ppermute | solution.py:44
  51.1 1.6 shard_map.88
  52.9 1.3 collective-permute-start.26
  54.9 4.2 %collective-permute-done.20 = bf16[320,128]{1,0:T(8,128)(2,1)S(1)} collective-permute-done((bf16[320,128]{1,0:T(8,128)(2,1)S(1)}, bf16[320,128]{1,0:T(8,128)(2,1)S(1)}, u32[]{:S(2)}, u32[]{:S(2)}) %collective-permute-start.20) | collective-permute-done | bytes 81952 | tf_op jit(solution)/shard_map/ppermute | solution.py:44
  59.7 3.9 %collective-permute-done.21 = bf16[320,128]{1,0:T(8,128)(2,1)S(1)} collective-permute-done((bf16[320,128]{1,0:T(8,128)(2,1)S(1)}, bf16[320,128]{1,0:T(8,128)(2,1)S(1)}, u32[]{:S(2)}, u32[]{:S(2)}) %collective-permute-start.21) | collective-permute-done | bytes 81952 | tf_op jit(solution)/shard_map/ppermute | solution.py:44
  64.3 2.4 %collective-permute-start.23 = (bf16[320,128]{1,0:T(8,128)(2,1)}, bf16[320,128]{1,0:T(8,128)(2,1)}, u32[]{:S(2)}, u32[]{:S(2)}) collective-permute-start(bf16[320,128]{1,0:T(8,128)(2,1)} %add_convert_fusion.5), channel_id=1, source_target_pairs={{0,8},{8,16},{16,24},{24,0},{1,9},{9,17},{17,25},{25,1},{2,10},{10... | collective-permute-start | bytes 245768 | tf_op jit(solution)/shard_map/ppermute | solution.py:59
  66.7 1.7 collective-permute-start.25
  68.4 2.3 %shard_map.89 = bf16[2,2,2,48,1792]{4,3,2,1,0:T(8,128)(2,1)} custom-call(s32[3,8]{1,0:T(4,128)S(1)} %pad_add_fusion.tab_ref, bf16[4,48,128]{2,1,0:T(8,128)(2,1)S(1)} %bitcast.80, bf16[384,768]{1,0:T(8,128)(2,1)S(1)} %shard_map.83.refs_0_, bf16[384,1024]{1,0:T(8,128)(2,1)S(1)} %shard_map.84.refs_1_, bf16[384,768]{1,0:T(8,128)(2,1)S(1)} %shard_map.85.refs_2_, ...), custom_call_target="tpu_custom_call" | custom-call | flops 1024 | bytes 1024 | tf_op jit(solution)/shard_map/pallas_call | solution.py:173
  70.6 1.5 collective-permute-start.22
  73.3 3.7 %collective-permute-start.27 = (bf16[2,2,48,1792]{3,2,1,0:T(8,128)(2,1)S(1)}, bf16[2,2,48,1792]{3,2,1,0:T(8,128)(2,1)S(1)}, u32[]{:S(2)}, u32[]{:S(2)}) collective-permute-start(bf16[2,2,48,1792]{3,2,1,0:T(8,128)(2,1)S(1)} %fusion.8), channel_id=1, source_target_pairs={{8,16},{16,8},{9,17},{17,9},{10,18},{18,10},{11,19},{19,11},{12,20... | collective-permute-start | bytes 2064392 | tf_op jit(solution)/shard_map/ppermute | solution.py:277
  77.1 6.6 %shard_map.91.refs_0_ = bf16[640,1792]{1,0:T(8,128)(2,1)S(1)} custom-call(bf16[640,2048]{1,0:T(8,128)(2,1)S(1)} %bitcast.84, bf16[2048,1792]{1,0:T(8,128)(2,1)S(1)} %bitcast.66), custom_call_target="tpu_custom_call" | custom-call | flops 68719476736 | bytes 7340032 | tf_op jit(solution)/shard_map/pallas_call | solution.py:127
  83.7 6.6 %shard_map.92.refs_1_ = bf16[640,1792]{1,0:T(8,128)(2,1)S(1)} custom-call(bf16[640,2048]{1,0:T(8,128)(2,1)S(1)} %bitcast.85, bf16[2048,1792]{1,0:T(8,128)(2,1)S(1)} %bitcast.70), custom_call_target="tpu_custom_call" | custom-call | flops 68719476736 | bytes 7340032 | tf_op jit(solution)/shard_map/pallas_call | solution.py:127
  90.4 1.1 add_convert_fusion.4
  92.5 1.0 shard_map.94
  94.6 1.0 shard_map.96
  95.6 11.8 %collective-permute-done.22 = bf16[2,2,2,48,1792]{4,3,2,1,0:T(8,128)(2,1)} collective-permute-done((bf16[2,2,2,48,1792]{4,3,2,1,0:T(8,128)(2,1)}, bf16[2,2,2,48,1792]{4,3,2,1,0:T(8,128)(2,1)}, u32[]{:S(2)}, u32[]{:S(2)}) %collective-permute-start.22) | collective-permute-done | bytes 1376288 | tf_op jit(solution)/shard_map/ppermute | solution.py:265
  107.4 1.3 collective-permute-start.30
  108.7 1.3 collective-permute-start.32
  110.0 27.5 %collective-permute-done.30 = bf16[1,2,2,80,1792]{4,3,2,1,0:T(8,128)(2,1)S(1)} collective-permute-done((bf16[1,2,2,80,1792]{4,3,2,1,0:T(8,128)(2,1)S(1)}, bf16[1,2,2,80,1792]{4,3,2,1,0:T(8,128)(2,1)S(1)}, u32[]{:S(2)}, u32[]{:S(2)}) %collective-permute-start.30) | collective-permute-done | bytes 1146912 | tf_op jit(solution)/shard_map/ppermute | solution.py:265
  137.8 2.1 %collective-permute-start.34 = (bf16[2,2,80,1792]{3,2,1,0:T(8,128)(2,1)S(1)}, bf16[2,2,80,1792]{3,2,1,0:T(8,128)(2,1)S(1)}, u32[]{:S(2)}, u32[]{:S(2)}) collective-permute-start(bf16[2,2,80,1792]{3,2,1,0:T(8,128)(2,1)S(1)} %fusion.5), channel_id=1, source_target_pairs={{8,16},{16,8},{9,17},{17,9},{10,18},{18,10},{11,19},{19,11},{12,20... | collective-permute-start | bytes 3440648 | tf_op jit(solution)/shard_map/ppermute | solution.py:207
  139.9 1.3 fusion.2
  141.2 1.3 collective-permute-start.29
  142.5 1.5 fusion.9
  144.0 3.9 %collective-permute-start.28 = (bf16[2,2,48,1792]{3,2,1,0:T(8,128)(2,1)S(1)}, bf16[2,2,48,1792]{3,2,1,0:T(8,128)(2,1)S(1)}, u32[]{:S(2)}, u32[]{:S(2)}) collective-permute-start(bf16[2,2,48,1792]{3,2,1,0:T(8,128)(2,1)S(1)} %fusion.9), channel_id=1, source_target_pairs={{8,16},{16,8},{9,17},{17,9},{10,18},{18,10},{11,19},{19,11},{12,20... | collective-permute-start | bytes 2064392 | tf_op jit(solution)/shard_map/ppermute | solution.py:207
  147.9 1.3 collective-permute-start.31
  149.2 12.8 %collective-permute-done.32 = bf16[1,2,2,80,1792]{4,3,2,1,0:T(8,128)(2,1)S(1)} collective-permute-done((bf16[1,2,2,80,1792]{4,3,2,1,0:T(8,128)(2,1)S(1)}, bf16[1,2,2,80,1792]{4,3,2,1,0:T(8,128)(2,1)S(1)}, u32[]{:S(2)}, u32[]{:S(2)}) %collective-permute-start.32) | collective-permute-done | bytes 1146912 | tf_op jit(solution)/shard_map/ppermute | solution.py:265
  162.3 1.9 collective-permute-start.33
  164.3 3.6 %collective-permute-done.34 = bf16[2,2,80,1792]{3,2,1,0:T(8,128)(2,1)S(1)} collective-permute-done((bf16[2,2,80,1792]{3,2,1,0:T(8,128)(2,1)S(1)}, bf16[2,2,80,1792]{3,2,1,0:T(8,128)(2,1)S(1)}, u32[]{:S(2)}, u32[]{:S(2)}) %collective-permute-start.34) | collective-permute-done | bytes 1146912 | tf_op jit(solution)/shard_map/ppermute | solution.py:207
  168.2 1.4 collective-permute-start.35
  169.5 13.1 %collective-permute-done.28 = bf16[2,2,48,1792]{3,2,1,0:T(8,128)(2,1)S(1)} collective-permute-done((bf16[2,2,48,1792]{3,2,1,0:T(8,128)(2,1)S(1)}, bf16[2,2,48,1792]{3,2,1,0:T(8,128)(2,1)S(1)}, u32[]{:S(2)}, u32[]{:S(2)}) %collective-permute-start.28) | collective-permute-done | bytes 688160 | tf_op jit(solution)/shard_map/ppermute | solution.py:207
  182.6 1.4 fusion.3
  185.2 18.2 %collective-permute-done.33 = bf16[2,2,80,1792]{3,2,1,0:T(8,128)(2,1)S(1)} collective-permute-done((bf16[2,2,80,1792]{3,2,1,0:T(8,128)(2,1)S(1)}, bf16[2,2,80,1792]{3,2,1,0:T(8,128)(2,1)S(1)}, u32[]{:S(2)}, u32[]{:S(2)}) %collective-permute-start.33) | collective-permute-done | bytes 1146912 | tf_op jit(solution)/shard_map/ppermute | solution.py:207
  (103 shorter events, 23.0 us)
Async XLA Ops:
  0.9 7.9 %collective-permute-start.1 = (bf16[48,2048]{1,0:T(8,128)(2,1)S(1)}, bf16[48,2048]{1,0:T(8,128)(2,1)S(1)}, u32[]{:S(2)}, u32[]{:S(2)}) collective-permute-start(bf16[48,2048]{1,0:T(8,128)(2,1)S(1)} %slice.30.refs_0_), channel_id=1, source_target_pairs={{0,2},{1,3},{2,0},{3,1},{4,6},{5,7},{6,4},{7,5},{8,10},{9,11},{10,... | collective-permute-start | bytes 589832 | tf_op jit(solution)/shard_map/ppermute | solution.py:44
  2.5 10.6 %collective-permute-start.3 = (bf16[48,2048]{1,0:T(8,128)(2,1)S(1)}, bf16[48,2048]{1,0:T(8,128)(2,1)S(1)}, u32[]{:S(2)}, u32[]{:S(2)}) collective-permute-start(bf16[48,2048]{1,0:T(8,128)(2,1)S(1)} %slice.30.refs_0_), channel_id=1, source_target_pairs={{0,4},{1,5},{2,6},{3,7},{4,0},{5,1},{6,2},{7,3},{8,12},{9,13},{10,... | collective-permute-start | bytes 589832 | tf_op jit(solution)/shard_map/ppermute | solution.py:44
  4.0 9.1 %collective-permute-start.5 = (bf16[48,2048]{1,0:T(8,128)(2,1)S(1)}, bf16[48,2048]{1,0:T(8,128)(2,1)S(1)}, u32[]{:S(2)}, u32[]{:S(2)}) collective-permute-start(bf16[48,2048]{1,0:T(8,128)(2,1)S(1)} %slice.30.refs_0_), channel_id=1, source_target_pairs={{0,6},{1,7},{2,4},{3,5},{4,2},{5,3},{6,0},{7,1},{8,14},{9,15},{10,... | collective-permute-start | bytes 589832 | tf_op jit(solution)/shard_map/ppermute | solution.py:44
  4.5 9.1 %collective-permute-start = (bf16[48,2048]{1,0:T(8,128)(2,1)S(1)}, bf16[48,2048]{1,0:T(8,128)(2,1)S(1)}, u32[]{:S(2)}, u32[]{:S(2)}) collective-permute-start(bf16[48,2048]{1,0:T(8,128)(2,1)S(1)} %slice.30.refs_0_), channel_id=1, source_target_pairs={{0,1},{1,0},{2,3},{3,2},{4,5},{5,4},{6,7},{7,6},{8,9},{9,8},{10,11... | collective-permute-start | bytes 589832 | tf_op jit(solution)/shard_map/ppermute | solution.py:44
  8.8 4.8 %collective-permute-start.2 = (bf16[48,2048]{1,0:T(8,128)(2,1)S(1)}, bf16[48,2048]{1,0:T(8,128)(2,1)S(1)}, u32[]{:S(2)}, u32[]{:S(2)}) collective-permute-start(bf16[48,2048]{1,0:T(8,128)(2,1)S(1)} %collective-permute-done.1.refs_2_), channel_id=1, source_target_pairs={{0,1},{1,0},{2,3},{3,2},{4,5},{5,4},{6,7},{7,6},{8,9},{9,8},{10,11... | collective-permute-start | bytes 589832 | tf_op jit(solution)/shard_map/ppermute | solution.py:44
  13.1 1.4 collective-permute-start.4
  13.1 1.7 collective-permute-start.6
  14.8 1.6 copy-start.1
  16.4 1.7 copy-start.3
  17.8 1.3 collective-permute-start.7
  19.1 6.1 %collective-permute-start.8 = (bf16[192,128]{1,0:T(8,128)(2,1)S(1)}, bf16[192,128]{1,0:T(8,128)(2,1)S(1)}, u32[]{:S(2)}, u32[]{:S(2)}) collective-permute-start(bf16[192,128]{1,0:T(8,128)(2,1)S(1)} %add_convert_fusion.12), channel_id=1, source_target_pairs={{0,2},{1,3},{2,0},{3,1},{4,6},{5,7},{6,4},{7,5},{8,10},{9,11},{10,... | collective-permute-start | bytes 147464 | tf_op jit(solution)/shard_map/ppermute | solution.py:44
  20.1 3.1 %copy-start = (bf16[2048,1792]{1,0:T(8,128)(2,1)S(1)}, bf16[2048,1792]{1,0:T(8,128)(2,1)}, u32[]{:S(2)}) copy-start(bf16[2048,1792]{1,0:T(8,128)(2,1)} %weight_ref.10) | copy-start | bytes 22020100
  23.2 11.4 %slice-start.4 = ((s8[7340032]{0:T(1024)(128)(4,1)}), s8[4194304]{0:T(1024)(128)(4,1)S(1)}, s32[]{:S(2)}) async-start(s8[7340032]{0:T(1024)(128)(4,1)} %bitcast.67), calls=%async_computation.4 | async-start | bytes 8388608
  25.3 9.3 %slice-start.5 = ((s8[7340032]{0:T(1024)(128)(4,1)}), s8[3145728]{0:T(1024)(128)(4,1)S(1)}, s32[]{:S(2)}) async-start(s8[7340032]{0:T(1024)(128)(4,1)} %bitcast.67), calls=%async_computation.5 | async-start | bytes 6291456
  25.3 4.2 %collective-permute-start.9 = (bf16[192,128]{1,0:T(8,128)(2,1)S(1)}, bf16[192,128]{1,0:T(8,128)(2,1)S(1)}, u32[]{:S(2)}, u32[]{:S(2)}) collective-permute-start(bf16[192,128]{1,0:T(8,128)(2,1)S(1)} %add_convert_fusion.11), channel_id=1, source_target_pairs={{0,4},{1,5},{2,6},{3,7},{4,0},{5,1},{6,2},{7,3},{8,12},{9,13},{10,... | collective-permute-start | bytes 147464 | tf_op jit(solution)/shard_map/ppermute | solution.py:44
  29.4 7.2 %collective-permute-start.10 = (bf16[192,128]{1,0:T(8,128)(2,1)S(1)}, bf16[192,128]{1,0:T(8,128)(2,1)S(1)}, u32[]{:S(2)}, u32[]{:S(2)}) collective-permute-start(bf16[192,128]{1,0:T(8,128)(2,1)S(1)} %add_convert_fusion.10), channel_id=1, source_target_pairs={{0,8},{8,0},{16,24},{24,16},{1,9},{9,1},{17,25},{25,17},{2,10},{10... | collective-permute-start | bytes 147464 | tf_op jit(solution)/shard_map/ppermute | solution.py:44
  31.1 11.6 %collective-permute-start.12 = (bf16[80,2048]{1,0:T(8,128)(2,1)S(1)}, bf16[80,2048]{1,0:T(8,128)(2,1)S(1)}, u32[]{:S(2)}, u32[]{:S(2)}) collective-permute-start(bf16[80,2048]{1,0:T(8,128)(2,1)S(1)} %slice.31.refs_0_), channel_id=1, source_target_pairs={{0,2},{1,3},{2,0},{3,1},{4,6},{5,7},{6,4},{7,5},{8,10},{9,11},{10,... | collective-permute-start | bytes 983048 | tf_op jit(solution)/shard_map/ppermute | solution.py:44
  32.3 15.8 %collective-permute-start.13 = (bf16[80,2048]{1,0:T(8,128)(2,1)S(1)}, bf16[80,2048]{1,0:T(8,128)(2,1)S(1)}, u32[]{:S(2)}, u32[]{:S(2)}) collective-permute-start(bf16[80,2048]{1,0:T(8,128)(2,1)S(1)} %slice.31.refs_0_), channel_id=1, source_target_pairs={{0,4},{1,5},{2,6},{3,7},{4,0},{5,1},{6,2},{7,3},{8,12},{9,13},{10,... | collective-permute-start | bytes 983048 | tf_op jit(solution)/shard_map/ppermute | solution.py:44
  33.7 14.4 %collective-permute-start.14 = (bf16[80,2048]{1,0:T(8,128)(2,1)S(1)}, bf16[80,2048]{1,0:T(8,128)(2,1)S(1)}, u32[]{:S(2)}, u32[]{:S(2)}) collective-permute-start(bf16[80,2048]{1,0:T(8,128)(2,1)S(1)} %slice.31.refs_0_), channel_id=1, source_target_pairs={{0,6},{1,7},{2,4},{3,5},{4,2},{5,3},{6,0},{7,1},{8,14},{9,15},{10,... | collective-permute-start | bytes 983048 | tf_op jit(solution)/shard_map/ppermute | solution.py:44
  34.6 7.2 %slice-start = ((s8[7340032]{0:T(1024)(128)(4,1)}), s8[4194304]{0:T(1024)(128)(4,1)S(1)}, s32[]{:S(2)}) async-start(s8[7340032]{0:T(1024)(128)(4,1)} %bitcast.63), calls=%async_computation | async-start | bytes 8388608
  36.6 5.1 %slice-start.1 = ((s8[7340032]{0:T(1024)(128)(4,1)}), s8[3145728]{0:T(1024)(128)(4,1)S(1)}, s32[]{:S(2)}) async-start(s8[7340032]{0:T(1024)(128)(4,1)} %bitcast.63), calls=%async_computation.1 | async-start | bytes 6291456
  36.7 5.1 %collective-permute-start.11 = (bf16[192,128]{1,0:T(8,128)(2,1)S(1)}, bf16[192,128]{1,0:T(8,128)(2,1)S(1)}, u32[]{:S(2)}, u32[]{:S(2)}) collective-permute-start(bf16[192,128]{1,0:T(8,128)(2,1)S(1)} %add_convert_fusion.9), channel_id=1, source_target_pairs={{0,16},{8,24},{16,0},{24,8},{1,17},{9,25},{17,1},{25,9},{2,18},{10... | collective-permute-start | bytes 147464 | tf_op jit(solution)/shard_map/ppermute | solution.py:44
  41.8 9.3 %copy-start.2 = (bf16[8,64,2048]{2,1,0:T(8,128)(2,1)S(1)}, bf16[8,64,2048]{2,1,0:T(8,128)(2,1)}, u32[]{:S(2)}) copy-start(bf16[8,64,2048]{2,1,0:T(8,128)(2,1)} %refs_8_.3) | copy-start | bytes 6291460
  48.1 1.6 collective-permute-start.15
  48.1 2.1 %collective-permute-start.16 = (bf16[80,2048]{1,0:T(8,128)(2,1)S(1)}, bf16[80,2048]{1,0:T(8,128)(2,1)S(1)}, u32[]{:S(2)}, u32[]{:S(2)}) collective-permute-start(bf16[80,2048]{1,0:T(8,128)(2,1)S(1)} %collective-permute-done.12.refs_2_), channel_id=1, source_target_pairs={{0,1},{1,0},{2,3},{3,2},{4,5},{5,4},{6,7},{7,6},{8,9},{9,8},{10,11... | collective-permute-start | bytes 983048 | tf_op jit(solution)/shard_map/ppermute | solution.py:44
  48.6 2.1 %collective-permute-start.17 = (bf16[80,2048]{1,0:T(8,128)(2,1)S(1)}, bf16[80,2048]{1,0:T(8,128)(2,1)S(1)}, u32[]{:S(2)}, u32[]{:S(2)}) collective-permute-start(bf16[80,2048]{1,0:T(8,128)(2,1)S(1)} %collective-permute-done.13.refs_4_), channel_id=1, source_target_pairs={{0,1},{1,0},{2,3},{3,2},{4,5},{5,4},{6,7},{7,6},{8,9},{9,8},{10,11... | collective-permute-start | bytes 983048 | tf_op jit(solution)/shard_map/ppermute | solution.py:44
  48.6 2.5 %collective-permute-start.18 = (bf16[80,2048]{1,0:T(8,128)(2,1)S(1)}, bf16[80,2048]{1,0:T(8,128)(2,1)S(1)}, u32[]{:S(2)}, u32[]{:S(2)}) collective-permute-start(bf16[80,2048]{1,0:T(8,128)(2,1)S(1)} %collective-permute-done.14.refs_6_), channel_id=1, source_target_pairs={{0,1},{1,0},{2,3},{3,2},{4,5},{5,4},{6,7},{7,6},{8,9},{9,8},{10,11... | collective-permute-start | bytes 983048 | tf_op jit(solution)/shard_map/ppermute | solution.py:44
  52.7 1.5 collective-permute-start.19
  52.9 20.2 %collective-permute-start.26 = (bf16[1,2,2,48,1792]{4,3,2,1,0:T(8,128)(2,1)S(1)}, bf16[1,2,2,48,1792]{4,3,2,1,0:T(8,128)(2,1)S(1)}, u32[]{:S(2)}, u32[]{:S(2)}) collective-permute-start(bf16[1,2,2,48,1792]{4,3,2,1,0:T(8,128)(2,1)S(1)} %shard_map.87), channel_id=1, source_target_pairs={{0,8},{24,16},{1,9},{25,17},{2,10},{26,18},{3,11},{27,19},{4,12},{... | collective-permute-start | bytes 2064392 | tf_op jit(solution)/shard_map/ppermute | solution.py:265
  54.3 4.8 %collective-permute-start.20 = (bf16[320,128]{1,0:T(8,128)(2,1)S(1)}, bf16[320,128]{1,0:T(8,128)(2,1)S(1)}, u32[]{:S(2)}, u32[]{:S(2)}) collective-permute-start(bf16[320,128]{1,0:T(8,128)(2,1)S(1)} %add_convert_fusion.7), channel_id=1, source_target_pairs={{0,2},{1,3},{2,0},{3,1},{4,6},{5,7},{6,4},{7,5},{8,10},{9,11},{10,... | collective-permute-start | bytes 245768 | tf_op jit(solution)/shard_map/ppermute | solution.py:44
  59.1 4.5 %collective-permute-start.21 = (bf16[320,128]{1,0:T(8,128)(2,1)S(1)}, bf16[320,128]{1,0:T(8,128)(2,1)S(1)}, u32[]{:S(2)}, u32[]{:S(2)}) collective-permute-start(bf16[320,128]{1,0:T(8,128)(2,1)S(1)} %add_convert_fusion.6), channel_id=1, source_target_pairs={{0,4},{1,5},{2,6},{3,7},{4,0},{5,1},{6,2},{7,3},{8,12},{9,13},{10,... | collective-permute-start | bytes 245768 | tf_op jit(solution)/shard_map/ppermute | solution.py:44
  64.3 26.1 %collective-permute-start.23 = (bf16[320,128]{1,0:T(8,128)(2,1)}, bf16[320,128]{1,0:T(8,128)(2,1)}, u32[]{:S(2)}, u32[]{:S(2)}) collective-permute-start(bf16[320,128]{1,0:T(8,128)(2,1)} %add_convert_fusion.5), channel_id=1, source_target_pairs={{0,8},{8,16},{16,24},{24,0},{1,9},{9,17},{17,25},{25,1},{2,10},{10... | collective-permute-start | bytes 245768 | tf_op jit(solution)/shard_map/ppermute | solution.py:59
  66.7 23.7 %collective-permute-start.24 = (bf16[320,128]{1,0:T(8,128)(2,1)}, bf16[320,128]{1,0:T(8,128)(2,1)}, u32[]{:S(2)}, u32[]{:S(2)}) collective-permute-start(bf16[320,128]{1,0:T(8,128)(2,1)} %add_convert_fusion.5), channel_id=1, source_target_pairs={{0,16},{8,24},{16,0},{24,8},{1,17},{9,25},{17,1},{25,9},{2,18},{10... | collective-permute-start | bytes 245768 | tf_op jit(solution)/shard_map/ppermute | solution.py:59
  66.7 23.7 %collective-permute-start.25 = (bf16[320,128]{1,0:T(8,128)(2,1)}, bf16[320,128]{1,0:T(8,128)(2,1)}, u32[]{:S(2)}, u32[]{:S(2)}) collective-permute-start(bf16[320,128]{1,0:T(8,128)(2,1)} %add_convert_fusion.5), channel_id=1, source_target_pairs={{0,24},{8,0},{16,8},{24,16},{1,25},{9,1},{17,9},{25,17},{2,26},{10... | collective-permute-start | bytes 245768 | tf_op jit(solution)/shard_map/ppermute | solution.py:59
  68.4 8.7 %slice-start.2 = ((s8[7340032]{0:T(1024)(128)(4,1)}), s8[4194304]{0:T(1024)(128)(4,1)S(1)}, s32[]{:S(2)}) async-start(s8[7340032]{0:T(1024)(128)(4,1)} %bitcast.65), calls=%async_computation.2 | async-start | bytes 8388608
  70.6 6.4 %slice-start.3 = ((s8[7340032]{0:T(1024)(128)(4,1)}), s8[3145728]{0:T(1024)(128)(4,1)S(1)}, s32[]{:S(2)}) async-start(s8[7340032]{0:T(1024)(128)(4,1)} %bitcast.65), calls=%async_computation.3 | async-start | bytes 6291456
  70.6 36.8 %collective-permute-start.22 = (bf16[2,2,2,48,1792]{4,3,2,1,0:T(8,128)(2,1)}, bf16[2,2,2,48,1792]{4,3,2,1,0:T(8,128)(2,1)}, u32[]{:S(2)}, u32[]{:S(2)}) collective-permute-start(bf16[2,2,2,48,1792]{4,3,2,1,0:T(8,128)(2,1)} %shard_map.89), channel_id=1, source_target_pairs={{0,8},{24,16},{1,9},{25,17},{2,10},{26,18},{3,11},{27,19},{4,12},{... | collective-permute-start | bytes 4128776 | tf_op jit(solution)/shard_map/ppermute | solution.py:265
  72.2 11.5 %slice-start.6 = ((s8[7340032]{0:T(1024)(128)(4,1)}), s8[3145728]{0:T(1024)(128)(4,1)S(1)}, s32[]{:S(2)}) async-start(s8[7340032]{0:T(1024)(128)(4,1)} %bitcast.69), calls=%async_computation.6 | async-start | bytes 6291456
  73.3 19.1 %collective-permute-start.27 = (bf16[2,2,48,1792]{3,2,1,0:T(8,128)(2,1)S(1)}, bf16[2,2,48,1792]{3,2,1,0:T(8,128)(2,1)S(1)}, u32[]{:S(2)}, u32[]{:S(2)}) collective-permute-start(bf16[2,2,48,1792]{3,2,1,0:T(8,128)(2,1)S(1)} %fusion.8), channel_id=1, source_target_pairs={{8,16},{16,8},{9,17},{17,9},{10,18},{18,10},{11,19},{19,11},{12,20... | collective-permute-start | bytes 2064392 | tf_op jit(solution)/shard_map/ppermute | solution.py:277
  77.1 6.6 %slice-start.7 = ((s8[7340032]{0:T(1024)(128)(4,1)}), s8[4194304]{0:T(1024)(128)(4,1)S(1)}, s32[]{:S(2)}) async-start(s8[7340032]{0:T(1024)(128)(4,1)} %bitcast.69), calls=%async_computation.7 | async-start | bytes 8388608
  107.4 30.1 %collective-permute-start.30 = (bf16[1,2,2,80,1792]{4,3,2,1,0:T(8,128)(2,1)S(1)}, bf16[1,2,2,80,1792]{4,3,2,1,0:T(8,128)(2,1)S(1)}, u32[]{:S(2)}, u32[]{:S(2)}) collective-permute-start(bf16[1,2,2,80,1792]{4,3,2,1,0:T(8,128)(2,1)S(1)} %shard_map.93), channel_id=1, source_target_pairs={{0,8},{24,16},{1,9},{25,17},{2,10},{26,18},{3,11},{27,19},{4,12},{... | collective-permute-start | bytes 3440648 | tf_op jit(solution)/shard_map/ppermute | solution.py:265
  108.7 53.4 %collective-permute-start.32 = (bf16[1,2,2,80,1792]{4,3,2,1,0:T(8,128)(2,1)S(1)}, bf16[1,2,2,80,1792]{4,3,2,1,0:T(8,128)(2,1)S(1)}, u32[]{:S(2)}, u32[]{:S(2)}) collective-permute-start(bf16[1,2,2,80,1792]{4,3,2,1,0:T(8,128)(2,1)S(1)} %shard_map.94), channel_id=1, source_target_pairs={{0,8},{24,16},{1,9},{25,17},{2,10},{26,18},{3,11},{27,19},{4,12},{... | collective-permute-start | bytes 3440648 | tf_op jit(solution)/shard_map/ppermute | solution.py:265
  137.8 30.1 %collective-permute-start.34 = (bf16[2,2,80,1792]{3,2,1,0:T(8,128)(2,1)S(1)}, bf16[2,2,80,1792]{3,2,1,0:T(8,128)(2,1)S(1)}, u32[]{:S(2)}, u32[]{:S(2)}) collective-permute-start(bf16[2,2,80,1792]{3,2,1,0:T(8,128)(2,1)S(1)} %fusion.5), channel_id=1, source_target_pairs={{8,16},{16,8},{9,17},{17,9},{10,18},{18,10},{11,19},{19,11},{12,20... | collective-permute-start | bytes 3440648 | tf_op jit(solution)/shard_map/ppermute | solution.py:207
  141.2 28.4 %collective-permute-start.29 = (bf16[2,2,48,1792]{3,2,1,0:T(8,128)(2,1)S(1)}, bf16[2,2,48,1792]{3,2,1,0:T(8,128)(2,1)S(1)}, u32[]{:S(2)}, u32[]{:S(2)}) collective-permute-start(bf16[2,2,48,1792]{3,2,1,0:T(8,128)(2,1)S(1)} %fusion.2), channel_id=1, source_target_pairs={{16,24},{8,0},{17,25},{9,1},{18,26},{10,2},{19,27},{11,3},{20,28},... | collective-permute-start | bytes 2064392 | tf_op jit(solution)/shard_map/ppermute | solution.py:207
  144.0 38.6 %collective-permute-start.28 = (bf16[2,2,48,1792]{3,2,1,0:T(8,128)(2,1)S(1)}, bf16[2,2,48,1792]{3,2,1,0:T(8,128)(2,1)S(1)}, u32[]{:S(2)}, u32[]{:S(2)}) collective-permute-start(bf16[2,2,48,1792]{3,2,1,0:T(8,128)(2,1)S(1)} %fusion.9), channel_id=1, source_target_pairs={{8,16},{16,8},{9,17},{17,9},{10,18},{18,10},{11,19},{19,11},{12,20... | collective-permute-start | bytes 2064392 | tf_op jit(solution)/shard_map/ppermute | solution.py:207
  147.9 37.3 %collective-permute-start.31 = (bf16[1,2,2,80,1792]{4,3,2,1,0:T(8,128)(2,1)S(1)}, bf16[1,2,2,80,1792]{4,3,2,1,0:T(8,128)(2,1)S(1)}, u32[]{:S(2)}, u32[]{:S(2)}) collective-permute-start(bf16[1,2,2,80,1792]{4,3,2,1,0:T(8,128)(2,1)S(1)} %shard_map.95), channel_id=1, source_target_pairs={{0,8},{24,16},{1,9},{25,17},{2,10},{26,18},{3,11},{27,19},{4,12},{... | collective-permute-start | bytes 3440648 | tf_op jit(solution)/shard_map/ppermute | solution.py:265
  162.3 41.0 %collective-permute-start.33 = (bf16[2,2,80,1792]{3,2,1,0:T(8,128)(2,1)S(1)}, bf16[2,2,80,1792]{3,2,1,0:T(8,128)(2,1)S(1)}, u32[]{:S(2)}, u32[]{:S(2)}) collective-permute-start(bf16[2,2,80,1792]{3,2,1,0:T(8,128)(2,1)S(1)} %fusion.4), channel_id=1, source_target_pairs={{8,16},{16,8},{9,17},{17,9},{10,18},{18,10},{11,19},{19,11},{12,20... | collective-permute-start | bytes 3440648 | tf_op jit(solution)/shard_map/ppermute | solution.py:207
  168.2 35.2 %collective-permute-start.35 = (bf16[2,2,80,1792]{3,2,1,0:T(8,128)(2,1)S(1)}, bf16[2,2,80,1792]{3,2,1,0:T(8,128)(2,1)S(1)}, u32[]{:S(2)}, u32[]{:S(2)}) collective-permute-start(bf16[2,2,80,1792]{3,2,1,0:T(8,128)(2,1)S(1)} %fusion), channel_id=1, source_target_pairs={{16,24},{8,0},{17,25},{9,1},{18,26},{10,2},{19,27},{11,3},{20,28},... | collective-permute-start | bytes 3440648 | tf_op jit(solution)/shard_map/ppermute | solution.py:207

commit v7 on v6

--- a/solution.py
+++ b/solution.py
@@ -284,12 +284,14 @@
     for slot in range(1, nseq):
         sent.append(terms(parts, inner, 0, rows, slot, 1, (sent[-1], second_hop)))
     rest_hop = after(rest_hop, sent[-1])
+    third_hop = lax.ppermute(add(rest[0], rest_hop[0]), "seq", hop_pairs(1, nseq))
     hops = []
     for slot in range(nseq - 1):
         hops.append(first_hop(after(sent[slot], hops[slot - 2] if slot > 1 else rest_hop)))
 
+    hops[0] = after(hops[0], third_hop)
     totals = [
-        scatter_line(own, [head_hop[0]] + [rest_hop[slot] for slot in range(nseq - 2)], nseq, {(1, 1): second_hop}),
+        scatter_line(own, [head_hop[0]] + [rest_hop[slot] for slot in range(nseq - 2)], nseq, {(1, 1): second_hop, (1, 2): third_hop}),
         scatter_line([term[0] for term in sent], [hop[0] for hop in hops], nseq),
     ]
     out = [(jax.nn.silu(total[0]) * total[1]).astype(jnp.bfloat16) for total in totals]

time: 206 us -> 195 us (0.947)
  the two profiles are of different devices: /device:TPU:16 before, /device:TPU:0 now
where the time goes in v7:
time: 195 us
  waiting for transfers between devices  87.6 us (45%)
  starting transfers between devices  53.9 us (28%)
  Pallas kernels  33.9 us (17%)
  other arithmetic  12.8 us (7%)
  local copies, waits for them, and re-layouts  5.99 us (3%)
    ppermute x5, waiting for transfers between devices, first_hop(): return lax.ppermute(send, 'seq', hop_pairs(0, nseq))  55.4 us
    ppermute x5, starting transfers between devices, first_hop(): return lax.ppermute(send, 'seq', hop_pairs(0, nseq))  25.1 us
    ppermute x22, waiting for transfers between devices, swap(): return lax.ppermute(x, axis, [(i, i ^ mask) for i in range(size)])  23.6 us
    pallas_call x6, Pallas kernels, project(): pl.pallas_call(project_kernel, out_shape=jax.ShapeDtypeStruct((rows, coun...  22.6 us
    ppermute x22, starting transfers between devices, swap(): return lax.ppermute(x, axis, [(i, i ^ mask) for i in range(size)])  17.7 us
    ppermute x4, waiting for transfers between devices, scatter_line(): arrived[level, step] = lax.ppermute(send, 'seq', hop_pairs(level, nseq))  8.62 us
    pallas_call x7, Pallas kernels, add_low_rank(): pl.pallas_call(functools.partial(low_rank_kernel, first, each, start, wid...  8.25 us
    convert_element_type x14, other arithmetic, add(): return (x.astype(jnp.float32) + y.astype(jnp.float32)).astype(x.dtype)  5.61 us
  transfers between devices with their start and end apart: 36, of which 19 were waited for; matrix products, arithmetic and copies ran while one was open for 6% of the time, Pallas kernels for 16%

profile of v7, /device:TPU:0, one launch (start us, length us, event | category | flops | bytes accessed | tf_op | source)
XLA Modules:
  0.0 194.6 jit_solution(10813760577143475508)
XLA Ops:
  0.9 3.0 %collective-permute-start.1 = (bf16[48,2048]{1,0:T(8,128)(2,1)S(1)}, bf16[48,2048]{1,0:T(8,128)(2,1)S(1)}, u32[]{:S(2)}, u32[]{:S(2)}) collective-permute-start(bf16[48,2048]{1,0:T(8,128)(2,1)S(1)} %slice.30.refs_0_), channel_id=1, source_target_pairs={{0,2},{1,3},{2,0},{3,1},{4,6},{5,7},{6,4},{7,5},{8,10},{9,11},{10,... | collective-permute-start | bytes 589832 | tf_op jit(solution)/shard_map/ppermute | solution.py:44
  3.9 1.5 collective-permute-start.3
  8.2 1.5 collective-permute-done.1.refs_2_
  9.7 4.8 %collective-permute-done.3.refs_4_ = bf16[48,2048]{1,0:T(8,128)(2,1)S(1)} collective-permute-done((bf16[48,2048]{1,0:T(8,128)(2,1)S(1)}, bf16[48,2048]{1,0:T(8,128)(2,1)S(1)}, u32[]{:S(2)}, u32[]{:S(2)}) %collective-permute-start.3) | collective-permute-done | bytes 196640 | tf_op jit(solution)/shard_map/ppermute | solution.py:44
  16.2 1.6 copy-done.1
  17.8 1.4 shard_map.82
  20.6 1.0 collective-permute-start.8
  21.6 3.1 %copy-done = bf16[2048,1792]{1,0:T(8,128)(2,1)S(1)} copy-done((bf16[2048,1792]{1,0:T(8,128)(2,1)S(1)}, bf16[2048,1792]{1,0:T(8,128)(2,1)}, u32[]{:S(2)}) %copy-start) | copy-done | bytes 7340056
  24.7 2.0 %shard_map.83.refs_0_ = bf16[384,768]{1,0:T(8,128)(2,1)S(1)} custom-call(bf16[384,2048]{1,0:T(8,128)(2,1)S(1)} %bitcast.71, bf16[2048,1792]{1,0:T(8,128)(2,1)S(1)} %copy-done), custom_call_target="tpu_custom_call" | custom-call | flops 1207959552 | bytes 3145728 | tf_op jit(solution)/shard_map/pallas_call | solution.py:127
  26.7 1.2 collective-permute-start.9
  27.9 2.7 %shard_map.84.refs_1_ = bf16[384,1024]{1,0:T(8,128)(2,1)S(1)} custom-call(bf16[384,2048]{1,0:T(8,128)(2,1)S(1)} %bitcast.72, bf16[2048,1792]{1,0:T(8,128)(2,1)S(1)} %copy-done), custom_call_target="tpu_custom_call" | custom-call | flops 1610612736 | bytes 4194304 | tf_op jit(solution)/shard_map/pallas_call | solution.py:127
  30.9 1.6 collective-permute-start.10
  32.5 1.2 collective-permute-start.12
  33.8 1.4 collective-permute-start.13
  36.0 2.0 %shard_map.85.refs_2_ = bf16[384,768]{1,0:T(8,128)(2,1)S(1)} custom-call(bf16[384,2048]{1,0:T(8,128)(2,1)S(1)} %bitcast.73, bf16[2048,1792]{1,0:T(8,128)(2,1)S(1)} %bitcast.68), custom_call_target="tpu_custom_call" | custom-call | flops 1207959552 | bytes 3145728 | tf_op jit(solution)/shard_map/pallas_call | solution.py:127
  38.1 2.7 %collective-permute-start.11 = (bf16[192,128]{1,0:T(8,128)(2,1)S(1)}, bf16[192,128]{1,0:T(8,128)(2,1)S(1)}, u32[]{:S(2)}, u32[]{:S(2)}) collective-permute-start(bf16[192,128]{1,0:T(8,128)(2,1)S(1)} %add_convert_fusion.9), channel_id=1, source_target_pairs={{0,16},{8,24},{16,0},{24,8},{1,17},{9,25},{17,1},{25,9},{2,18},{10... | collective-permute-start | bytes 147464 | tf_op jit(solution)/shard_map/ppermute | solution.py:44
  40.8 2.7 %shard_map.86.refs_3_ = bf16[384,1024]{1,0:T(8,128)(2,1)S(1)} custom-call(bf16[384,2048]{1,0:T(8,128)(2,1)S(1)} %bitcast.74, bf16[2048,1792]{1,0:T(8,128)(2,1)S(1)} %bitcast.68), custom_call_target="tpu_custom_call" | custom-call | flops 1610612736 | bytes 4194304 | tf_op jit(solution)/shard_map/pallas_call | solution.py:127
  44.6 4.9 %collective-permute-done.13.refs_4_ = bf16[80,2048]{1,0:T(8,128)(2,1)S(1)} collective-permute-done((bf16[80,2048]{1,0:T(8,128)(2,1)S(1)}, bf16[80,2048]{1,0:T(8,128)(2,1)S(1)}, u32[]{:S(2)}, u32[]{:S(2)}) %collective-permute-start.13) | collective-permute-done | bytes 327712 | tf_op jit(solution)/shard_map/ppermute | solution.py:44
  52.6 1.6 shard_map.88
  54.4 2.4 %collective-permute-start.26 = (bf16[1,2,2,48,1792]{4,3,2,1,0:T(8,128)(2,1)S(1)}, bf16[1,2,2,48,1792]{4,3,2,1,0:T(8,128)(2,1)S(1)}, u32[]{:S(2)}, u32[]{:S(2)}) collective-permute-start(bf16[1,2,2,48,1792]{4,3,2,1,0:T(8,128)(2,1)S(1)} %shard_map.87), channel_id=1, source_target_pairs={{0,8},{24,16},{1,9},{25,17},{2,10},{26,18},{3,11},{27,19},{4,12},{... | collective-permute-start | bytes 2064392 | tf_op jit(solution)/shard_map/ppermute | solution.py:265
  57.4 3.9 %collective-permute-done.20 = bf16[320,128]{1,0:T(8,128)(2,1)S(1)} collective-permute-done((bf16[320,128]{1,0:T(8,128)(2,1)S(1)}, bf16[320,128]{1,0:T(8,128)(2,1)S(1)}, u32[]{:S(2)}, u32[]{:S(2)}) %collective-permute-start.20) | collective-permute-done | bytes 81952 | tf_op jit(solution)/shard_map/ppermute | solution.py:44
  61.9 3.9 %collective-permute-done.21 = bf16[320,128]{1,0:T(8,128)(2,1)S(1)} collective-permute-done((bf16[320,128]{1,0:T(8,128)(2,1)S(1)}, bf16[320,128]{1,0:T(8,128)(2,1)S(1)}, u32[]{:S(2)}, u32[]{:S(2)}) %collective-permute-start.21) | collective-permute-done | bytes 81952 | tf_op jit(solution)/shard_map/ppermute | solution.py:44
  66.6 4.2 %collective-permute-start.24 = (bf16[320,128]{1,0:T(8,128)(2,1)}, bf16[320,128]{1,0:T(8,128)(2,1)}, u32[]{:S(2)}, u32[]{:S(2)}) collective-permute-start(bf16[320,128]{1,0:T(8,128)(2,1)} %add_convert_fusion.5), channel_id=1, source_target_pairs={{0,16},{8,24},{16,0},{24,8},{1,17},{9,25},{17,1},{25,9},{2,18},{10... | collective-permute-start | bytes 245768 | tf_op jit(solution)/shard_map/ppermute | solution.py:59
  71.2 2.2 %shard_map.89 = bf16[2,2,2,48,1792]{4,3,2,1,0:T(8,128)(2,1)} custom-call(s32[3,8]{1,0:T(4,128)S(1)} %pad_add_fusion.tab_ref, bf16[4,48,128]{2,1,0:T(8,128)(2,1)S(1)} %bitcast.80, bf16[384,768]{1,0:T(8,128)(2,1)S(1)} %shard_map.83.refs_0_, bf16[384,1024]{1,0:T(8,128)(2,1)S(1)} %shard_map.84.refs_1_, bf16[384,768]{1,0:T(8,128)(2,1)S(1)} %shard_map.85.refs_2_, ...), custom_call_target="tpu_custom_call" | custom-call | flops 1024 | bytes 1024 | tf_op jit(solution)/shard_map/pallas_call | solution.py:173
  73.5 4.5 %collective-permute-start.22 = (bf16[2,2,2,48,1792]{4,3,2,1,0:T(8,128)(2,1)}, bf16[2,2,2,48,1792]{4,3,2,1,0:T(8,128)(2,1)}, u32[]{:S(2)}, u32[]{:S(2)}) collective-permute-start(bf16[2,2,2,48,1792]{4,3,2,1,0:T(8,128)(2,1)} %shard_map.89), channel_id=1, source_target_pairs={{0,8},{24,16},{1,9},{25,17},{2,10},{26,18},{3,11},{27,19},{4,12},{... | collective-permute-start | bytes 4128776 | tf_op jit(solution)/shard_map/ppermute | solution.py:265
  78.0 1.0 fusion.8
  79.0 1.6 collective-permute-start.27
  81.9 6.6 %shard_map.91.refs_0_ = bf16[640,1792]{1,0:T(8,128)(2,1)S(1)} custom-call(bf16[640,2048]{1,0:T(8,128)(2,1)S(1)} %bitcast.84, bf16[2048,1792]{1,0:T(8,128)(2,1)S(1)} %bitcast.66), custom_call_target="tpu_custom_call" | custom-call | flops 68719476736 | bytes 7340032 | tf_op jit(solution)/shard_map/pallas_call | solution.py:127
  88.5 6.6 %shard_map.92.refs_1_ = bf16[640,1792]{1,0:T(8,128)(2,1)S(1)} custom-call(bf16[640,2048]{1,0:T(8,128)(2,1)S(1)} %bitcast.85, bf16[2048,1792]{1,0:T(8,128)(2,1)S(1)} %bitcast.70), custom_call_target="tpu_custom_call" | custom-call | flops 68719476736 | bytes 7340032 | tf_op jit(solution)/shard_map/pallas_call | solution.py:127
  95.1 1.1 add_convert_fusion.4
  96.2 1.0 shard_map.93
  97.2 1.0 shard_map.94
  98.3 1.0 shard_map.95
  99.3 1.0 shard_map.96
  100.3 6.5 %collective-permute-done.22 = bf16[2,2,2,48,1792]{4,3,2,1,0:T(8,128)(2,1)} collective-permute-done((bf16[2,2,2,48,1792]{4,3,2,1,0:T(8,128)(2,1)}, bf16[2,2,2,48,1792]{4,3,2,1,0:T(8,128)(2,1)}, u32[]{:S(2)}, u32[]{:S(2)}) %collective-permute-start.22) | collective-permute-done | bytes 1376288 | tf_op jit(solution)/shard_map/ppermute | solution.py:265
  106.8 4.4 %collective-permute-start.30 = (bf16[1,2,2,80,1792]{4,3,2,1,0:T(8,128)(2,1)S(1)}, bf16[1,2,2,80,1792]{4,3,2,1,0:T(8,128)(2,1)S(1)}, u32[]{:S(2)}, u32[]{:S(2)}) collective-permute-start(bf16[1,2,2,80,1792]{4,3,2,1,0:T(8,128)(2,1)S(1)} %shard_map.93), channel_id=1, source_target_pairs={{0,8},{24,16},{1,9},{25,17},{2,10},{26,18},{3,11},{27,19},{4,12},{... | collective-permute-start | bytes 3440648 | tf_op jit(solution)/shard_map/ppermute | solution.py:265
  111.3 1.5 fusion.9
  113.5 5.4 %collective-permute-start.32 = (bf16[1,2,2,80,1792]{4,3,2,1,0:T(8,128)(2,1)S(1)}, bf16[1,2,2,80,1792]{4,3,2,1,0:T(8,128)(2,1)S(1)}, u32[]{:S(2)}, u32[]{:S(2)}) collective-permute-start(bf16[1,2,2,80,1792]{4,3,2,1,0:T(8,128)(2,1)S(1)} %shard_map.94), channel_id=1, source_target_pairs={{0,8},{24,16},{1,9},{25,17},{2,10},{26,18},{3,11},{27,19},{4,12},{... | collective-permute-start | bytes 3440648 | tf_op jit(solution)/shard_map/ppermute | solution.py:265
  118.8 18.1 %collective-permute-done.30 = bf16[1,2,2,80,1792]{4,3,2,1,0:T(8,128)(2,1)S(1)} collective-permute-done((bf16[1,2,2,80,1792]{4,3,2,1,0:T(8,128)(2,1)S(1)}, bf16[1,2,2,80,1792]{4,3,2,1,0:T(8,128)(2,1)S(1)}, u32[]{:S(2)}, u32[]{:S(2)}) %collective-permute-start.30) | collective-permute-done | bytes 1146912 | tf_op jit(solution)/shard_map/ppermute | solution.py:265
  137.9 1.5 fusion.2
  139.4 1.3 collective-permute-start.29
  140.7 8.4 %collective-permute-start.31 = (bf16[1,2,2,80,1792]{4,3,2,1,0:T(8,128)(2,1)S(1)}, bf16[1,2,2,80,1792]{4,3,2,1,0:T(8,128)(2,1)S(1)}, u32[]{:S(2)}, u32[]{:S(2)}) collective-permute-start(bf16[1,2,2,80,1792]{4,3,2,1,0:T(8,128)(2,1)S(1)} %shard_map.95), channel_id=1, source_target_pairs={{0,8},{24,16},{1,9},{25,17},{2,10},{26,18},{3,11},{27,19},{4,12},{... | collective-permute-start | bytes 3440648 | tf_op jit(solution)/shard_map/ppermute | solution.py:265
  149.1 12.4 %collective-permute-done.32 = bf16[1,2,2,80,1792]{4,3,2,1,0:T(8,128)(2,1)S(1)} collective-permute-done((bf16[1,2,2,80,1792]{4,3,2,1,0:T(8,128)(2,1)S(1)}, bf16[1,2,2,80,1792]{4,3,2,1,0:T(8,128)(2,1)S(1)}, u32[]{:S(2)}, u32[]{:S(2)}) %collective-permute-start.32) | collective-permute-done | bytes 1146912 | tf_op jit(solution)/shard_map/ppermute | solution.py:265
  162.8 1.3 collective-permute-start.35
  164.1 1.4 fusion.3
  165.7 18.4 %collective-permute-done.31 = bf16[1,2,2,80,1792]{4,3,2,1,0:T(8,128)(2,1)S(1)} collective-permute-done((bf16[1,2,2,80,1792]{4,3,2,1,0:T(8,128)(2,1)S(1)}, bf16[1,2,2,80,1792]{4,3,2,1,0:T(8,128)(2,1)S(1)}, u32[]{:S(2)}, u32[]{:S(2)}) %collective-permute-start.31) | collective-permute-done | bytes 1146912 | tf_op jit(solution)/shard_map/ppermute | solution.py:265
  184.1 8.6 %collective-permute-done.35 = bf16[2,2,80,1792]{3,2,1,0:T(8,128)(2,1)S(1)} collective-permute-done((bf16[2,2,80,1792]{3,2,1,0:T(8,128)(2,1)S(1)}, bf16[2,2,80,1792]{3,2,1,0:T(8,128)(2,1)S(1)}, u32[]{:S(2)}, u32[]{:S(2)}) %collective-permute-start.35) | collective-permute-done | bytes 1146912 | tf_op jit(solution)/shard_map/ppermute | solution.py:207
  193.6 1.0 pad_maximum_fusion
  (103 shorter events, 19.9 us)
Async XLA Ops:
  0.9 8.7 %collective-permute-start.1 = (bf16[48,2048]{1,0:T(8,128)(2,1)S(1)}, bf16[48,2048]{1,0:T(8,128)(2,1)S(1)}, u32[]{:S(2)}, u32[]{:S(2)}) collective-permute-start(bf16[48,2048]{1,0:T(8,128)(2,1)S(1)} %slice.30.refs_0_), channel_id=1, source_target_pairs={{0,2},{1,3},{2,0},{3,1},{4,6},{5,7},{6,4},{7,5},{8,10},{9,11},{10,... | collective-permute-start | bytes 589832 | tf_op jit(solution)/shard_map/ppermute | solution.py:44
  3.9 10.6 %collective-permute-start.3 = (bf16[48,2048]{1,0:T(8,128)(2,1)S(1)}, bf16[48,2048]{1,0:T(8,128)(2,1)S(1)}, u32[]{:S(2)}, u32[]{:S(2)}) collective-permute-start(bf16[48,2048]{1,0:T(8,128)(2,1)S(1)} %slice.30.refs_0_), channel_id=1, source_target_pairs={{0,4},{1,5},{2,6},{3,7},{4,0},{5,1},{6,2},{7,3},{8,12},{9,13},{10,... | collective-permute-start | bytes 589832 | tf_op jit(solution)/shard_map/ppermute | solution.py:44
  5.5 9.1 %collective-permute-start.5 = (bf16[48,2048]{1,0:T(8,128)(2,1)S(1)}, bf16[48,2048]{1,0:T(8,128)(2,1)S(1)}, u32[]{:S(2)}, u32[]{:S(2)}) collective-permute-start(bf16[48,2048]{1,0:T(8,128)(2,1)S(1)} %slice.30.refs_0_), channel_id=1, source_target_pairs={{0,6},{1,7},{2,4},{3,5},{4,2},{5,3},{6,0},{7,1},{8,14},{9,15},{10,... | collective-permute-start | bytes 589832 | tf_op jit(solution)/shard_map/ppermute | solution.py:44
  5.5 9.6 %collective-permute-start = (bf16[48,2048]{1,0:T(8,128)(2,1)S(1)}, bf16[48,2048]{1,0:T(8,128)(2,1)S(1)}, u32[]{:S(2)}, u32[]{:S(2)}) collective-permute-start(bf16[48,2048]{1,0:T(8,128)(2,1)S(1)} %slice.30.refs_0_), channel_id=1, source_target_pairs={{0,1},{1,0},{2,3},{3,2},{4,5},{5,4},{6,7},{7,6},{8,9},{9,8},{10,11... | collective-permute-start | bytes 589832 | tf_op jit(solution)/shard_map/ppermute | solution.py:44
  9.7 5.4 %collective-permute-start.2 = (bf16[48,2048]{1,0:T(8,128)(2,1)S(1)}, bf16[48,2048]{1,0:T(8,128)(2,1)S(1)}, u32[]{:S(2)}, u32[]{:S(2)}) collective-permute-start(bf16[48,2048]{1,0:T(8,128)(2,1)S(1)} %collective-permute-done.1.refs_2_), channel_id=1, source_target_pairs={{0,1},{1,0},{2,3},{3,2},{4,5},{5,4},{6,7},{7,6},{8,9},{9,8},{10,11... | collective-permute-start | bytes 589832 | tf_op jit(solution)/shard_map/ppermute | solution.py:44
  14.5 1.4 collective-permute-start.4
  14.5 1.7 collective-permute-start.6
  16.2 1.6 copy-start.1
  17.8 1.7 copy-start.3
  19.3 1.3 collective-permute-start.7
  20.6 6.1 %collective-permute-start.8 = (bf16[192,128]{1,0:T(8,128)(2,1)S(1)}, bf16[192,128]{1,0:T(8,128)(2,1)S(1)}, u32[]{:S(2)}, u32[]{:S(2)}) collective-permute-start(bf16[192,128]{1,0:T(8,128)(2,1)S(1)} %add_convert_fusion.12), channel_id=1, source_target_pairs={{0,2},{1,3},{2,0},{3,1},{4,6},{5,7},{6,4},{7,5},{8,10},{9,11},{10,... | collective-permute-start | bytes 147464 | tf_op jit(solution)/shard_map/ppermute | solution.py:44
  21.6 3.1 %copy-start = (bf16[2048,1792]{1,0:T(8,128)(2,1)S(1)}, bf16[2048,1792]{1,0:T(8,128)(2,1)}, u32[]{:S(2)}) copy-start(bf16[2048,1792]{1,0:T(8,128)(2,1)} %weight_ref.10) | copy-start | bytes 22020100
  24.7 11.4 %slice-start.4 = ((s8[7340032]{0:T(1024)(128)(4,1)}), s8[4194304]{0:T(1024)(128)(4,1)S(1)}, s32[]{:S(2)}) async-start(s8[7340032]{0:T(1024)(128)(4,1)} %bitcast.67), calls=%async_computation.4 | async-start | bytes 8388608
  26.7 9.3 %slice-start.5 = ((s8[7340032]{0:T(1024)(128)(4,1)}), s8[3145728]{0:T(1024)(128)(4,1)S(1)}, s32[]{:S(2)}) async-start(s8[7340032]{0:T(1024)(128)(4,1)} %bitcast.67), calls=%async_computation.5 | async-start | bytes 6291456
  26.7 4.2 %collective-permute-start.9 = (bf16[192,128]{1,0:T(8,128)(2,1)S(1)}, bf16[192,128]{1,0:T(8,128)(2,1)S(1)}, u32[]{:S(2)}, u32[]{:S(2)}) collective-permute-start(bf16[192,128]{1,0:T(8,128)(2,1)S(1)} %add_convert_fusion.11), channel_id=1, source_target_pairs={{0,4},{1,5},{2,6},{3,7},{4,0},{5,1},{6,2},{7,3},{8,12},{9,13},{10,... | collective-permute-start | bytes 147464 | tf_op jit(solution)/shard_map/ppermute | solution.py:44
  30.9 7.2 %collective-permute-start.10 = (bf16[192,128]{1,0:T(8,128)(2,1)S(1)}, bf16[192,128]{1,0:T(8,128)(2,1)S(1)}, u32[]{:S(2)}, u32[]{:S(2)}) collective-permute-start(bf16[192,128]{1,0:T(8,128)(2,1)S(1)} %add_convert_fusion.10), channel_id=1, source_target_pairs={{0,8},{8,0},{16,24},{24,16},{1,9},{9,1},{17,25},{25,17},{2,10},{10... | collective-permute-start | bytes 147464 | tf_op jit(solution)/shard_map/ppermute | solution.py:44
  32.5 12.1 %collective-permute-start.12 = (bf16[80,2048]{1,0:T(8,128)(2,1)S(1)}, bf16[80,2048]{1,0:T(8,128)(2,1)S(1)}, u32[]{:S(2)}, u32[]{:S(2)}) collective-permute-start(bf16[80,2048]{1,0:T(8,128)(2,1)S(1)} %slice.31.refs_0_), channel_id=1, source_target_pairs={{0,2},{1,3},{2,0},{3,1},{4,6},{5,7},{6,4},{7,5},{8,10},{9,11},{10,... | collective-permute-start | bytes 983048 | tf_op jit(solution)/shard_map/ppermute | solution.py:44
  33.8 15.8 %collective-permute-start.13 = (bf16[80,2048]{1,0:T(8,128)(2,1)S(1)}, bf16[80,2048]{1,0:T(8,128)(2,1)S(1)}, u32[]{:S(2)}, u32[]{:S(2)}) collective-permute-start(bf16[80,2048]{1,0:T(8,128)(2,1)S(1)} %slice.31.refs_0_), channel_id=1, source_target_pairs={{0,4},{1,5},{2,6},{3,7},{4,0},{5,1},{6,2},{7,3},{8,12},{9,13},{10,... | collective-permute-start | bytes 983048 | tf_op jit(solution)/shard_map/ppermute | solution.py:44
  35.1 14.4 %collective-permute-start.14 = (bf16[80,2048]{1,0:T(8,128)(2,1)S(1)}, bf16[80,2048]{1,0:T(8,128)(2,1)S(1)}, u32[]{:S(2)}, u32[]{:S(2)}) collective-permute-start(bf16[80,2048]{1,0:T(8,128)(2,1)S(1)} %slice.31.refs_0_), channel_id=1, source_target_pairs={{0,6},{1,7},{2,4},{3,5},{4,2},{5,3},{6,0},{7,1},{8,14},{9,15},{10,... | collective-permute-start | bytes 983048 | tf_op jit(solution)/shard_map/ppermute | solution.py:44
  36.0 7.6 %slice-start = ((s8[7340032]{0:T(1024)(128)(4,1)}), s8[4194304]{0:T(1024)(128)(4,1)S(1)}, s32[]{:S(2)}) async-start(s8[7340032]{0:T(1024)(128)(4,1)} %bitcast.63), calls=%async_computation | async-start | bytes 8388608
  38.1 5.5 %slice-start.1 = ((s8[7340032]{0:T(1024)(128)(4,1)}), s8[3145728]{0:T(1024)(128)(4,1)S(1)}, s32[]{:S(2)}) async-start(s8[7340032]{0:T(1024)(128)(4,1)} %bitcast.63), calls=%async_computation.1 | async-start | bytes 6291456
  38.1 5.5 %collective-permute-start.11 = (bf16[192,128]{1,0:T(8,128)(2,1)S(1)}, bf16[192,128]{1,0:T(8,128)(2,1)S(1)}, u32[]{:S(2)}, u32[]{:S(2)}) collective-permute-start(bf16[192,128]{1,0:T(8,128)(2,1)S(1)} %add_convert_fusion.9), channel_id=1, source_target_pairs={{0,16},{8,24},{16,0},{24,8},{1,17},{9,25},{17,1},{25,9},{2,18},{10... | collective-permute-start | bytes 147464 | tf_op jit(solution)/shard_map/ppermute | solution.py:44
  43.6 8.9 %copy-start.2 = (bf16[8,64,2048]{2,1,0:T(8,128)(2,1)S(1)}, bf16[8,64,2048]{2,1,0:T(8,128)(2,1)}, u32[]{:S(2)}) copy-start(bf16[8,64,2048]{2,1,0:T(8,128)(2,1)} %refs_8_.3) | copy-start | bytes 6291460
  49.5 1.6 collective-permute-start.15
  49.5 2.1 %collective-permute-start.16 = (bf16[80,2048]{1,0:T(8,128)(2,1)S(1)}, bf16[80,2048]{1,0:T(8,128)(2,1)S(1)}, u32[]{:S(2)}, u32[]{:S(2)}) collective-permute-start(bf16[80,2048]{1,0:T(8,128)(2,1)S(1)} %collective-permute-done.12.refs_2_), channel_id=1, source_target_pairs={{0,1},{1,0},{2,3},{3,2},{4,5},{5,4},{6,7},{7,6},{8,9},{9,8},{10,11... | collective-permute-start | bytes 983048 | tf_op jit(solution)/shard_map/ppermute | solution.py:44
  50.0 2.1 %collective-permute-start.17 = (bf16[80,2048]{1,0:T(8,128)(2,1)S(1)}, bf16[80,2048]{1,0:T(8,128)(2,1)S(1)}, u32[]{:S(2)}, u32[]{:S(2)}) collective-permute-start(bf16[80,2048]{1,0:T(8,128)(2,1)S(1)} %collective-permute-done.13.refs_4_), channel_id=1, source_target_pairs={{0,1},{1,0},{2,3},{3,2},{4,5},{5,4},{6,7},{7,6},{8,9},{9,8},{10,11... | collective-permute-start | bytes 983048 | tf_op jit(solution)/shard_map/ppermute | solution.py:44
  50.0 2.5 %collective-permute-start.18 = (bf16[80,2048]{1,0:T(8,128)(2,1)S(1)}, bf16[80,2048]{1,0:T(8,128)(2,1)S(1)}, u32[]{:S(2)}, u32[]{:S(2)}) collective-permute-start(bf16[80,2048]{1,0:T(8,128)(2,1)S(1)} %collective-permute-done.14.refs_6_), channel_id=1, source_target_pairs={{0,1},{1,0},{2,3},{3,2},{4,5},{5,4},{6,7},{7,6},{8,9},{9,8},{10,11... | collective-permute-start | bytes 983048 | tf_op jit(solution)/shard_map/ppermute | solution.py:44
  54.2 2.6 %collective-permute-start.19 = (bf16[320,128]{1,0:T(8,128)(2,1)S(1)}, bf16[320,128]{1,0:T(8,128)(2,1)S(1)}, u32[]{:S(2)}, u32[]{:S(2)}) collective-permute-start(bf16[320,128]{1,0:T(8,128)(2,1)S(1)} %bitcast.82), channel_id=1, source_target_pairs={{0,1},{1,0},{2,3},{3,2},{4,5},{5,4},{6,7},{7,6},{8,9},{9,8},{10,11... | collective-permute-start | bytes 245768 | tf_op jit(solution)/shard_map/ppermute | solution.py:44
  54.4 23.6 %collective-permute-start.26 = (bf16[1,2,2,48,1792]{4,3,2,1,0:T(8,128)(2,1)S(1)}, bf16[1,2,2,48,1792]{4,3,2,1,0:T(8,128)(2,1)S(1)}, u32[]{:S(2)}, u32[]{:S(2)}) collective-permute-start(bf16[1,2,2,48,1792]{4,3,2,1,0:T(8,128)(2,1)S(1)} %shard_map.87), channel_id=1, source_target_pairs={{0,8},{24,16},{1,9},{25,17},{2,10},{26,18},{3,11},{27,19},{4,12},{... | collective-permute-start | bytes 2064392 | tf_op jit(solution)/shard_map/ppermute | solution.py:265
  56.8 4.5 %collective-permute-start.20 = (bf16[320,128]{1,0:T(8,128)(2,1)S(1)}, bf16[320,128]{1,0:T(8,128)(2,1)S(1)}, u32[]{:S(2)}, u32[]{:S(2)}) collective-permute-start(bf16[320,128]{1,0:T(8,128)(2,1)S(1)} %add_convert_fusion.7), channel_id=1, source_target_pairs={{0,2},{1,3},{2,0},{3,1},{4,6},{5,7},{6,4},{7,5},{8,10},{9,11},{10,... | collective-permute-start | bytes 245768 | tf_op jit(solution)/shard_map/ppermute | solution.py:44
  61.4 4.5 %collective-permute-start.21 = (bf16[320,128]{1,0:T(8,128)(2,1)S(1)}, bf16[320,128]{1,0:T(8,128)(2,1)S(1)}, u32[]{:S(2)}, u32[]{:S(2)}) collective-permute-start(bf16[320,128]{1,0:T(8,128)(2,1)S(1)} %add_convert_fusion.6), channel_id=1, source_target_pairs={{0,4},{1,5},{2,6},{3,7},{4,0},{5,1},{6,2},{7,3},{8,12},{9,13},{10,... | collective-permute-start | bytes 245768 | tf_op jit(solution)/shard_map/ppermute | solution.py:44
  66.5 28.5 %collective-permute-start.23 = (bf16[320,128]{1,0:T(8,128)(2,1)}, bf16[320,128]{1,0:T(8,128)(2,1)}, u32[]{:S(2)}, u32[]{:S(2)}) collective-permute-start(bf16[320,128]{1,0:T(8,128)(2,1)} %add_convert_fusion.5), channel_id=1, source_target_pairs={{0,8},{8,16},{16,24},{24,0},{1,9},{9,17},{17,25},{25,1},{2,10},{10... | collective-permute-start | bytes 245768 | tf_op jit(solution)/shard_map/ppermute | solution.py:59
  66.6 28.6 %collective-permute-start.24 = (bf16[320,128]{1,0:T(8,128)(2,1)}, bf16[320,128]{1,0:T(8,128)(2,1)}, u32[]{:S(2)}, u32[]{:S(2)}) collective-permute-start(bf16[320,128]{1,0:T(8,128)(2,1)} %add_convert_fusion.5), channel_id=1, source_target_pairs={{0,16},{8,24},{16,0},{24,8},{1,17},{9,25},{17,1},{25,9},{2,18},{10... | collective-permute-start | bytes 245768 | tf_op jit(solution)/shard_map/ppermute | solution.py:59
  70.7 24.4 %collective-permute-start.25 = (bf16[320,128]{1,0:T(8,128)(2,1)}, bf16[320,128]{1,0:T(8,128)(2,1)}, u32[]{:S(2)}, u32[]{:S(2)}) collective-permute-start(bf16[320,128]{1,0:T(8,128)(2,1)} %add_convert_fusion.5), channel_id=1, source_target_pairs={{0,24},{8,0},{16,8},{24,16},{1,25},{9,1},{17,9},{25,17},{2,26},{10... | collective-permute-start | bytes 245768 | tf_op jit(solution)/shard_map/ppermute | solution.py:59
  73.5 33.4 %collective-permute-start.22 = (bf16[2,2,2,48,1792]{4,3,2,1,0:T(8,128)(2,1)}, bf16[2,2,2,48,1792]{4,3,2,1,0:T(8,128)(2,1)}, u32[]{:S(2)}, u32[]{:S(2)}) collective-permute-start(bf16[2,2,2,48,1792]{4,3,2,1,0:T(8,128)(2,1)} %shard_map.89), channel_id=1, source_target_pairs={{0,8},{24,16},{1,9},{25,17},{2,10},{26,18},{3,11},{27,19},{4,12},{... | collective-permute-start | bytes 4128776 | tf_op jit(solution)/shard_map/ppermute | solution.py:265
  78.0 3.6 %slice-start.2 = ((s8[7340032]{0:T(1024)(128)(4,1)}), s8[4194304]{0:T(1024)(128)(4,1)S(1)}, s32[]{:S(2)}) async-start(s8[7340032]{0:T(1024)(128)(4,1)} %bitcast.65), calls=%async_computation.2 | async-start | bytes 8388608
  79.0 2.8 %slice-start.3 = ((s8[7340032]{0:T(1024)(128)(4,1)}), s8[3145728]{0:T(1024)(128)(4,1)S(1)}, s32[]{:S(2)}) async-start(s8[7340032]{0:T(1024)(128)(4,1)} %bitcast.65), calls=%async_computation.3 | async-start | bytes 6291456
  79.0 18.2 %collective-permute-start.27 = (bf16[2,2,48,1792]{3,2,1,0:T(8,128)(2,1)}, bf16[2,2,48,1792]{3,2,1,0:T(8,128)(2,1)}, u32[]{:S(2)}, u32[]{:S(2)}) collective-permute-start(bf16[2,2,48,1792]{3,2,1,0:T(8,128)(2,1)} %fusion.8), channel_id=1, source_target_pairs={{8,16},{16,8},{9,17},{17,9},{10,18},{18,10},{11,19},{19,11},{12,20... | collective-permute-start | bytes 2064392 | tf_op jit(solution)/shard_map/ppermute | solution.py:277
  80.6 7.8 %slice-start.6 = ((s8[7340032]{0:T(1024)(128)(4,1)}), s8[3145728]{0:T(1024)(128)(4,1)S(1)}, s32[]{:S(2)}) async-start(s8[7340032]{0:T(1024)(128)(4,1)} %bitcast.69), calls=%async_computation.6 | async-start | bytes 6291456
  81.8 6.6 %slice-start.7 = ((s8[7340032]{0:T(1024)(128)(4,1)}), s8[4194304]{0:T(1024)(128)(4,1)S(1)}, s32[]{:S(2)}) async-start(s8[7340032]{0:T(1024)(128)(4,1)} %bitcast.69), calls=%async_computation.7 | async-start | bytes 8388608
  106.8 30.1 %collective-permute-start.30 = (bf16[1,2,2,80,1792]{4,3,2,1,0:T(8,128)(2,1)S(1)}, bf16[1,2,2,80,1792]{4,3,2,1,0:T(8,128)(2,1)S(1)}, u32[]{:S(2)}, u32[]{:S(2)}) collective-permute-start(bf16[1,2,2,80,1792]{4,3,2,1,0:T(8,128)(2,1)S(1)} %shard_map.93), channel_id=1, source_target_pairs={{0,8},{24,16},{1,9},{25,17},{2,10},{26,18},{3,11},{27,19},{4,12},{... | collective-permute-start | bytes 3440648 | tf_op jit(solution)/shard_map/ppermute | solution.py:265
  112.7 6.1 %collective-permute-start.28 = (bf16[2,2,48,1792]{3,2,1,0:T(8,128)(2,1)S(1)}, bf16[2,2,48,1792]{3,2,1,0:T(8,128)(2,1)S(1)}, u32[]{:S(2)}, u32[]{:S(2)}) collective-permute-start(bf16[2,2,48,1792]{3,2,1,0:T(8,128)(2,1)S(1)} %fusion.9), channel_id=1, source_target_pairs={{8,16},{16,8},{9,17},{17,9},{10,18},{18,10},{11,19},{19,11},{12,20... | collective-permute-start | bytes 2064392 | tf_op jit(solution)/shard_map/ppermute | solution.py:287
  113.5 48.0 %collective-permute-start.32 = (bf16[1,2,2,80,1792]{4,3,2,1,0:T(8,128)(2,1)S(1)}, bf16[1,2,2,80,1792]{4,3,2,1,0:T(8,128)(2,1)S(1)}, u32[]{:S(2)}, u32[]{:S(2)}) collective-permute-start(bf16[1,2,2,80,1792]{4,3,2,1,0:T(8,128)(2,1)S(1)} %shard_map.94), channel_id=1, source_target_pairs={{0,8},{24,16},{1,9},{25,17},{2,10},{26,18},{3,11},{27,19},{4,12},{... | collective-permute-start | bytes 3440648 | tf_op jit(solution)/shard_map/ppermute | solution.py:265
  137.2 25.3 %collective-permute-start.34 = (bf16[2,2,80,1792]{3,2,1,0:T(8,128)(2,1)S(1)}, bf16[2,2,80,1792]{3,2,1,0:T(8,128)(2,1)S(1)}, u32[]{:S(2)}, u32[]{:S(2)}) collective-permute-start(bf16[2,2,80,1792]{3,2,1,0:T(8,128)(2,1)S(1)} %fusion.5), channel_id=1, source_target_pairs={{8,16},{16,8},{9,17},{17,9},{10,18},{18,10},{11,19},{19,11},{12,20... | collective-permute-start | bytes 3440648 | tf_op jit(solution)/shard_map/ppermute | solution.py:207
  139.4 24.7 %collective-permute-start.29 = (bf16[2,2,48,1792]{3,2,1,0:T(8,128)(2,1)S(1)}, bf16[2,2,48,1792]{3,2,1,0:T(8,128)(2,1)S(1)}, u32[]{:S(2)}, u32[]{:S(2)}) collective-permute-start(bf16[2,2,48,1792]{3,2,1,0:T(8,128)(2,1)S(1)} %fusion.2), channel_id=1, source_target_pairs={{16,24},{8,0},{17,25},{9,1},{18,26},{10,2},{19,27},{11,3},{20,28},... | collective-permute-start | bytes 2064392 | tf_op jit(solution)/shard_map/ppermute | solution.py:207
  140.7 43.4 %collective-permute-start.31 = (bf16[1,2,2,80,1792]{4,3,2,1,0:T(8,128)(2,1)S(1)}, bf16[1,2,2,80,1792]{4,3,2,1,0:T(8,128)(2,1)S(1)}, u32[]{:S(2)}, u32[]{:S(2)}) collective-permute-start(bf16[1,2,2,80,1792]{4,3,2,1,0:T(8,128)(2,1)S(1)} %shard_map.95), channel_id=1, source_target_pairs={{0,8},{24,16},{1,9},{25,17},{2,10},{26,18},{3,11},{27,19},{4,12},{... | collective-permute-start | bytes 3440648 | tf_op jit(solution)/shard_map/ppermute | solution.py:265
  161.8 22.4 %collective-permute-start.33 = (bf16[2,2,80,1792]{3,2,1,0:T(8,128)(2,1)S(1)}, bf16[2,2,80,1792]{3,2,1,0:T(8,128)(2,1)S(1)}, u32[]{:S(2)}, u32[]{:S(2)}) collective-permute-start(bf16[2,2,80,1792]{3,2,1,0:T(8,128)(2,1)S(1)} %fusion.4), channel_id=1, source_target_pairs={{8,16},{16,8},{9,17},{17,9},{10,18},{18,10},{11,19},{19,11},{12,20... | collective-permute-start | bytes 3440648 | tf_op jit(solution)/shard_map/ppermute | solution.py:207
  162.8 29.9 %collective-permute-start.35 = (bf16[2,2,80,1792]{3,2,1,0:T(8,128)(2,1)S(1)}, bf16[2,2,80,1792]{3,2,1,0:T(8,128)(2,1)S(1)}, u32[]{:S(2)}, u32[]{:S(2)}) collective-permute-start(bf16[2,2,80,1792]{3,2,1,0:T(8,128)(2,1)S(1)} %fusion), channel_id=1, source_target_pairs={{16,24},{8,0},{17,25},{9,1},{18,26},{10,2},{19,27},{11,3},{20,28},... | collective-permute-start | bytes 3440648 | tf_op jit(solution)/shard_map/ppermute | solution.py:207

commit v8 on v7

--- a/solution.py
+++ b/solution.py
@@ -65,6 +65,7 @@
 
 def sum_beside(x, axis, size, beside):
     done = []
+    steps = [x]
     mask = 1
     while mask < size:
         other = swap(x, axis, size, mask)
@@ -72,8 +73,9 @@
             done.append(beside(x))
             other = after(other, done[-1]) if done[-1] is not None else other
         x = add(x, other)
+        steps.append(x)
         mask *= 2
-    return x, done
+    return steps, done
 
 
 def assemble_kernel(segs, group, tab_ref, *refs):
@@ -137,7 +139,7 @@
         cost_estimate=pl.CostEstimate(
             flops=hint or 2 * rows * width * count * tile, bytes_accessed=2 * width * count * tile, transcendentals=0
         ),
-    )(x, weight)
+    )(x, pltpu.with_memory_space_constraint(weight, pltpu.HBM))
 
 
 def low_rank_kernel(first, each, start, widths, tab_ref, inner_ref, *refs):
@@ -251,11 +253,12 @@
         weight, begin, count = left.pop(0)
         return project(after(x, gate), weight, begin, count, tile)
 
-    shared, parts = sum_beside(mine.reshape(-1, mine.shape[2]), "tp", ntp, piece)
-    chips = gather_chips(after(tokens[rows:], shared), ntp)
-    inner, more = sum_beside(shared, "seq", nseq, piece)
+    steps, parts = sum_beside(mine.reshape(-1, mine.shape[2]), "tp", ntp, piece)
+    shared = steps[-1]
+    chips = gather_chips(after(tokens[rows:], steps[-2]), ntp)
+    sums, more = sum_beside(shared, "seq", nseq, piece)
     parts = [part for part in parts + more if part is not None]
-    inner = inner.reshape(mine.shape)
+    inner = sums[-1].reshape(mine.shape)
 
     def terms(parts, inner, start, rows, first, count, gate, hint=1 << 10):
         given = after(inner, gate) if gate is not None else inner
@@ -268,7 +271,8 @@
     pieces = gather_cores(list(after(tuple(chips), head)), ntp)
     (x,), mine = assemble(pieces, (later,), down_pool, down_table, AHEAD)
     head_hop = first_hop(head)
-    shared, _ = sum_beside(mine.reshape(-1, mine.shape[2]), "tp", ntp, lambda gate: None)
+    steps, _ = sum_beside(mine.reshape(-1, mine.shape[2]), "tp", ntp, lambda gate: None)
+    shared = steps[-1]
     rest = terms(parts, inner, 0, rows, 1, nseq - 2, shared)
     rest_hop = first_hop(rest)
     kept = terms(parts, inner, 0, rows, nseq - 1, 1, rest)

time: 195 us -> 192 us (0.985)
  Pallas kernels: 33.9 us -> 44.2 us
  waiting for transfers between devices: 87.6 us -> 81.4 us
  starting transfers between devices: 53.9 us -> 49.6 us
  local copies, waits for them, and re-layouts: 5.99 us -> 2.65 us
    pallas_call x6, Pallas kernels: 22.6 us -> 32.9 us  [project(): pl.pallas_call(project_kernel, out_shape=jax.ShapeDtypeStruct((rows, coun...]
    ppermute x22, waiting for transfers between devices: 23.6 us -> 16.9 us  [swap(): return lax.ppermute(x, axis, [(i, i ^ mask) for i in range(size)])]
    ppermute x5, starting transfers between devices: 25.1 us -> 20.2 us  [first_hop(): return lax.ppermute(send, 'seq', hop_pairs(0, nseq))]
    unnamed x24 -> x10, local copies, waits for them, and re-layouts: 4.95 us -> 1.61 us
    ppermute x5, waiting for transfers between devices: 55.4 us -> 58.2 us  [first_hop(): return lax.ppermute(send, 'seq', hop_pairs(0, nseq))]
    ppermute x4, waiting for transfers between devices: 8.62 us -> 6.28 us  [scatter_line(): arrived[level, step] = lax.ppermute(send, 'seq', hop_pairs(level, nseq))]
  transfers between devices with their start and end apart: 36 -> 36, of which waited for: 19 -> 16; matrix products, arithmetic and copies ran while one was open for 6% -> 6% of each run, Pallas kernels for 16% -> 22%
where the time goes in v8:
time: 192 us; the launch traced here: 191 us
  waiting for transfers between devices  81.4 us (42%)
  starting transfers between devices  49.6 us (26%)
  Pallas kernels  44.2 us (23%)
  other arithmetic  12.8 us (7%)
  local copies, waits for them, and re-layouts  2.65 us (1%)
    ppermute x5, waiting for transfers between devices, first_hop(): return lax.ppermute(send, 'seq', hop_pairs(0, nseq))  58.2 us
    pallas_call x6, Pallas kernels, project(): pl.pallas_call(project_kernel, out_shape=jax.ShapeDtypeStruct((rows, coun...  32.9 us
    ppermute x5, starting transfers between devices, first_hop(): return lax.ppermute(send, 'seq', hop_pairs(0, nseq))  20.2 us
    ppermute x22, starting transfers between devices, swap(): return lax.ppermute(x, axis, [(i, i ^ mask) for i in range(size)])  19.1 us
    ppermute x22, waiting for transfers between devices, swap(): return lax.ppermute(x, axis, [(i, i ^ mask) for i in range(size)])  16.9 us
    pallas_call x7, Pallas kernels, add_low_rank(): pl.pallas_call(functools.partial(low_rank_kernel, first, each, start, wid...  8.26 us
    ppermute x4, waiting for transfers between devices, scatter_line(): arrived[level, step] = lax.ppermute(send, 'seq', hop_pairs(level, nseq))  6.28 us
    convert_element_type x14, other arithmetic, add(): return (x.astype(jnp.float32) + y.astype(jnp.float32)).astype(x.dtype)  5.63 us
  transfers between devices with their start and end apart: 36, of which 16 were waited for; matrix products, arithmetic and copies ran while one was open for 6% of the time, Pallas kernels for 22%

profile of v8, /device:TPU:0, one launch (start us, length us, event | category | flops | bytes accessed | tf_op | source)
XLA Modules:
  0.0 191.1 jit_solution(16339327693303753832)
XLA Ops:
  0.9 3.0 %collective-permute-start.1 = (bf16[48,2048]{1,0:T(8,128)(2,1)S(1)}, bf16[48,2048]{1,0:T(8,128)(2,1)S(1)}, u32[]{:S(2)}, u32[]{:S(2)}) collective-permute-start(bf16[48,2048]{1,0:T(8,128)(2,1)S(1)} %slice.30.refs_0_), channel_id=1, source_target_pairs={{0,2},{1,3},{2,0},{3,1},{4,6},{5,7},{6,4},{7,5},{8,10},{9,11},{10,... | collective-permute-start | bytes 589832 | tf_op jit(solution)/shard_map/ppermute | solution.py:44
  3.9 1.5 collective-permute-start.3
  8.2 1.5 collective-permute-done.1.refs_2_
  9.7 4.8 %collective-permute-done.3.refs_4_ = bf16[48,2048]{1,0:T(8,128)(2,1)S(1)} collective-permute-done((bf16[48,2048]{1,0:T(8,128)(2,1)S(1)}, bf16[48,2048]{1,0:T(8,128)(2,1)S(1)}, u32[]{:S(2)}, u32[]{:S(2)}) %collective-permute-start.3) | collective-permute-done | bytes 196640 | tf_op jit(solution)/shard_map/ppermute | solution.py:44
  16.2 1.6 copy-done
  17.8 1.4 shard_map.82
  20.6 1.0 collective-permute-start.8
  21.6 3.6 %shard_map.83.refs_0_ = bf16[384,768]{1,0:T(8,128)(2,1)S(1)} custom-call(bf16[384,2048]{1,0:T(8,128)(2,1)S(1)} %bitcast.65, bf16[2048,1792]{1,0:T(8,128)(2,1)} %weight_ref.10), custom_call_target="tpu_custom_call" | custom-call | flops 1207959552 | bytes 3145728 | tf_op jit(solution)/shard_map/pallas_call | solution.py:129
  25.3 1.2 collective-permute-start.9
  26.4 1.5 collective-permute-start.12
  28.4 1.5 collective-permute-start.14
  29.9 4.3 %shard_map.84.refs_1_ = bf16[384,1024]{1,0:T(8,128)(2,1)S(1)} custom-call(bf16[384,2048]{1,0:T(8,128)(2,1)S(1)} %bitcast.66, bf16[2048,1792]{1,0:T(8,128)(2,1)} %weight_ref.10), custom_call_target="tpu_custom_call" | custom-call | flops 1610612736 | bytes 4194304 | tf_op jit(solution)/shard_map/pallas_call | solution.py:129
  34.3 1.6 collective-permute-start.10
  35.9 3.8 %shard_map.85.refs_2_ = bf16[384,768]{1,0:T(8,128)(2,1)S(1)} custom-call(bf16[384,2048]{1,0:T(8,128)(2,1)S(1)} %bitcast.67, bf16[2048,1792]{1,0:T(8,128)(2,1)} %weight_ref.11), custom_call_target="tpu_custom_call" | custom-call | flops 1207959552 | bytes 3145728 | tf_op jit(solution)/shard_map/pallas_call | solution.py:129
  39.8 2.7 %collective-permute-start.11 = (bf16[192,128]{1,0:T(8,128)(2,1)S(1)}, bf16[192,128]{1,0:T(8,128)(2,1)S(1)}, u32[]{:S(2)}, u32[]{:S(2)}) collective-permute-start(bf16[192,128]{1,0:T(8,128)(2,1)S(1)} %add_convert_fusion.9), channel_id=1, source_target_pairs={{0,16},{8,24},{16,0},{24,8},{1,17},{9,25},{17,1},{25,9},{2,18},{10... | collective-permute-start | bytes 147464 | tf_op jit(solution)/shard_map/ppermute | solution.py:44
  42.4 4.3 %shard_map.86.refs_3_ = bf16[384,1024]{1,0:T(8,128)(2,1)S(1)} custom-call(bf16[384,2048]{1,0:T(8,128)(2,1)S(1)} %bitcast.68, bf16[2048,1792]{1,0:T(8,128)(2,1)} %weight_ref.11), custom_call_target="tpu_custom_call" | custom-call | flops 1610612736 | bytes 4194304 | tf_op jit(solution)/shard_map/pallas_call | solution.py:129
  50.9 1.6 shard_map.88
  52.8 2.4 %collective-permute-start.26 = (bf16[1,2,2,48,1792]{4,3,2,1,0:T(8,128)(2,1)S(1)}, bf16[1,2,2,48,1792]{4,3,2,1,0:T(8,128)(2,1)S(1)}, u32[]{:S(2)}, u32[]{:S(2)}) collective-permute-start(bf16[1,2,2,48,1792]{4,3,2,1,0:T(8,128)(2,1)S(1)} %shard_map.87), channel_id=1, source_target_pairs={{0,8},{24,16},{1,9},{25,17},{2,10},{26,18},{3,11},{27,19},{4,12},{... | collective-permute-start | bytes 2064392 | tf_op jit(solution)/shard_map/ppermute | solution.py:268
  55.2 1.6 collective-permute-start.20
  56.8 3.0 %collective-permute-done.20 = bf16[320,128]{1,0:T(8,128)(2,1)S(1)} collective-permute-done((bf16[320,128]{1,0:T(8,128)(2,1)S(1)}, bf16[320,128]{1,0:T(8,128)(2,1)S(1)}, u32[]{:S(2)}, u32[]{:S(2)}) %collective-permute-start.20) | collective-permute-done | bytes 81952 | tf_op jit(solution)/shard_map/ppermute | solution.py:44
  59.8 1.0 collective-permute-start.21
  60.8 3.5 %collective-permute-done.21 = bf16[320,128]{1,0:T(8,128)(2,1)S(1)} collective-permute-done((bf16[320,128]{1,0:T(8,128)(2,1)S(1)}, bf16[320,128]{1,0:T(8,128)(2,1)S(1)}, u32[]{:S(2)}, u32[]{:S(2)}) %collective-permute-start.21) | collective-permute-done | bytes 81952 | tf_op jit(solution)/shard_map/ppermute | solution.py:44
  64.9 2.2 %collective-permute-start.24 = (bf16[320,128]{1,0:T(8,128)(2,1)}, bf16[320,128]{1,0:T(8,128)(2,1)}, u32[]{:S(2)}, u32[]{:S(2)}) collective-permute-start(bf16[320,128]{1,0:T(8,128)(2,1)} %add_convert_fusion.5), channel_id=1, source_target_pairs={{0,16},{8,24},{16,0},{24,8},{1,17},{9,25},{17,1},{25,9},{2,18},{10... | collective-permute-start | bytes 245768 | tf_op jit(solution)/shard_map/ppermute | solution.py:59
  67.1 1.6 collective-permute-start.25
  68.8 2.2 %shard_map.89 = bf16[2,2,2,48,1792]{4,3,2,1,0:T(8,128)(2,1)} custom-call(s32[3,8]{1,0:T(4,128)S(1)} %pad_add_fusion.tab_ref, bf16[4,48,128]{2,1,0:T(8,128)(2,1)S(1)} %bitcast.74, bf16[384,768]{1,0:T(8,128)(2,1)S(1)} %shard_map.83.refs_0_, bf16[384,1024]{1,0:T(8,128)(2,1)S(1)} %shard_map.84.refs_1_, bf16[384,768]{1,0:T(8,128)(2,1)S(1)} %shard_map.85.refs_2_, ...), custom_call_target="tpu_custom_call" | custom-call | flops 1024 | bytes 1024 | tf_op jit(solution)/shard_map/pallas_call | solution.py:175
  71.0 3.6 %collective-permute-start.22 = (bf16[2,2,2,48,1792]{4,3,2,1,0:T(8,128)(2,1)}, bf16[2,2,2,48,1792]{4,3,2,1,0:T(8,128)(2,1)}, u32[]{:S(2)}, u32[]{:S(2)}) collective-permute-start(bf16[2,2,2,48,1792]{4,3,2,1,0:T(8,128)(2,1)} %shard_map.89), channel_id=1, source_target_pairs={{0,8},{24,16},{1,9},{25,17},{2,10},{26,18},{3,11},{27,19},{4,12},{... | collective-permute-start | bytes 4128776 | tf_op jit(solution)/shard_map/ppermute | solution.py:268
  74.6 1.0 fusion.8
  75.6 1.5 collective-permute-start.27
  78.1 8.4 %shard_map.91.refs_0_ = bf16[640,1792]{1,0:T(8,128)(2,1)S(1)} custom-call(bf16[640,2048]{1,0:T(8,128)(2,1)S(1)} %bitcast.78, bf16[2048,1792]{1,0:T(8,128)(2,1)} %weight_ref.10), custom_call_target="tpu_custom_call" | custom-call | flops 68719476736 | bytes 7340032 | tf_op jit(solution)/shard_map/pallas_call | solution.py:129
  86.5 8.4 %shard_map.92.refs_1_ = bf16[640,1792]{1,0:T(8,128)(2,1)S(1)} custom-call(bf16[640,2048]{1,0:T(8,128)(2,1)S(1)} %bitcast.79, bf16[2048,1792]{1,0:T(8,128)(2,1)} %weight_ref.11), custom_call_target="tpu_custom_call" | custom-call | flops 68719476736 | bytes 7340032 | tf_op jit(solution)/shard_map/pallas_call | solution.py:129
  94.9 1.1 add_convert_fusion.4
  96.0 1.0 shard_map.93
  97.0 1.0 shard_map.94
  98.1 1.0 shard_map.95
  99.1 1.0 shard_map.96
  100.1 5.1 %collective-permute-done.22 = bf16[2,2,2,48,1792]{4,3,2,1,0:T(8,128)(2,1)} collective-permute-done((bf16[2,2,2,48,1792]{4,3,2,1,0:T(8,128)(2,1)}, bf16[2,2,2,48,1792]{4,3,2,1,0:T(8,128)(2,1)}, u32[]{:S(2)}, u32[]{:S(2)}) %collective-permute-start.22) | collective-permute-done | bytes 1376288 | tf_op jit(solution)/shard_map/ppermute | solution.py:268
  105.2 4.4 %collective-permute-start.30 = (bf16[1,2,2,80,1792]{4,3,2,1,0:T(8,128)(2,1)S(1)}, bf16[1,2,2,80,1792]{4,3,2,1,0:T(8,128)(2,1)S(1)}, u32[]{:S(2)}, u32[]{:S(2)}) collective-permute-start(bf16[1,2,2,80,1792]{4,3,2,1,0:T(8,128)(2,1)S(1)} %shard_map.93), channel_id=1, source_target_pairs={{0,8},{24,16},{1,9},{25,17},{2,10},{26,18},{3,11},{27,19},{4,12},{... | collective-permute-start | bytes 3440648 | tf_op jit(solution)/shard_map/ppermute | solution.py:268
  109.7 1.5 fusion.9
  111.8 3.3 %collective-permute-start.32 = (bf16[1,2,2,80,1792]{4,3,2,1,0:T(8,128)(2,1)S(1)}, bf16[1,2,2,80,1792]{4,3,2,1,0:T(8,128)(2,1)S(1)}, u32[]{:S(2)}, u32[]{:S(2)}) collective-permute-start(bf16[1,2,2,80,1792]{4,3,2,1,0:T(8,128)(2,1)S(1)} %shard_map.94), channel_id=1, source_target_pairs={{0,8},{24,16},{1,9},{25,17},{2,10},{26,18},{3,11},{27,19},{4,12},{... | collective-permute-start | bytes 3440648 | tf_op jit(solution)/shard_map/ppermute | solution.py:268
  115.1 20.1 %collective-permute-done.30 = bf16[1,2,2,80,1792]{4,3,2,1,0:T(8,128)(2,1)S(1)} collective-permute-done((bf16[1,2,2,80,1792]{4,3,2,1,0:T(8,128)(2,1)S(1)}, bf16[1,2,2,80,1792]{4,3,2,1,0:T(8,128)(2,1)S(1)}, u32[]{:S(2)}, u32[]{:S(2)}) %collective-permute-start.30) | collective-permute-done | bytes 1146912 | tf_op jit(solution)/shard_map/ppermute | solution.py:268
  136.5 1.5 fusion.2
  138.0 1.3 collective-permute-start.29
  139.3 6.5 %collective-permute-start.31 = (bf16[1,2,2,80,1792]{4,3,2,1,0:T(8,128)(2,1)S(1)}, bf16[1,2,2,80,1792]{4,3,2,1,0:T(8,128)(2,1)S(1)}, u32[]{:S(2)}, u32[]{:S(2)}) collective-permute-start(bf16[1,2,2,80,1792]{4,3,2,1,0:T(8,128)(2,1)S(1)} %shard_map.95), channel_id=1, source_target_pairs={{0,8},{24,16},{1,9},{25,17},{2,10},{26,18},{3,11},{27,19},{4,12},{... | collective-permute-start | bytes 3440648 | tf_op jit(solution)/shard_map/ppermute | solution.py:268
  145.7 14.1 %collective-permute-done.32 = bf16[1,2,2,80,1792]{4,3,2,1,0:T(8,128)(2,1)S(1)} collective-permute-done((bf16[1,2,2,80,1792]{4,3,2,1,0:T(8,128)(2,1)S(1)}, bf16[1,2,2,80,1792]{4,3,2,1,0:T(8,128)(2,1)S(1)}, u32[]{:S(2)}, u32[]{:S(2)}) %collective-permute-start.32) | collective-permute-done | bytes 1146912 | tf_op jit(solution)/shard_map/ppermute | solution.py:268
  161.2 1.3 collective-permute-start.35
  162.5 1.4 fusion.3
  164.1 18.8 %collective-permute-done.31 = bf16[1,2,2,80,1792]{4,3,2,1,0:T(8,128)(2,1)S(1)} collective-permute-done((bf16[1,2,2,80,1792]{4,3,2,1,0:T(8,128)(2,1)S(1)}, bf16[1,2,2,80,1792]{4,3,2,1,0:T(8,128)(2,1)S(1)}, u32[]{:S(2)}, u32[]{:S(2)}) %collective-permute-start.31) | collective-permute-done | bytes 1146912 | tf_op jit(solution)/shard_map/ppermute | solution.py:268
  183.0 6.3 %collective-permute-done.35 = bf16[2,2,80,1792]{3,2,1,0:T(8,128)(2,1)S(1)} collective-permute-done((bf16[2,2,80,1792]{3,2,1,0:T(8,128)(2,1)S(1)}, bf16[2,2,80,1792]{3,2,1,0:T(8,128)(2,1)S(1)}, u32[]{:S(2)}, u32[]{:S(2)}) %collective-permute-start.35) | collective-permute-done | bytes 1146912 | tf_op jit(solution)/shard_map/ppermute | solution.py:209
  (86 shorter events, 18.5 us)
Async XLA Ops:
  0.9 8.7 %collective-permute-start.1 = (bf16[48,2048]{1,0:T(8,128)(2,1)S(1)}, bf16[48,2048]{1,0:T(8,128)(2,1)S(1)}, u32[]{:S(2)}, u32[]{:S(2)}) collective-permute-start(bf16[48,2048]{1,0:T(8,128)(2,1)S(1)} %slice.30.refs_0_), channel_id=1, source_target_pairs={{0,2},{1,3},{2,0},{3,1},{4,6},{5,7},{6,4},{7,5},{8,10},{9,11},{10,... | collective-permute-start | bytes 589832 | tf_op jit(solution)/shard_map/ppermute | solution.py:44
  3.9 10.6 %collective-permute-start.3 = (bf16[48,2048]{1,0:T(8,128)(2,1)S(1)}, bf16[48,2048]{1,0:T(8,128)(2,1)S(1)}, u32[]{:S(2)}, u32[]{:S(2)}) collective-permute-start(bf16[48,2048]{1,0:T(8,128)(2,1)S(1)} %slice.30.refs_0_), channel_id=1, source_target_pairs={{0,4},{1,5},{2,6},{3,7},{4,0},{5,1},{6,2},{7,3},{8,12},{9,13},{10,... | collective-permute-start | bytes 589832 | tf_op jit(solution)/shard_map/ppermute | solution.py:44
  5.5 9.1 %collective-permute-start.5 = (bf16[48,2048]{1,0:T(8,128)(2,1)S(1)}, bf16[48,2048]{1,0:T(8,128)(2,1)S(1)}, u32[]{:S(2)}, u32[]{:S(2)}) collective-permute-start(bf16[48,2048]{1,0:T(8,128)(2,1)S(1)} %slice.30.refs_0_), channel_id=1, source_target_pairs={{0,6},{1,7},{2,4},{3,5},{4,2},{5,3},{6,0},{7,1},{8,14},{9,15},{10,... | collective-permute-start | bytes 589832 | tf_op jit(solution)/shard_map/ppermute | solution.py:44
  5.5 9.6 %collective-permute-start = (bf16[48,2048]{1,0:T(8,128)(2,1)S(1)}, bf16[48,2048]{1,0:T(8,128)(2,1)S(1)}, u32[]{:S(2)}, u32[]{:S(2)}) collective-permute-start(bf16[48,2048]{1,0:T(8,128)(2,1)S(1)} %slice.30.refs_0_), channel_id=1, source_target_pairs={{0,1},{1,0},{2,3},{3,2},{4,5},{5,4},{6,7},{7,6},{8,9},{9,8},{10,11... | collective-permute-start | bytes 589832 | tf_op jit(solution)/shard_map/ppermute | solution.py:44
  9.7 5.4 %collective-permute-start.2 = (bf16[48,2048]{1,0:T(8,128)(2,1)S(1)}, bf16[48,2048]{1,0:T(8,128)(2,1)S(1)}, u32[]{:S(2)}, u32[]{:S(2)}) collective-permute-start(bf16[48,2048]{1,0:T(8,128)(2,1)S(1)} %collective-permute-done.1.refs_2_), channel_id=1, source_target_pairs={{0,1},{1,0},{2,3},{3,2},{4,5},{5,4},{6,7},{7,6},{8,9},{9,8},{10,11... | collective-permute-start | bytes 589832 | tf_op jit(solution)/shard_map/ppermute | solution.py:44
  14.5 1.4 collective-permute-start.4
  14.5 1.7 collective-permute-start.6
  16.2 1.6 copy-start
  17.8 1.7 copy-start.2
  19.3 1.3 collective-permute-start.7
  20.6 4.7 %collective-permute-start.8 = (bf16[192,128]{1,0:T(8,128)(2,1)S(1)}, bf16[192,128]{1,0:T(8,128)(2,1)S(1)}, u32[]{:S(2)}, u32[]{:S(2)}) collective-permute-start(bf16[192,128]{1,0:T(8,128)(2,1)S(1)} %add_convert_fusion.12), channel_id=1, source_target_pairs={{0,2},{1,3},{2,0},{3,1},{4,6},{5,7},{6,4},{7,5},{8,10},{9,11},{10,... | collective-permute-start | bytes 147464 | tf_op jit(solution)/shard_map/ppermute | solution.py:44
  25.3 9.0 %collective-permute-start.9 = (bf16[192,128]{1,0:T(8,128)(2,1)S(1)}, bf16[192,128]{1,0:T(8,128)(2,1)S(1)}, u32[]{:S(2)}, u32[]{:S(2)}) collective-permute-start(bf16[192,128]{1,0:T(8,128)(2,1)S(1)} %add_convert_fusion.11), channel_id=1, source_target_pairs={{0,4},{1,5},{2,6},{3,7},{4,0},{5,1},{6,2},{7,3},{8,12},{9,13},{10,... | collective-permute-start | bytes 147464 | tf_op jit(solution)/shard_map/ppermute | solution.py:44
  26.4 21.4 %collective-permute-start.12 = (bf16[80,2048]{1,0:T(8,128)(2,1)S(1)}, bf16[80,2048]{1,0:T(8,128)(2,1)S(1)}, u32[]{:S(2)}, u32[]{:S(2)}) collective-permute-start(bf16[80,2048]{1,0:T(8,128)(2,1)S(1)} %slice.31.refs_0_), channel_id=1, source_target_pairs={{0,2},{1,3},{2,0},{3,1},{4,6},{5,7},{6,4},{7,5},{8,10},{9,11},{10,... | collective-permute-start | bytes 983048 | tf_op jit(solution)/shard_map/ppermute | solution.py:44
  27.9 19.9 %collective-permute-start.13 = (bf16[80,2048]{1,0:T(8,128)(2,1)S(1)}, bf16[80,2048]{1,0:T(8,128)(2,1)S(1)}, u32[]{:S(2)}, u32[]{:S(2)}) collective-permute-start(bf16[80,2048]{1,0:T(8,128)(2,1)S(1)} %slice.31.refs_0_), channel_id=1, source_target_pairs={{0,4},{1,5},{2,6},{3,7},{4,0},{5,1},{6,2},{7,3},{8,12},{9,13},{10,... | collective-permute-start | bytes 983048 | tf_op jit(solution)/shard_map/ppermute | solution.py:44
  28.4 19.4 %collective-permute-start.14 = (bf16[80,2048]{1,0:T(8,128)(2,1)S(1)}, bf16[80,2048]{1,0:T(8,128)(2,1)S(1)}, u32[]{:S(2)}, u32[]{:S(2)}) collective-permute-start(bf16[80,2048]{1,0:T(8,128)(2,1)S(1)} %slice.31.refs_0_), channel_id=1, source_target_pairs={{0,6},{1,7},{2,4},{3,5},{4,2},{5,3},{6,0},{7,1},{8,14},{9,15},{10,... | collective-permute-start | bytes 983048 | tf_op jit(solution)/shard_map/ppermute | solution.py:44
  34.3 5.4 %collective-permute-start.10 = (bf16[192,128]{1,0:T(8,128)(2,1)S(1)}, bf16[192,128]{1,0:T(8,128)(2,1)S(1)}, u32[]{:S(2)}, u32[]{:S(2)}) collective-permute-start(bf16[192,128]{1,0:T(8,128)(2,1)S(1)} %add_convert_fusion.10), channel_id=1, source_target_pairs={{0,8},{8,0},{16,24},{24,16},{1,9},{9,1},{17,25},{25,17},{2,10},{10... | collective-permute-start | bytes 147464 | tf_op jit(solution)/shard_map/ppermute | solution.py:44
  35.9 10.9 %slice-start = ((s8[7340032]{0:T(1024)(128)(4,1)}), s8[4194304]{0:T(1024)(128)(4,1)S(1)}, s32[]{:S(2)}) async-start(s8[7340032]{0:T(1024)(128)(4,1)} %bitcast.63), calls=%async_computation | async-start | bytes 8388608
  39.8 7.1 %slice-start.1 = ((s8[7340032]{0:T(1024)(128)(4,1)}), s8[3145728]{0:T(1024)(128)(4,1)S(1)}, s32[]{:S(2)}) async-start(s8[7340032]{0:T(1024)(128)(4,1)} %bitcast.63), calls=%async_computation.1 | async-start | bytes 6291456
  39.8 7.0 %collective-permute-start.11 = (bf16[192,128]{1,0:T(8,128)(2,1)S(1)}, bf16[192,128]{1,0:T(8,128)(2,1)S(1)}, u32[]{:S(2)}, u32[]{:S(2)}) collective-permute-start(bf16[192,128]{1,0:T(8,128)(2,1)S(1)} %add_convert_fusion.9), channel_id=1, source_target_pairs={{0,16},{8,24},{16,0},{24,8},{1,17},{9,25},{17,1},{25,9},{2,18},{10... | collective-permute-start | bytes 147464 | tf_op jit(solution)/shard_map/ppermute | solution.py:44
  46.8 4.1 %copy-start.1 = (bf16[8,64,2048]{2,1,0:T(8,128)(2,1)S(1)}, bf16[8,64,2048]{2,1,0:T(8,128)(2,1)}, u32[]{:S(2)}) copy-start(bf16[8,64,2048]{2,1,0:T(8,128)(2,1)} %refs_8_.3) | copy-start | bytes 6291460
  47.8 1.7 collective-permute-start.15
  47.9 2.1 %collective-permute-start.16 = (bf16[80,2048]{1,0:T(8,128)(2,1)S(1)}, bf16[80,2048]{1,0:T(8,128)(2,1)S(1)}, u32[]{:S(2)}, u32[]{:S(2)}) collective-permute-start(bf16[80,2048]{1,0:T(8,128)(2,1)S(1)} %collective-permute-done.12.refs_2_), channel_id=1, source_target_pairs={{0,1},{1,0},{2,3},{3,2},{4,5},{5,4},{6,7},{7,6},{8,9},{9,8},{10,11... | collective-permute-start | bytes 983048 | tf_op jit(solution)/shard_map/ppermute | solution.py:44
  48.4 2.1 %collective-permute-start.17 = (bf16[80,2048]{1,0:T(8,128)(2,1)S(1)}, bf16[80,2048]{1,0:T(8,128)(2,1)S(1)}, u32[]{:S(2)}, u32[]{:S(2)}) collective-permute-start(bf16[80,2048]{1,0:T(8,128)(2,1)S(1)} %collective-permute-done.13.refs_4_), channel_id=1, source_target_pairs={{0,1},{1,0},{2,3},{3,2},{4,5},{5,4},{6,7},{7,6},{8,9},{9,8},{10,11... | collective-permute-start | bytes 983048 | tf_op jit(solution)/shard_map/ppermute | solution.py:44
  48.5 2.4 %collective-permute-start.18 = (bf16[80,2048]{1,0:T(8,128)(2,1)S(1)}, bf16[80,2048]{1,0:T(8,128)(2,1)S(1)}, u32[]{:S(2)}, u32[]{:S(2)}) collective-permute-start(bf16[80,2048]{1,0:T(8,128)(2,1)S(1)} %collective-permute-done.14.refs_6_), channel_id=1, source_target_pairs={{0,1},{1,0},{2,3},{3,2},{4,5},{5,4},{6,7},{7,6},{8,9},{9,8},{10,11... | collective-permute-start | bytes 983048 | tf_op jit(solution)/shard_map/ppermute | solution.py:44
  52.6 2.6 %collective-permute-start.19 = (bf16[320,128]{1,0:T(8,128)(2,1)S(1)}, bf16[320,128]{1,0:T(8,128)(2,1)S(1)}, u32[]{:S(2)}, u32[]{:S(2)}) collective-permute-start(bf16[320,128]{1,0:T(8,128)(2,1)S(1)} %bitcast.76), channel_id=1, source_target_pairs={{0,1},{1,0},{2,3},{3,2},{4,5},{5,4},{6,7},{7,6},{8,9},{9,8},{10,11... | collective-permute-start | bytes 245768 | tf_op jit(solution)/shard_map/ppermute | solution.py:44
  52.8 21.8 %collective-permute-start.26 = (bf16[1,2,2,48,1792]{4,3,2,1,0:T(8,128)(2,1)S(1)}, bf16[1,2,2,48,1792]{4,3,2,1,0:T(8,128)(2,1)S(1)}, u32[]{:S(2)}, u32[]{:S(2)}) collective-permute-start(bf16[1,2,2,48,1792]{4,3,2,1,0:T(8,128)(2,1)S(1)} %shard_map.87), channel_id=1, source_target_pairs={{0,8},{24,16},{1,9},{25,17},{2,10},{26,18},{3,11},{27,19},{4,12},{... | collective-permute-start | bytes 2064392 | tf_op jit(solution)/shard_map/ppermute | solution.py:268
  55.2 4.5 %collective-permute-start.20 = (bf16[320,128]{1,0:T(8,128)(2,1)S(1)}, bf16[320,128]{1,0:T(8,128)(2,1)S(1)}, u32[]{:S(2)}, u32[]{:S(2)}) collective-permute-start(bf16[320,128]{1,0:T(8,128)(2,1)S(1)} %add_convert_fusion.7), channel_id=1, source_target_pairs={{0,2},{1,3},{2,0},{3,1},{4,6},{5,7},{6,4},{7,5},{8,10},{9,11},{10,... | collective-permute-start | bytes 245768 | tf_op jit(solution)/shard_map/ppermute | solution.py:44
  59.8 4.5 %collective-permute-start.21 = (bf16[320,128]{1,0:T(8,128)(2,1)S(1)}, bf16[320,128]{1,0:T(8,128)(2,1)S(1)}, u32[]{:S(2)}, u32[]{:S(2)}) collective-permute-start(bf16[320,128]{1,0:T(8,128)(2,1)S(1)} %add_convert_fusion.6), channel_id=1, source_target_pairs={{0,4},{1,5},{2,6},{3,7},{4,0},{5,1},{6,2},{7,3},{8,12},{9,13},{10,... | collective-permute-start | bytes 245768 | tf_op jit(solution)/shard_map/ppermute | solution.py:44
  64.9 30.0 %collective-permute-start.23 = (bf16[320,128]{1,0:T(8,128)(2,1)}, bf16[320,128]{1,0:T(8,128)(2,1)}, u32[]{:S(2)}, u32[]{:S(2)}) collective-permute-start(bf16[320,128]{1,0:T(8,128)(2,1)} %add_convert_fusion.5), channel_id=1, source_target_pairs={{0,8},{8,16},{16,24},{24,0},{1,9},{9,17},{17,25},{25,1},{2,10},{10... | collective-permute-start | bytes 245768 | tf_op jit(solution)/shard_map/ppermute | solution.py:59
  64.9 30.0 %collective-permute-start.24 = (bf16[320,128]{1,0:T(8,128)(2,1)}, bf16[320,128]{1,0:T(8,128)(2,1)}, u32[]{:S(2)}, u32[]{:S(2)}) collective-permute-start(bf16[320,128]{1,0:T(8,128)(2,1)} %add_convert_fusion.5), channel_id=1, source_target_pairs={{0,16},{8,24},{16,0},{24,8},{1,17},{9,25},{17,1},{25,9},{2,18},{10... | collective-permute-start | bytes 245768 | tf_op jit(solution)/shard_map/ppermute | solution.py:59
  67.1 27.8 %collective-permute-start.25 = (bf16[320,128]{1,0:T(8,128)(2,1)}, bf16[320,128]{1,0:T(8,128)(2,1)}, u32[]{:S(2)}, u32[]{:S(2)}) collective-permute-start(bf16[320,128]{1,0:T(8,128)(2,1)} %add_convert_fusion.5), channel_id=1, source_target_pairs={{0,24},{8,0},{16,8},{24,16},{1,25},{9,1},{17,9},{25,17},{2,26},{10... | collective-permute-start | bytes 245768 | tf_op jit(solution)/shard_map/ppermute | solution.py:59
  71.0 34.2 %collective-permute-start.22 = (bf16[2,2,2,48,1792]{4,3,2,1,0:T(8,128)(2,1)}, bf16[2,2,2,48,1792]{4,3,2,1,0:T(8,128)(2,1)}, u32[]{:S(2)}, u32[]{:S(2)}) collective-permute-start(bf16[2,2,2,48,1792]{4,3,2,1,0:T(8,128)(2,1)} %shard_map.89), channel_id=1, source_target_pairs={{0,8},{24,16},{1,9},{25,17},{2,10},{26,18},{3,11},{27,19},{4,12},{... | collective-permute-start | bytes 4128776 | tf_op jit(solution)/shard_map/ppermute | solution.py:268
  75.6 21.4 %collective-permute-start.27 = (bf16[2,2,48,1792]{3,2,1,0:T(8,128)(2,1)}, bf16[2,2,48,1792]{3,2,1,0:T(8,128)(2,1)}, u32[]{:S(2)}, u32[]{:S(2)}) collective-permute-start(bf16[2,2,48,1792]{3,2,1,0:T(8,128)(2,1)} %fusion.8), channel_id=1, source_target_pairs={{8,16},{16,8},{9,17},{17,9},{10,18},{18,10},{11,19},{19,11},{12,20... | collective-permute-start | bytes 2064392 | tf_op jit(solution)/shard_map/ppermute | solution.py:281
  105.2 30.1 %collective-permute-start.30 = (bf16[1,2,2,80,1792]{4,3,2,1,0:T(8,128)(2,1)S(1)}, bf16[1,2,2,80,1792]{4,3,2,1,0:T(8,128)(2,1)S(1)}, u32[]{:S(2)}, u32[]{:S(2)}) collective-permute-start(bf16[1,2,2,80,1792]{4,3,2,1,0:T(8,128)(2,1)S(1)} %shard_map.93), channel_id=1, source_target_pairs={{0,8},{24,16},{1,9},{25,17},{2,10},{26,18},{3,11},{27,19},{4,12},{... | collective-permute-start | bytes 3440648 | tf_op jit(solution)/shard_map/ppermute | solution.py:268
  111.1 4.0 %collective-permute-start.28 = (bf16[2,2,48,1792]{3,2,1,0:T(8,128)(2,1)S(1)}, bf16[2,2,48,1792]{3,2,1,0:T(8,128)(2,1)S(1)}, u32[]{:S(2)}, u32[]{:S(2)}) collective-permute-start(bf16[2,2,48,1792]{3,2,1,0:T(8,128)(2,1)S(1)} %fusion.9), channel_id=1, source_target_pairs={{8,16},{16,8},{9,17},{17,9},{10,18},{18,10},{11,19},{19,11},{12,20... | collective-permute-start | bytes 2064392 | tf_op jit(solution)/shard_map/ppermute | solution.py:291
  111.8 48.0 %collective-permute-start.32 = (bf16[1,2,2,80,1792]{4,3,2,1,0:T(8,128)(2,1)S(1)}, bf16[1,2,2,80,1792]{4,3,2,1,0:T(8,128)(2,1)S(1)}, u32[]{:S(2)}, u32[]{:S(2)}) collective-permute-start(bf16[1,2,2,80,1792]{4,3,2,1,0:T(8,128)(2,1)S(1)} %shard_map.94), channel_id=1, source_target_pairs={{0,8},{24,16},{1,9},{25,17},{2,10},{26,18},{3,11},{27,19},{4,12},{... | collective-permute-start | bytes 3440648 | tf_op jit(solution)/shard_map/ppermute | solution.py:268
  135.6 25.3 %collective-permute-start.34 = (bf16[2,2,80,1792]{3,2,1,0:T(8,128)(2,1)S(1)}, bf16[2,2,80,1792]{3,2,1,0:T(8,128)(2,1)S(1)}, u32[]{:S(2)}, u32[]{:S(2)}) collective-permute-start(bf16[2,2,80,1792]{3,2,1,0:T(8,128)(2,1)S(1)} %fusion.5), channel_id=1, source_target_pairs={{8,16},{16,8},{9,17},{17,9},{10,18},{18,10},{11,19},{19,11},{12,20... | collective-permute-start | bytes 3440648 | tf_op jit(solution)/shard_map/ppermute | solution.py:209
  138.0 24.5 %collective-permute-start.29 = (bf16[2,2,48,1792]{3,2,1,0:T(8,128)(2,1)S(1)}, bf16[2,2,48,1792]{3,2,1,0:T(8,128)(2,1)S(1)}, u32[]{:S(2)}, u32[]{:S(2)}) collective-permute-start(bf16[2,2,48,1792]{3,2,1,0:T(8,128)(2,1)S(1)} %fusion.2), channel_id=1, source_target_pairs={{16,24},{8,0},{17,25},{9,1},{18,26},{10,2},{19,27},{11,3},{20,28},... | collective-permute-start | bytes 2064392 | tf_op jit(solution)/shard_map/ppermute | solution.py:209
  139.3 43.7 %collective-permute-start.31 = (bf16[1,2,2,80,1792]{4,3,2,1,0:T(8,128)(2,1)S(1)}, bf16[1,2,2,80,1792]{4,3,2,1,0:T(8,128)(2,1)S(1)}, u32[]{:S(2)}, u32[]{:S(2)}) collective-permute-start(bf16[1,2,2,80,1792]{4,3,2,1,0:T(8,128)(2,1)S(1)} %shard_map.95), channel_id=1, source_target_pairs={{0,8},{24,16},{1,9},{25,17},{2,10},{26,18},{3,11},{27,19},{4,12},{... | collective-permute-start | bytes 3440648 | tf_op jit(solution)/shard_map/ppermute | solution.py:268
  160.1 22.8 %collective-permute-start.33 = (bf16[2,2,80,1792]{3,2,1,0:T(8,128)(2,1)S(1)}, bf16[2,2,80,1792]{3,2,1,0:T(8,128)(2,1)S(1)}, u32[]{:S(2)}, u32[]{:S(2)}) collective-permute-start(bf16[2,2,80,1792]{3,2,1,0:T(8,128)(2,1)S(1)} %fusion.4), channel_id=1, source_target_pairs={{8,16},{16,8},{9,17},{17,9},{10,18},{18,10},{11,19},{19,11},{12,20... | collective-permute-start | bytes 3440648 | tf_op jit(solution)/shard_map/ppermute | solution.py:209
  161.2 28.1 %collective-permute-start.35 = (bf16[2,2,80,1792]{3,2,1,0:T(8,128)(2,1)S(1)}, bf16[2,2,80,1792]{3,2,1,0:T(8,128)(2,1)S(1)}, u32[]{:S(2)}, u32[]{:S(2)}) collective-permute-start(bf16[2,2,80,1792]{3,2,1,0:T(8,128)(2,1)S(1)} %fusion), channel_id=1, source_target_pairs={{16,24},{8,0},{17,25},{9,1},{18,26},{10,2},{19,27},{11,3},{20,28},... | collective-permute-start | bytes 3440648 | tf_op jit(solution)/shard_map/ppermute | solution.py:209

commit v9 on v8

--- a/solution.py
+++ b/solution.py
@@ -139,15 +139,15 @@
         cost_estimate=pl.CostEstimate(
             flops=hint or 2 * rows * width * count * tile, bytes_accessed=2 * width * count * tile, transcendentals=0
         ),
-    )(x, pltpu.with_memory_space_constraint(weight, pltpu.HBM))
+    )(x, weight)
 
 
 def low_rank_kernel(first, each, start, widths, tab_ref, inner_ref, *refs):
-    parts, ups, out_ref = refs[:2 * len(widths)], refs[2 * len(widths):-1], refs[-1]
+    parts, ups, outs = refs[:2 * len(widths)], refs[2 * len(widths):2 * len(widths) + each], refs[2 * len(widths) + each:]
     slot = first + pl.program_id(0)
     lanes = inner_ref.shape[2]
     rank = lanes // 2
-    rows = out_ref.shape[3]
+    rows = outs[0].shape[3]
     lane = lax.broadcasted_iota(jnp.int32, (rows, lanes), 1)
     for e in range(each):
         seg = tab_ref[2, slot * each + e]
@@ -160,11 +160,14 @@
                 factor = ups[e][0, which, :, column:column + width]
                 low = jnp.dot(inner, jnp.concatenate([factor, factor], axis=0), preferred_element_type=jnp.float32)
                 term = parts[which * len(widths) + n][e * rows:(e + 1) * rows].astype(jnp.float32) + low
-                out_ref[0, which, e, :, column:column + width] = term.astype(jnp.bfloat16)
+                if len(outs) == 2:
+                    outs[which][0, 0, e, :, column:column + width] = term.astype(jnp.bfloat16)
+                else:
+                    outs[0][0, which, e, :, column:column + width] = term.astype(jnp.bfloat16)
                 column += width
 
 
-def add_low_rank(parts, inner, start, rows, first, count, up_pool, table, each, hint=1 << 10):
+def add_low_rank(parts, inner, start, rows, first, count, up_pool, table, each, hint=1 << 10, halves=1):
     columns = up_pool.shape[3]
     rank = up_pool.shape[2]
     widths = [part.shape[1] for part in parts[:len(parts) // 2]]
@@ -174,14 +177,14 @@
 
     return pl.pallas_call(
         functools.partial(low_rank_kernel, first, each, start, widths),
-        out_shape=jax.ShapeDtypeStruct((count, 2, each, rows, columns), jnp.bfloat16),
+        out_shape=[jax.ShapeDtypeStruct((count, 2 // halves, each, rows, columns), jnp.bfloat16)] * halves,
         grid_spec=pltpu.PrefetchScalarGridSpec(
             num_scalar_prefetch=1,
             grid=(count,),
             in_specs=[pl.BlockSpec(inner.shape, lambda n, tab: (0, 0, 0))]
             + [pl.BlockSpec((each * rows, part.shape[1]), lambda n, tab: (first + n, 0)) for part in parts]
             + [up_spec(e) for e in range(each)],
-            out_specs=pl.BlockSpec((1, 2, each, rows, columns), lambda n, tab: (n, 0, 0, 0, 0)),
+            out_specs=[pl.BlockSpec((1, 2 // halves, each, rows, columns), lambda n, tab: (n, 0, 0, 0, 0))] * halves,
         ),
         compiler_params=pltpu.CompilerParams(vmem_limit_bytes=24 << 20),
         cost_estimate=pl.CostEstimate(flops=hint, bytes_accessed=1 << 10, transcendentals=0),
@@ -251,6 +254,8 @@
         if not left:
             return None
         weight, begin, count = left.pop(0)
+        if weight is gate_weight:
+            weight = pltpu.with_memory_space_constraint(weight, pltpu.HBM)
         return project(after(x, gate), weight, begin, count, tile)
 
     steps, parts = sum_beside(mine.reshape(-1, mine.shape[2]), "tp", ntp, piece)
@@ -260,9 +265,10 @@
     parts = [part for part in parts + more if part is not None]
     inner = sums[-1].reshape(mine.shape)
 
-    def terms(parts, inner, start, rows, first, count, gate, hint=1 << 10):
+    def terms(parts, inner, start, rows, first, count, gate, hint=1 << 10, halves=1):
         given = after(inner, gate) if gate is not None else inner
-        return add_low_rank(parts, given, start, rows, first, count, up_pool, up_table, each, hint)
+        made = add_low_rank(parts, given, start, rows, first, count, up_pool, up_table, each, hint, halves)
+        return made if halves == 2 else made[0]
 
     def first_hop(send):
         return lax.ppermute(send, "seq", hop_pairs(0, nseq))
@@ -284,20 +290,24 @@
 
     rows = later
     parts = [project(x, weight, 0, tiles, tile, AHEAD) for weight in (gate_weight, up_weight)]
-    sent = [terms(parts, inner, 0, rows, 0, 1, None)]
+    sent = [terms(parts, inner, 0, rows, 0, 1, None, halves=2)]
     for slot in range(1, nseq):
-        sent.append(terms(parts, inner, 0, rows, slot, 1, (sent[-1], second_hop)))
-    rest_hop = after(rest_hop, sent[-1])
+        sent.append(terms(parts, inner, 0, rows, slot, 1, (sent[-1][0], second_hop), halves=2))
+    rest_hop = after(rest_hop, sent[-1][0])
     third_hop = lax.ppermute(add(rest[0], rest_hop[0]), "seq", hop_pairs(1, nseq))
+    line = [half for slot in range(nseq - 1) for half in sent[slot]]
     hops = []
-    for slot in range(nseq - 1):
-        hops.append(first_hop(after(sent[slot], hops[slot - 2] if slot > 1 else rest_hop)))
-
-    hops[0] = after(hops[0], third_hop)
-    totals = [
-        scatter_line(own, [head_hop[0]] + [rest_hop[slot] for slot in range(nseq - 2)], nseq, {(1, 1): second_hop, (1, 2): third_hop}),
-        scatter_line([term[0] for term in sent], [hop[0] for hop in hops], nseq),
+    for n, half in enumerate(line):
+        hops.append(first_hop(after(half, hops[n - 2] if n > 1 else rest_hop)))
+    hops[:2] = after(tuple(hops[:2]), third_hop)
+
+    firsts = [head_hop[0]] + [rest_hop[slot] for slot in range(nseq - 2)]
+    totals = [scatter_line(own, firsts, nseq, {(1, 1): second_hop, (1, 2): third_hop})]
+    halves = [
+        scatter_line([term[which][0, 0] for term in sent], [hop[0, 0] for hop in hops[which::2]], nseq)
+        for which in range(2)
     ]
+    totals.append(halves)
     out = [(jax.nn.silu(total[0]) * total[1]).astype(jnp.bfloat16) for total in totals]
     return jnp.concatenate(out, axis=1).reshape(-1, columns)
 

time: 192 us -> 199 us (1.036)
  starting transfers between devices: 49.6 us -> 67.3 us
  Pallas kernels: 44.2 us -> 37.5 us
  waiting for transfers between devices: 81.4 us -> 77.1 us
    ppermute x5 -> x8, starting transfers between devices: 20.2 us -> 35.3 us  [first_hop(): return lax.ppermute(send, 'seq', hop_pairs(0, nseq))]
    ppermute x5 -> x8, waiting for transfers between devices: 58.2 us -> 49.2 us  [first_hop(): return lax.ppermute(send, 'seq', hop_pairs(0, nseq))]
    pallas_call x6, Pallas kernels: 32.9 us -> 26.2 us  [project(): pl.pallas_call(project_kernel, out_shape=jax.ShapeDtypeStruct((rows, coun...]
    ppermute x4 -> x7, waiting for transfers between devices: 6.28 us -> 10.5 us  [scatter_line(): arrived[level, step] = lax.ppermute(send, 'seq', hop_pairs(level, nseq))]
    ppermute x4 -> x7, starting transfers between devices: 4.23 us -> 6.64 us  [scatter_line(): arrived[level, step] = lax.ppermute(send, 'seq', hop_pairs(level, nseq))]
    convert_element_type x14 -> x17, other arithmetic: 5.63 us -> 5.63 us  [add(): return (x.astype(jnp.float32) + y.astype(jnp.float32)).astype(x.dtype)]
  transfers between devices with their start and end apart: 36 -> 42, of which waited for: 16 -> 21; matrix products, arithmetic and copies ran while one was open for 6% -> 5% of each run, Pallas kernels for 22% -> 17%
where the time goes in v9:
time: 199 us; the launch traced here: 198 us
  waiting for transfers between devices  77.1 us (39%)
  starting transfers between devices  67.3 us (34%)
  Pallas kernels  37.5 us (19%)
  other arithmetic  12.7 us (6%)
  local copies, waits for them, and re-layouts  2.89 us (1%)
    ppermute x8, waiting for transfers between devices, first_hop(): return lax.ppermute(send, 'seq', hop_pairs(0, nseq))  49.2 us
    ppermute x8, starting transfers between devices, first_hop(): return lax.ppermute(send, 'seq', hop_pairs(0, nseq))  35.3 us
    pallas_call x6, Pallas kernels, project(): pl.pallas_call(project_kernel, out_shape=jax.ShapeDtypeStruct((rows, coun...  26.2 us
    ppermute x22, starting transfers between devices, swap(): return lax.ppermute(x, axis, [(i, i ^ mask) for i in range(size)])  19.1 us
    ppermute x22, waiting for transfers between devices, swap(): return lax.ppermute(x, axis, [(i, i ^ mask) for i in range(size)])  17.4 us
    ppermute x7, waiting for transfers between devices, scatter_line(): arrived[level, step] = lax.ppermute(send, 'seq', hop_pairs(level, nseq))  10.5 us
    pallas_call x7, Pallas kernels, add_low_rank(): pl.pallas_call(functools.partial(low_rank_kernel, first, each, start, wid...  8.25 us
    ppermute x7, starting transfers between devices, scatter_line(): arrived[level, step] = lax.ppermute(send, 'seq', hop_pairs(level, nseq))  6.64 us
  transfers between devices with their start and end apart: 42, of which 21 were waited for; matrix products, arithmetic and copies ran while one was open for 5% of the time, Pallas kernels for 17%

profile of v9, /device:TPU:0, one launch (start us, length us, event | category | flops | bytes accessed | tf_op | source)
XLA Modules:
  0.0 198.1 jit_solution(7672374283112863002)
XLA Ops:
  0.9 3.0 %collective-permute-start.1 = (bf16[48,2048]{1,0:T(8,128)(2,1)S(1)}, bf16[48,2048]{1,0:T(8,128)(2,1)S(1)}, u32[]{:S(2)}, u32[]{:S(2)}) collective-permute-start(bf16[48,2048]{1,0:T(8,128)(2,1)S(1)} %slice.24.refs_0_), channel_id=1, source_target_pairs={{0,2},{1,3},{2,0},{3,1},{4,6},{5,7},{6,4},{7,5},{8,10},{9,11},{10,... | collective-permute-start | bytes 589832 | tf_op jit(solution)/shard_map/ppermute | solution.py:44
  3.9 1.5 collective-permute-start.3
  8.2 1.5 collective-permute-done.1.refs_2_
  9.7 4.8 %collective-permute-done.3.refs_4_ = bf16[48,2048]{1,0:T(8,128)(2,1)S(1)} collective-permute-done((bf16[48,2048]{1,0:T(8,128)(2,1)S(1)}, bf16[48,2048]{1,0:T(8,128)(2,1)S(1)}, u32[]{:S(2)}, u32[]{:S(2)}) %collective-permute-start.3) | collective-permute-done | bytes 196640 | tf_op jit(solution)/shard_map/ppermute | solution.py:44
  16.2 1.6 copy-done
  17.8 1.4 shard_map.82
  21.6 3.8 %shard_map.83.refs_0_ = bf16[384,768]{1,0:T(8,128)(2,1)S(1)} custom-call(bf16[384,2048]{1,0:T(8,128)(2,1)S(1)} %bitcast.78, bf16[2048,1792]{1,0:T(8,128)(2,1)} %weight_ref.10), custom_call_target="tpu_custom_call" | custom-call | flops 1207959552 | bytes 3145728 | tf_op jit(solution)/shard_map/pallas_call | solution.py:129
  25.4 1.2 collective-permute-start.9
  26.6 1.5 collective-permute-start.12
  28.6 1.5 collective-permute-start.14
  30.1 4.3 %shard_map.84.refs_1_ = bf16[384,1024]{1,0:T(8,128)(2,1)S(1)} custom-call(bf16[384,2048]{1,0:T(8,128)(2,1)S(1)} %bitcast.79, bf16[2048,1792]{1,0:T(8,128)(2,1)} %weight_ref.10), custom_call_target="tpu_custom_call" | custom-call | flops 1610612736 | bytes 4194304 | tf_op jit(solution)/shard_map/pallas_call | solution.py:129
  34.5 1.6 collective-permute-start.10
  36.1 2.0 %shard_map.85.refs_2_ = bf16[384,768]{1,0:T(8,128)(2,1)S(1)} custom-call(bf16[384,2048]{1,0:T(8,128)(2,1)S(1)} %bitcast.80, bf16[2048,1792]{1,0:T(8,128)(2,1)S(1)} %bitcast.75), custom_call_target="tpu_custom_call" | custom-call | flops 1207959552 | bytes 3145728 | tf_op jit(solution)/shard_map/pallas_call | solution.py:129
  38.6 2.7 %collective-permute-start.11 = (bf16[192,128]{1,0:T(8,128)(2,1)S(1)}, bf16[192,128]{1,0:T(8,128)(2,1)S(1)}, u32[]{:S(2)}, u32[]{:S(2)}) collective-permute-start(bf16[192,128]{1,0:T(8,128)(2,1)S(1)} %add_convert_fusion.11), channel_id=1, source_target_pairs={{0,16},{8,24},{16,0},{24,8},{1,17},{9,25},{17,1},{25,9},{2,18},{10... | collective-permute-start | bytes 147464 | tf_op jit(solution)/shard_map/ppermute | solution.py:44
  41.3 2.7 %shard_map.86.refs_3_ = bf16[384,1024]{1,0:T(8,128)(2,1)S(1)} custom-call(bf16[384,2048]{1,0:T(8,128)(2,1)S(1)} %bitcast.81, bf16[2048,1792]{1,0:T(8,128)(2,1)S(1)} %bitcast.75), custom_call_target="tpu_custom_call" | custom-call | flops 1610612736 | bytes 4194304 | tf_op jit(solution)/shard_map/pallas_call | solution.py:129
  48.2 1.7 shard_map.88
  50.1 3.5 %collective-permute-start.26 = (bf16[1,2,2,48,1792]{4,3,2,1,0:T(8,128)(2,1)S(1)}, bf16[1,2,2,48,1792]{4,3,2,1,0:T(8,128)(2,1)S(1)}, u32[]{:S(2)}, u32[]{:S(2)}) collective-permute-start(bf16[1,2,2,48,1792]{4,3,2,1,0:T(8,128)(2,1)S(1)} %shard_map.87), channel_id=1, source_target_pairs={{0,8},{24,16},{1,9},{25,17},{2,10},{26,18},{3,11},{27,19},{4,12},{... | collective-permute-start | bytes 2064392 | tf_op jit(solution)/shard_map/ppermute | solution.py:274
  53.6 1.6 collective-permute-start.20
  55.2 3.0 %collective-permute-done.20 = bf16[320,128]{1,0:T(8,128)(2,1)S(1)} collective-permute-done((bf16[320,128]{1,0:T(8,128)(2,1)S(1)}, bf16[320,128]{1,0:T(8,128)(2,1)S(1)}, u32[]{:S(2)}, u32[]{:S(2)}) %collective-permute-start.20) | collective-permute-done | bytes 81952 | tf_op jit(solution)/shard_map/ppermute | solution.py:44
  59.2 3.5 %collective-permute-done.21 = bf16[320,128]{1,0:T(8,128)(2,1)S(1)} collective-permute-done((bf16[320,128]{1,0:T(8,128)(2,1)S(1)}, bf16[320,128]{1,0:T(8,128)(2,1)S(1)}, u32[]{:S(2)}, u32[]{:S(2)}) %collective-permute-start.21) | collective-permute-done | bytes 81952 | tf_op jit(solution)/shard_map/ppermute | solution.py:44
  63.4 2.8 %collective-permute-start.24 = (bf16[320,128]{1,0:T(8,128)(2,1)}, bf16[320,128]{1,0:T(8,128)(2,1)}, u32[]{:S(2)}, u32[]{:S(2)}) collective-permute-start(bf16[320,128]{1,0:T(8,128)(2,1)} %add_convert_fusion.7), channel_id=1, source_target_pairs={{0,16},{8,24},{16,0},{24,8},{1,17},{9,25},{17,1},{25,9},{2,18},{10... | collective-permute-start | bytes 245768 | tf_op jit(solution)/shard_map/ppermute | solution.py:59
  66.1 1.1 collective-permute-start.25
  67.2 2.2 %shard_map.89 = bf16[2,2,2,48,1792]{4,3,2,1,0:T(8,128)(2,1)} custom-call(s32[3,8]{1,0:T(4,128)S(1)} %pad_add_fusion.tab_ref, bf16[4,48,128]{2,1,0:T(8,128)(2,1)S(1)} %bitcast.87, bf16[384,768]{1,0:T(8,128)(2,1)S(1)} %shard_map.83.refs_0_, bf16[384,1024]{1,0:T(8,128)(2,1)S(1)} %shard_map.84.refs_1_, bf16[384,768]{1,0:T(8,128)(2,1)S(1)} %shard_map.85.refs_2_, ...), custom_call_target="tpu_custom_call" | custom-call | flops 1024 | bytes 1024 | tf_op jit(solution)/shard_map/pallas_call | solution.py:178
  69.4 4.0 %collective-permute-start.22 = (bf16[2,2,2,48,1792]{4,3,2,1,0:T(8,128)(2,1)}, bf16[2,2,2,48,1792]{4,3,2,1,0:T(8,128)(2,1)}, u32[]{:S(2)}, u32[]{:S(2)}) collective-permute-start(bf16[2,2,2,48,1792]{4,3,2,1,0:T(8,128)(2,1)} %shard_map.89), channel_id=1, source_target_pairs={{0,8},{24,16},{1,9},{25,17},{2,10},{26,18},{3,11},{27,19},{4,12},{... | collective-permute-start | bytes 4128776 | tf_op jit(solution)/shard_map/ppermute | solution.py:274
  74.4 1.7 collective-permute-start.27
  77.3 6.7 %shard_map.91.refs_0_ = bf16[640,1792]{1,0:T(8,128)(2,1)S(1)} custom-call(bf16[640,2048]{1,0:T(8,128)(2,1)S(1)} %bitcast.91, bf16[2048,1792]{1,0:T(8,128)(2,1)S(1)} %bitcast.73), custom_call_target="tpu_custom_call" | custom-call | flops 68719476736 | bytes 7340032 | tf_op jit(solution)/shard_map/pallas_call | solution.py:129
  83.9 6.7 %shard_map.92.refs_1_ = bf16[640,1792]{1,0:T(8,128)(2,1)S(1)} custom-call(bf16[640,2048]{1,0:T(8,128)(2,1)S(1)} %bitcast.92, bf16[2048,1792]{1,0:T(8,128)(2,1)S(1)} %bitcast.77), custom_call_target="tpu_custom_call" | custom-call | flops 68719476736 | bytes 7340032 | tf_op jit(solution)/shard_map/pallas_call | solution.py:129
  95.9 7.7 %collective-permute-done.22 = bf16[2,2,2,48,1792]{4,3,2,1,0:T(8,128)(2,1)} collective-permute-done((bf16[2,2,2,48,1792]{4,3,2,1,0:T(8,128)(2,1)}, bf16[2,2,2,48,1792]{4,3,2,1,0:T(8,128)(2,1)}, u32[]{:S(2)}, u32[]{:S(2)}) %collective-permute-start.22) | collective-permute-done | bytes 1376288 | tf_op jit(solution)/shard_map/ppermute | solution.py:274
  103.6 1.5 fusion.9
  105.8 7.0 %collective-permute-start.30 = (bf16[1,1,2,80,1792]{4,3,2,1,0:T(8,128)(2,1)S(1)}, bf16[1,1,2,80,1792]{4,3,2,1,0:T(8,128)(2,1)S(1)}, u32[]{:S(2)}, u32[]{:S(2)}) collective-permute-start(bf16[1,1,2,80,1792]{4,3,2,1,0:T(8,128)(2,1)S(1)} %get-tuple-element.75), channel_id=1, source_target_pairs={{0,8},{24,16},{1,9},{25,17},{2,10},{26,18},{3,11},{27,19},{4,12},{... | collective-permute-start | bytes 1720328 | tf_op jit(solution)/shard_map/ppermute | solution.py:274
  112.8 1.3 collective-permute-start.34
  114.1 1.5 fusion
  115.6 1.3 collective-permute-start.29
  116.9 9.3 %collective-permute-done.30 = bf16[1,1,2,80,1792]{4,3,2,1,0:T(8,128)(2,1)S(1)} collective-permute-done((bf16[1,1,2,80,1792]{4,3,2,1,0:T(8,128)(2,1)S(1)}, bf16[1,1,2,80,1792]{4,3,2,1,0:T(8,128)(2,1)S(1)}, u32[]{:S(2)}, u32[]{:S(2)}) %collective-permute-start.30) | collective-permute-done | bytes 573472 | tf_op jit(solution)/shard_map/ppermute | solution.py:274
  126.1 4.4 %collective-permute-start.31 = (bf16[1,1,2,80,1792]{4,3,2,1,0:T(8,128)(2,1)S(1)}, bf16[1,1,2,80,1792]{4,3,2,1,0:T(8,128)(2,1)S(1)}, u32[]{:S(2)}, u32[]{:S(2)}) collective-permute-start(bf16[1,1,2,80,1792]{4,3,2,1,0:T(8,128)(2,1)S(1)} %get-tuple-element.76), channel_id=1, source_target_pairs={{0,8},{24,16},{1,9},{25,17},{2,10},{26,18},{3,11},{27,19},{4,12},{... | collective-permute-start | bytes 1720328 | tf_op jit(solution)/shard_map/ppermute | solution.py:274
  130.6 7.9 %collective-permute-done.34 = bf16[1,1,2,80,1792]{4,3,2,1,0:T(8,128)(2,1)S(1)} collective-permute-done((bf16[1,1,2,80,1792]{4,3,2,1,0:T(8,128)(2,1)S(1)}, bf16[1,1,2,80,1792]{4,3,2,1,0:T(8,128)(2,1)S(1)}, u32[]{:S(2)}, u32[]{:S(2)}) %collective-permute-start.34) | collective-permute-done | bytes 573472 | tf_op jit(solution)/shard_map/ppermute | solution.py:274
  138.4 4.4 %collective-permute-start.37 = (bf16[1,1,2,80,1792]{4,3,2,1,0:T(8,128)(2,1)S(1)}, bf16[1,1,2,80,1792]{4,3,2,1,0:T(8,128)(2,1)S(1)}, u32[]{:S(2)}, u32[]{:S(2)}) collective-permute-start(bf16[1,1,2,80,1792]{4,3,2,1,0:T(8,128)(2,1)S(1)} %get-tuple-element.84), channel_id=1, source_target_pairs={{0,8},{24,16},{1,9},{25,17},{2,10},{26,18},{3,11},{27,19},{4,12},{... | collective-permute-start | bytes 1720328 | tf_op jit(solution)/shard_map/ppermute | solution.py:274
  144.6 6.2 %collective-permute-done.31 = bf16[1,1,2,80,1792]{4,3,2,1,0:T(8,128)(2,1)S(1)} collective-permute-done((bf16[1,1,2,80,1792]{4,3,2,1,0:T(8,128)(2,1)S(1)}, bf16[1,1,2,80,1792]{4,3,2,1,0:T(8,128)(2,1)S(1)}, u32[]{:S(2)}, u32[]{:S(2)}) %collective-permute-start.31) | collective-permute-done | bytes 573472 | tf_op jit(solution)/shard_map/ppermute | solution.py:274
  150.7 4.4 %collective-permute-start.32 = (bf16[1,1,2,80,1792]{4,3,2,1,0:T(8,128)(2,1)S(1)}, bf16[1,1,2,80,1792]{4,3,2,1,0:T(8,128)(2,1)S(1)}, u32[]{:S(2)}, u32[]{:S(2)}) collective-permute-start(bf16[1,1,2,80,1792]{4,3,2,1,0:T(8,128)(2,1)S(1)} %get-tuple-element.77), channel_id=1, source_target_pairs={{0,8},{24,16},{1,9},{25,17},{2,10},{26,18},{3,11},{27,19},{4,12},{... | collective-permute-start | bytes 1720328 | tf_op jit(solution)/shard_map/ppermute | solution.py:274
  155.3 7.7 %collective-permute-done.37 = bf16[1,1,2,80,1792]{4,3,2,1,0:T(8,128)(2,1)S(1)} collective-permute-done((bf16[1,1,2,80,1792]{4,3,2,1,0:T(8,128)(2,1)S(1)}, bf16[1,1,2,80,1792]{4,3,2,1,0:T(8,128)(2,1)S(1)}, u32[]{:S(2)}, u32[]{:S(2)}) %collective-permute-start.37) | collective-permute-done | bytes 573472 | tf_op jit(solution)/shard_map/ppermute | solution.py:274
  163.9 6.3 %collective-permute-start.38 = (bf16[1,1,2,80,1792]{4,3,2,1,0:T(8,128)(2,1)S(1)}, bf16[1,1,2,80,1792]{4,3,2,1,0:T(8,128)(2,1)S(1)}, u32[]{:S(2)}, u32[]{:S(2)}) collective-permute-start(bf16[1,1,2,80,1792]{4,3,2,1,0:T(8,128)(2,1)S(1)} %get-tuple-element.85), channel_id=1, source_target_pairs={{0,8},{24,16},{1,9},{25,17},{2,10},{26,18},{3,11},{27,19},{4,12},{... | collective-permute-start | bytes 1720328 | tf_op jit(solution)/shard_map/ppermute | solution.py:274
  171.2 1.3 collective-permute-start.36
  172.5 2.8 %collective-permute-done.32 = bf16[1,1,2,80,1792]{4,3,2,1,0:T(8,128)(2,1)S(1)} collective-permute-done((bf16[1,1,2,80,1792]{4,3,2,1,0:T(8,128)(2,1)S(1)}, bf16[1,1,2,80,1792]{4,3,2,1,0:T(8,128)(2,1)S(1)}, u32[]{:S(2)}, u32[]{:S(2)}) %collective-permute-start.32) | collective-permute-done | bytes 573472 | tf_op jit(solution)/shard_map/ppermute | solution.py:274
  175.3 1.3 collective-permute-start.41
  176.6 1.4 fusion.1
  178.2 7.6 %collective-permute-done.38 = bf16[1,1,2,80,1792]{4,3,2,1,0:T(8,128)(2,1)S(1)} collective-permute-done((bf16[1,1,2,80,1792]{4,3,2,1,0:T(8,128)(2,1)S(1)}, bf16[1,1,2,80,1792]{4,3,2,1,0:T(8,128)(2,1)S(1)}, u32[]{:S(2)}, u32[]{:S(2)}) %collective-permute-start.38) | collective-permute-done | bytes 573472 | tf_op jit(solution)/shard_map/ppermute | solution.py:274
  185.8 3.2 %collective-permute-done.36 = bf16[2,80,1792]{2,1,0:T(8,128)(2,1)S(1)} collective-permute-done((bf16[2,80,1792]{2,1,0:T(8,128)(2,1)S(1)}, bf16[2,80,1792]{2,1,0:T(8,128)(2,1)S(1)}, u32[]{:S(2)}, u32[]{:S(2)}) %collective-permute-start.36) | collective-permute-done | bytes 573472 | tf_op jit(solution)/shard_map/ppermute | solution.py:212
  189.0 7.3 %collective-permute-done.41 = bf16[2,80,1792]{2,1,0:T(8,128)(2,1)S(1)} collective-permute-done((bf16[2,80,1792]{2,1,0:T(8,128)(2,1)S(1)}, bf16[2,80,1792]{2,1,0:T(8,128)(2,1)S(1)}, u32[]{:S(2)}, u32[]{:S(2)}) %collective-permute-start.41) | collective-permute-done | bytes 573472 | tf_op jit(solution)/shard_map/ppermute | solution.py:212
  (115 shorter events, 28.4 us)
Async XLA Ops:
  0.9 8.7 %collective-permute-start.1 = (bf16[48,2048]{1,0:T(8,128)(2,1)S(1)}, bf16[48,2048]{1,0:T(8,128)(2,1)S(1)}, u32[]{:S(2)}, u32[]{:S(2)}) collective-permute-start(bf16[48,2048]{1,0:T(8,128)(2,1)S(1)} %slice.24.refs_0_), channel_id=1, source_target_pairs={{0,2},{1,3},{2,0},{3,1},{4,6},{5,7},{6,4},{7,5},{8,10},{9,11},{10,... | collective-permute-start | bytes 589832 | tf_op jit(solution)/shard_map/ppermute | solution.py:44
  3.9 10.6 %collective-permute-start.3 = (bf16[48,2048]{1,0:T(8,128)(2,1)S(1)}, bf16[48,2048]{1,0:T(8,128)(2,1)S(1)}, u32[]{:S(2)}, u32[]{:S(2)}) collective-permute-start(bf16[48,2048]{1,0:T(8,128)(2,1)S(1)} %slice.24.refs_0_), channel_id=1, source_target_pairs={{0,4},{1,5},{2,6},{3,7},{4,0},{5,1},{6,2},{7,3},{8,12},{9,13},{10,... | collective-permute-start | bytes 589832 | tf_op jit(solution)/shard_map/ppermute | solution.py:44
  5.5 9.1 %collective-permute-start.5 = (bf16[48,2048]{1,0:T(8,128)(2,1)S(1)}, bf16[48,2048]{1,0:T(8,128)(2,1)S(1)}, u32[]{:S(2)}, u32[]{:S(2)}) collective-permute-start(bf16[48,2048]{1,0:T(8,128)(2,1)S(1)} %slice.24.refs_0_), channel_id=1, source_target_pairs={{0,6},{1,7},{2,4},{3,5},{4,2},{5,3},{6,0},{7,1},{8,14},{9,15},{10,... | collective-permute-start | bytes 589832 | tf_op jit(solution)/shard_map/ppermute | solution.py:44
  5.5 9.6 %collective-permute-start = (bf16[48,2048]{1,0:T(8,128)(2,1)S(1)}, bf16[48,2048]{1,0:T(8,128)(2,1)S(1)}, u32[]{:S(2)}, u32[]{:S(2)}) collective-permute-start(bf16[48,2048]{1,0:T(8,128)(2,1)S(1)} %slice.24.refs_0_), channel_id=1, source_target_pairs={{0,1},{1,0},{2,3},{3,2},{4,5},{5,4},{6,7},{7,6},{8,9},{9,8},{10,11... | collective-permute-start | bytes 589832 | tf_op jit(solution)/shard_map/ppermute | solution.py:44
  9.7 5.4 %collective-permute-start.2 = (bf16[48,2048]{1,0:T(8,128)(2,1)S(1)}, bf16[48,2048]{1,0:T(8,128)(2,1)S(1)}, u32[]{:S(2)}, u32[]{:S(2)}) collective-permute-start(bf16[48,2048]{1,0:T(8,128)(2,1)S(1)} %collective-permute-done.1.refs_2_), channel_id=1, source_target_pairs={{0,1},{1,0},{2,3},{3,2},{4,5},{5,4},{6,7},{7,6},{8,9},{9,8},{10,11... | collective-permute-start | bytes 589832 | tf_op jit(solution)/shard_map/ppermute | solution.py:44
  14.5 1.4 collective-permute-start.4
  14.5 1.7 collective-permute-start.6
  19.3 1.3 collective-permute-start.7
  20.6 4.8 %collective-permute-start.8 = (bf16[192,128]{1,0:T(8,128)(2,1)S(1)}, bf16[192,128]{1,0:T(8,128)(2,1)S(1)}, u32[]{:S(2)}, u32[]{:S(2)}) collective-permute-start(bf16[192,128]{1,0:T(8,128)(2,1)S(1)} %add_convert_fusion.14), channel_id=1, source_target_pairs={{0,2},{1,3},{2,0},{3,1},{4,6},{5,7},{6,4},{7,5},{8,10},{9,11},{10,... | collective-permute-start | bytes 147464 | tf_op jit(solution)/shard_map/ppermute | solution.py:44
  21.6 14.5 %slice-start.4 = ((s8[7340032]{0:T(1024)(128)(4,1)}), s8[4194304]{0:T(1024)(128)(4,1)S(1)}, s32[]{:S(2)}) async-start(s8[7340032]{0:T(1024)(128)(4,1)} %bitcast.74), calls=%async_computation.4 | async-start | bytes 8388608
  25.4 10.7 %slice-start.5 = ((s8[7340032]{0:T(1024)(128)(4,1)}), s8[3145728]{0:T(1024)(128)(4,1)S(1)}, s32[]{:S(2)}) async-start(s8[7340032]{0:T(1024)(128)(4,1)} %bitcast.74), calls=%async_computation.5 | async-start | bytes 6291456
  25.4 9.0 %collective-permute-start.9 = (bf16[192,128]{1,0:T(8,128)(2,1)S(1)}, bf16[192,128]{1,0:T(8,128)(2,1)S(1)}, u32[]{:S(2)}, u32[]{:S(2)}) collective-permute-start(bf16[192,128]{1,0:T(8,128)(2,1)S(1)} %add_convert_fusion.13), channel_id=1, source_target_pairs={{0,4},{1,5},{2,6},{3,7},{4,0},{5,1},{6,2},{7,3},{8,12},{9,13},{10,... | collective-permute-start | bytes 147464 | tf_op jit(solution)/shard_map/ppermute | solution.py:44
  26.6 18.5 %collective-permute-start.12 = (bf16[80,2048]{1,0:T(8,128)(2,1)S(1)}, bf16[80,2048]{1,0:T(8,128)(2,1)S(1)}, u32[]{:S(2)}, u32[]{:S(2)}) collective-permute-start(bf16[80,2048]{1,0:T(8,128)(2,1)S(1)} %slice.25.refs_0_), channel_id=1, source_target_pairs={{0,2},{1,3},{2,0},{3,1},{4,6},{5,7},{6,4},{7,5},{8,10},{9,11},{10,... | collective-permute-start | bytes 983048 | tf_op jit(solution)/shard_map/ppermute | solution.py:44
  28.1 17.0 %collective-permute-start.13 = (bf16[80,2048]{1,0:T(8,128)(2,1)S(1)}, bf16[80,2048]{1,0:T(8,128)(2,1)S(1)}, u32[]{:S(2)}, u32[]{:S(2)}) collective-permute-start(bf16[80,2048]{1,0:T(8,128)(2,1)S(1)} %slice.25.refs_0_), channel_id=1, source_target_pairs={{0,4},{1,5},{2,6},{3,7},{4,0},{5,1},{6,2},{7,3},{8,12},{9,13},{10,... | collective-permute-start | bytes 983048 | tf_op jit(solution)/shard_map/ppermute | solution.py:44
  28.6 16.5 %collective-permute-start.14 = (bf16[80,2048]{1,0:T(8,128)(2,1)S(1)}, bf16[80,2048]{1,0:T(8,128)(2,1)S(1)}, u32[]{:S(2)}, u32[]{:S(2)}) collective-permute-start(bf16[80,2048]{1,0:T(8,128)(2,1)S(1)} %slice.25.refs_0_), channel_id=1, source_target_pairs={{0,6},{1,7},{2,4},{3,5},{4,2},{5,3},{6,0},{7,1},{8,14},{9,15},{10,... | collective-permute-start | bytes 983048 | tf_op jit(solution)/shard_map/ppermute | solution.py:44
  34.5 4.2 %collective-permute-start.10 = (bf16[192,128]{1,0:T(8,128)(2,1)S(1)}, bf16[192,128]{1,0:T(8,128)(2,1)S(1)}, u32[]{:S(2)}, u32[]{:S(2)}) collective-permute-start(bf16[192,128]{1,0:T(8,128)(2,1)S(1)} %add_convert_fusion.12), channel_id=1, source_target_pairs={{0,8},{8,0},{16,24},{24,16},{1,9},{9,1},{17,25},{25,17},{2,10},{10... | collective-permute-start | bytes 147464 | tf_op jit(solution)/shard_map/ppermute | solution.py:44
  36.1 7.9 %slice-start = ((s8[7340032]{0:T(1024)(128)(4,1)}), s8[4194304]{0:T(1024)(128)(4,1)S(1)}, s32[]{:S(2)}) async-start(s8[7340032]{0:T(1024)(128)(4,1)} %bitcast.70), calls=%async_computation | async-start | bytes 8388608
  38.6 5.4 %slice-start.1 = ((s8[7340032]{0:T(1024)(128)(4,1)}), s8[3145728]{0:T(1024)(128)(4,1)S(1)}, s32[]{:S(2)}) async-start(s8[7340032]{0:T(1024)(128)(4,1)} %bitcast.70), calls=%async_computation.1 | async-start | bytes 6291456
  38.6 5.4 %collective-permute-start.11 = (bf16[192,128]{1,0:T(8,128)(2,1)S(1)}, bf16[192,128]{1,0:T(8,128)(2,1)S(1)}, u32[]{:S(2)}, u32[]{:S(2)}) collective-permute-start(bf16[192,128]{1,0:T(8,128)(2,1)S(1)} %add_convert_fusion.11), channel_id=1, source_target_pairs={{0,16},{8,24},{16,0},{24,8},{1,17},{9,25},{17,1},{25,9},{2,18},{10... | collective-permute-start | bytes 147464 | tf_op jit(solution)/shard_map/ppermute | solution.py:44
  45.1 1.7 collective-permute-start.15
  45.2 2.1 %collective-permute-start.16 = (bf16[80,2048]{1,0:T(8,128)(2,1)S(1)}, bf16[80,2048]{1,0:T(8,128)(2,1)S(1)}, u32[]{:S(2)}, u32[]{:S(2)}) collective-permute-start(bf16[80,2048]{1,0:T(8,128)(2,1)S(1)} %collective-permute-done.12.refs_2_), channel_id=1, source_target_pairs={{0,1},{1,0},{2,3},{3,2},{4,5},{5,4},{6,7},{7,6},{8,9},{9,8},{10,11... | collective-permute-start | bytes 983048 | tf_op jit(solution)/shard_map/ppermute | solution.py:44
  45.7 2.1 %collective-permute-start.17 = (bf16[80,2048]{1,0:T(8,128)(2,1)S(1)}, bf16[80,2048]{1,0:T(8,128)(2,1)S(1)}, u32[]{:S(2)}, u32[]{:S(2)}) collective-permute-start(bf16[80,2048]{1,0:T(8,128)(2,1)S(1)} %collective-permute-done.13.refs_4_), channel_id=1, source_target_pairs={{0,1},{1,0},{2,3},{3,2},{4,5},{5,4},{6,7},{7,6},{8,9},{9,8},{10,11... | collective-permute-start | bytes 983048 | tf_op jit(solution)/shard_map/ppermute | solution.py:44
  45.7 2.4 %collective-permute-start.18 = (bf16[80,2048]{1,0:T(8,128)(2,1)S(1)}, bf16[80,2048]{1,0:T(8,128)(2,1)S(1)}, u32[]{:S(2)}, u32[]{:S(2)}) collective-permute-start(bf16[80,2048]{1,0:T(8,128)(2,1)S(1)} %collective-permute-done.14.refs_6_), channel_id=1, source_target_pairs={{0,1},{1,0},{2,3},{3,2},{4,5},{5,4},{6,7},{7,6},{8,9},{9,8},{10,11... | collective-permute-start | bytes 983048 | tf_op jit(solution)/shard_map/ppermute | solution.py:44
  49.9 3.7 %collective-permute-start.19 = (bf16[320,128]{1,0:T(8,128)(2,1)S(1)}, bf16[320,128]{1,0:T(8,128)(2,1)S(1)}, u32[]{:S(2)}, u32[]{:S(2)}) collective-permute-start(bf16[320,128]{1,0:T(8,128)(2,1)S(1)} %bitcast.89), channel_id=1, source_target_pairs={{0,1},{1,0},{2,3},{3,2},{4,5},{5,4},{6,7},{7,6},{8,9},{9,8},{10,11... | collective-permute-start | bytes 245768 | tf_op jit(solution)/shard_map/ppermute | solution.py:44
  50.1 23.3 %collective-permute-start.26 = (bf16[1,2,2,48,1792]{4,3,2,1,0:T(8,128)(2,1)S(1)}, bf16[1,2,2,48,1792]{4,3,2,1,0:T(8,128)(2,1)S(1)}, u32[]{:S(2)}, u32[]{:S(2)}) collective-permute-start(bf16[1,2,2,48,1792]{4,3,2,1,0:T(8,128)(2,1)S(1)} %shard_map.87), channel_id=1, source_target_pairs={{0,8},{24,16},{1,9},{25,17},{2,10},{26,18},{3,11},{27,19},{4,12},{... | collective-permute-start | bytes 2064392 | tf_op jit(solution)/shard_map/ppermute | solution.py:274
  53.6 4.5 %collective-permute-start.20 = (bf16[320,128]{1,0:T(8,128)(2,1)S(1)}, bf16[320,128]{1,0:T(8,128)(2,1)S(1)}, u32[]{:S(2)}, u32[]{:S(2)}) collective-permute-start(bf16[320,128]{1,0:T(8,128)(2,1)S(1)} %add_convert_fusion.9), channel_id=1, source_target_pairs={{0,2},{1,3},{2,0},{3,1},{4,6},{5,7},{6,4},{7,5},{8,10},{9,11},{10,... | collective-permute-start | bytes 245768 | tf_op jit(solution)/shard_map/ppermute | solution.py:44
  58.2 4.5 %collective-permute-start.21 = (bf16[320,128]{1,0:T(8,128)(2,1)S(1)}, bf16[320,128]{1,0:T(8,128)(2,1)S(1)}, u32[]{:S(2)}, u32[]{:S(2)}) collective-permute-start(bf16[320,128]{1,0:T(8,128)(2,1)S(1)} %add_convert_fusion.8), channel_id=1, source_target_pairs={{0,4},{1,5},{2,6},{3,7},{4,0},{5,1},{6,2},{7,3},{8,12},{9,13},{10,... | collective-permute-start | bytes 245768 | tf_op jit(solution)/shard_map/ppermute | solution.py:44
  63.4 27.3 %collective-permute-start.23 = (bf16[320,128]{1,0:T(8,128)(2,1)}, bf16[320,128]{1,0:T(8,128)(2,1)}, u32[]{:S(2)}, u32[]{:S(2)}) collective-permute-start(bf16[320,128]{1,0:T(8,128)(2,1)} %add_convert_fusion.7), channel_id=1, source_target_pairs={{0,8},{8,16},{16,24},{24,0},{1,9},{9,17},{17,25},{25,1},{2,10},{10... | collective-permute-start | bytes 245768 | tf_op jit(solution)/shard_map/ppermute | solution.py:59
  63.4 27.3 %collective-permute-start.24 = (bf16[320,128]{1,0:T(8,128)(2,1)}, bf16[320,128]{1,0:T(8,128)(2,1)}, u32[]{:S(2)}, u32[]{:S(2)}) collective-permute-start(bf16[320,128]{1,0:T(8,128)(2,1)} %add_convert_fusion.7), channel_id=1, source_target_pairs={{0,16},{8,24},{16,0},{24,8},{1,17},{9,25},{17,1},{25,9},{2,18},{10... | collective-permute-start | bytes 245768 | tf_op jit(solution)/shard_map/ppermute | solution.py:59
  66.1 24.6 %collective-permute-start.25 = (bf16[320,128]{1,0:T(8,128)(2,1)}, bf16[320,128]{1,0:T(8,128)(2,1)}, u32[]{:S(2)}, u32[]{:S(2)}) collective-permute-start(bf16[320,128]{1,0:T(8,128)(2,1)} %add_convert_fusion.7), channel_id=1, source_target_pairs={{0,24},{8,0},{16,8},{24,16},{1,25},{9,1},{17,9},{25,17},{2,26},{10... | collective-permute-start | bytes 245768 | tf_op jit(solution)/shard_map/ppermute | solution.py:59
  69.4 34.2 %collective-permute-start.22 = (bf16[2,2,2,48,1792]{4,3,2,1,0:T(8,128)(2,1)}, bf16[2,2,2,48,1792]{4,3,2,1,0:T(8,128)(2,1)}, u32[]{:S(2)}, u32[]{:S(2)}) collective-permute-start(bf16[2,2,2,48,1792]{4,3,2,1,0:T(8,128)(2,1)} %shard_map.89), channel_id=1, source_target_pairs={{0,8},{24,16},{1,9},{25,17},{2,10},{26,18},{3,11},{27,19},{4,12},{... | collective-permute-start | bytes 4128776 | tf_op jit(solution)/shard_map/ppermute | solution.py:274
  74.4 18.4 %collective-permute-start.27 = (bf16[2,2,48,1792]{3,2,1,0:T(8,128)(2,1)}, bf16[2,2,48,1792]{3,2,1,0:T(8,128)(2,1)}, u32[]{:S(2)}, u32[]{:S(2)}) collective-permute-start(bf16[2,2,48,1792]{3,2,1,0:T(8,128)(2,1)} %fusion.8), channel_id=1, source_target_pairs={{8,16},{16,8},{9,17},{17,9},{10,18},{18,10},{11,19},{19,11},{12,20... | collective-permute-start | bytes 2064392 | tf_op jit(solution)/shard_map/ppermute | solution.py:287
  76.1 7.9 %slice-start.6 = ((s8[7340032]{0:T(1024)(128)(4,1)}), s8[3145728]{0:T(1024)(128)(4,1)S(1)}, s32[]{:S(2)}) async-start(s8[7340032]{0:T(1024)(128)(4,1)} %bitcast.76), calls=%async_computation.6 | async-start | bytes 6291456
  77.3 6.7 %slice-start.7 = ((s8[7340032]{0:T(1024)(128)(4,1)}), s8[4194304]{0:T(1024)(128)(4,1)S(1)}, s32[]{:S(2)}) async-start(s8[7340032]{0:T(1024)(128)(4,1)} %bitcast.76), calls=%async_computation.7 | async-start | bytes 8388608
  105.1 37.8 %collective-permute-start.28 = (bf16[2,2,48,1792]{3,2,1,0:T(8,128)(2,1)S(1)}, bf16[2,2,48,1792]{3,2,1,0:T(8,128)(2,1)S(1)}, u32[]{:S(2)}, u32[]{:S(2)}) collective-permute-start(bf16[2,2,48,1792]{3,2,1,0:T(8,128)(2,1)S(1)} %fusion.9), channel_id=1, source_target_pairs={{8,16},{16,8},{9,17},{17,9},{10,18},{18,10},{11,19},{19,11},{12,20... | collective-permute-start | bytes 2064392 | tf_op jit(solution)/shard_map/ppermute | solution.py:297
  105.8 20.3 %collective-permute-start.30 = (bf16[1,1,2,80,1792]{4,3,2,1,0:T(8,128)(2,1)S(1)}, bf16[1,1,2,80,1792]{4,3,2,1,0:T(8,128)(2,1)S(1)}, u32[]{:S(2)}, u32[]{:S(2)}) collective-permute-start(bf16[1,1,2,80,1792]{4,3,2,1,0:T(8,128)(2,1)S(1)} %get-tuple-element.75), channel_id=1, source_target_pairs={{0,8},{24,16},{1,9},{25,17},{2,10},{26,18},{3,11},{27,19},{4,12},{... | collective-permute-start | bytes 1720328 | tf_op jit(solution)/shard_map/ppermute | solution.py:274
  112.8 25.7 %collective-permute-start.34 = (bf16[1,1,2,80,1792]{4,3,2,1,0:T(8,128)(2,1)S(1)}, bf16[1,1,2,80,1792]{4,3,2,1,0:T(8,128)(2,1)S(1)}, u32[]{:S(2)}, u32[]{:S(2)}) collective-permute-start(bf16[1,1,2,80,1792]{4,3,2,1,0:T(8,128)(2,1)S(1)} %get-tuple-element.79), channel_id=1, source_target_pairs={{0,8},{24,16},{1,9},{25,17},{2,10},{26,18},{3,11},{27,19},{4,12},{... | collective-permute-start | bytes 1720328 | tf_op jit(solution)/shard_map/ppermute | solution.py:274
  115.6 55.6 %collective-permute-start.29 = (bf16[2,2,48,1792]{3,2,1,0:T(8,128)(2,1)S(1)}, bf16[2,2,48,1792]{3,2,1,0:T(8,128)(2,1)S(1)}, u32[]{:S(2)}, u32[]{:S(2)}) collective-permute-start(bf16[2,2,48,1792]{3,2,1,0:T(8,128)(2,1)S(1)} %fusion), channel_id=1, source_target_pairs={{16,24},{8,0},{17,25},{9,1},{18,26},{10,2},{19,27},{11,3},{20,28},... | collective-permute-start | bytes 2064392 | tf_op jit(solution)/shard_map/ppermute | solution.py:212
  126.1 24.6 %collective-permute-start.31 = (bf16[1,1,2,80,1792]{4,3,2,1,0:T(8,128)(2,1)S(1)}, bf16[1,1,2,80,1792]{4,3,2,1,0:T(8,128)(2,1)S(1)}, u32[]{:S(2)}, u32[]{:S(2)}) collective-permute-start(bf16[1,1,2,80,1792]{4,3,2,1,0:T(8,128)(2,1)S(1)} %get-tuple-element.76), channel_id=1, source_target_pairs={{0,8},{24,16},{1,9},{25,17},{2,10},{26,18},{3,11},{27,19},{4,12},{... | collective-permute-start | bytes 1720328 | tf_op jit(solution)/shard_map/ppermute | solution.py:274
  138.4 24.6 %collective-permute-start.37 = (bf16[1,1,2,80,1792]{4,3,2,1,0:T(8,128)(2,1)S(1)}, bf16[1,1,2,80,1792]{4,3,2,1,0:T(8,128)(2,1)S(1)}, u32[]{:S(2)}, u32[]{:S(2)}) collective-permute-start(bf16[1,1,2,80,1792]{4,3,2,1,0:T(8,128)(2,1)S(1)} %get-tuple-element.84), channel_id=1, source_target_pairs={{0,8},{24,16},{1,9},{25,17},{2,10},{26,18},{3,11},{27,19},{4,12},{... | collective-permute-start | bytes 1720328 | tf_op jit(solution)/shard_map/ppermute | solution.py:274
  143.0 20.8 %collective-permute-start.35 = (bf16[2,80,1792]{2,1,0:T(8,128)(2,1)S(1)}, bf16[2,80,1792]{2,1,0:T(8,128)(2,1)S(1)}, u32[]{:S(2)}, u32[]{:S(2)}) collective-permute-start(bf16[2,80,1792]{2,1,0:T(8,128)(2,1)S(1)} %fusion.13), channel_id=1, source_target_pairs={{8,16},{16,8},{9,17},{17,9},{10,18},{18,10},{11,19},{19,11},{12,20... | collective-permute-start | bytes 1720328 | tf_op jit(solution)/shard_map/ppermute | solution.py:212
  143.9 26.5 %collective-permute-start.40 = (bf16[2,80,1792]{2,1,0:T(8,128)(2,1)S(1)}, bf16[2,80,1792]{2,1,0:T(8,128)(2,1)S(1)}, u32[]{:S(2)}, u32[]{:S(2)}) collective-permute-start(bf16[2,80,1792]{2,1,0:T(8,128)(2,1)S(1)} %fusion.15), channel_id=1, source_target_pairs={{8,16},{16,8},{9,17},{17,9},{10,18},{18,10},{11,19},{19,11},{12,20... | collective-permute-start | bytes 1720328 | tf_op jit(solution)/shard_map/ppermute | solution.py:212
  150.7 24.6 %collective-permute-start.32 = (bf16[1,1,2,80,1792]{4,3,2,1,0:T(8,128)(2,1)S(1)}, bf16[1,1,2,80,1792]{4,3,2,1,0:T(8,128)(2,1)S(1)}, u32[]{:S(2)}, u32[]{:S(2)}) collective-permute-start(bf16[1,1,2,80,1792]{4,3,2,1,0:T(8,128)(2,1)S(1)} %get-tuple-element.77), channel_id=1, source_target_pairs={{0,8},{24,16},{1,9},{25,17},{2,10},{26,18},{3,11},{27,19},{4,12},{... | collective-permute-start | bytes 1720328 | tf_op jit(solution)/shard_map/ppermute | solution.py:274
  163.0 15.2 %collective-permute-start.33 = (bf16[2,80,1792]{2,1,0:T(8,128)(2,1)S(1)}, bf16[2,80,1792]{2,1,0:T(8,128)(2,1)S(1)}, u32[]{:S(2)}, u32[]{:S(2)}) collective-permute-start(bf16[2,80,1792]{2,1,0:T(8,128)(2,1)S(1)} %fusion.12), channel_id=1, source_target_pairs={{8,16},{16,8},{9,17},{17,9},{10,18},{18,10},{11,19},{19,11},{12,20... | collective-permute-start | bytes 1720328 | tf_op jit(solution)/shard_map/ppermute | solution.py:212
  163.9 22.0 %collective-permute-start.38 = (bf16[1,1,2,80,1792]{4,3,2,1,0:T(8,128)(2,1)S(1)}, bf16[1,1,2,80,1792]{4,3,2,1,0:T(8,128)(2,1)S(1)}, u32[]{:S(2)}, u32[]{:S(2)}) collective-permute-start(bf16[1,1,2,80,1792]{4,3,2,1,0:T(8,128)(2,1)S(1)} %get-tuple-element.85), channel_id=1, source_target_pairs={{0,8},{24,16},{1,9},{25,17},{2,10},{26,18},{3,11},{27,19},{4,12},{... | collective-permute-start | bytes 1720328 | tf_op jit(solution)/shard_map/ppermute | solution.py:274
  170.3 15.5 %collective-permute-start.39 = (bf16[2,80,1792]{2,1,0:T(8,128)(2,1)S(1)}, bf16[2,80,1792]{2,1,0:T(8,128)(2,1)S(1)}, u32[]{:S(2)}, u32[]{:S(2)}) collective-permute-start(bf16[2,80,1792]{2,1,0:T(8,128)(2,1)S(1)} %fusion.14), channel_id=1, source_target_pairs={{8,16},{16,8},{9,17},{17,9},{10,18},{18,10},{11,19},{19,11},{12,20... | collective-permute-start | bytes 1720328 | tf_op jit(solution)/shard_map/ppermute | solution.py:212
  171.2 17.8 %collective-permute-start.36 = (bf16[2,80,1792]{2,1,0:T(8,128)(2,1)S(1)}, bf16[2,80,1792]{2,1,0:T(8,128)(2,1)S(1)}, u32[]{:S(2)}, u32[]{:S(2)}) collective-permute-start(bf16[2,80,1792]{2,1,0:T(8,128)(2,1)S(1)} %fusion.3), channel_id=1, source_target_pairs={{16,24},{8,0},{17,25},{9,1},{18,26},{10,2},{19,27},{11,3},{20,28},... | collective-permute-start | bytes 1720328 | tf_op jit(solution)/shard_map/ppermute | solution.py:212
  175.3 21.0 %collective-permute-start.41 = (bf16[2,80,1792]{2,1,0:T(8,128)(2,1)S(1)}, bf16[2,80,1792]{2,1,0:T(8,128)(2,1)S(1)}, u32[]{:S(2)}, u32[]{:S(2)}) collective-permute-start(bf16[2,80,1792]{2,1,0:T(8,128)(2,1)S(1)} %fusion.2), channel_id=1, source_target_pairs={{16,24},{8,0},{17,25},{9,1},{18,26},{10,2},{19,27},{11,3},{20,28},... | collective-permute-start | bytes 1720328 | tf_op jit(solution)/shard_map/ppermute | solution.py:212
  (5 other events, 13.9 us)

commit v10 on v8

--- a/solution.py
+++ b/solution.py
@@ -139,7 +139,7 @@
         cost_estimate=pl.CostEstimate(
             flops=hint or 2 * rows * width * count * tile, bytes_accessed=2 * width * count * tile, transcendentals=0
         ),
-    )(x, pltpu.with_memory_space_constraint(weight, pltpu.HBM))
+    )(x, weight)
 
 
 def low_rank_kernel(first, each, start, widths, tab_ref, inner_ref, *refs):
@@ -251,6 +251,8 @@
         if not left:
             return None
         weight, begin, count = left.pop(0)
+        if weight is gate_weight:
+            weight = pltpu.with_memory_space_constraint(weight, pltpu.HBM)
         return project(after(x, gate), weight, begin, count, tile)
 
     steps, parts = sum_beside(mine.reshape(-1, mine.shape[2]), "tp", ntp, piece)

time: 192 us -> 191 us (level)
  Pallas kernels: 44.2 us -> 37.3 us
  waiting for transfers between devices: 81.4 us -> 84.2 us
  starting transfers between devices: 49.6 us -> 52.3 us
    pallas_call x6, Pallas kernels: 32.9 us -> 26 us  [project(): pl.pallas_call(project_kernel, out_shape=jax.ShapeDtypeStruct((rows, coun...]
    ppermute x5, starting transfers between devices: 20.2 us -> 22.8 us  [first_hop(): return lax.ppermute(send, 'seq', hop_pairs(0, nseq))]
  transfers between devices with their start and end apart: 36 -> 36, of which waited for: 16 -> 17; matrix products, arithmetic and copies ran while one was open for 6% -> 6% of each run, Pallas kernels for 22% -> 18%
where the time goes in v10:
time: 191 us; the launch traced here: 190 us
  waiting for transfers between devices  84.2 us (44%)
  starting transfers between devices  52.3 us (27%)
  Pallas kernels  37.3 us (20%)
  other arithmetic  12.7 us (7%)
  local copies, waits for them, and re-layouts  2.91 us (2%)
    ppermute x5, waiting for transfers between devices, first_hop(): return lax.ppermute(send, 'seq', hop_pairs(0, nseq))  59.9 us
    pallas_call x6, Pallas kernels, project(): pl.pallas_call(project_kernel, out_shape=jax.ShapeDtypeStruct((rows, coun...  26 us
    ppermute x5, starting transfers between devices, first_hop(): return lax.ppermute(send, 'seq', hop_pairs(0, nseq))  22.8 us
    ppermute x22, starting transfers between devices, swap(): return lax.ppermute(x, axis, [(i, i ^ mask) for i in range(size)])  19.1 us
    ppermute x22, waiting for transfers between devices, swap(): return lax.ppermute(x, axis, [(i, i ^ mask) for i in range(size)])  17.4 us
    pallas_call x7, Pallas kernels, add_low_rank(): pl.pallas_call(functools.partial(low_rank_kernel, first, each, start, wid...  8.26 us
    ppermute x4, waiting for transfers between devices, scatter_line(): arrived[level, step] = lax.ppermute(send, 'seq', hop_pairs(level, nseq))  6.81 us
    convert_element_type x14, other arithmetic, add(): return (x.astype(jnp.float32) + y.astype(jnp.float32)).astype(x.dtype)  5.61 us
  transfers between devices with their start and end apart: 36, of which 17 were waited for; matrix products, arithmetic and copies ran while one was open for 6% of the time, Pallas kernels for 18%

profile of v10, /device:TPU:0, one launch (start us, length us, event | category | flops | bytes accessed | tf_op | source)
XLA Modules:
  0.0 190.0 jit_solution(9562650636841288584)
XLA Ops:
  0.9 3.0 %collective-permute-start.1 = (bf16[48,2048]{1,0:T(8,128)(2,1)S(1)}, bf16[48,2048]{1,0:T(8,128)(2,1)S(1)}, u32[]{:S(2)}, u32[]{:S(2)}) collective-permute-start(bf16[48,2048]{1,0:T(8,128)(2,1)S(1)} %slice.30.refs_0_), channel_id=1, source_target_pairs={{0,2},{1,3},{2,0},{3,1},{4,6},{5,7},{6,4},{7,5},{8,10},{9,11},{10,... | collective-permute-start | bytes 589832 | tf_op jit(solution)/shard_map/ppermute | solution.py:44
  3.9 1.5 collective-permute-start.3
  8.2 1.5 collective-permute-done.1.refs_2_
  9.7 4.8 %collective-permute-done.3.refs_4_ = bf16[48,2048]{1,0:T(8,128)(2,1)S(1)} collective-permute-done((bf16[48,2048]{1,0:T(8,128)(2,1)S(1)}, bf16[48,2048]{1,0:T(8,128)(2,1)S(1)}, u32[]{:S(2)}, u32[]{:S(2)}) %collective-permute-start.3) | collective-permute-done | bytes 196640 | tf_op jit(solution)/shard_map/ppermute | solution.py:44
  16.2 1.6 copy-done
  17.8 1.4 shard_map.82
  20.6 1.0 collective-permute-start.8
  21.6 3.8 %shard_map.83.refs_0_ = bf16[384,768]{1,0:T(8,128)(2,1)S(1)} custom-call(bf16[384,2048]{1,0:T(8,128)(2,1)S(1)} %bitcast.71, bf16[2048,1792]{1,0:T(8,128)(2,1)} %weight_ref.10), custom_call_target="tpu_custom_call" | custom-call | flops 1207959552 | bytes 3145728 | tf_op jit(solution)/shard_map/pallas_call | solution.py:129
  25.4 1.2 collective-permute-start.9
  26.6 1.5 collective-permute-start.12
  28.6 1.5 collective-permute-start.14
  30.1 4.3 %shard_map.84.refs_1_ = bf16[384,1024]{1,0:T(8,128)(2,1)S(1)} custom-call(bf16[384,2048]{1,0:T(8,128)(2,1)S(1)} %bitcast.72, bf16[2048,1792]{1,0:T(8,128)(2,1)} %weight_ref.10), custom_call_target="tpu_custom_call" | custom-call | flops 1610612736 | bytes 4194304 | tf_op jit(solution)/shard_map/pallas_call | solution.py:129
  34.5 1.6 collective-permute-start.10
  36.1 2.0 %shard_map.85.refs_2_ = bf16[384,768]{1,0:T(8,128)(2,1)S(1)} custom-call(bf16[384,2048]{1,0:T(8,128)(2,1)S(1)} %bitcast.73, bf16[2048,1792]{1,0:T(8,128)(2,1)S(1)} %bitcast.68), custom_call_target="tpu_custom_call" | custom-call | flops 1207959552 | bytes 3145728 | tf_op jit(solution)/shard_map/pallas_call | solution.py:129
  38.6 2.7 %collective-permute-start.11 = (bf16[192,128]{1,0:T(8,128)(2,1)S(1)}, bf16[192,128]{1,0:T(8,128)(2,1)S(1)}, u32[]{:S(2)}, u32[]{:S(2)}) collective-permute-start(bf16[192,128]{1,0:T(8,128)(2,1)S(1)} %add_convert_fusion.9), channel_id=1, source_target_pairs={{0,16},{8,24},{16,0},{24,8},{1,17},{9,25},{17,1},{25,9},{2,18},{10... | collective-permute-start | bytes 147464 | tf_op jit(solution)/shard_map/ppermute | solution.py:44
  41.3 2.7 %shard_map.86.refs_3_ = bf16[384,1024]{1,0:T(8,128)(2,1)S(1)} custom-call(bf16[384,2048]{1,0:T(8,128)(2,1)S(1)} %bitcast.74, bf16[2048,1792]{1,0:T(8,128)(2,1)S(1)} %bitcast.68), custom_call_target="tpu_custom_call" | custom-call | flops 1610612736 | bytes 4194304 | tf_op jit(solution)/shard_map/pallas_call | solution.py:129
  48.2 1.6 shard_map.88
  50.0 3.5 %collective-permute-start.26 = (bf16[1,2,2,48,1792]{4,3,2,1,0:T(8,128)(2,1)S(1)}, bf16[1,2,2,48,1792]{4,3,2,1,0:T(8,128)(2,1)S(1)}, u32[]{:S(2)}, u32[]{:S(2)}) collective-permute-start(bf16[1,2,2,48,1792]{4,3,2,1,0:T(8,128)(2,1)S(1)} %shard_map.87), channel_id=1, source_target_pairs={{0,8},{24,16},{1,9},{25,17},{2,10},{26,18},{3,11},{27,19},{4,12},{... | collective-permute-start | bytes 2064392 | tf_op jit(solution)/shard_map/ppermute | solution.py:270
  53.6 1.6 collective-permute-start.20
  55.2 3.0 %collective-permute-done.20 = bf16[320,128]{1,0:T(8,128)(2,1)S(1)} collective-permute-done((bf16[320,128]{1,0:T(8,128)(2,1)S(1)}, bf16[320,128]{1,0:T(8,128)(2,1)S(1)}, u32[]{:S(2)}, u32[]{:S(2)}) %collective-permute-start.20) | collective-permute-done | bytes 81952 | tf_op jit(solution)/shard_map/ppermute | solution.py:44
  58.1 1.0 collective-permute-start.21
  59.1 3.5 %collective-permute-done.21 = bf16[320,128]{1,0:T(8,128)(2,1)S(1)} collective-permute-done((bf16[320,128]{1,0:T(8,128)(2,1)S(1)}, bf16[320,128]{1,0:T(8,128)(2,1)S(1)}, u32[]{:S(2)}, u32[]{:S(2)}) %collective-permute-start.21) | collective-permute-done | bytes 81952 | tf_op jit(solution)/shard_map/ppermute | solution.py:44
  63.3 2.8 %collective-permute-start.24 = (bf16[320,128]{1,0:T(8,128)(2,1)}, bf16[320,128]{1,0:T(8,128)(2,1)}, u32[]{:S(2)}, u32[]{:S(2)}) collective-permute-start(bf16[320,128]{1,0:T(8,128)(2,1)} %add_convert_fusion.5), channel_id=1, source_target_pairs={{0,16},{8,24},{16,0},{24,8},{1,17},{9,25},{17,1},{25,9},{2,18},{10... | collective-permute-start | bytes 245768 | tf_op jit(solution)/shard_map/ppermute | solution.py:59
  66.1 1.1 collective-permute-start.25
  67.1 2.2 %shard_map.89 = bf16[2,2,2,48,1792]{4,3,2,1,0:T(8,128)(2,1)} custom-call(s32[3,8]{1,0:T(4,128)S(1)} %pad_add_fusion.tab_ref, bf16[4,48,128]{2,1,0:T(8,128)(2,1)S(1)} %bitcast.80, bf16[384,768]{1,0:T(8,128)(2,1)S(1)} %shard_map.83.refs_0_, bf16[384,1024]{1,0:T(8,128)(2,1)S(1)} %shard_map.84.refs_1_, bf16[384,768]{1,0:T(8,128)(2,1)S(1)} %shard_map.85.refs_2_, ...), custom_call_target="tpu_custom_call" | custom-call | flops 1024 | bytes 1024 | tf_op jit(solution)/shard_map/pallas_call | solution.py:175
  69.4 4.0 %collective-permute-start.22 = (bf16[2,2,2,48,1792]{4,3,2,1,0:T(8,128)(2,1)}, bf16[2,2,2,48,1792]{4,3,2,1,0:T(8,128)(2,1)}, u32[]{:S(2)}, u32[]{:S(2)}) collective-permute-start(bf16[2,2,2,48,1792]{4,3,2,1,0:T(8,128)(2,1)} %shard_map.89), channel_id=1, source_target_pairs={{0,8},{24,16},{1,9},{25,17},{2,10},{26,18},{3,11},{27,19},{4,12},{... | collective-permute-start | bytes 4128776 | tf_op jit(solution)/shard_map/ppermute | solution.py:270
  73.3 1.0 fusion.8
  74.3 1.6 collective-permute-start.27
  77.2 6.6 %shard_map.91.refs_0_ = bf16[640,1792]{1,0:T(8,128)(2,1)S(1)} custom-call(bf16[640,2048]{1,0:T(8,128)(2,1)S(1)} %bitcast.84, bf16[2048,1792]{1,0:T(8,128)(2,1)S(1)} %bitcast.66), custom_call_target="tpu_custom_call" | custom-call | flops 68719476736 | bytes 7340032 | tf_op jit(solution)/shard_map/pallas_call | solution.py:129
  83.8 6.6 %shard_map.92.refs_1_ = bf16[640,1792]{1,0:T(8,128)(2,1)S(1)} custom-call(bf16[640,2048]{1,0:T(8,128)(2,1)S(1)} %bitcast.85, bf16[2048,1792]{1,0:T(8,128)(2,1)S(1)} %bitcast.70), custom_call_target="tpu_custom_call" | custom-call | flops 68719476736 | bytes 7340032 | tf_op jit(solution)/shard_map/pallas_call | solution.py:129
  90.5 1.1 add_convert_fusion.4
  91.5 1.0 shard_map.93
  92.6 1.0 shard_map.94
  93.6 1.0 shard_map.95
  94.6 1.0 shard_map.96
  95.7 7.9 %collective-permute-done.22 = bf16[2,2,2,48,1792]{4,3,2,1,0:T(8,128)(2,1)} collective-permute-done((bf16[2,2,2,48,1792]{4,3,2,1,0:T(8,128)(2,1)}, bf16[2,2,2,48,1792]{4,3,2,1,0:T(8,128)(2,1)}, u32[]{:S(2)}, u32[]{:S(2)}) %collective-permute-start.22) | collective-permute-done | bytes 1376288 | tf_op jit(solution)/shard_map/ppermute | solution.py:270
  103.6 4.4 %collective-permute-start.30 = (bf16[1,2,2,80,1792]{4,3,2,1,0:T(8,128)(2,1)S(1)}, bf16[1,2,2,80,1792]{4,3,2,1,0:T(8,128)(2,1)S(1)}, u32[]{:S(2)}, u32[]{:S(2)}) collective-permute-start(bf16[1,2,2,80,1792]{4,3,2,1,0:T(8,128)(2,1)S(1)} %shard_map.93), channel_id=1, source_target_pairs={{0,8},{24,16},{1,9},{25,17},{2,10},{26,18},{3,11},{27,19},{4,12},{... | collective-permute-start | bytes 3440648 | tf_op jit(solution)/shard_map/ppermute | solution.py:270
  108.0 1.5 fusion.9
  110.2 3.8 %collective-permute-start.32 = (bf16[1,2,2,80,1792]{4,3,2,1,0:T(8,128)(2,1)S(1)}, bf16[1,2,2,80,1792]{4,3,2,1,0:T(8,128)(2,1)S(1)}, u32[]{:S(2)}, u32[]{:S(2)}) collective-permute-start(bf16[1,2,2,80,1792]{4,3,2,1,0:T(8,128)(2,1)S(1)} %shard_map.94), channel_id=1, source_target_pairs={{0,8},{24,16},{1,9},{25,17},{2,10},{26,18},{3,11},{27,19},{4,12},{... | collective-permute-start | bytes 3440648 | tf_op jit(solution)/shard_map/ppermute | solution.py:270
  114.1 19.6 %collective-permute-done.30 = bf16[1,2,2,80,1792]{4,3,2,1,0:T(8,128)(2,1)S(1)} collective-permute-done((bf16[1,2,2,80,1792]{4,3,2,1,0:T(8,128)(2,1)S(1)}, bf16[1,2,2,80,1792]{4,3,2,1,0:T(8,128)(2,1)S(1)}, u32[]{:S(2)}, u32[]{:S(2)}) %collective-permute-start.30) | collective-permute-done | bytes 1146912 | tf_op jit(solution)/shard_map/ppermute | solution.py:270
  134.9 1.5 fusion.2
  136.3 1.3 collective-permute-start.29
  137.6 7.0 %collective-permute-start.31 = (bf16[1,2,2,80,1792]{4,3,2,1,0:T(8,128)(2,1)S(1)}, bf16[1,2,2,80,1792]{4,3,2,1,0:T(8,128)(2,1)S(1)}, u32[]{:S(2)}, u32[]{:S(2)}) collective-permute-start(bf16[1,2,2,80,1792]{4,3,2,1,0:T(8,128)(2,1)S(1)} %shard_map.95), channel_id=1, source_target_pairs={{0,8},{24,16},{1,9},{25,17},{2,10},{26,18},{3,11},{27,19},{4,12},{... | collective-permute-start | bytes 3440648 | tf_op jit(solution)/shard_map/ppermute | solution.py:270
  144.6 13.6 %collective-permute-done.32 = bf16[1,2,2,80,1792]{4,3,2,1,0:T(8,128)(2,1)S(1)} collective-permute-done((bf16[1,2,2,80,1792]{4,3,2,1,0:T(8,128)(2,1)S(1)}, bf16[1,2,2,80,1792]{4,3,2,1,0:T(8,128)(2,1)S(1)}, u32[]{:S(2)}, u32[]{:S(2)}) %collective-permute-start.32) | collective-permute-done | bytes 1146912 | tf_op jit(solution)/shard_map/ppermute | solution.py:270
  159.5 1.3 collective-permute-start.35
  160.9 1.4 fusion.3
  162.5 18.9 %collective-permute-done.31 = bf16[1,2,2,80,1792]{4,3,2,1,0:T(8,128)(2,1)S(1)} collective-permute-done((bf16[1,2,2,80,1792]{4,3,2,1,0:T(8,128)(2,1)S(1)}, bf16[1,2,2,80,1792]{4,3,2,1,0:T(8,128)(2,1)S(1)}, u32[]{:S(2)}, u32[]{:S(2)}) %collective-permute-start.31) | collective-permute-done | bytes 1146912 | tf_op jit(solution)/shard_map/ppermute | solution.py:270
  181.3 6.8 %collective-permute-done.35 = bf16[2,2,80,1792]{3,2,1,0:T(8,128)(2,1)S(1)} collective-permute-done((bf16[2,2,80,1792]{3,2,1,0:T(8,128)(2,1)S(1)}, bf16[2,2,80,1792]{3,2,1,0:T(8,128)(2,1)S(1)}, u32[]{:S(2)}, u32[]{:S(2)}) %collective-permute-start.35) | collective-permute-done | bytes 1146912 | tf_op jit(solution)/shard_map/ppermute | solution.py:209
  (101 shorter events, 19.2 us)
Async XLA Ops:
  0.9 8.7 %collective-permute-start.1 = (bf16[48,2048]{1,0:T(8,128)(2,1)S(1)}, bf16[48,2048]{1,0:T(8,128)(2,1)S(1)}, u32[]{:S(2)}, u32[]{:S(2)}) collective-permute-start(bf16[48,2048]{1,0:T(8,128)(2,1)S(1)} %slice.30.refs_0_), channel_id=1, source_target_pairs={{0,2},{1,3},{2,0},{3,1},{4,6},{5,7},{6,4},{7,5},{8,10},{9,11},{10,... | collective-permute-start | bytes 589832 | tf_op jit(solution)/shard_map/ppermute | solution.py:44
  3.9 10.6 %collective-permute-start.3 = (bf16[48,2048]{1,0:T(8,128)(2,1)S(1)}, bf16[48,2048]{1,0:T(8,128)(2,1)S(1)}, u32[]{:S(2)}, u32[]{:S(2)}) collective-permute-start(bf16[48,2048]{1,0:T(8,128)(2,1)S(1)} %slice.30.refs_0_), channel_id=1, source_target_pairs={{0,4},{1,5},{2,6},{3,7},{4,0},{5,1},{6,2},{7,3},{8,12},{9,13},{10,... | collective-permute-start | bytes 589832 | tf_op jit(solution)/shard_map/ppermute | solution.py:44
  5.5 9.1 %collective-permute-start.5 = (bf16[48,2048]{1,0:T(8,128)(2,1)S(1)}, bf16[48,2048]{1,0:T(8,128)(2,1)S(1)}, u32[]{:S(2)}, u32[]{:S(2)}) collective-permute-start(bf16[48,2048]{1,0:T(8,128)(2,1)S(1)} %slice.30.refs_0_), channel_id=1, source_target_pairs={{0,6},{1,7},{2,4},{3,5},{4,2},{5,3},{6,0},{7,1},{8,14},{9,15},{10,... | collective-permute-start | bytes 589832 | tf_op jit(solution)/shard_map/ppermute | solution.py:44
  5.5 9.6 %collective-permute-start = (bf16[48,2048]{1,0:T(8,128)(2,1)S(1)}, bf16[48,2048]{1,0:T(8,128)(2,1)S(1)}, u32[]{:S(2)}, u32[]{:S(2)}) collective-permute-start(bf16[48,2048]{1,0:T(8,128)(2,1)S(1)} %slice.30.refs_0_), channel_id=1, source_target_pairs={{0,1},{1,0},{2,3},{3,2},{4,5},{5,4},{6,7},{7,6},{8,9},{9,8},{10,11... | collective-permute-start | bytes 589832 | tf_op jit(solution)/shard_map/ppermute | solution.py:44
  9.7 5.4 %collective-permute-start.2 = (bf16[48,2048]{1,0:T(8,128)(2,1)S(1)}, bf16[48,2048]{1,0:T(8,128)(2,1)S(1)}, u32[]{:S(2)}, u32[]{:S(2)}) collective-permute-start(bf16[48,2048]{1,0:T(8,128)(2,1)S(1)} %collective-permute-done.1.refs_2_), channel_id=1, source_target_pairs={{0,1},{1,0},{2,3},{3,2},{4,5},{5,4},{6,7},{7,6},{8,9},{9,8},{10,11... | collective-permute-start | bytes 589832 | tf_op jit(solution)/shard_map/ppermute | solution.py:44
  14.5 1.4 collective-permute-start.4
  14.5 1.7 collective-permute-start.6
  16.2 1.6 copy-start
  17.8 1.7 copy-start.2
  19.3 1.3 collective-permute-start.7
  20.6 4.8 %collective-permute-start.8 = (bf16[192,128]{1,0:T(8,128)(2,1)S(1)}, bf16[192,128]{1,0:T(8,128)(2,1)S(1)}, u32[]{:S(2)}, u32[]{:S(2)}) collective-permute-start(bf16[192,128]{1,0:T(8,128)(2,1)S(1)} %add_convert_fusion.12), channel_id=1, source_target_pairs={{0,2},{1,3},{2,0},{3,1},{4,6},{5,7},{6,4},{7,5},{8,10},{9,11},{10,... | collective-permute-start | bytes 147464 | tf_op jit(solution)/shard_map/ppermute | solution.py:44
  21.6 14.5 %slice-start.4 = ((s8[7340032]{0:T(1024)(128)(4,1)}), s8[4194304]{0:T(1024)(128)(4,1)S(1)}, s32[]{:S(2)}) async-start(s8[7340032]{0:T(1024)(128)(4,1)} %bitcast.67), calls=%async_computation.4 | async-start | bytes 8388608
  25.4 10.7 %slice-start.5 = ((s8[7340032]{0:T(1024)(128)(4,1)}), s8[3145728]{0:T(1024)(128)(4,1)S(1)}, s32[]{:S(2)}) async-start(s8[7340032]{0:T(1024)(128)(4,1)} %bitcast.67), calls=%async_computation.5 | async-start | bytes 6291456
  25.4 9.0 %collective-permute-start.9 = (bf16[192,128]{1,0:T(8,128)(2,1)S(1)}, bf16[192,128]{1,0:T(8,128)(2,1)S(1)}, u32[]{:S(2)}, u32[]{:S(2)}) collective-permute-start(bf16[192,128]{1,0:T(8,128)(2,1)S(1)} %add_convert_fusion.11), channel_id=1, source_target_pairs={{0,4},{1,5},{2,6},{3,7},{4,0},{5,1},{6,2},{7,3},{8,12},{9,13},{10,... | collective-permute-start | bytes 147464 | tf_op jit(solution)/shard_map/ppermute | solution.py:44
  26.6 18.5 %collective-permute-start.12 = (bf16[80,2048]{1,0:T(8,128)(2,1)S(1)}, bf16[80,2048]{1,0:T(8,128)(2,1)S(1)}, u32[]{:S(2)}, u32[]{:S(2)}) collective-permute-start(bf16[80,2048]{1,0:T(8,128)(2,1)S(1)} %slice.31.refs_0_), channel_id=1, source_target_pairs={{0,2},{1,3},{2,0},{3,1},{4,6},{5,7},{6,4},{7,5},{8,10},{9,11},{10,... | collective-permute-start | bytes 983048 | tf_op jit(solution)/shard_map/ppermute | solution.py:44
  28.1 17.0 %collective-permute-start.13 = (bf16[80,2048]{1,0:T(8,128)(2,1)S(1)}, bf16[80,2048]{1,0:T(8,128)(2,1)S(1)}, u32[]{:S(2)}, u32[]{:S(2)}) collective-permute-start(bf16[80,2048]{1,0:T(8,128)(2,1)S(1)} %slice.31.refs_0_), channel_id=1, source_target_pairs={{0,4},{1,5},{2,6},{3,7},{4,0},{5,1},{6,2},{7,3},{8,12},{9,13},{10,... | collective-permute-start | bytes 983048 | tf_op jit(solution)/shard_map/ppermute | solution.py:44
  28.6 16.5 %collective-permute-start.14 = (bf16[80,2048]{1,0:T(8,128)(2,1)S(1)}, bf16[80,2048]{1,0:T(8,128)(2,1)S(1)}, u32[]{:S(2)}, u32[]{:S(2)}) collective-permute-start(bf16[80,2048]{1,0:T(8,128)(2,1)S(1)} %slice.31.refs_0_), channel_id=1, source_target_pairs={{0,6},{1,7},{2,4},{3,5},{4,2},{5,3},{6,0},{7,1},{8,14},{9,15},{10,... | collective-permute-start | bytes 983048 | tf_op jit(solution)/shard_map/ppermute | solution.py:44
  34.5 4.2 %collective-permute-start.10 = (bf16[192,128]{1,0:T(8,128)(2,1)S(1)}, bf16[192,128]{1,0:T(8,128)(2,1)S(1)}, u32[]{:S(2)}, u32[]{:S(2)}) collective-permute-start(bf16[192,128]{1,0:T(8,128)(2,1)S(1)} %add_convert_fusion.10), channel_id=1, source_target_pairs={{0,8},{8,0},{16,24},{24,16},{1,9},{9,1},{17,25},{25,17},{2,10},{10... | collective-permute-start | bytes 147464 | tf_op jit(solution)/shard_map/ppermute | solution.py:44
  36.1 7.9 %slice-start = ((s8[7340032]{0:T(1024)(128)(4,1)}), s8[4194304]{0:T(1024)(128)(4,1)S(1)}, s32[]{:S(2)}) async-start(s8[7340032]{0:T(1024)(128)(4,1)} %bitcast.63), calls=%async_computation | async-start | bytes 8388608
  38.6 5.4 %slice-start.1 = ((s8[7340032]{0:T(1024)(128)(4,1)}), s8[3145728]{0:T(1024)(128)(4,1)S(1)}, s32[]{:S(2)}) async-start(s8[7340032]{0:T(1024)(128)(4,1)} %bitcast.63), calls=%async_computation.1 | async-start | bytes 6291456
  38.6 5.4 %collective-permute-start.11 = (bf16[192,128]{1,0:T(8,128)(2,1)S(1)}, bf16[192,128]{1,0:T(8,128)(2,1)S(1)}, u32[]{:S(2)}, u32[]{:S(2)}) collective-permute-start(bf16[192,128]{1,0:T(8,128)(2,1)S(1)} %add_convert_fusion.9), channel_id=1, source_target_pairs={{0,16},{8,24},{16,0},{24,8},{1,17},{9,25},{17,1},{25,9},{2,18},{10... | collective-permute-start | bytes 147464 | tf_op jit(solution)/shard_map/ppermute | solution.py:44
  44.1 4.1 %copy-start.1 = (bf16[8,64,2048]{2,1,0:T(8,128)(2,1)S(1)}, bf16[8,64,2048]{2,1,0:T(8,128)(2,1)}, u32[]{:S(2)}) copy-start(bf16[8,64,2048]{2,1,0:T(8,128)(2,1)} %refs_8_.3) | copy-start | bytes 6291460
  45.1 1.7 collective-permute-start.15
  45.2 2.1 %collective-permute-start.16 = (bf16[80,2048]{1,0:T(8,128)(2,1)S(1)}, bf16[80,2048]{1,0:T(8,128)(2,1)S(1)}, u32[]{:S(2)}, u32[]{:S(2)}) collective-permute-start(bf16[80,2048]{1,0:T(8,128)(2,1)S(1)} %collective-permute-done.12.refs_2_), channel_id=1, source_target_pairs={{0,1},{1,0},{2,3},{3,2},{4,5},{5,4},{6,7},{7,6},{8,9},{9,8},{10,11... | collective-permute-start | bytes 983048 | tf_op jit(solution)/shard_map/ppermute | solution.py:44
  45.7 2.1 %collective-permute-start.17 = (bf16[80,2048]{1,0:T(8,128)(2,1)S(1)}, bf16[80,2048]{1,0:T(8,128)(2,1)S(1)}, u32[]{:S(2)}, u32[]{:S(2)}) collective-permute-start(bf16[80,2048]{1,0:T(8,128)(2,1)S(1)} %collective-permute-done.13.refs_4_), channel_id=1, source_target_pairs={{0,1},{1,0},{2,3},{3,2},{4,5},{5,4},{6,7},{7,6},{8,9},{9,8},{10,11... | collective-permute-start | bytes 983048 | tf_op jit(solution)/shard_map/ppermute | solution.py:44
  45.7 2.4 %collective-permute-start.18 = (bf16[80,2048]{1,0:T(8,128)(2,1)S(1)}, bf16[80,2048]{1,0:T(8,128)(2,1)S(1)}, u32[]{:S(2)}, u32[]{:S(2)}) collective-permute-start(bf16[80,2048]{1,0:T(8,128)(2,1)S(1)} %collective-permute-done.14.refs_6_), channel_id=1, source_target_pairs={{0,1},{1,0},{2,3},{3,2},{4,5},{5,4},{6,7},{7,6},{8,9},{9,8},{10,11... | collective-permute-start | bytes 983048 | tf_op jit(solution)/shard_map/ppermute | solution.py:44
  49.8 3.7 %collective-permute-start.19 = (bf16[320,128]{1,0:T(8,128)(2,1)S(1)}, bf16[320,128]{1,0:T(8,128)(2,1)S(1)}, u32[]{:S(2)}, u32[]{:S(2)}) collective-permute-start(bf16[320,128]{1,0:T(8,128)(2,1)S(1)} %bitcast.82), channel_id=1, source_target_pairs={{0,1},{1,0},{2,3},{3,2},{4,5},{5,4},{6,7},{7,6},{8,9},{9,8},{10,11... | collective-permute-start | bytes 245768 | tf_op jit(solution)/shard_map/ppermute | solution.py:44
  50.0 23.3 %collective-permute-start.26 = (bf16[1,2,2,48,1792]{4,3,2,1,0:T(8,128)(2,1)S(1)}, bf16[1,2,2,48,1792]{4,3,2,1,0:T(8,128)(2,1)S(1)}, u32[]{:S(2)}, u32[]{:S(2)}) collective-permute-start(bf16[1,2,2,48,1792]{4,3,2,1,0:T(8,128)(2,1)S(1)} %shard_map.87), channel_id=1, source_target_pairs={{0,8},{24,16},{1,9},{25,17},{2,10},{26,18},{3,11},{27,19},{4,12},{... | collective-permute-start | bytes 2064392 | tf_op jit(solution)/shard_map/ppermute | solution.py:270
  53.6 4.5 %collective-permute-start.20 = (bf16[320,128]{1,0:T(8,128)(2,1)S(1)}, bf16[320,128]{1,0:T(8,128)(2,1)S(1)}, u32[]{:S(2)}, u32[]{:S(2)}) collective-permute-start(bf16[320,128]{1,0:T(8,128)(2,1)S(1)} %add_convert_fusion.7), channel_id=1, source_target_pairs={{0,2},{1,3},{2,0},{3,1},{4,6},{5,7},{6,4},{7,5},{8,10},{9,11},{10,... | collective-permute-start | bytes 245768 | tf_op jit(solution)/shard_map/ppermute | solution.py:44
  58.1 4.5 %collective-permute-start.21 = (bf16[320,128]{1,0:T(8,128)(2,1)S(1)}, bf16[320,128]{1,0:T(8,128)(2,1)S(1)}, u32[]{:S(2)}, u32[]{:S(2)}) collective-permute-start(bf16[320,128]{1,0:T(8,128)(2,1)S(1)} %add_convert_fusion.6), channel_id=1, source_target_pairs={{0,4},{1,5},{2,6},{3,7},{4,0},{5,1},{6,2},{7,3},{8,12},{9,13},{10,... | collective-permute-start | bytes 245768 | tf_op jit(solution)/shard_map/ppermute | solution.py:44
  63.3 27.1 %collective-permute-start.23 = (bf16[320,128]{1,0:T(8,128)(2,1)}, bf16[320,128]{1,0:T(8,128)(2,1)}, u32[]{:S(2)}, u32[]{:S(2)}) collective-permute-start(bf16[320,128]{1,0:T(8,128)(2,1)} %add_convert_fusion.5), channel_id=1, source_target_pairs={{0,8},{8,16},{16,24},{24,0},{1,9},{9,17},{17,25},{25,1},{2,10},{10... | collective-permute-start | bytes 245768 | tf_op jit(solution)/shard_map/ppermute | solution.py:59
  63.3 27.2 %collective-permute-start.24 = (bf16[320,128]{1,0:T(8,128)(2,1)}, bf16[320,128]{1,0:T(8,128)(2,1)}, u32[]{:S(2)}, u32[]{:S(2)}) collective-permute-start(bf16[320,128]{1,0:T(8,128)(2,1)} %add_convert_fusion.5), channel_id=1, source_target_pairs={{0,16},{8,24},{16,0},{24,8},{1,17},{9,25},{17,1},{25,9},{2,18},{10... | collective-permute-start | bytes 245768 | tf_op jit(solution)/shard_map/ppermute | solution.py:59
  66.1 24.4 %collective-permute-start.25 = (bf16[320,128]{1,0:T(8,128)(2,1)}, bf16[320,128]{1,0:T(8,128)(2,1)}, u32[]{:S(2)}, u32[]{:S(2)}) collective-permute-start(bf16[320,128]{1,0:T(8,128)(2,1)} %add_convert_fusion.5), channel_id=1, source_target_pairs={{0,24},{8,0},{16,8},{24,16},{1,25},{9,1},{17,9},{25,17},{2,26},{10... | collective-permute-start | bytes 245768 | tf_op jit(solution)/shard_map/ppermute | solution.py:59
  69.4 34.2 %collective-permute-start.22 = (bf16[2,2,2,48,1792]{4,3,2,1,0:T(8,128)(2,1)}, bf16[2,2,2,48,1792]{4,3,2,1,0:T(8,128)(2,1)}, u32[]{:S(2)}, u32[]{:S(2)}) collective-permute-start(bf16[2,2,2,48,1792]{4,3,2,1,0:T(8,128)(2,1)} %shard_map.89), channel_id=1, source_target_pairs={{0,8},{24,16},{1,9},{25,17},{2,10},{26,18},{3,11},{27,19},{4,12},{... | collective-permute-start | bytes 4128776 | tf_op jit(solution)/shard_map/ppermute | solution.py:270
  73.3 3.6 %slice-start.2 = ((s8[7340032]{0:T(1024)(128)(4,1)}), s8[4194304]{0:T(1024)(128)(4,1)S(1)}, s32[]{:S(2)}) async-start(s8[7340032]{0:T(1024)(128)(4,1)} %bitcast.65), calls=%async_computation.2 | async-start | bytes 8388608
  74.3 2.8 %slice-start.3 = ((s8[7340032]{0:T(1024)(128)(4,1)}), s8[3145728]{0:T(1024)(128)(4,1)S(1)}, s32[]{:S(2)}) async-start(s8[7340032]{0:T(1024)(128)(4,1)} %bitcast.65), calls=%async_computation.3 | async-start | bytes 6291456
  74.3 18.2 %collective-permute-start.27 = (bf16[2,2,48,1792]{3,2,1,0:T(8,128)(2,1)}, bf16[2,2,48,1792]{3,2,1,0:T(8,128)(2,1)}, u32[]{:S(2)}, u32[]{:S(2)}) collective-permute-start(bf16[2,2,48,1792]{3,2,1,0:T(8,128)(2,1)} %fusion.8), channel_id=1, source_target_pairs={{8,16},{16,8},{9,17},{17,9},{10,18},{18,10},{11,19},{19,11},{12,20... | collective-permute-start | bytes 2064392 | tf_op jit(solution)/shard_map/ppermute | solution.py:283
  76.0 7.8 %slice-start.6 = ((s8[7340032]{0:T(1024)(128)(4,1)}), s8[3145728]{0:T(1024)(128)(4,1)S(1)}, s32[]{:S(2)}) async-start(s8[7340032]{0:T(1024)(128)(4,1)} %bitcast.69), calls=%async_computation.6 | async-start | bytes 6291456
  77.2 6.6 %slice-start.7 = ((s8[7340032]{0:T(1024)(128)(4,1)}), s8[4194304]{0:T(1024)(128)(4,1)S(1)}, s32[]{:S(2)}) async-start(s8[7340032]{0:T(1024)(128)(4,1)} %bitcast.69), calls=%async_computation.7 | async-start | bytes 8388608
  103.6 30.1 %collective-permute-start.30 = (bf16[1,2,2,80,1792]{4,3,2,1,0:T(8,128)(2,1)S(1)}, bf16[1,2,2,80,1792]{4,3,2,1,0:T(8,128)(2,1)S(1)}, u32[]{:S(2)}, u32[]{:S(2)}) collective-permute-start(bf16[1,2,2,80,1792]{4,3,2,1,0:T(8,128)(2,1)S(1)} %shard_map.93), channel_id=1, source_target_pairs={{0,8},{24,16},{1,9},{25,17},{2,10},{26,18},{3,11},{27,19},{4,12},{... | collective-permute-start | bytes 3440648 | tf_op jit(solution)/shard_map/ppermute | solution.py:270
  109.5 4.6 %collective-permute-start.28 = (bf16[2,2,48,1792]{3,2,1,0:T(8,128)(2,1)S(1)}, bf16[2,2,48,1792]{3,2,1,0:T(8,128)(2,1)S(1)}, u32[]{:S(2)}, u32[]{:S(2)}) collective-permute-start(bf16[2,2,48,1792]{3,2,1,0:T(8,128)(2,1)S(1)} %fusion.9), channel_id=1, source_target_pairs={{8,16},{16,8},{9,17},{17,9},{10,18},{18,10},{11,19},{19,11},{12,20... | collective-permute-start | bytes 2064392 | tf_op jit(solution)/shard_map/ppermute | solution.py:293
  110.2 48.0 %collective-permute-start.32 = (bf16[1,2,2,80,1792]{4,3,2,1,0:T(8,128)(2,1)S(1)}, bf16[1,2,2,80,1792]{4,3,2,1,0:T(8,128)(2,1)S(1)}, u32[]{:S(2)}, u32[]{:S(2)}) collective-permute-start(bf16[1,2,2,80,1792]{4,3,2,1,0:T(8,128)(2,1)S(1)} %shard_map.94), channel_id=1, source_target_pairs={{0,8},{24,16},{1,9},{25,17},{2,10},{26,18},{3,11},{27,19},{4,12},{... | collective-permute-start | bytes 3440648 | tf_op jit(solution)/shard_map/ppermute | solution.py:270
  133.9 25.3 %collective-permute-start.34 = (bf16[2,2,80,1792]{3,2,1,0:T(8,128)(2,1)S(1)}, bf16[2,2,80,1792]{3,2,1,0:T(8,128)(2,1)S(1)}, u32[]{:S(2)}, u32[]{:S(2)}) collective-permute-start(bf16[2,2,80,1792]{3,2,1,0:T(8,128)(2,1)S(1)} %fusion.5), channel_id=1, source_target_pairs={{8,16},{16,8},{9,17},{17,9},{10,18},{18,10},{11,19},{19,11},{12,20... | collective-permute-start | bytes 3440648 | tf_op jit(solution)/shard_map/ppermute | solution.py:209
  136.3 24.5 %collective-permute-start.29 = (bf16[2,2,48,1792]{3,2,1,0:T(8,128)(2,1)S(1)}, bf16[2,2,48,1792]{3,2,1,0:T(8,128)(2,1)S(1)}, u32[]{:S(2)}, u32[]{:S(2)}) collective-permute-start(bf16[2,2,48,1792]{3,2,1,0:T(8,128)(2,1)S(1)} %fusion.2), channel_id=1, source_target_pairs={{16,24},{8,0},{17,25},{9,1},{18,26},{10,2},{19,27},{11,3},{20,28},... | collective-permute-start | bytes 2064392 | tf_op jit(solution)/shard_map/ppermute | solution.py:209
  137.6 43.7 %collective-permute-start.31 = (bf16[1,2,2,80,1792]{4,3,2,1,0:T(8,128)(2,1)S(1)}, bf16[1,2,2,80,1792]{4,3,2,1,0:T(8,128)(2,1)S(1)}, u32[]{:S(2)}, u32[]{:S(2)}) collective-permute-start(bf16[1,2,2,80,1792]{4,3,2,1,0:T(8,128)(2,1)S(1)} %shard_map.95), channel_id=1, source_target_pairs={{0,8},{24,16},{1,9},{25,17},{2,10},{26,18},{3,11},{27,19},{4,12},{... | collective-permute-start | bytes 3440648 | tf_op jit(solution)/shard_map/ppermute | solution.py:270
  158.5 22.8 %collective-permute-start.33 = (bf16[2,2,80,1792]{3,2,1,0:T(8,128)(2,1)S(1)}, bf16[2,2,80,1792]{3,2,1,0:T(8,128)(2,1)S(1)}, u32[]{:S(2)}, u32[]{:S(2)}) collective-permute-start(bf16[2,2,80,1792]{3,2,1,0:T(8,128)(2,1)S(1)} %fusion.4), channel_id=1, source_target_pairs={{8,16},{16,8},{9,17},{17,9},{10,18},{18,10},{11,19},{19,11},{12,20... | collective-permute-start | bytes 3440648 | tf_op jit(solution)/shard_map/ppermute | solution.py:209
  159.5 28.6 %collective-permute-start.35 = (bf16[2,2,80,1792]{3,2,1,0:T(8,128)(2,1)S(1)}, bf16[2,2,80,1792]{3,2,1,0:T(8,128)(2,1)S(1)}, u32[]{:S(2)}, u32[]{:S(2)}) collective-permute-start(bf16[2,2,80,1792]{3,2,1,0:T(8,128)(2,1)S(1)} %fusion), channel_id=1, source_target_pairs={{16,24},{8,0},{17,25},{9,1},{18,26},{10,2},{19,27},{11,3},{20,28},... | collective-permute-start | bytes 3440648 | tf_op jit(solution)/shard_map/ppermute | solution.py:209

commit v11 on v10

--- a/solution.py
+++ b/solution.py
@@ -207,10 +207,13 @@
             slot = step - level if level < nseq // 2 else step
             send = add(own[slot], arrived[level - 1, step - 1])
             arrived[level, step] = lax.ppermute(send, "seq", hop_pairs(level, nseq))
-    total = own[nseq - 1].astype(jnp.float32)
-    for level in range(nseq - 1):
-        total = total + arrived[level, last].astype(jnp.float32)
-    return total
+    totals = []
+    for which in range(2):
+        total = own[nseq - 1][which].astype(jnp.float32)
+        for level in range(nseq - 1):
+            total = total + arrived[level, last][which].astype(jnp.float32)
+        totals.append(total)
+    return totals
 
 
 def after(x, gate):
@@ -275,9 +278,9 @@
     head_hop = first_hop(head)
     steps, _ = sum_beside(mine.reshape(-1, mine.shape[2]), "tp", ntp, lambda gate: None)
     shared = steps[-1]
-    rest = terms(parts, inner, 0, rows, 1, nseq - 2, shared)
-    rest_hop = first_hop(rest)
-    kept = terms(parts, inner, 0, rows, nseq - 1, 1, rest)
+    rest = terms(parts, inner, 0, rows, 1, nseq - 2, mine)
+    kept = terms(parts, inner, 0, rows, nseq - 1, 1, (rest, shared))
+    rest_hop = first_hop(after(rest, kept))
     inner = sum_one_step(shared, "seq", nseq).reshape(mine.shape)
     second = add(head[0], after(head_hop, rest)[0])
     second_hop = lax.ppermute(second, "seq", hop_pairs(1, nseq))
@@ -285,7 +288,8 @@
     own = [head[0]] + [rest[slot] for slot in range(nseq - 2)] + [kept[0]]
 
     rows = later
-    parts = [project(x, weight, 0, tiles, tile, AHEAD) for weight in (gate_weight, up_weight)]
+    gate_part = project(x, gate_weight, 0, tiles, tile, AHEAD)
+    parts = [gate_part, project(after(x, gate_part), up_weight, 0, tiles, tile, 1 << 10)]
     sent = [terms(parts, inner, 0, rows, 0, 1, None)]
     for slot in range(1, nseq):
         sent.append(terms(parts, inner, 0, rows, slot, 1, (sent[-1], second_hop)))

time: 191 us -> 188 us (0.984)
  other arithmetic: 12.7 us -> 6.4 us
  waiting for transfers between devices: 84.2 us -> 90.3 us
    ppermute x5, waiting for transfers between devices: 59.9 us -> 73 us  [first_hop(): return lax.ppermute(send, 'seq', hop_pairs(0, nseq))]
    ppermute x22, waiting for transfers between devices: 17.4 us -> 11.9 us  [swap(): return lax.ppermute(x, axis, [(i, i ^ mask) for i in range(size)])]
    ppermute x3, starting transfers between devices: 3.83 us -> 8.12 us  [sum_one_step(): lax.ppermute(x, axis, [(i, (i + k) % size) for i in range(size)])]
    convert_element_type x14, other arithmetic: 5.61 us -> 1.47 us  [add(): return (x.astype(jnp.float32) + y.astype(jnp.float32)).astype(x.dtype)]
    ppermute x5, starting transfers between devices: 22.8 us -> 18.8 us  [first_hop(): return lax.ppermute(send, 'seq', hop_pairs(0, nseq))]
    ppermute x4, waiting for transfers between devices: 6.81 us -> 4.53 us  [scatter_line(): arrived[level, step] = lax.ppermute(send, 'seq', hop_pairs(level, nseq))]
    add x2 -> x0, other arithmetic: 1.94 us -> none  [scatter_line(): total = total + arrived[level, last].astype(jnp.float32)]
  transfers between devices with their start and end apart: 36 -> 36, of which waited for: 17 -> 15; matrix products, arithmetic and copies ran while one was open for 6% -> 3% of each run, Pallas kernels for 18% -> 19%
where the time goes in v11:
time: 188 us
  waiting for transfers between devices  90.3 us (48%)
  starting transfers between devices  51.4 us (27%)
  Pallas kernels  36.5 us (19%)
  other arithmetic  6.4 us (3%)
  local copies, waits for them, and re-layouts  2.69 us (1%)
    ppermute x5, waiting for transfers between devices, first_hop(): return lax.ppermute(send, 'seq', hop_pairs(0, nseq))  73 us
    pallas_call x6, Pallas kernels, project(): pl.pallas_call(project_kernel, out_shape=jax.ShapeDtypeStruct((rows, coun...  26 us
    ppermute x22, starting transfers between devices, swap(): return lax.ppermute(x, axis, [(i, i ^ mask) for i in range(size)])  19 us
    ppermute x5, starting transfers between devices, first_hop(): return lax.ppermute(send, 'seq', hop_pairs(0, nseq))  18.8 us
    ppermute x22, waiting for transfers between devices, swap(): return lax.ppermute(x, axis, [(i, i ^ mask) for i in range(size)])  11.9 us
    ppermute x3, starting transfers between devices, sum_one_step(): lax.ppermute(x, axis, [(i, (i + k) % size) for i in range(size)])  8.12 us
    pallas_call x7, Pallas kernels, add_low_rank(): pl.pallas_call(functools.partial(low_rank_kernel, first, each, start, wid...  7.4 us
    ppermute x4, waiting for transfers between devices, scatter_line(): arrived[level, step] = lax.ppermute(send, 'seq', hop_pairs(level, nseq))  4.53 us
  transfers between devices with their start and end apart: 36, of which 15 were waited for; matrix products, arithmetic and copies ran while one was open for 3% of the time, Pallas kernels for 19%

profile of v11, /device:TPU:0, one launch (start us, length us, event | category | flops | bytes accessed | tf_op | source)
XLA Modules:
  0.0 187.9 jit_solution(9477312339558399263)
XLA Ops:
  0.0 0.9 slice.74.refs_0_
  0.9 3.0 %collective-permute-start.1 = (bf16[48,2048]{1,0:T(8,128)(2,1)S(1)}, bf16[48,2048]{1,0:T(8,128)(2,1)S(1)}, u32[]{:S(2)}, u32[]{:S(2)}) collective-permute-start(bf16[48,2048]{1,0:T(8,128)(2,1)S(1)} %slice.74.refs_0_), channel_id=1, source_target_pairs={{0,2},{1,3},{2,0},{3,1},{4,6},{5,7},{6,4},{7,5},{8,10},{9,11},{10,... | collective-permute-start | bytes 589832 | tf_op jit(solution)/shard_map/ppermute | solution.py:44
  3.9 1.5 collective-permute-start.3
  8.2 1.5 collective-permute-done.1.refs_2_
  9.7 4.8 %collective-permute-done.3.refs_4_ = bf16[48,2048]{1,0:T(8,128)(2,1)S(1)} collective-permute-done((bf16[48,2048]{1,0:T(8,128)(2,1)S(1)}, bf16[48,2048]{1,0:T(8,128)(2,1)S(1)}, u32[]{:S(2)}, u32[]{:S(2)}) %collective-permute-start.3) | collective-permute-done | bytes 196640 | tf_op jit(solution)/shard_map/ppermute | solution.py:44
  16.2 1.6 copy-done
  17.8 1.4 shard_map.82
  19.6 0.9 collective-permute-done.7
  20.6 1.0 collective-permute-start.8
  21.6 3.8 %shard_map.83.refs_0_ = bf16[384,768]{1,0:T(8,128)(2,1)S(1)} custom-call(bf16[384,2048]{1,0:T(8,128)(2,1)S(1)} %bitcast.95, bf16[2048,1792]{1,0:T(8,128)(2,1)} %weight_ref.10), custom_call_target="tpu_custom_call" | custom-call | flops 1207959552 | bytes 3145728 | tf_op jit(solution)/shard_map/pallas_call | solution.py:129
  25.4 1.2 collective-permute-start.9
  26.6 1.5 collective-permute-start.12
  28.6 1.5 collective-permute-start.14
  30.1 4.3 %shard_map.84.refs_1_ = bf16[384,1024]{1,0:T(8,128)(2,1)S(1)} custom-call(bf16[384,2048]{1,0:T(8,128)(2,1)S(1)} %bitcast.96, bf16[2048,1792]{1,0:T(8,128)(2,1)} %weight_ref.10), custom_call_target="tpu_custom_call" | custom-call | flops 1610612736 | bytes 4194304 | tf_op jit(solution)/shard_map/pallas_call | solution.py:129
  34.5 1.6 collective-permute-start.10
  36.1 2.0 %shard_map.85.refs_2_ = bf16[384,768]{1,0:T(8,128)(2,1)S(1)} custom-call(bf16[384,2048]{1,0:T(8,128)(2,1)S(1)} %bitcast.97, bf16[2048,1792]{1,0:T(8,128)(2,1)S(1)} %bitcast.90), custom_call_target="tpu_custom_call" | custom-call | flops 1207959552 | bytes 3145728 | tf_op jit(solution)/shard_map/pallas_call | solution.py:129
  38.6 2.7 %collective-permute-start.11 = (bf16[192,128]{1,0:T(8,128)(2,1)S(1)}, bf16[192,128]{1,0:T(8,128)(2,1)S(1)}, u32[]{:S(2)}, u32[]{:S(2)}) collective-permute-start(bf16[192,128]{1,0:T(8,128)(2,1)S(1)} %add_convert_fusion.9), channel_id=1, source_target_pairs={{0,16},{8,24},{16,0},{24,8},{1,17},{9,25},{17,1},{25,9},{2,18},{10... | collective-permute-start | bytes 147464 | tf_op jit(solution)/shard_map/ppermute | solution.py:44
  41.3 2.7 %shard_map.86.refs_3_ = bf16[384,1024]{1,0:T(8,128)(2,1)S(1)} custom-call(bf16[384,2048]{1,0:T(8,128)(2,1)S(1)} %bitcast.98, bf16[2048,1792]{1,0:T(8,128)(2,1)S(1)} %bitcast.90), custom_call_target="tpu_custom_call" | custom-call | flops 1610612736 | bytes 4194304 | tf_op jit(solution)/shard_map/pallas_call | solution.py:129
  44.1 1.0 shard_map.87
  46.2 3.5 %collective-permute-start.26 = (bf16[1,2,2,48,1792]{4,3,2,1,0:T(8,128)(2,1)S(1)}, bf16[1,2,2,48,1792]{4,3,2,1,0:T(8,128)(2,1)S(1)}, u32[]{:S(2)}, u32[]{:S(2)}) collective-permute-start(bf16[1,2,2,48,1792]{4,3,2,1,0:T(8,128)(2,1)S(1)} %shard_map.87), channel_id=1, source_target_pairs={{0,8},{24,16},{1,9},{25,17},{2,10},{26,18},{3,11},{27,19},{4,12},{... | collective-permute-start | bytes 2064392 | tf_op jit(solution)/shard_map/ppermute | solution.py:273
  49.7 1.6 shard_map.88
  51.4 1.3 collective-permute-done.19
  52.7 1.6 collective-permute-start.20
  54.3 1.4 shard_map.89
  55.7 1.6 collective-permute-done.20
  57.3 1.0 collective-permute-start.21
  58.3 6.2 %collective-permute-done.26 = bf16[1,2,2,48,1792]{4,3,2,1,0:T(8,128)(2,1)S(1)} collective-permute-done((bf16[1,2,2,48,1792]{4,3,2,1,0:T(8,128)(2,1)S(1)}, bf16[1,2,2,48,1792]{4,3,2,1,0:T(8,128)(2,1)S(1)}, u32[]{:S(2)}, u32[]{:S(2)}) %collective-permute-start.26) | collective-permute-done | bytes 688160 | tf_op jit(solution)/shard_map/ppermute | solution.py:273
  65.5 5.0 %collective-permute-start.23 = (bf16[320,128]{1,0:T(8,128)(2,1)S(1)}, bf16[320,128]{1,0:T(8,128)(2,1)S(1)}, u32[]{:S(2)}, u32[]{:S(2)}) collective-permute-start(bf16[320,128]{1,0:T(8,128)(2,1)S(1)} %add_convert_fusion.5), channel_id=1, source_target_pairs={{0,8},{8,16},{16,24},{24,0},{1,9},{9,17},{17,25},{25,1},{2,10},{10... | collective-permute-start | bytes 245768 | tf_op jit(solution)/shard_map/ppermute | solution.py:59
  70.8 2.8 %collective-permute-start.25 = (bf16[320,128]{1,0:T(8,128)(2,1)S(1)}, bf16[320,128]{1,0:T(8,128)(2,1)S(1)}, u32[]{:S(2)}, u32[]{:S(2)}) collective-permute-start(bf16[320,128]{1,0:T(8,128)(2,1)S(1)} %add_convert_fusion.5), channel_id=1, source_target_pairs={{0,24},{8,0},{16,8},{24,16},{1,25},{9,1},{17,9},{25,17},{2,26},{10... | collective-permute-start | bytes 245768 | tf_op jit(solution)/shard_map/ppermute | solution.py:59
  73.6 1.0 shard_map.90
  74.6 1.6 collective-permute-start.22
  76.3 6.6 %shard_map.91.refs_0_ = bf16[640,1792]{1,0:T(8,128)(2,1)S(1)} custom-call(bf16[640,2048]{1,0:T(8,128)(2,1)S(1)} %bitcast.99, bf16[2048,1792]{1,0:T(8,128)(2,1)S(1)} %bitcast.94), custom_call_target="tpu_custom_call" | custom-call | flops 68719476736 | bytes 7340032 | tf_op jit(solution)/shard_map/pallas_call | solution.py:129
  82.9 6.6 %shard_map.92.refs_1_ = bf16[640,1792]{1,0:T(8,128)(2,1)S(1)} custom-call(bf16[640,2048]{1,0:T(8,128)(2,1)S(1)} %bitcast.100, bf16[2048,1792]{1,0:T(8,128)(2,1)S(1)} %bitcast.92), custom_call_target="tpu_custom_call" | custom-call | flops 1024 | bytes 7340032 | tf_op jit(solution)/shard_map/pallas_call | solution.py:129
  90.4 1.0 shard_map.93
  91.5 1.0 shard_map.94
  92.5 1.0 shard_map.95
  93.6 1.0 shard_map.96
  94.6 10.4 %collective-permute-done.22 = bf16[2,2,2,48,1792]{4,3,2,1,0:T(8,128)(2,1)S(1)} collective-permute-done((bf16[2,2,2,48,1792]{4,3,2,1,0:T(8,128)(2,1)S(1)}, bf16[2,2,2,48,1792]{4,3,2,1,0:T(8,128)(2,1)S(1)}, u32[]{:S(2)}, u32[]{:S(2)}) %collective-permute-start.22) | collective-permute-done | bytes 1376288 | tf_op jit(solution)/shard_map/ppermute | solution.py:273
  105.0 4.4 %collective-permute-start.30 = (bf16[1,2,2,80,1792]{4,3,2,1,0:T(8,128)(2,1)S(1)}, bf16[1,2,2,80,1792]{4,3,2,1,0:T(8,128)(2,1)S(1)}, u32[]{:S(2)}, u32[]{:S(2)}) collective-permute-start(bf16[1,2,2,80,1792]{4,3,2,1,0:T(8,128)(2,1)S(1)} %shard_map.93), channel_id=1, source_target_pairs={{0,8},{24,16},{1,9},{25,17},{2,10},{26,18},{3,11},{27,19},{4,12},{... | collective-permute-start | bytes 3440648 | tf_op jit(solution)/shard_map/ppermute | solution.py:273
  110.4 3.1 %collective-permute-start.32 = (bf16[1,2,2,80,1792]{4,3,2,1,0:T(8,128)(2,1)S(1)}, bf16[1,2,2,80,1792]{4,3,2,1,0:T(8,128)(2,1)S(1)}, u32[]{:S(2)}, u32[]{:S(2)}) collective-permute-start(bf16[1,2,2,80,1792]{4,3,2,1,0:T(8,128)(2,1)S(1)} %shard_map.94), channel_id=1, source_target_pairs={{0,8},{24,16},{1,9},{25,17},{2,10},{26,18},{3,11},{27,19},{4,12},{... | collective-permute-start | bytes 3440648 | tf_op jit(solution)/shard_map/ppermute | solution.py:273
  113.5 21.6 %collective-permute-done.30 = bf16[1,2,2,80,1792]{4,3,2,1,0:T(8,128)(2,1)S(1)} collective-permute-done((bf16[1,2,2,80,1792]{4,3,2,1,0:T(8,128)(2,1)S(1)}, bf16[1,2,2,80,1792]{4,3,2,1,0:T(8,128)(2,1)S(1)}, u32[]{:S(2)}, u32[]{:S(2)}) %collective-permute-start.30) | collective-permute-done | bytes 1146912 | tf_op jit(solution)/shard_map/ppermute | solution.py:273
  136.3 1.3 collective-permute-start.29
  137.6 6.1 %collective-permute-start.31 = (bf16[1,2,2,80,1792]{4,3,2,1,0:T(8,128)(2,1)S(1)}, bf16[1,2,2,80,1792]{4,3,2,1,0:T(8,128)(2,1)S(1)}, u32[]{:S(2)}, u32[]{:S(2)}) collective-permute-start(bf16[1,2,2,80,1792]{4,3,2,1,0:T(8,128)(2,1)S(1)} %shard_map.95), channel_id=1, source_target_pairs={{0,8},{24,16},{1,9},{25,17},{2,10},{26,18},{3,11},{27,19},{4,12},{... | collective-permute-start | bytes 3440648 | tf_op jit(solution)/shard_map/ppermute | solution.py:273
  143.7 16.0 %collective-permute-done.32 = bf16[1,2,2,80,1792]{4,3,2,1,0:T(8,128)(2,1)S(1)} collective-permute-done((bf16[1,2,2,80,1792]{4,3,2,1,0:T(8,128)(2,1)S(1)}, bf16[1,2,2,80,1792]{4,3,2,1,0:T(8,128)(2,1)S(1)}, u32[]{:S(2)}, u32[]{:S(2)}) %collective-permute-start.32) | collective-permute-done | bytes 1146912 | tf_op jit(solution)/shard_map/ppermute | solution.py:273
  161.0 1.3 collective-permute-start.35
  162.8 18.8 %collective-permute-done.31 = bf16[1,2,2,80,1792]{4,3,2,1,0:T(8,128)(2,1)S(1)} collective-permute-done((bf16[1,2,2,80,1792]{4,3,2,1,0:T(8,128)(2,1)S(1)}, bf16[1,2,2,80,1792]{4,3,2,1,0:T(8,128)(2,1)S(1)}, u32[]{:S(2)}, u32[]{:S(2)}) %collective-permute-start.31) | collective-permute-done | bytes 1146912 | tf_op jit(solution)/shard_map/ppermute | solution.py:273
  181.6 4.5 %collective-permute-done.35 = bf16[2,2,80,1792]{3,2,1,0:T(8,128)(2,1)S(1)} collective-permute-done((bf16[2,2,80,1792]{3,2,1,0:T(8,128)(2,1)S(1)}, bf16[2,2,80,1792]{3,2,1,0:T(8,128)(2,1)S(1)}, u32[]{:S(2)}, u32[]{:S(2)}) %collective-permute-start.35) | collective-permute-done | bytes 1146912 | tf_op jit(solution)/shard_map/ppermute | solution.py:209
  186.9 1.0 pad_maximum_fusion
  (99 shorter events, 13.8 us)
Async XLA Ops:
  0.9 8.7 %collective-permute-start.1 = (bf16[48,2048]{1,0:T(8,128)(2,1)S(1)}, bf16[48,2048]{1,0:T(8,128)(2,1)S(1)}, u32[]{:S(2)}, u32[]{:S(2)}) collective-permute-start(bf16[48,2048]{1,0:T(8,128)(2,1)S(1)} %slice.74.refs_0_), channel_id=1, source_target_pairs={{0,2},{1,3},{2,0},{3,1},{4,6},{5,7},{6,4},{7,5},{8,10},{9,11},{10,... | collective-permute-start | bytes 589832 | tf_op jit(solution)/shard_map/ppermute | solution.py:44
  3.9 10.6 %collective-permute-start.3 = (bf16[48,2048]{1,0:T(8,128)(2,1)S(1)}, bf16[48,2048]{1,0:T(8,128)(2,1)S(1)}, u32[]{:S(2)}, u32[]{:S(2)}) collective-permute-start(bf16[48,2048]{1,0:T(8,128)(2,1)S(1)} %slice.74.refs_0_), channel_id=1, source_target_pairs={{0,4},{1,5},{2,6},{3,7},{4,0},{5,1},{6,2},{7,3},{8,12},{9,13},{10,... | collective-permute-start | bytes 589832 | tf_op jit(solution)/shard_map/ppermute | solution.py:44
  5.5 9.1 %collective-permute-start.5 = (bf16[48,2048]{1,0:T(8,128)(2,1)S(1)}, bf16[48,2048]{1,0:T(8,128)(2,1)S(1)}, u32[]{:S(2)}, u32[]{:S(2)}) collective-permute-start(bf16[48,2048]{1,0:T(8,128)(2,1)S(1)} %slice.74.refs_0_), channel_id=1, source_target_pairs={{0,6},{1,7},{2,4},{3,5},{4,2},{5,3},{6,0},{7,1},{8,14},{9,15},{10,... | collective-permute-start | bytes 589832 | tf_op jit(solution)/shard_map/ppermute | solution.py:44
  5.5 9.6 %collective-permute-start = (bf16[48,2048]{1,0:T(8,128)(2,1)S(1)}, bf16[48,2048]{1,0:T(8,128)(2,1)S(1)}, u32[]{:S(2)}, u32[]{:S(2)}) collective-permute-start(bf16[48,2048]{1,0:T(8,128)(2,1)S(1)} %slice.74.refs_0_), channel_id=1, source_target_pairs={{0,1},{1,0},{2,3},{3,2},{4,5},{5,4},{6,7},{7,6},{8,9},{9,8},{10,11... | collective-permute-start | bytes 589832 | tf_op jit(solution)/shard_map/ppermute | solution.py:44
  9.7 5.4 %collective-permute-start.2 = (bf16[48,2048]{1,0:T(8,128)(2,1)S(1)}, bf16[48,2048]{1,0:T(8,128)(2,1)S(1)}, u32[]{:S(2)}, u32[]{:S(2)}) collective-permute-start(bf16[48,2048]{1,0:T(8,128)(2,1)S(1)} %collective-permute-done.1.refs_2_), channel_id=1, source_target_pairs={{0,1},{1,0},{2,3},{3,2},{4,5},{5,4},{6,7},{7,6},{8,9},{9,8},{10,11... | collective-permute-start | bytes 589832 | tf_op jit(solution)/shard_map/ppermute | solution.py:44
  14.5 1.4 collective-permute-start.4
  14.5 1.7 collective-permute-start.6
  16.2 1.6 copy-start
  17.8 1.7 copy-start.2
  19.3 1.3 collective-permute-start.7
  20.6 4.8 %collective-permute-start.8 = (bf16[192,128]{1,0:T(8,128)(2,1)S(1)}, bf16[192,128]{1,0:T(8,128)(2,1)S(1)}, u32[]{:S(2)}, u32[]{:S(2)}) collective-permute-start(bf16[192,128]{1,0:T(8,128)(2,1)S(1)} %add_convert_fusion.12), channel_id=1, source_target_pairs={{0,2},{1,3},{2,0},{3,1},{4,6},{5,7},{6,4},{7,5},{8,10},{9,11},{10,... | collective-permute-start | bytes 147464 | tf_op jit(solution)/shard_map/ppermute | solution.py:44
  21.6 14.5 %slice-start.2 = ((s8[7340032]{0:T(1024)(128)(4,1)}), s8[4194304]{0:T(1024)(128)(4,1)S(1)}, s32[]{:S(2)}) async-start(s8[7340032]{0:T(1024)(128)(4,1)} %bitcast.89), calls=%async_computation.2 | async-start | bytes 8388608
  25.4 10.7 %slice-start.3 = ((s8[7340032]{0:T(1024)(128)(4,1)}), s8[3145728]{0:T(1024)(128)(4,1)S(1)}, s32[]{:S(2)}) async-start(s8[7340032]{0:T(1024)(128)(4,1)} %bitcast.89), calls=%async_computation.3 | async-start | bytes 6291456
  25.4 9.0 %collective-permute-start.9 = (bf16[192,128]{1,0:T(8,128)(2,1)S(1)}, bf16[192,128]{1,0:T(8,128)(2,1)S(1)}, u32[]{:S(2)}, u32[]{:S(2)}) collective-permute-start(bf16[192,128]{1,0:T(8,128)(2,1)S(1)} %add_convert_fusion.11), channel_id=1, source_target_pairs={{0,4},{1,5},{2,6},{3,7},{4,0},{5,1},{6,2},{7,3},{8,12},{9,13},{10,... | collective-permute-start | bytes 147464 | tf_op jit(solution)/shard_map/ppermute | solution.py:44
  26.6 18.5 %collective-permute-start.12 = (bf16[80,2048]{1,0:T(8,128)(2,1)S(1)}, bf16[80,2048]{1,0:T(8,128)(2,1)S(1)}, u32[]{:S(2)}, u32[]{:S(2)}) collective-permute-start(bf16[80,2048]{1,0:T(8,128)(2,1)S(1)} %slice.75.refs_0_), channel_id=1, source_target_pairs={{0,2},{1,3},{2,0},{3,1},{4,6},{5,7},{6,4},{7,5},{8,10},{9,11},{10,... | collective-permute-start | bytes 983048 | tf_op jit(solution)/shard_map/ppermute | solution.py:44
  28.1 17.0 %collective-permute-start.13 = (bf16[80,2048]{1,0:T(8,128)(2,1)S(1)}, bf16[80,2048]{1,0:T(8,128)(2,1)S(1)}, u32[]{:S(2)}, u32[]{:S(2)}) collective-permute-start(bf16[80,2048]{1,0:T(8,128)(2,1)S(1)} %slice.75.refs_0_), channel_id=1, source_target_pairs={{0,4},{1,5},{2,6},{3,7},{4,0},{5,1},{6,2},{7,3},{8,12},{9,13},{10,... | collective-permute-start | bytes 983048 | tf_op jit(solution)/shard_map/ppermute | solution.py:44
  28.6 16.5 %collective-permute-start.14 = (bf16[80,2048]{1,0:T(8,128)(2,1)S(1)}, bf16[80,2048]{1,0:T(8,128)(2,1)S(1)}, u32[]{:S(2)}, u32[]{:S(2)}) collective-permute-start(bf16[80,2048]{1,0:T(8,128)(2,1)S(1)} %slice.75.refs_0_), channel_id=1, source_target_pairs={{0,6},{1,7},{2,4},{3,5},{4,2},{5,3},{6,0},{7,1},{8,14},{9,15},{10,... | collective-permute-start | bytes 983048 | tf_op jit(solution)/shard_map/ppermute | solution.py:44
  34.5 4.2 %collective-permute-start.10 = (bf16[192,128]{1,0:T(8,128)(2,1)S(1)}, bf16[192,128]{1,0:T(8,128)(2,1)S(1)}, u32[]{:S(2)}, u32[]{:S(2)}) collective-permute-start(bf16[192,128]{1,0:T(8,128)(2,1)S(1)} %add_convert_fusion.10), channel_id=1, source_target_pairs={{0,8},{8,0},{16,24},{24,16},{1,9},{9,1},{17,25},{25,17},{2,10},{10... | collective-permute-start | bytes 147464 | tf_op jit(solution)/shard_map/ppermute | solution.py:44
  36.1 7.9 %slice-start = ((s8[7340032]{0:T(1024)(128)(4,1)}), s8[4194304]{0:T(1024)(128)(4,1)S(1)}, s32[]{:S(2)}) async-start(s8[7340032]{0:T(1024)(128)(4,1)} %bitcast.87), calls=%async_computation | async-start | bytes 8388608
  38.6 5.4 %slice-start.1 = ((s8[7340032]{0:T(1024)(128)(4,1)}), s8[3145728]{0:T(1024)(128)(4,1)S(1)}, s32[]{:S(2)}) async-start(s8[7340032]{0:T(1024)(128)(4,1)} %bitcast.87), calls=%async_computation.1 | async-start | bytes 6291456
  38.6 5.4 %collective-permute-start.11 = (bf16[192,128]{1,0:T(8,128)(2,1)S(1)}, bf16[192,128]{1,0:T(8,128)(2,1)S(1)}, u32[]{:S(2)}, u32[]{:S(2)}) collective-permute-start(bf16[192,128]{1,0:T(8,128)(2,1)S(1)} %add_convert_fusion.9), channel_id=1, source_target_pairs={{0,16},{8,24},{16,0},{24,8},{1,17},{9,25},{17,1},{25,9},{2,18},{10... | collective-permute-start | bytes 147464 | tf_op jit(solution)/shard_map/ppermute | solution.py:44
  44.1 5.7 %copy-start.1 = (bf16[8,64,2048]{2,1,0:T(8,128)(2,1)S(1)}, bf16[8,64,2048]{2,1,0:T(8,128)(2,1)}, u32[]{:S(2)}) copy-start(bf16[8,64,2048]{2,1,0:T(8,128)(2,1)} %refs_8_.3) | copy-start | bytes 6291460
  45.1 4.6 %collective-permute-start.15 = (bf16[80,2048]{1,0:T(8,128)(2,1)S(1)}, bf16[80,2048]{1,0:T(8,128)(2,1)S(1)}, u32[]{:S(2)}, u32[]{:S(2)}) collective-permute-start(bf16[80,2048]{1,0:T(8,128)(2,1)S(1)} %slice.75.refs_0_), channel_id=1, source_target_pairs={{0,1},{1,0},{2,3},{3,2},{4,5},{5,4},{6,7},{7,6},{8,9},{9,8},{10,11... | collective-permute-start | bytes 983048 | tf_op jit(solution)/shard_map/ppermute | solution.py:44
  45.2 4.5 %collective-permute-start.16 = (bf16[80,2048]{1,0:T(8,128)(2,1)S(1)}, bf16[80,2048]{1,0:T(8,128)(2,1)S(1)}, u32[]{:S(2)}, u32[]{:S(2)}) collective-permute-start(bf16[80,2048]{1,0:T(8,128)(2,1)S(1)} %collective-permute-done.12.refs_2_), channel_id=1, source_target_pairs={{0,1},{1,0},{2,3},{3,2},{4,5},{5,4},{6,7},{7,6},{8,9},{9,8},{10,11... | collective-permute-start | bytes 983048 | tf_op jit(solution)/shard_map/ppermute | solution.py:44
  45.7 4.1 %collective-permute-start.17 = (bf16[80,2048]{1,0:T(8,128)(2,1)S(1)}, bf16[80,2048]{1,0:T(8,128)(2,1)S(1)}, u32[]{:S(2)}, u32[]{:S(2)}) collective-permute-start(bf16[80,2048]{1,0:T(8,128)(2,1)S(1)} %collective-permute-done.13.refs_4_), channel_id=1, source_target_pairs={{0,1},{1,0},{2,3},{3,2},{4,5},{5,4},{6,7},{7,6},{8,9},{9,8},{10,11... | collective-permute-start | bytes 983048 | tf_op jit(solution)/shard_map/ppermute | solution.py:44
  45.7 4.0 %collective-permute-start.18 = (bf16[80,2048]{1,0:T(8,128)(2,1)S(1)}, bf16[80,2048]{1,0:T(8,128)(2,1)S(1)}, u32[]{:S(2)}, u32[]{:S(2)}) collective-permute-start(bf16[80,2048]{1,0:T(8,128)(2,1)S(1)} %collective-permute-done.14.refs_6_), channel_id=1, source_target_pairs={{0,1},{1,0},{2,3},{3,2},{4,5},{5,4},{6,7},{7,6},{8,9},{9,8},{10,11... | collective-permute-start | bytes 983048 | tf_op jit(solution)/shard_map/ppermute | solution.py:44
  46.2 18.4 %collective-permute-start.26 = (bf16[1,2,2,48,1792]{4,3,2,1,0:T(8,128)(2,1)S(1)}, bf16[1,2,2,48,1792]{4,3,2,1,0:T(8,128)(2,1)S(1)}, u32[]{:S(2)}, u32[]{:S(2)}) collective-permute-start(bf16[1,2,2,48,1792]{4,3,2,1,0:T(8,128)(2,1)S(1)} %shard_map.87), channel_id=1, source_target_pairs={{0,8},{24,16},{1,9},{25,17},{2,10},{26,18},{3,11},{27,19},{4,12},{... | collective-permute-start | bytes 2064392 | tf_op jit(solution)/shard_map/ppermute | solution.py:273
  51.4 1.3 collective-permute-start.19
  52.7 4.6 %collective-permute-start.20 = (bf16[320,128]{1,0:T(8,128)(2,1)S(1)}, bf16[320,128]{1,0:T(8,128)(2,1)S(1)}, u32[]{:S(2)}, u32[]{:S(2)}) collective-permute-start(bf16[320,128]{1,0:T(8,128)(2,1)S(1)} %add_convert_fusion.7), channel_id=1, source_target_pairs={{0,2},{1,3},{2,0},{3,1},{4,6},{5,7},{6,4},{7,5},{8,10},{9,11},{10,... | collective-permute-start | bytes 245768 | tf_op jit(solution)/shard_map/ppermute | solution.py:44
  57.3 8.1 %collective-permute-start.21 = (bf16[320,128]{1,0:T(8,128)(2,1)S(1)}, bf16[320,128]{1,0:T(8,128)(2,1)S(1)}, u32[]{:S(2)}, u32[]{:S(2)}) collective-permute-start(bf16[320,128]{1,0:T(8,128)(2,1)S(1)} %add_convert_fusion.6), channel_id=1, source_target_pairs={{0,4},{1,5},{2,6},{3,7},{4,0},{5,1},{6,2},{7,3},{8,12},{9,13},{10,... | collective-permute-start | bytes 245768 | tf_op jit(solution)/shard_map/ppermute | solution.py:44
  64.7 26.8 %collective-permute-start.27 = (bf16[2,2,48,1792]{3,2,1,0:T(8,128)(2,1)S(1)}, bf16[2,2,48,1792]{3,2,1,0:T(8,128)(2,1)S(1)}, u32[]{:S(2)}, u32[]{:S(2)}) collective-permute-start(bf16[2,2,48,1792]{3,2,1,0:T(8,128)(2,1)S(1)} %fusion.6), channel_id=1, source_target_pairs={{8,16},{16,8},{9,17},{17,9},{10,18},{18,10},{11,19},{19,11},{12,20... | collective-permute-start | bytes 2064392 | tf_op jit(solution)/shard_map/ppermute | solution.py:286
  65.4 10.8 %slice-start.6 = ((s8[7340032]{0:T(1024)(128)(4,1)}), s8[4194304]{0:T(1024)(128)(4,1)S(1)}, s32[]{:S(2)}) async-start(s8[7340032]{0:T(1024)(128)(4,1)} %bitcast.93), calls=%async_computation.6 | async-start | bytes 8388608
  65.5 10.8 %slice-start.7 = ((s8[7340032]{0:T(1024)(128)(4,1)}), s8[3145728]{0:T(1024)(128)(4,1)S(1)}, s32[]{:S(2)}) async-start(s8[7340032]{0:T(1024)(128)(4,1)} %bitcast.93), calls=%async_computation.7 | async-start | bytes 6291456
  65.5 24.0 %collective-permute-start.23 = (bf16[320,128]{1,0:T(8,128)(2,1)S(1)}, bf16[320,128]{1,0:T(8,128)(2,1)S(1)}, u32[]{:S(2)}, u32[]{:S(2)}) collective-permute-start(bf16[320,128]{1,0:T(8,128)(2,1)S(1)} %add_convert_fusion.5), channel_id=1, source_target_pairs={{0,8},{8,16},{16,24},{24,0},{1,9},{9,17},{17,25},{25,1},{2,10},{10... | collective-permute-start | bytes 245768 | tf_op jit(solution)/shard_map/ppermute | solution.py:59
  70.5 19.8 %collective-permute-start.24 = (bf16[320,128]{1,0:T(8,128)(2,1)S(1)}, bf16[320,128]{1,0:T(8,128)(2,1)S(1)}, u32[]{:S(2)}, u32[]{:S(2)}) collective-permute-start(bf16[320,128]{1,0:T(8,128)(2,1)S(1)} %add_convert_fusion.5), channel_id=1, source_target_pairs={{0,16},{8,24},{16,0},{24,8},{1,17},{9,25},{17,1},{25,9},{2,18},{10... | collective-permute-start | bytes 245768 | tf_op jit(solution)/shard_map/ppermute | solution.py:59
  70.8 19.6 %collective-permute-start.25 = (bf16[320,128]{1,0:T(8,128)(2,1)S(1)}, bf16[320,128]{1,0:T(8,128)(2,1)S(1)}, u32[]{:S(2)}, u32[]{:S(2)}) collective-permute-start(bf16[320,128]{1,0:T(8,128)(2,1)S(1)} %add_convert_fusion.5), channel_id=1, source_target_pairs={{0,24},{8,0},{16,8},{24,16},{1,25},{9,1},{17,9},{25,17},{2,26},{10... | collective-permute-start | bytes 245768 | tf_op jit(solution)/shard_map/ppermute | solution.py:59
  73.6 9.2 %slice-start.4 = ((s8[7340032]{0:T(1024)(128)(4,1)}), s8[4194304]{0:T(1024)(128)(4,1)S(1)}, s32[]{:S(2)}) async-start(s8[7340032]{0:T(1024)(128)(4,1)} %bitcast.91), calls=%async_computation.4 | async-start | bytes 8388608
  74.6 8.3 %slice-start.5 = ((s8[7340032]{0:T(1024)(128)(4,1)}), s8[3145728]{0:T(1024)(128)(4,1)S(1)}, s32[]{:S(2)}) async-start(s8[7340032]{0:T(1024)(128)(4,1)} %bitcast.91), calls=%async_computation.5 | async-start | bytes 6291456
  74.6 30.4 %collective-permute-start.22 = (bf16[2,2,2,48,1792]{4,3,2,1,0:T(8,128)(2,1)S(1)}, bf16[2,2,2,48,1792]{4,3,2,1,0:T(8,128)(2,1)S(1)}, u32[]{:S(2)}, u32[]{:S(2)}) collective-permute-start(bf16[2,2,2,48,1792]{4,3,2,1,0:T(8,128)(2,1)S(1)} %shard_map.89), channel_id=1, source_target_pairs={{0,8},{24,16},{1,9},{25,17},{2,10},{26,18},{3,11},{27,19},{4,12},{... | collective-permute-start | bytes 4128776 | tf_op jit(solution)/shard_map/ppermute | solution.py:273
  105.0 30.1 %collective-permute-start.30 = (bf16[1,2,2,80,1792]{4,3,2,1,0:T(8,128)(2,1)S(1)}, bf16[1,2,2,80,1792]{4,3,2,1,0:T(8,128)(2,1)S(1)}, u32[]{:S(2)}, u32[]{:S(2)}) collective-permute-start(bf16[1,2,2,80,1792]{4,3,2,1,0:T(8,128)(2,1)S(1)} %shard_map.93), channel_id=1, source_target_pairs={{0,8},{24,16},{1,9},{25,17},{2,10},{26,18},{3,11},{27,19},{4,12},{... | collective-permute-start | bytes 3440648 | tf_op jit(solution)/shard_map/ppermute | solution.py:273
  109.7 3.8 %collective-permute-start.28 = (bf16[2,2,48,1792]{3,2,1,0:T(8,128)(2,1)S(1)}, bf16[2,2,48,1792]{3,2,1,0:T(8,128)(2,1)S(1)}, u32[]{:S(2)}, u32[]{:S(2)}) collective-permute-start(bf16[2,2,48,1792]{3,2,1,0:T(8,128)(2,1)S(1)} %fusion.7), channel_id=1, source_target_pairs={{8,16},{16,8},{9,17},{17,9},{10,18},{18,10},{11,19},{19,11},{12,20... | collective-permute-start | bytes 2064392 | tf_op jit(solution)/shard_map/ppermute | solution.py:297
  110.4 49.3 %collective-permute-start.32 = (bf16[1,2,2,80,1792]{4,3,2,1,0:T(8,128)(2,1)S(1)}, bf16[1,2,2,80,1792]{4,3,2,1,0:T(8,128)(2,1)S(1)}, u32[]{:S(2)}, u32[]{:S(2)}) collective-permute-start(bf16[1,2,2,80,1792]{4,3,2,1,0:T(8,128)(2,1)S(1)} %shard_map.94), channel_id=1, source_target_pairs={{0,8},{24,16},{1,9},{25,17},{2,10},{26,18},{3,11},{27,19},{4,12},{... | collective-permute-start | bytes 3440648 | tf_op jit(solution)/shard_map/ppermute | solution.py:273
  135.4 25.3 %collective-permute-start.34 = (bf16[2,2,80,1792]{3,2,1,0:T(8,128)(2,1)S(1)}, bf16[2,2,80,1792]{3,2,1,0:T(8,128)(2,1)S(1)}, u32[]{:S(2)}, u32[]{:S(2)}) collective-permute-start(bf16[2,2,80,1792]{3,2,1,0:T(8,128)(2,1)S(1)} %fusion.3), channel_id=1, source_target_pairs={{8,16},{16,8},{9,17},{17,9},{10,18},{18,10},{11,19},{19,11},{12,20... | collective-permute-start | bytes 3440648 | tf_op jit(solution)/shard_map/ppermute | solution.py:209
  136.3 26.0 %collective-permute-start.29 = (bf16[2,2,48,1792]{3,2,1,0:T(8,128)(2,1)S(1)}, bf16[2,2,48,1792]{3,2,1,0:T(8,128)(2,1)S(1)}, u32[]{:S(2)}, u32[]{:S(2)}) collective-permute-start(bf16[2,2,48,1792]{3,2,1,0:T(8,128)(2,1)S(1)} %fusion.1), channel_id=1, source_target_pairs={{16,24},{8,0},{17,25},{9,1},{18,26},{10,2},{19,27},{11,3},{20,28},... | collective-permute-start | bytes 2064392 | tf_op jit(solution)/shard_map/ppermute | solution.py:209
  137.6 44.0 %collective-permute-start.31 = (bf16[1,2,2,80,1792]{4,3,2,1,0:T(8,128)(2,1)S(1)}, bf16[1,2,2,80,1792]{4,3,2,1,0:T(8,128)(2,1)S(1)}, u32[]{:S(2)}, u32[]{:S(2)}) collective-permute-start(bf16[1,2,2,80,1792]{4,3,2,1,0:T(8,128)(2,1)S(1)} %shard_map.95), channel_id=1, source_target_pairs={{0,8},{24,16},{1,9},{25,17},{2,10},{26,18},{3,11},{27,19},{4,12},{... | collective-permute-start | bytes 3440648 | tf_op jit(solution)/shard_map/ppermute | solution.py:273
  160.0 21.6 %collective-permute-start.33 = (bf16[2,2,80,1792]{3,2,1,0:T(8,128)(2,1)S(1)}, bf16[2,2,80,1792]{3,2,1,0:T(8,128)(2,1)S(1)}, u32[]{:S(2)}, u32[]{:S(2)}) collective-permute-start(bf16[2,2,80,1792]{3,2,1,0:T(8,128)(2,1)S(1)} %fusion.2), channel_id=1, source_target_pairs={{8,16},{16,8},{9,17},{17,9},{10,18},{18,10},{11,19},{19,11},{12,20... | collective-permute-start | bytes 3440648 | tf_op jit(solution)/shard_map/ppermute | solution.py:209
  161.0 25.1 %collective-permute-start.35 = (bf16[2,2,80,1792]{3,2,1,0:T(8,128)(2,1)S(1)}, bf16[2,2,80,1792]{3,2,1,0:T(8,128)(2,1)S(1)}, u32[]{:S(2)}, u32[]{:S(2)}) collective-permute-start(bf16[2,2,80,1792]{3,2,1,0:T(8,128)(2,1)S(1)} %fusion), channel_id=1, source_target_pairs={{16,24},{8,0},{17,25},{9,1},{18,26},{10,2},{19,27},{11,3},{20,28},... | collective-permute-start | bytes 3440648 | tf_op jit(solution)/shard_map/ppermute | solution.py:209

commit v12 on v11

--- a/solution.py
+++ b/solution.py
@@ -279,8 +279,8 @@
     steps, _ = sum_beside(mine.reshape(-1, mine.shape[2]), "tp", ntp, lambda gate: None)
     shared = steps[-1]
     rest = terms(parts, inner, 0, rows, 1, nseq - 2, mine)
-    kept = terms(parts, inner, 0, rows, nseq - 1, 1, (rest, shared))
-    rest_hop = first_hop(after(rest, kept))
+    kept = terms(parts, inner, 0, rows, nseq - 1, 1, rest)
+    rest_hop = first_hop(after(rest, shared))
     inner = sum_one_step(shared, "seq", nseq).reshape(mine.shape)
     second = add(head[0], after(head_hop, rest)[0])
     second_hop = lax.ppermute(second, "seq", hop_pairs(1, nseq))

time: 188 us -> 189 us (level)
  transfers between devices with their start and end apart: 36 -> 36, of which waited for: 15 -> 15; matrix products, arithmetic and copies ran while one was open for 3% -> 2% of each run, Pallas kernels for 19% -> 19%
where the time goes in v12:
time: 189 us; the launch traced here: 188 us
  waiting for transfers between devices  90.8 us (48%)
  starting transfers between devices  51.1 us (27%)
  Pallas kernels  36.5 us (19%)
  other arithmetic  6.4 us (3%)
  local copies, waits for them, and re-layouts  2.69 us (1%)
    ppermute x5, waiting for transfers between devices, first_hop(): return lax.ppermute(send, 'seq', hop_pairs(0, nseq))  73 us
    pallas_call x6, Pallas kernels, project(): pl.pallas_call(project_kernel, out_shape=jax.ShapeDtypeStruct((rows, coun...  26 us
    ppermute x22, starting transfers between devices, swap(): return lax.ppermute(x, axis, [(i, i ^ mask) for i in range(size)])  19 us
    ppermute x5, starting transfers between devices, first_hop(): return lax.ppermute(send, 'seq', hop_pairs(0, nseq))  18.6 us
    ppermute x22, waiting for transfers between devices, swap(): return lax.ppermute(x, axis, [(i, i ^ mask) for i in range(size)])  10.9 us
    ppermute x3, starting transfers between devices, sum_one_step(): lax.ppermute(x, axis, [(i, (i + k) % size) for i in range(size)])  8.12 us
    pallas_call x7, Pallas kernels, add_low_rank(): pl.pallas_call(functools.partial(low_rank_kernel, first, each, start, wid...  7.41 us
    ppermute x4, waiting for transfers between devices, scatter_line(): arrived[level, step] = lax.ppermute(send, 'seq', hop_pairs(level, nseq))  4.89 us
  transfers between devices with their start and end apart: 36, of which 15 were waited for; matrix products, arithmetic and copies ran while one was open for 2% of the time, Pallas kernels for 19%

profile of v12, /device:TPU:0, one launch (start us, length us, event | category | flops | bytes accessed | tf_op | source)
XLA Modules:
  0.0 188.2 jit_solution(9048300115347653374)
XLA Ops:
  0.0 0.9 slice.74.refs_0_
  0.9 3.0 %collective-permute-start.1 = (bf16[48,2048]{1,0:T(8,128)(2,1)S(1)}, bf16[48,2048]{1,0:T(8,128)(2,1)S(1)}, u32[]{:S(2)}, u32[]{:S(2)}) collective-permute-start(bf16[48,2048]{1,0:T(8,128)(2,1)S(1)} %slice.74.refs_0_), channel_id=1, source_target_pairs={{0,2},{1,3},{2,0},{3,1},{4,6},{5,7},{6,4},{7,5},{8,10},{9,11},{10,... | collective-permute-start | bytes 589832 | tf_op jit(solution)/shard_map/ppermute | solution.py:44
  3.9 1.5 collective-permute-start.3
  8.2 1.5 collective-permute-done.1.refs_2_
  9.7 4.8 %collective-permute-done.3.refs_4_ = bf16[48,2048]{1,0:T(8,128)(2,1)S(1)} collective-permute-done((bf16[48,2048]{1,0:T(8,128)(2,1)S(1)}, bf16[48,2048]{1,0:T(8,128)(2,1)S(1)}, u32[]{:S(2)}, u32[]{:S(2)}) %collective-permute-start.3) | collective-permute-done | bytes 196640 | tf_op jit(solution)/shard_map/ppermute | solution.py:44
  16.2 1.6 copy-done
  17.8 1.4 shard_map.82
  19.6 0.9 collective-permute-done.7
  20.6 1.0 collective-permute-start.8
  21.6 3.8 %shard_map.83.refs_0_ = bf16[384,768]{1,0:T(8,128)(2,1)S(1)} custom-call(bf16[384,2048]{1,0:T(8,128)(2,1)S(1)} %bitcast.95, bf16[2048,1792]{1,0:T(8,128)(2,1)} %weight_ref.10), custom_call_target="tpu_custom_call" | custom-call | flops 1207959552 | bytes 3145728 | tf_op jit(solution)/shard_map/pallas_call | solution.py:129
  25.4 1.2 collective-permute-start.9
  26.6 1.5 collective-permute-start.12
  28.6 1.5 collective-permute-start.14
  30.1 4.3 %shard_map.84.refs_1_ = bf16[384,1024]{1,0:T(8,128)(2,1)S(1)} custom-call(bf16[384,2048]{1,0:T(8,128)(2,1)S(1)} %bitcast.96, bf16[2048,1792]{1,0:T(8,128)(2,1)} %weight_ref.10), custom_call_target="tpu_custom_call" | custom-call | flops 1610612736 | bytes 4194304 | tf_op jit(solution)/shard_map/pallas_call | solution.py:129
  34.5 1.6 collective-permute-start.10
  36.1 2.0 %shard_map.85.refs_2_ = bf16[384,768]{1,0:T(8,128)(2,1)S(1)} custom-call(bf16[384,2048]{1,0:T(8,128)(2,1)S(1)} %bitcast.97, bf16[2048,1792]{1,0:T(8,128)(2,1)S(1)} %bitcast.90), custom_call_target="tpu_custom_call" | custom-call | flops 1207959552 | bytes 3145728 | tf_op jit(solution)/shard_map/pallas_call | solution.py:129
  38.6 2.7 %collective-permute-start.11 = (bf16[192,128]{1,0:T(8,128)(2,1)S(1)}, bf16[192,128]{1,0:T(8,128)(2,1)S(1)}, u32[]{:S(2)}, u32[]{:S(2)}) collective-permute-start(bf16[192,128]{1,0:T(8,128)(2,1)S(1)} %add_convert_fusion.9), channel_id=1, source_target_pairs={{0,16},{8,24},{16,0},{24,8},{1,17},{9,25},{17,1},{25,9},{2,18},{10... | collective-permute-start | bytes 147464 | tf_op jit(solution)/shard_map/ppermute | solution.py:44
  41.3 2.7 %shard_map.86.refs_3_ = bf16[384,1024]{1,0:T(8,128)(2,1)S(1)} custom-call(bf16[384,2048]{1,0:T(8,128)(2,1)S(1)} %bitcast.98, bf16[2048,1792]{1,0:T(8,128)(2,1)S(1)} %bitcast.90), custom_call_target="tpu_custom_call" | custom-call | flops 1610612736 | bytes 4194304 | tf_op jit(solution)/shard_map/pallas_call | solution.py:129
  44.1 1.0 shard_map.87
  46.2 3.5 %collective-permute-start.26 = (bf16[1,2,2,48,1792]{4,3,2,1,0:T(8,128)(2,1)S(1)}, bf16[1,2,2,48,1792]{4,3,2,1,0:T(8,128)(2,1)S(1)}, u32[]{:S(2)}, u32[]{:S(2)}) collective-permute-start(bf16[1,2,2,48,1792]{4,3,2,1,0:T(8,128)(2,1)S(1)} %shard_map.87), channel_id=1, source_target_pairs={{0,8},{24,16},{1,9},{25,17},{2,10},{26,18},{3,11},{27,19},{4,12},{... | collective-permute-start | bytes 2064392 | tf_op jit(solution)/shard_map/ppermute | solution.py:273
  49.7 1.6 shard_map.88
  51.4 1.3 collective-permute-done.19
  52.7 1.6 collective-permute-start.20
  54.3 1.4 shard_map.89
  55.7 1.0 shard_map.90
  57.3 1.0 collective-permute-start.21
  58.3 6.2 %collective-permute-done.26 = bf16[1,2,2,48,1792]{4,3,2,1,0:T(8,128)(2,1)S(1)} collective-permute-done((bf16[1,2,2,48,1792]{4,3,2,1,0:T(8,128)(2,1)S(1)}, bf16[1,2,2,48,1792]{4,3,2,1,0:T(8,128)(2,1)S(1)}, u32[]{:S(2)}, u32[]{:S(2)}) %collective-permute-start.26) | collective-permute-done | bytes 688160 | tf_op jit(solution)/shard_map/ppermute | solution.py:273
  65.5 5.0 %collective-permute-start.23 = (bf16[320,128]{1,0:T(8,128)(2,1)S(1)}, bf16[320,128]{1,0:T(8,128)(2,1)S(1)}, u32[]{:S(2)}, u32[]{:S(2)}) collective-permute-start(bf16[320,128]{1,0:T(8,128)(2,1)S(1)} %add_convert_fusion.5), channel_id=1, source_target_pairs={{0,8},{8,16},{16,24},{24,0},{1,9},{9,17},{17,25},{25,1},{2,10},{10... | collective-permute-start | bytes 245768 | tf_op jit(solution)/shard_map/ppermute | solution.py:59
  70.8 2.8 %collective-permute-start.25 = (bf16[320,128]{1,0:T(8,128)(2,1)S(1)}, bf16[320,128]{1,0:T(8,128)(2,1)S(1)}, u32[]{:S(2)}, u32[]{:S(2)}) collective-permute-start(bf16[320,128]{1,0:T(8,128)(2,1)S(1)} %add_convert_fusion.5), channel_id=1, source_target_pairs={{0,24},{8,0},{16,8},{24,16},{1,25},{9,1},{17,9},{25,17},{2,26},{10... | collective-permute-start | bytes 245768 | tf_op jit(solution)/shard_map/ppermute | solution.py:59
  73.6 1.4 collective-permute-start.22
  75.0 6.6 %shard_map.91.refs_0_ = bf16[640,1792]{1,0:T(8,128)(2,1)S(1)} custom-call(bf16[640,2048]{1,0:T(8,128)(2,1)S(1)} %bitcast.99, bf16[2048,1792]{1,0:T(8,128)(2,1)S(1)} %bitcast.94), custom_call_target="tpu_custom_call" | custom-call | flops 68719476736 | bytes 7340032 | tf_op jit(solution)/shard_map/pallas_call | solution.py:129
  81.7 6.6 %shard_map.92.refs_1_ = bf16[640,1792]{1,0:T(8,128)(2,1)S(1)} custom-call(bf16[640,2048]{1,0:T(8,128)(2,1)S(1)} %bitcast.100, bf16[2048,1792]{1,0:T(8,128)(2,1)S(1)} %bitcast.92), custom_call_target="tpu_custom_call" | custom-call | flops 1024 | bytes 7340032 | tf_op jit(solution)/shard_map/pallas_call | solution.py:129
  88.3 2.1 %collective-permute-done.24 = bf16[320,128]{1,0:T(8,128)(2,1)S(1)} collective-permute-done((bf16[320,128]{1,0:T(8,128)(2,1)S(1)}, bf16[320,128]{1,0:T(8,128)(2,1)S(1)}, u32[]{:S(2)}, u32[]{:S(2)}) %collective-permute-start.24) | collective-permute-done | bytes 81952 | tf_op jit(solution)/shard_map/ppermute | solution.py:59
  90.4 1.0 shard_map.93
  91.5 1.0 shard_map.94
  92.5 1.0 shard_map.95
  93.6 1.0 shard_map.96
  94.6 10.0 %collective-permute-done.22 = bf16[2,2,2,48,1792]{4,3,2,1,0:T(8,128)(2,1)S(1)} collective-permute-done((bf16[2,2,2,48,1792]{4,3,2,1,0:T(8,128)(2,1)S(1)}, bf16[2,2,2,48,1792]{4,3,2,1,0:T(8,128)(2,1)S(1)}, u32[]{:S(2)}, u32[]{:S(2)}) %collective-permute-start.22) | collective-permute-done | bytes 1376288 | tf_op jit(solution)/shard_map/ppermute | solution.py:273
  104.6 4.4 %collective-permute-start.30 = (bf16[1,2,2,80,1792]{4,3,2,1,0:T(8,128)(2,1)S(1)}, bf16[1,2,2,80,1792]{4,3,2,1,0:T(8,128)(2,1)S(1)}, u32[]{:S(2)}, u32[]{:S(2)}) collective-permute-start(bf16[1,2,2,80,1792]{4,3,2,1,0:T(8,128)(2,1)S(1)} %shard_map.93), channel_id=1, source_target_pairs={{0,8},{24,16},{1,9},{25,17},{2,10},{26,18},{3,11},{27,19},{4,12},{... | collective-permute-start | bytes 3440648 | tf_op jit(solution)/shard_map/ppermute | solution.py:273
  109.9 3.1 %collective-permute-start.32 = (bf16[1,2,2,80,1792]{4,3,2,1,0:T(8,128)(2,1)S(1)}, bf16[1,2,2,80,1792]{4,3,2,1,0:T(8,128)(2,1)S(1)}, u32[]{:S(2)}, u32[]{:S(2)}) collective-permute-start(bf16[1,2,2,80,1792]{4,3,2,1,0:T(8,128)(2,1)S(1)} %shard_map.94), channel_id=1, source_target_pairs={{0,8},{24,16},{1,9},{25,17},{2,10},{26,18},{3,11},{27,19},{4,12},{... | collective-permute-start | bytes 3440648 | tf_op jit(solution)/shard_map/ppermute | solution.py:273
  113.1 21.6 %collective-permute-done.30 = bf16[1,2,2,80,1792]{4,3,2,1,0:T(8,128)(2,1)S(1)} collective-permute-done((bf16[1,2,2,80,1792]{4,3,2,1,0:T(8,128)(2,1)S(1)}, bf16[1,2,2,80,1792]{4,3,2,1,0:T(8,128)(2,1)S(1)}, u32[]{:S(2)}, u32[]{:S(2)}) %collective-permute-start.30) | collective-permute-done | bytes 1146912 | tf_op jit(solution)/shard_map/ppermute | solution.py:273
  135.9 1.3 collective-permute-start.29
  137.2 6.1 %collective-permute-start.31 = (bf16[1,2,2,80,1792]{4,3,2,1,0:T(8,128)(2,1)S(1)}, bf16[1,2,2,80,1792]{4,3,2,1,0:T(8,128)(2,1)S(1)}, u32[]{:S(2)}, u32[]{:S(2)}) collective-permute-start(bf16[1,2,2,80,1792]{4,3,2,1,0:T(8,128)(2,1)S(1)} %shard_map.95), channel_id=1, source_target_pairs={{0,8},{24,16},{1,9},{25,17},{2,10},{26,18},{3,11},{27,19},{4,12},{... | collective-permute-start | bytes 3440648 | tf_op jit(solution)/shard_map/ppermute | solution.py:273
  143.3 16.0 %collective-permute-done.32 = bf16[1,2,2,80,1792]{4,3,2,1,0:T(8,128)(2,1)S(1)} collective-permute-done((bf16[1,2,2,80,1792]{4,3,2,1,0:T(8,128)(2,1)S(1)}, bf16[1,2,2,80,1792]{4,3,2,1,0:T(8,128)(2,1)S(1)}, u32[]{:S(2)}, u32[]{:S(2)}) %collective-permute-start.32) | collective-permute-done | bytes 1146912 | tf_op jit(solution)/shard_map/ppermute | solution.py:273
  160.6 1.3 collective-permute-start.35
  162.4 19.2 %collective-permute-done.31 = bf16[1,2,2,80,1792]{4,3,2,1,0:T(8,128)(2,1)S(1)} collective-permute-done((bf16[1,2,2,80,1792]{4,3,2,1,0:T(8,128)(2,1)S(1)}, bf16[1,2,2,80,1792]{4,3,2,1,0:T(8,128)(2,1)S(1)}, u32[]{:S(2)}, u32[]{:S(2)}) %collective-permute-start.31) | collective-permute-done | bytes 1146912 | tf_op jit(solution)/shard_map/ppermute | solution.py:273
  181.5 4.9 %collective-permute-done.35 = bf16[2,2,80,1792]{3,2,1,0:T(8,128)(2,1)S(1)} collective-permute-done((bf16[2,2,80,1792]{3,2,1,0:T(8,128)(2,1)S(1)}, bf16[2,2,80,1792]{3,2,1,0:T(8,128)(2,1)S(1)}, u32[]{:S(2)}, u32[]{:S(2)}) %collective-permute-start.35) | collective-permute-done | bytes 1146912 | tf_op jit(solution)/shard_map/ppermute | solution.py:209
  187.2 1.0 pad_maximum_fusion
  (99 shorter events, 13.5 us)
Async XLA Ops:
  0.9 8.7 %collective-permute-start.1 = (bf16[48,2048]{1,0:T(8,128)(2,1)S(1)}, bf16[48,2048]{1,0:T(8,128)(2,1)S(1)}, u32[]{:S(2)}, u32[]{:S(2)}) collective-permute-start(bf16[48,2048]{1,0:T(8,128)(2,1)S(1)} %slice.74.refs_0_), channel_id=1, source_target_pairs={{0,2},{1,3},{2,0},{3,1},{4,6},{5,7},{6,4},{7,5},{8,10},{9,11},{10,... | collective-permute-start | bytes 589832 | tf_op jit(solution)/shard_map/ppermute | solution.py:44
  3.9 10.6 %collective-permute-start.3 = (bf16[48,2048]{1,0:T(8,128)(2,1)S(1)}, bf16[48,2048]{1,0:T(8,128)(2,1)S(1)}, u32[]{:S(2)}, u32[]{:S(2)}) collective-permute-start(bf16[48,2048]{1,0:T(8,128)(2,1)S(1)} %slice.74.refs_0_), channel_id=1, source_target_pairs={{0,4},{1,5},{2,6},{3,7},{4,0},{5,1},{6,2},{7,3},{8,12},{9,13},{10,... | collective-permute-start | bytes 589832 | tf_op jit(solution)/shard_map/ppermute | solution.py:44
  5.5 9.1 %collective-permute-start.5 = (bf16[48,2048]{1,0:T(8,128)(2,1)S(1)}, bf16[48,2048]{1,0:T(8,128)(2,1)S(1)}, u32[]{:S(2)}, u32[]{:S(2)}) collective-permute-start(bf16[48,2048]{1,0:T(8,128)(2,1)S(1)} %slice.74.refs_0_), channel_id=1, source_target_pairs={{0,6},{1,7},{2,4},{3,5},{4,2},{5,3},{6,0},{7,1},{8,14},{9,15},{10,... | collective-permute-start | bytes 589832 | tf_op jit(solution)/shard_map/ppermute | solution.py:44
  5.5 9.6 %collective-permute-start = (bf16[48,2048]{1,0:T(8,128)(2,1)S(1)}, bf16[48,2048]{1,0:T(8,128)(2,1)S(1)}, u32[]{:S(2)}, u32[]{:S(2)}) collective-permute-start(bf16[48,2048]{1,0:T(8,128)(2,1)S(1)} %slice.74.refs_0_), channel_id=1, source_target_pairs={{0,1},{1,0},{2,3},{3,2},{4,5},{5,4},{6,7},{7,6},{8,9},{9,8},{10,11... | collective-permute-start | bytes 589832 | tf_op jit(solution)/shard_map/ppermute | solution.py:44
  9.7 5.4 %collective-permute-start.2 = (bf16[48,2048]{1,0:T(8,128)(2,1)S(1)}, bf16[48,2048]{1,0:T(8,128)(2,1)S(1)}, u32[]{:S(2)}, u32[]{:S(2)}) collective-permute-start(bf16[48,2048]{1,0:T(8,128)(2,1)S(1)} %collective-permute-done.1.refs_2_), channel_id=1, source_target_pairs={{0,1},{1,0},{2,3},{3,2},{4,5},{5,4},{6,7},{7,6},{8,9},{9,8},{10,11... | collective-permute-start | bytes 589832 | tf_op jit(solution)/shard_map/ppermute | solution.py:44
  14.5 1.4 collective-permute-start.4
  14.5 1.7 collective-permute-start.6
  16.2 1.6 copy-start
  17.8 1.7 copy-start.2
  19.3 1.3 collective-permute-start.7
  20.6 4.8 %collective-permute-start.8 = (bf16[192,128]{1,0:T(8,128)(2,1)S(1)}, bf16[192,128]{1,0:T(8,128)(2,1)S(1)}, u32[]{:S(2)}, u32[]{:S(2)}) collective-permute-start(bf16[192,128]{1,0:T(8,128)(2,1)S(1)} %add_convert_fusion.12), channel_id=1, source_target_pairs={{0,2},{1,3},{2,0},{3,1},{4,6},{5,7},{6,4},{7,5},{8,10},{9,11},{10,... | collective-permute-start | bytes 147464 | tf_op jit(solution)/shard_map/ppermute | solution.py:44
  21.6 14.5 %slice-start.2 = ((s8[7340032]{0:T(1024)(128)(4,1)}), s8[4194304]{0:T(1024)(128)(4,1)S(1)}, s32[]{:S(2)}) async-start(s8[7340032]{0:T(1024)(128)(4,1)} %bitcast.89), calls=%async_computation.2 | async-start | bytes 8388608
  25.4 10.7 %slice-start.3 = ((s8[7340032]{0:T(1024)(128)(4,1)}), s8[3145728]{0:T(1024)(128)(4,1)S(1)}, s32[]{:S(2)}) async-start(s8[7340032]{0:T(1024)(128)(4,1)} %bitcast.89), calls=%async_computation.3 | async-start | bytes 6291456
  25.4 9.0 %collective-permute-start.9 = (bf16[192,128]{1,0:T(8,128)(2,1)S(1)}, bf16[192,128]{1,0:T(8,128)(2,1)S(1)}, u32[]{:S(2)}, u32[]{:S(2)}) collective-permute-start(bf16[192,128]{1,0:T(8,128)(2,1)S(1)} %add_convert_fusion.11), channel_id=1, source_target_pairs={{0,4},{1,5},{2,6},{3,7},{4,0},{5,1},{6,2},{7,3},{8,12},{9,13},{10,... | collective-permute-start | bytes 147464 | tf_op jit(solution)/shard_map/ppermute | solution.py:44
  26.6 18.5 %collective-permute-start.12 = (bf16[80,2048]{1,0:T(8,128)(2,1)S(1)}, bf16[80,2048]{1,0:T(8,128)(2,1)S(1)}, u32[]{:S(2)}, u32[]{:S(2)}) collective-permute-start(bf16[80,2048]{1,0:T(8,128)(2,1)S(1)} %slice.75.refs_0_), channel_id=1, source_target_pairs={{0,2},{1,3},{2,0},{3,1},{4,6},{5,7},{6,4},{7,5},{8,10},{9,11},{10,... | collective-permute-start | bytes 983048 | tf_op jit(solution)/shard_map/ppermute | solution.py:44
  28.1 17.0 %collective-permute-start.13 = (bf16[80,2048]{1,0:T(8,128)(2,1)S(1)}, bf16[80,2048]{1,0:T(8,128)(2,1)S(1)}, u32[]{:S(2)}, u32[]{:S(2)}) collective-permute-start(bf16[80,2048]{1,0:T(8,128)(2,1)S(1)} %slice.75.refs_0_), channel_id=1, source_target_pairs={{0,4},{1,5},{2,6},{3,7},{4,0},{5,1},{6,2},{7,3},{8,12},{9,13},{10,... | collective-permute-start | bytes 983048 | tf_op jit(solution)/shard_map/ppermute | solution.py:44
  28.6 16.5 %collective-permute-start.14 = (bf16[80,2048]{1,0:T(8,128)(2,1)S(1)}, bf16[80,2048]{1,0:T(8,128)(2,1)S(1)}, u32[]{:S(2)}, u32[]{:S(2)}) collective-permute-start(bf16[80,2048]{1,0:T(8,128)(2,1)S(1)} %slice.75.refs_0_), channel_id=1, source_target_pairs={{0,6},{1,7},{2,4},{3,5},{4,2},{5,3},{6,0},{7,1},{8,14},{9,15},{10,... | collective-permute-start | bytes 983048 | tf_op jit(solution)/shard_map/ppermute | solution.py:44
  34.5 4.2 %collective-permute-start.10 = (bf16[192,128]{1,0:T(8,128)(2,1)S(1)}, bf16[192,128]{1,0:T(8,128)(2,1)S(1)}, u32[]{:S(2)}, u32[]{:S(2)}) collective-permute-start(bf16[192,128]{1,0:T(8,128)(2,1)S(1)} %add_convert_fusion.10), channel_id=1, source_target_pairs={{0,8},{8,0},{16,24},{24,16},{1,9},{9,1},{17,25},{25,17},{2,10},{10... | collective-permute-start | bytes 147464 | tf_op jit(solution)/shard_map/ppermute | solution.py:44
  36.1 7.9 %slice-start = ((s8[7340032]{0:T(1024)(128)(4,1)}), s8[4194304]{0:T(1024)(128)(4,1)S(1)}, s32[]{:S(2)}) async-start(s8[7340032]{0:T(1024)(128)(4,1)} %bitcast.87), calls=%async_computation | async-start | bytes 8388608
  38.6 5.4 %slice-start.1 = ((s8[7340032]{0:T(1024)(128)(4,1)}), s8[3145728]{0:T(1024)(128)(4,1)S(1)}, s32[]{:S(2)}) async-start(s8[7340032]{0:T(1024)(128)(4,1)} %bitcast.87), calls=%async_computation.1 | async-start | bytes 6291456
  38.6 5.4 %collective-permute-start.11 = (bf16[192,128]{1,0:T(8,128)(2,1)S(1)}, bf16[192,128]{1,0:T(8,128)(2,1)S(1)}, u32[]{:S(2)}, u32[]{:S(2)}) collective-permute-start(bf16[192,128]{1,0:T(8,128)(2,1)S(1)} %add_convert_fusion.9), channel_id=1, source_target_pairs={{0,16},{8,24},{16,0},{24,8},{1,17},{9,25},{17,1},{25,9},{2,18},{10... | collective-permute-start | bytes 147464 | tf_op jit(solution)/shard_map/ppermute | solution.py:44
  44.1 5.7 %copy-start.1 = (bf16[8,64,2048]{2,1,0:T(8,128)(2,1)S(1)}, bf16[8,64,2048]{2,1,0:T(8,128)(2,1)}, u32[]{:S(2)}) copy-start(bf16[8,64,2048]{2,1,0:T(8,128)(2,1)} %refs_8_.3) | copy-start | bytes 6291460
  45.1 4.6 %collective-permute-start.15 = (bf16[80,2048]{1,0:T(8,128)(2,1)S(1)}, bf16[80,2048]{1,0:T(8,128)(2,1)S(1)}, u32[]{:S(2)}, u32[]{:S(2)}) collective-permute-start(bf16[80,2048]{1,0:T(8,128)(2,1)S(1)} %slice.75.refs_0_), channel_id=1, source_target_pairs={{0,1},{1,0},{2,3},{3,2},{4,5},{5,4},{6,7},{7,6},{8,9},{9,8},{10,11... | collective-permute-start | bytes 983048 | tf_op jit(solution)/shard_map/ppermute | solution.py:44
  45.2 4.5 %collective-permute-start.16 = (bf16[80,2048]{1,0:T(8,128)(2,1)S(1)}, bf16[80,2048]{1,0:T(8,128)(2,1)S(1)}, u32[]{:S(2)}, u32[]{:S(2)}) collective-permute-start(bf16[80,2048]{1,0:T(8,128)(2,1)S(1)} %collective-permute-done.12.refs_2_), channel_id=1, source_target_pairs={{0,1},{1,0},{2,3},{3,2},{4,5},{5,4},{6,7},{7,6},{8,9},{9,8},{10,11... | collective-permute-start | bytes 983048 | tf_op jit(solution)/shard_map/ppermute | solution.py:44
  45.7 4.1 %collective-permute-start.17 = (bf16[80,2048]{1,0:T(8,128)(2,1)S(1)}, bf16[80,2048]{1,0:T(8,128)(2,1)S(1)}, u32[]{:S(2)}, u32[]{:S(2)}) collective-permute-start(bf16[80,2048]{1,0:T(8,128)(2,1)S(1)} %collective-permute-done.13.refs_4_), channel_id=1, source_target_pairs={{0,1},{1,0},{2,3},{3,2},{4,5},{5,4},{6,7},{7,6},{8,9},{9,8},{10,11... | collective-permute-start | bytes 983048 | tf_op jit(solution)/shard_map/ppermute | solution.py:44
  45.7 4.0 %collective-permute-start.18 = (bf16[80,2048]{1,0:T(8,128)(2,1)S(1)}, bf16[80,2048]{1,0:T(8,128)(2,1)S(1)}, u32[]{:S(2)}, u32[]{:S(2)}) collective-permute-start(bf16[80,2048]{1,0:T(8,128)(2,1)S(1)} %collective-permute-done.14.refs_6_), channel_id=1, source_target_pairs={{0,1},{1,0},{2,3},{3,2},{4,5},{5,4},{6,7},{7,6},{8,9},{9,8},{10,11... | collective-permute-start | bytes 983048 | tf_op jit(solution)/shard_map/ppermute | solution.py:44
  46.2 18.4 %collective-permute-start.26 = (bf16[1,2,2,48,1792]{4,3,2,1,0:T(8,128)(2,1)S(1)}, bf16[1,2,2,48,1792]{4,3,2,1,0:T(8,128)(2,1)S(1)}, u32[]{:S(2)}, u32[]{:S(2)}) collective-permute-start(bf16[1,2,2,48,1792]{4,3,2,1,0:T(8,128)(2,1)S(1)} %shard_map.87), channel_id=1, source_target_pairs={{0,8},{24,16},{1,9},{25,17},{2,10},{26,18},{3,11},{27,19},{4,12},{... | collective-permute-start | bytes 2064392 | tf_op jit(solution)/shard_map/ppermute | solution.py:273
  51.4 1.3 collective-permute-start.19
  52.7 4.6 %collective-permute-start.20 = (bf16[320,128]{1,0:T(8,128)(2,1)S(1)}, bf16[320,128]{1,0:T(8,128)(2,1)S(1)}, u32[]{:S(2)}, u32[]{:S(2)}) collective-permute-start(bf16[320,128]{1,0:T(8,128)(2,1)S(1)} %add_convert_fusion.7), channel_id=1, source_target_pairs={{0,2},{1,3},{2,0},{3,1},{4,6},{5,7},{6,4},{7,5},{8,10},{9,11},{10,... | collective-permute-start | bytes 245768 | tf_op jit(solution)/shard_map/ppermute | solution.py:44
  54.3 20.7 %slice-start.6 = ((s8[7340032]{0:T(1024)(128)(4,1)}), s8[4194304]{0:T(1024)(128)(4,1)S(1)}, s32[]{:S(2)}) async-start(s8[7340032]{0:T(1024)(128)(4,1)} %bitcast.93), calls=%async_computation.6 | async-start | bytes 8388608
  55.7 19.3 %slice-start.7 = ((s8[7340032]{0:T(1024)(128)(4,1)}), s8[3145728]{0:T(1024)(128)(4,1)S(1)}, s32[]{:S(2)}) async-start(s8[7340032]{0:T(1024)(128)(4,1)} %bitcast.93), calls=%async_computation.7 | async-start | bytes 6291456
  55.7 25.9 %slice-start.4 = ((s8[7340032]{0:T(1024)(128)(4,1)}), s8[4194304]{0:T(1024)(128)(4,1)S(1)}, s32[]{:S(2)}) async-start(s8[7340032]{0:T(1024)(128)(4,1)} %bitcast.91), calls=%async_computation.4 | async-start | bytes 8388608
  57.3 8.1 %collective-permute-start.21 = (bf16[320,128]{1,0:T(8,128)(2,1)S(1)}, bf16[320,128]{1,0:T(8,128)(2,1)S(1)}, u32[]{:S(2)}, u32[]{:S(2)}) collective-permute-start(bf16[320,128]{1,0:T(8,128)(2,1)S(1)} %add_convert_fusion.6), channel_id=1, source_target_pairs={{0,4},{1,5},{2,6},{3,7},{4,0},{5,1},{6,2},{7,3},{8,12},{9,13},{10,... | collective-permute-start | bytes 245768 | tf_op jit(solution)/shard_map/ppermute | solution.py:44
  64.7 26.8 %collective-permute-start.27 = (bf16[2,2,48,1792]{3,2,1,0:T(8,128)(2,1)S(1)}, bf16[2,2,48,1792]{3,2,1,0:T(8,128)(2,1)S(1)}, u32[]{:S(2)}, u32[]{:S(2)}) collective-permute-start(bf16[2,2,48,1792]{3,2,1,0:T(8,128)(2,1)S(1)} %fusion.6), channel_id=1, source_target_pairs={{8,16},{16,8},{9,17},{17,9},{10,18},{18,10},{11,19},{19,11},{12,20... | collective-permute-start | bytes 2064392 | tf_op jit(solution)/shard_map/ppermute | solution.py:286
  65.5 16.2 %slice-start.5 = ((s8[7340032]{0:T(1024)(128)(4,1)}), s8[3145728]{0:T(1024)(128)(4,1)S(1)}, s32[]{:S(2)}) async-start(s8[7340032]{0:T(1024)(128)(4,1)} %bitcast.91), calls=%async_computation.5 | async-start | bytes 6291456
  65.5 22.8 %collective-permute-start.23 = (bf16[320,128]{1,0:T(8,128)(2,1)S(1)}, bf16[320,128]{1,0:T(8,128)(2,1)S(1)}, u32[]{:S(2)}, u32[]{:S(2)}) collective-permute-start(bf16[320,128]{1,0:T(8,128)(2,1)S(1)} %add_convert_fusion.5), channel_id=1, source_target_pairs={{0,8},{8,16},{16,24},{24,0},{1,9},{9,17},{17,25},{25,1},{2,10},{10... | collective-permute-start | bytes 245768 | tf_op jit(solution)/shard_map/ppermute | solution.py:59
  70.5 19.9 %collective-permute-start.24 = (bf16[320,128]{1,0:T(8,128)(2,1)S(1)}, bf16[320,128]{1,0:T(8,128)(2,1)S(1)}, u32[]{:S(2)}, u32[]{:S(2)}) collective-permute-start(bf16[320,128]{1,0:T(8,128)(2,1)S(1)} %add_convert_fusion.5), channel_id=1, source_target_pairs={{0,16},{8,24},{16,0},{24,8},{1,17},{9,25},{17,1},{25,9},{2,18},{10... | collective-permute-start | bytes 245768 | tf_op jit(solution)/shard_map/ppermute | solution.py:59
  70.8 19.6 %collective-permute-start.25 = (bf16[320,128]{1,0:T(8,128)(2,1)S(1)}, bf16[320,128]{1,0:T(8,128)(2,1)S(1)}, u32[]{:S(2)}, u32[]{:S(2)}) collective-permute-start(bf16[320,128]{1,0:T(8,128)(2,1)S(1)} %add_convert_fusion.5), channel_id=1, source_target_pairs={{0,24},{8,0},{16,8},{24,16},{1,25},{9,1},{17,9},{25,17},{2,26},{10... | collective-permute-start | bytes 245768 | tf_op jit(solution)/shard_map/ppermute | solution.py:59
  73.6 31.0 %collective-permute-start.22 = (bf16[2,2,2,48,1792]{4,3,2,1,0:T(8,128)(2,1)S(1)}, bf16[2,2,2,48,1792]{4,3,2,1,0:T(8,128)(2,1)S(1)}, u32[]{:S(2)}, u32[]{:S(2)}) collective-permute-start(bf16[2,2,2,48,1792]{4,3,2,1,0:T(8,128)(2,1)S(1)} %shard_map.89), channel_id=1, source_target_pairs={{0,8},{24,16},{1,9},{25,17},{2,10},{26,18},{3,11},{27,19},{4,12},{... | collective-permute-start | bytes 4128776 | tf_op jit(solution)/shard_map/ppermute | solution.py:273
  104.6 30.1 %collective-permute-start.30 = (bf16[1,2,2,80,1792]{4,3,2,1,0:T(8,128)(2,1)S(1)}, bf16[1,2,2,80,1792]{4,3,2,1,0:T(8,128)(2,1)S(1)}, u32[]{:S(2)}, u32[]{:S(2)}) collective-permute-start(bf16[1,2,2,80,1792]{4,3,2,1,0:T(8,128)(2,1)S(1)} %shard_map.93), channel_id=1, source_target_pairs={{0,8},{24,16},{1,9},{25,17},{2,10},{26,18},{3,11},{27,19},{4,12},{... | collective-permute-start | bytes 3440648 | tf_op jit(solution)/shard_map/ppermute | solution.py:273
  109.2 3.8 %collective-permute-start.28 = (bf16[2,2,48,1792]{3,2,1,0:T(8,128)(2,1)S(1)}, bf16[2,2,48,1792]{3,2,1,0:T(8,128)(2,1)S(1)}, u32[]{:S(2)}, u32[]{:S(2)}) collective-permute-start(bf16[2,2,48,1792]{3,2,1,0:T(8,128)(2,1)S(1)} %fusion.7), channel_id=1, source_target_pairs={{8,16},{16,8},{9,17},{17,9},{10,18},{18,10},{11,19},{19,11},{12,20... | collective-permute-start | bytes 2064392 | tf_op jit(solution)/shard_map/ppermute | solution.py:297
  109.9 49.3 %collective-permute-start.32 = (bf16[1,2,2,80,1792]{4,3,2,1,0:T(8,128)(2,1)S(1)}, bf16[1,2,2,80,1792]{4,3,2,1,0:T(8,128)(2,1)S(1)}, u32[]{:S(2)}, u32[]{:S(2)}) collective-permute-start(bf16[1,2,2,80,1792]{4,3,2,1,0:T(8,128)(2,1)S(1)} %shard_map.94), channel_id=1, source_target_pairs={{0,8},{24,16},{1,9},{25,17},{2,10},{26,18},{3,11},{27,19},{4,12},{... | collective-permute-start | bytes 3440648 | tf_op jit(solution)/shard_map/ppermute | solution.py:273
  135.0 25.3 %collective-permute-start.34 = (bf16[2,2,80,1792]{3,2,1,0:T(8,128)(2,1)S(1)}, bf16[2,2,80,1792]{3,2,1,0:T(8,128)(2,1)S(1)}, u32[]{:S(2)}, u32[]{:S(2)}) collective-permute-start(bf16[2,2,80,1792]{3,2,1,0:T(8,128)(2,1)S(1)} %fusion.3), channel_id=1, source_target_pairs={{8,16},{16,8},{9,17},{17,9},{10,18},{18,10},{11,19},{19,11},{12,20... | collective-permute-start | bytes 3440648 | tf_op jit(solution)/shard_map/ppermute | solution.py:209
  135.9 26.0 %collective-permute-start.29 = (bf16[2,2,48,1792]{3,2,1,0:T(8,128)(2,1)S(1)}, bf16[2,2,48,1792]{3,2,1,0:T(8,128)(2,1)S(1)}, u32[]{:S(2)}, u32[]{:S(2)}) collective-permute-start(bf16[2,2,48,1792]{3,2,1,0:T(8,128)(2,1)S(1)} %fusion.1), channel_id=1, source_target_pairs={{16,24},{8,0},{17,25},{9,1},{18,26},{10,2},{19,27},{11,3},{20,28},... | collective-permute-start | bytes 2064392 | tf_op jit(solution)/shard_map/ppermute | solution.py:209
  137.2 44.3 %collective-permute-start.31 = (bf16[1,2,2,80,1792]{4,3,2,1,0:T(8,128)(2,1)S(1)}, bf16[1,2,2,80,1792]{4,3,2,1,0:T(8,128)(2,1)S(1)}, u32[]{:S(2)}, u32[]{:S(2)}) collective-permute-start(bf16[1,2,2,80,1792]{4,3,2,1,0:T(8,128)(2,1)S(1)} %shard_map.95), channel_id=1, source_target_pairs={{0,8},{24,16},{1,9},{25,17},{2,10},{26,18},{3,11},{27,19},{4,12},{... | collective-permute-start | bytes 3440648 | tf_op jit(solution)/shard_map/ppermute | solution.py:273
  159.5 22.0 %collective-permute-start.33 = (bf16[2,2,80,1792]{3,2,1,0:T(8,128)(2,1)S(1)}, bf16[2,2,80,1792]{3,2,1,0:T(8,128)(2,1)S(1)}, u32[]{:S(2)}, u32[]{:S(2)}) collective-permute-start(bf16[2,2,80,1792]{3,2,1,0:T(8,128)(2,1)S(1)} %fusion.2), channel_id=1, source_target_pairs={{8,16},{16,8},{9,17},{17,9},{10,18},{18,10},{11,19},{19,11},{12,20... | collective-permute-start | bytes 3440648 | tf_op jit(solution)/shard_map/ppermute | solution.py:209
  160.6 25.8 %collective-permute-start.35 = (bf16[2,2,80,1792]{3,2,1,0:T(8,128)(2,1)S(1)}, bf16[2,2,80,1792]{3,2,1,0:T(8,128)(2,1)S(1)}, u32[]{:S(2)}, u32[]{:S(2)}) collective-permute-start(bf16[2,2,80,1792]{3,2,1,0:T(8,128)(2,1)S(1)} %fusion), channel_id=1, source_target_pairs={{16,24},{8,0},{17,25},{9,1},{18,26},{10,2},{19,27},{11,3},{20,28},... | collective-permute-start | bytes 3440648 | tf_op jit(solution)/shard_map/ppermute | solution.py:209
